TPU v7x, 128 devices: a whole 4x4x4 slice. The times are simulated.
128 devices in a mesh: row: 16 (over z, x_lo, core), col: 8 (over x_hi, y).
Axes of the slice: x: 4 (x_hi: 2, x_lo: 2; x = x_hi * 2 + x_lo), y: 4, z: 4, core: 2. Of those that a mesh axis runs over, the one named last changes fastest.
Arguments:
- tokens: bfloat16 [384, 8192], P(None, 'row'), may hold values from -6 to 6
- grad_out: bfloat16 [384, 8192], P(None, 'row'), may hold values from -6 to 6
- gate_weight: bfloat16 [8192, 22016], P('row', 'col'), may hold values from -0.0625 to 0.0625
- up_weight: bfloat16 [8192, 22016], P('row', 'col'), may hold values from -0.0625 to 0.0625
- down_weight: bfloat16 [8192, 22016], P('row', 'col'), may hold values from -0.0390625 to 0.0390625
- gate_left: bfloat16 [8192, 128], P('row', 'col'), may hold values from -0.01953125 to 0.01953125
- up_left: bfloat16 [8192, 128], P('row', 'col'), may hold values from -0.01953125 to 0.01953125
- down_left: bfloat16 [8192, 128], P('row', 'col'), may hold values from -0.01171875 to 0.01171875
- gate_right: bfloat16 [128, 22016], P('row', 'col'), may hold values from -0.5 to 0.5
- up_right: bfloat16 [128, 22016], P('row', 'col'), may hold values from -0.5 to 0.5
- down_right: bfloat16 [128, 22016], P('row', 'col'), may hold values from -0.5 to 0.5
Outputs:
- mixed: bfloat16 [384, 8192], P('col', 'row')
- input_grad: bfloat16 [384, 8192], P('col', 'row')
- gate_grad: bfloat16 [8192, 22016], P('row', 'col')
- up_grad: bfloat16 [8192, 22016], P('row', 'col')
- down_grad: bfloat16 [8192, 22016], P('row', 'col')
All inputs are finite; a program needn't handle non-finite values.
Results may differ from a plain program's by a relative error of at most 0.0072.
Values may be sent and summed in bfloat16 or wider, within the bound.
No kernel may reach another device: no remote copies, remote signals or barrier semaphores. Data moves between devices by JAX's collectives and lax.ppermute only.
A program may use at most 128 MiB of HBM per device.

v0:
```python
import jax
import jax.numpy as jnp
from jax import lax
from jax.sharding import PartitionSpec as P

LAST_DIMS = (((1,), (1,)), ((), ()))
FIRST_DIMS = (((0,), (0,)), ((), ()))


def turned_gather(arrays, axis, dims):
    turned = [jnp.moveaxis(a, dim, 0) for a, dim in zip(arrays, dims)]
    widths = [t[0].size for t in turned]
    both = jnp.concatenate([t.reshape(-1, w) for t, w in zip(turned, widths)], axis=1)
    result = lax.all_gather(both, axis, axis=0, tiled=True)
    tiles = jnp.split(result, [sum(widths[:k]) for k in range(1, len(widths))], axis=1)
    return tuple(
        (
            jnp.moveaxis(b.reshape(-1, *t.shape[1:]), 0, dim)
            for b, t, dim in zip(tiles, turned, dims)
        )
    )


def side_by_side(arrays, axis, dim, along):
    both = jnp.concatenate(arrays, axis=along)
    result, at, gathered = (lax.all_gather(both, axis, axis=dim, tiled=True), 0, [])
    for a in arrays:
        gathered.append(lax.slice_in_dim(result, at, at + a.shape[along], axis=along))
        at += a.shape[along]
    return tuple(gathered)


def cut_along(value, dim, size):
    lengths = value.shape
    tiles = value.reshape(*lengths[:dim], size, lengths[dim] // size, *lengths[dim + 1 :])
    return jnp.moveaxis(tiles, dim, 0)


def sum_at_owner(value, axis, dim):
    size = lax.axis_size(axis)
    tiles = lax.all_to_all(cut_along(value, dim, size), axis, 0, 0, tiled=True)
    return jnp.sum(tiles, axis=0)


def merge_weight(base, left, right):
    delta = jnp.dot(left, right, preferred_element_type=jnp.float32)
    return (base.astype(jnp.float32) + delta).astype(jnp.bfloat16)


def activate(gate, up):
    return (gate * jax.nn.sigmoid(gate) * up).astype(jnp.bfloat16)


def derive(gate, up, back):
    sigma = jax.nn.sigmoid(gate)
    gate_delta = (back * up * sigma * (1.0 + gate * (1.0 - sigma))).astype(jnp.bfloat16)
    up_delta = (back * gate * sigma).astype(jnp.bfloat16)
    return (gate_delta, up_delta)


def shards(
    tokens,
    grad_out,
    gate_weight,
    up_weight,
    down_weight,
    gate_left,
    up_left,
    down_left,
    gate_right,
    up_right,
    down_right,
):
    lefts = turned_gather((gate_left, up_left, down_left), "col", (1, 1, 1))
    rights = side_by_side((gate_right, up_right, down_right), "row", 0, 1)
    merged_gate = merge_weight(gate_weight, lefts[0], rights[0])
    merged_up = merge_weight(up_weight, lefts[1], rights[1])
    merged_down = merge_weight(down_weight, lefts[2], rights[2])
    gate_part = jnp.dot(tokens, merged_gate, preferred_element_type=jnp.float32)
    up_part = jnp.dot(tokens, merged_up, preferred_element_type=jnp.float32)
    gate_rows, up_rows = (
        lax.psum_scatter(gate_part, "row", scatter_dimension=0, tiled=True),
        lax.psum_scatter(up_part, "row", scatter_dimension=0, tiled=True),
    )
    hidden = lax.all_gather(activate(gate_rows, up_rows), "row", axis=0, tiled=True)
    mixed = sum_at_owner(
        lax.dot_general(hidden, merged_down, LAST_DIMS, preferred_element_type=jnp.float32),
        "col",
        0,
    ).astype(jnp.bfloat16)
    back_part = jnp.dot(grad_out, merged_down, preferred_element_type=jnp.float32)
    back_block = lax.psum_scatter(back_part, "row", scatter_dimension=0, tiled=True)
    gate_block, up_block = derive(gate_rows, up_rows, back_block)
    gate_delta, up_delta = side_by_side((gate_block, up_block), "row", 0, 1)
    total = lax.dot_general(gate_delta, merged_gate, LAST_DIMS, preferred_element_type=jnp.float32)
    input_grad = sum_at_owner(
        total + lax.dot_general(up_delta, merged_up, LAST_DIMS, preferred_element_type=jnp.float32),
        "col",
        0,
    ).astype(jnp.bfloat16)
    gate_grad = lax.dot_general(
        tokens, gate_delta, FIRST_DIMS, preferred_element_type=jnp.float32
    ).astype(jnp.bfloat16)
    up_grad = lax.dot_general(
        tokens, up_delta, FIRST_DIMS, preferred_element_type=jnp.float32
    ).astype(jnp.bfloat16)
    down_grad = lax.dot_general(
        grad_out, hidden, FIRST_DIMS, preferred_element_type=jnp.float32
    ).astype(jnp.bfloat16)
    return (mixed, input_grad, gate_grad, up_grad, down_grad)


def solution(mesh):
    in_specs = (
        P(None, "row"),
        P(None, "row"),
        P("row", "col"),
        P("row", "col"),
        P("row", "col"),
        P("row", "col"),
        P("row", "col"),
        P("row", "col"),
        P("row", "col"),
        P("row", "col"),
        P("row", "col"),
    )
    out_specs = (
        P("col", "row"),
        P("col", "row"),
        P("row", "col"),
        P("row", "col"),
        P("row", "col"),
    )
    return jax.shard_map(shards, mesh=mesh, in_specs=in_specs, out_specs=out_specs, check_vma=False)
```

profile of v0, /device:TPU:0, one launch (start us, length us, event | category | flops | bytes accessed | tf_op | source)
XLA Modules:
  0.0 389.9 jit_solution(16315347881451261901)
XLA Ops:
  7.2 0.0 copy-start
  7.2 0.0 all-gather.4.cloned.1.call-start
  7.2 1.6 concatenate.10
  8.9 0.0 all-gather.4.cloned.1.call-update
  8.9 0.0 reduce-scatter.10.cloned.1.call-start
  8.9 0.8 pad_maximum_fusion.1
  9.7 37.8 %all_gather.12 = bf16[128,1536]{1,0:T(8,128)(2,1)} all-gather(bf16[16,1536]{1,0:T(8,128)(2,1)S(1)} %pad_maximum_fusion.1), channel_id=1, replica_groups=mesh['row'=16,'col'=8] {'col'}, dimensions={0}, use_global_device_ids=true | all-gather | bytes 442368 | tf_op jit(solution)/shard_map/all_gather | solution.py:14
  47.5 3.0 add_convert_fusion.2
  50.5 3.7 convolution_bitcast_fusion.2
  54.2 5.7 %copy.27 = f32[384,2752]{1,0:T(8,128)} copy(f32[384,2752]{0,1:T(8,128)} %convolution_bitcast_fusion.2) | data formatting | bytes 8454144
  59.9 0.0 reduce-scatter.10.cloned.1.call-update
  59.9 0.0 reduce-scatter.12.cloned.1.call-start
  60.0 3.4 add_convert_fusion.1
  63.4 0.0 copy-start.1
  63.4 1.5 copy-done.1
  65.0 3.7 convolution_bitcast_fusion.1
  68.7 5.9 %copy.29 = f32[384,2752]{1,0:T(8,128)} copy(f32[384,2752]{0,1:T(8,128)} %convolution_bitcast_fusion.1) | data formatting | bytes 8454144
  74.6 0.0 reduce-scatter.12.cloned.1.call-update
  74.7 0.0 reduce-scatter.14.cloned.1.call-start
  74.7 0.0 copy-start.3
  74.7 3.1 add_convert_fusion
  77.8 1.5 copy-done.2
  79.4 3.6 convolution_bitcast_fusion
  83.0 5.8 %copy.31 = f32[384,2752]{1,0:T(8,128)} copy(f32[384,2752]{0,1:T(8,128)} %convolution_bitcast_fusion) | data formatting | bytes 8454144
  88.8 0.0 reduce-scatter.14.cloned.1.call-update
  88.8 0.0 all-gather.6.cloned.1.call-start
  88.9 42.9 %reduce-scatter.10.cloned.1.call-done = f32[24,2752]{1,0:T(8,128)} async-done(((f32[384,2752]{1,0:T(8,128)}), f32[24,2752]{1,0:T(8,128)}) %reduce-scatter.10.cloned.1.call-update) | async-done | bytes 264208 | tf_op jit(solution)/shard_map/reduce_scatter | solution.py:82
  131.8 71.6 %reduce-scatter.12.cloned.1.call-done = f32[24,2752]{1,0:T(8,128)} async-done(((f32[384,2752]{1,0:T(8,128)}), f32[24,2752]{1,0:T(8,128)}) %reduce-scatter.12.cloned.1.call-update) | async-done | bytes 264208 | tf_op jit(solution)/shard_map/reduce_scatter | solution.py:83
  203.4 71.5 %reduce-scatter.14.cloned.1.call-done = f32[24,2752]{1,0:T(8,128)} async-done(((f32[384,2752]{1,0:T(8,128)}), f32[24,2752]{1,0:T(8,128)}) %reduce-scatter.14.cloned.1.call-update) | async-done | bytes 264208 | tf_op jit(solution)/shard_map/reduce_scatter | solution.py:92
  274.9 1.9 multiply_convert_fusion.1
  276.8 0.0 all-gather.6.cloned.1.call-update
  276.9 0.0 all-gather.8.cloned.1.call-start
  276.9 0.8 pad_maximum_fusion
  277.7 0.0 all-gather.8.cloned.1.call-update
  277.7 32.4 %all-gather.6.cloned.1.call-done = bf16[384,2752]{1,0:T(8,128)(2,1)} async-done(((bf16[24,2752]{1,0:T(8,128)(2,1)}), bf16[384,2752]{1,0:T(8,128)(2,1)}) %all-gather.6.cloned.1.call-update) | async-done | bytes 2113552 | tf_op jit(solution)/shard_map/all_gather | solution.py:85
  310.1 4.6 %fusion.18 = f32[384,512]{1,0:T(8,128)} fusion(bf16[384,2752]{1,0:T(8,128)(2,1)} %all-gather.6.cloned.1.call-done, bf16[512,2752]{0,1:T(8,128)(2,1)} %copy-done.2), kind=kOutput, calls=%fused_computation.31 | convolution fusion | flops 1082130432 | bytes 5718016 | tf_op jit(solution)/shard_map/dot_general | solution.py:87
  314.7 6.3 %all-to-all-start = ((f32[8,48,512]{2,1,0:T(8,128)}), f32[8,48,512]{2,1,0:T(8,128)}, u32[]{:S(2)}, u32[]{:S(2)}) async-start(f32[8,48,512]{2,1,0:T(8,128)} %bitcast.35), calls=%async_computation | async-start | bytes 1572864 | tf_op jit(solution)/shard_map/all_to_all | solution.py:41
  321.1 4.9 %fusion.2 = bf16[512,2752]{0,1:T(8,128)(2,1)} fusion(bf16[384,2752]{1,0:T(8,128)(2,1)} %all-gather.6.cloned.1.call-done, bf16[384,512]{1,0:T(8,128)(2,1)} %param.12), kind=kOutput, calls=%fused_computation.11 | convolution fusion | flops 1083539456 | bytes 5324800 | tf_op jit(solution)/shard_map/dot_general | solution.py:107
  325.9 16.9 %all-to-all-done = f32[8,48,512]{2,1,0:T(8,128)} async-done(((f32[8,48,512]{2,1,0:T(8,128)}), f32[8,48,512]{2,1,0:T(8,128)}, u32[]{:S(2)}, u32[]{:S(2)}) %all-to-all-start) | async-done | bytes 786464 | tf_op jit(solution)/shard_map/all_to_all | solution.py:41
  342.8 1.8 reduce_sum.18
  344.7 11.0 %all-gather.8.cloned.1.call-done = bf16[384,5504]{1,0:T(8,128)(2,1)} async-done(((bf16[24,5504]{1,0:T(8,128)(2,1)}), bf16[384,5504]{1,0:T(8,128)(2,1)}) %all-gather.8.cloned.1.call-update) | async-done | bytes 4227088 | tf_op jit(solution)/shard_map/all_gather | solution.py:26
  355.6 3.9 %fusion.4 = f32[384,512]{1,0:T(8,128)S(1)} fusion(bf16[512,2752]{0,1:T(8,128)(2,1)} %copy-done.1, bf16[384,5504]{1,0:T(8,128)(2,1)} %all-gather.8.cloned.1.call-done), kind=kOutput, calls=%fused_computation.13 | convolution fusion | flops 1082130432 | bytes 5767168 | tf_op jit(solution)/shard_map/dot_general | solution.py:97
  359.6 2.2 fusion.9
  361.8 6.8 %all-to-all-start.1 = ((f32[8,48,512]{2,1,0:T(8,128)}), f32[8,48,512]{2,1,0:T(8,128)S(1)}, u32[]{:S(2)}, u32[]{:S(2)}) async-start(f32[8,48,512]{2,1,0:T(8,128)} %bitcast.34), calls=%async_computation.1 | async-start | bytes 1572864 | tf_op jit(solution)/shard_map/all_to_all | solution.py:41
  368.6 5.0 %fusion = bf16[512,2752]{0,1:T(8,128)(2,1)} fusion(bf16[384,512]{1,0:T(8,128)(2,1)S(1)} %copy-done, bf16[384,5504]{1,0:T(8,128)(2,1)} %all-gather.8.cloned.1.call-done), kind=kOutput, calls=%fused_computation.9 | convolution fusion | flops 1083539456 | bytes 5373952 | tf_op jit(solution)/shard_map/dot_general | solution.py:101
  373.6 4.4 %fusion.1 = bf16[512,2752]{0,1:T(8,128)(2,1)} fusion(bf16[384,512]{1,0:T(8,128)(2,1)S(1)} %copy-done, bf16[384,5504]{1,0:T(8,128)(2,1)S(1)} %bitcast.40), kind=kOutput, calls=%fused_computation.10 | convolution fusion | flops 1083539456 | bytes 5373952 | tf_op jit(solution)/shard_map/dot_general | solution.py:104
  378.0 4.4 %all-to-all-done.1 = f32[8,48,512]{2,1,0:T(8,128)S(1)} async-done(((f32[8,48,512]{2,1,0:T(8,128)}), f32[8,48,512]{2,1,0:T(8,128)S(1)}, u32[]{:S(2)}, u32[]{:S(2)}) %all-to-all-start.1) | async-done | bytes 786464 | tf_op jit(solution)/shard_map/all_to_all | solution.py:41
  382.4 0.7 reduce_sum.19
  (11 shorter events, 0.0 us)
Async XLA Ops:
  7.2 43.3 %copy-start = (bf16[384,512]{1,0:T(8,128)(2,1)S(1)}, bf16[384,512]{1,0:T(8,128)(2,1)}, u32[]{:S(2)}) copy-start(bf16[384,512]{1,0:T(8,128)(2,1)} %param.11) | copy-start | bytes 1179652
  7.2 40.3 %all-gather.4.cloned.1.call-start = ((), (), s32[]{:S(2)}) async-start(), calls=%async_computation.5 | async-start | bytes 2263040 | tf_op jit(solution)/shard_map/all_gather | solution.py:26
  8.9 122.9 %reduce-scatter.10.cloned.1.call-start = ((), (), s32[]{:S(2)}) async-start(), calls=%async_computation.8 | async-start | bytes 4595712 | tf_op jit(solution)/shard_map/reduce_scatter | solution.py:82
  59.9 143.5 %reduce-scatter.12.cloned.1.call-start = ((), (), s32[]{:S(2)}) async-start(), calls=%async_computation.9 | async-start | bytes 4595712 | tf_op jit(solution)/shard_map/reduce_scatter | solution.py:83
  63.4 1.6 copy-start.1
  74.7 200.3 %reduce-scatter.14.cloned.1.call-start = ((), (), s32[]{:S(2)}) async-start(), calls=%async_computation.10 | async-start | bytes 4595712 | tf_op jit(solution)/shard_map/reduce_scatter | solution.py:92
  74.7 4.6 %copy-start.3 = (bf16[384,512]{1,0:T(8,128)(2,1)S(1)}, bf16[384,512]{1,0:T(8,128)(2,1)}, u32[]{:S(2)}) copy-start(bf16[384,512]{1,0:T(8,128)(2,1)} %param.12) | copy-start | bytes 1179652
  77.8 1.6 copy-start.2
  88.8 221.3 %all-gather.6.cloned.1.call-start = ((), (), s32[]{:S(2)}) async-start(), calls=%async_computation.6 | async-start | bytes 2297856 | tf_op jit(solution)/shard_map/all_gather | solution.py:85
  276.9 78.8 %all-gather.8.cloned.1.call-start = ((), (), s32[]{:S(2)}) async-start(), calls=%async_computation.7 | async-start | bytes 4491264 | tf_op jit(solution)/shard_map/all_gather | solution.py:26
  314.7 28.1 %all-to-all-start = ((f32[8,48,512]{2,1,0:T(8,128)}), f32[8,48,512]{2,1,0:T(8,128)}, u32[]{:S(2)}, u32[]{:S(2)}) async-start(f32[8,48,512]{2,1,0:T(8,128)} %bitcast.35), calls=%async_computation | async-start | bytes 1572864 | tf_op jit(solution)/shard_map/all_to_all | solution.py:41
  355.6 3.9 %copy-start.4 = (bf16[384,5504]{1,0:T(8,128)(2,1)S(1)}, bf16[384,5504]{1,0:T(8,128)(2,1)}, u32[]{:S(2)}) copy-start(bf16[384,5504]{1,0:T(8,128)(2,1)} %all-gather.8.cloned.1.call-done) | copy-start | bytes 12681220
  361.8 11.8 %slice-start = ((s8[4227072]{0:T(1024)(128)(4,1)}), s8[32768]{0:T(1024)(128)(4,1)S(1)}, s32[]{:S(2)}) async-start(s8[4227072]{0:T(1024)(128)(4,1)} %bitcast.39), calls=%async_computation.11 | async-start | bytes 65536
  361.8 20.6 %all-to-all-start.1 = ((f32[8,48,512]{2,1,0:T(8,128)}), f32[8,48,512]{2,1,0:T(8,128)S(1)}, u32[]{:S(2)}, u32[]{:S(2)}) async-start(f32[8,48,512]{2,1,0:T(8,128)} %bitcast.34), calls=%async_computation.1 | async-start | bytes 1572864 | tf_op jit(solution)/shard_map/all_to_all | solution.py:41
  368.6 5.0 %slice-start.1 = ((s8[4227072]{0:T(1024)(128)(4,1)}), s8[4194304]{0:T(1024)(128)(4,1)S(1)}, s32[]{:S(2)}) async-start(s8[4227072]{0:T(1024)(128)(4,1)} %bitcast.39), calls=%async_computation.12 | async-start | bytes 8388608
Sparse Core Ops, SparseCore 0:
  10.3 36.7 all-gather.3
  60.1 71.7 reduce-scatter.9
  134.2 69.1 reduce-scatter.11
  205.7 69.1 reduce-scatter.13
  277.0 33.0 all-gather.5
  311.7 43.9 all-gather.7
where the time goes:
time: 391 us; the launch traced here: 390 us
  waiting for transfers between devices  251 us (64%)
  matrix products  45.5 us (12%)
  blocking collectives  37.8 us (10%)
  local copies, waits for them, and re-layouts  22.2 us (6%)
  between operations  14.2 us (4%)
  starting transfers between devices  13.4 us (3%)
  other arithmetic  5.99 us (2%)
    reduce_scatter x1, waiting for transfers between devices, shards(): lax.psum_scatter(up_part, 'row', scatter_dimension=0, tiled=True)  71.6 us
    reduce_scatter x1, waiting for transfers between devices, shards(): lax.psum_scatter(back_part, 'row', scatter_dimension=0, tiled=True)  71.5 us
    reduce_scatter x1, waiting for transfers between devices, shards(): lax.psum_scatter(gate_part, 'row', scatter_dimension=0, tiled=True)  42.9 us
    all_gather x1, blocking collectives, turned_gather(): result = lax.all_gather(both, axis, axis=0, tiled=True)  37.8 us
    all_gather x1, waiting for transfers between devices, shards(): lax.all_gather(activate(gate_rows, up_rows), 'row', axis=0, tiled=True)  32.4 us
    all_to_all x2, waiting for transfers between devices, sum_at_owner(): tiles = lax.all_to_all(cut_along(value, dim, size), axis, 0, 0, tiled=True)  21.3 us
    unnamed x17, local copies, waits for them, and re-layouts  20.6 us
    all_to_all x2, starting transfers between devices, sum_at_owner(): tiles = lax.all_to_all(cut_along(value, dim, size), axis, 0, 0, tiled=True)  13.2 us
  transfers between devices with their start and end apart: 8, of which 7 were waited for; matrix products, arithmetic and copies ran while one was open for 12% of the time, Pallas kernels for 0%

commit v1 on v0

v1 whole, which is shorter than its diff:
```python
import jax
import jax.numpy as jnp
from jax import lax
from jax.sharding import PartitionSpec as P

BF = jnp.bfloat16
F32 = jnp.float32
ROWS = 24


def dot(a, b, dims):
    return lax.dot_general(a, b, (dims, ((), ())), preferred_element_type=F32)


NN = ((1,), (0,))
NT = ((1,), (1,))
TN = ((0,), (0,))


def row_send(x, dz, da, dc):
    pairs = []
    for z in range(4):
        for a in range(2):
            for c in range(2):
                to = ((z + dz) % 4) * 4 + ((a + da) % 2) * 2 + (c + dc) % 2
                pairs.append((z * 4 + a * 2 + c, to))
    return lax.ppermute(x, "row", pairs)


def col_send(x, dh, dy):
    pairs = []
    for h in range(2):
        for y in range(4):
            pairs.append((h * 4 + y, ((h + dh) % 2) * 4 + (y + dy) % 4))
    return lax.ppermute(x, "col", pairs)


def row_reduce(mine, theirs, z_first):
    n = mine.shape[1]
    got = row_send(theirs, 0, 0, 1)
    total = (mine + got.astype(F32)).reshape(4, 2, ROWS, n)
    if z_first:
        own = total[0]
        parts = [row_send(total[d].astype(BF), d, 0, 0) for d in (1, 3, 2)]
        for p in parts:
            own = own + p.astype(F32)
        return own[0] + row_send(own[1].astype(BF), 0, 1, 0).astype(F32)
    own = total[:, 0] + row_send(total[:, 1].astype(BF), 0, 1, 0).astype(F32)
    parts = [row_send(own[d].astype(BF), d, 0, 0) for d in (1, 3, 2)]
    own = own[0]
    for p in parts:
        own = own + p.astype(F32)
    return own


def row_gather(x, z_last):
    rows, n = x.shape
    if z_last:
        pair = jnp.stack([x, row_send(x, 0, 1, 0)])
        got = {d: row_send(pair, d, 0, 0) for d in (1, 3, 2)}
        half = jnp.stack([pair, got[3], got[2], got[1]])
    else:
        got = {d: row_send(x, d, 0, 0) for d in (1, 3, 2)}
        four = jnp.stack([x, got[3], got[2], got[1]])
        half = jnp.stack([four, row_send(four, 0, 1, 0)], axis=1)
    half = half.reshape(8 * rows, n)
    return jnp.concatenate([half, row_send(half, 0, 0, 1)], axis=0)


def col_reduce(part, order):
    spread = dot(order, part.astype(BF), NN).astype(BF).reshape(2, 4, 48, -1)
    own = spread[0].astype(F32) + col_send(spread[1], 1, 0).astype(F32)
    parts = [col_send(own[d].astype(BF), 0, d) for d in (1, 3, 2)]
    own = own[0]
    for p in parts:
        own = own + p.astype(F32)
    return own.astype(BF)


def shards(
    tokens,
    grad_out,
    gate_weight,
    up_weight,
    down_weight,
    gate_left,
    up_left,
    down_left,
    gate_right,
    up_right,
    down_right,
):
    n = gate_weight.shape[1]
    row, col = lax.axis_index("row"), lax.axis_index("col")
    z, a, c = row // 4, (row // 2) % 2, row % 2
    h, y = col // 4, col % 4

    def local_block(k):
        dc, dz, da = k // 8, (k // 2) % 4, k % 2
        return (z + dz) % 4, (a + da) % 2, (c + dc) % 2

    k = jnp.arange(384)
    bz, ba, bc = local_block(k // ROWS)
    held = ((bc * 4 + bz) * 2 + ba) * ROWS + k % ROWS
    order = (held[:, None] == k[None, :]).astype(BF)
    dest = ((h + k // 192) % 2) * 4 + (y + (k // 48) % 4) % 4
    leave = ((dest * 48 + k % 48)[:, None] == held[None, :]).astype(BF)

    j = jnp.arange(128)
    rz, ra, rc = local_block(j // 8)
    right_rank = (rz * 4 + ra * 2 + rc) * 8 + j % 8
    m = jnp.arange(384)
    my, mh, mt, mi = (m // 96), (m // 48) % 2, (m // 16) % 3, m % 16
    left_rank = (((h - mh) % 2) * 4 + (y - my) % 4) * 16 + mi
    match = ((left_rank + 128 * mt)[None, :] == m[:, None]).astype(BF)
    sort = (right_rank[None, :] == j[:, None]).astype(BF)

    rights = row_gather(jnp.concatenate([gate_right, up_right, down_right], axis=1), True)
    rights = dot(sort, rights, NN).astype(BF)
    right_g, right_u, right_d = (rights[:, n * t : n * (t + 1)] for t in range(3))
    lefts = jnp.concatenate([gate_left.T, up_left.T, down_left.T], axis=0)
    lefts = jnp.stack([lefts, col_send(lefts, 1, 0)])
    lefts = jnp.stack([lefts] + [col_send(lefts, 0, d) for d in (1, 2, 3)])
    lefts = dot(match, lefts.reshape(384, 512), NN).astype(BF)

    tok = dot(order, tokens, NN).astype(BF)
    out = dot(order, grad_out, NN).astype(BF)

    def halves(x, w):
        return dot(x[:192], w, NN), dot(x[192:], w, NN).astype(BF)

    gate_rows = row_reduce(*halves(tok, gate_weight), False)
    low = jnp.concatenate([dot(tok, lefts[:256], NT), dot(out, lefts[256:], NT)], axis=1)
    up_mine, up_theirs = halves(tok, up_weight)
    up_rows = row_reduce(
        jnp.concatenate([low[:192], up_mine], axis=1),
        jnp.concatenate([low[192:].astype(BF), up_theirs], axis=1),
        True,
    )
    back_rows = row_reduce(*halves(out, down_weight), False)
    low = up_rows[:, :384].astype(BF)
    gate = gate_rows + dot(low[:, :128], right_g, NN)
    up = up_rows[:, 384:] + dot(low[:, 128:256], right_u, NN)
    back = back_rows + dot(low[:, 256:], right_d, NN)

    sigma = jax.nn.sigmoid(gate)
    hidden = row_gather((gate * sigma * up).astype(BF), True)
    gate_delta = (back * up * sigma * (1.0 + gate * (1.0 - sigma))).astype(BF)
    up_delta = (back * gate * sigma).astype(BF)
    gate_delta = row_gather(gate_delta, False)
    up_delta = row_gather(up_delta, True)

    def through(x, w, right, left):
        return dot(x, w, NT) + dot(dot(x, right, NT).astype(BF), left, NN)

    mixed = col_reduce(through(hidden, down_weight, right_d, lefts[256:]), leave)
    input_grad = col_reduce(
        through(gate_delta, gate_weight, right_g, lefts[:128])
        + through(up_delta, up_weight, right_u, lefts[128:256]),
        leave,
    )
    gate_grad = dot(tok, gate_delta, TN).astype(BF)
    up_grad = dot(tok, up_delta, TN).astype(BF)
    down_grad = dot(out, hidden, TN).astype(BF)
    return mixed, input_grad, gate_grad, up_grad, down_grad


def solution(mesh):
    arg = P("row", "col")
    in_specs = (P(None, "row"), P(None, "row")) + (arg,) * 9
    out_specs = (P("col", "row"), P("col", "row")) + (arg,) * 3
    return jax.shard_map(shards, mesh=mesh, in_specs=in_specs, out_specs=out_specs, check_vma=False)
```

time: 391 us -> 201 us (0.51)
  waiting for transfers between devices: 251 us -> 57.7 us
  starting transfers between devices: 13.4 us -> 55.7 us
  blocking collectives: 37.8 us -> 0 us
  matrix products: 45.5 us -> 63.1 us
  local copies, waits for them, and re-layouts: 22.2 us -> 8.18 us
  between operations: 14.2 us -> 1.2 us
  other arithmetic: 5.99 us -> 14.5 us
    reduce_scatter x3 -> x0, waiting for transfers between devices: 186 us -> none  [the longest x1 71.6 us: shards(): lax.psum_scatter(up_part, 'row', scatter_dimension=0, tiled=True)]
    ppermute x0 -> x47, waiting for transfers between devices: none -> 57.7 us  [the longest x35 50.8 us: row_send(): return lax.ppermute(x, 'row', pairs)]
    ppermute x0 -> x47, starting transfers between devices: none -> 55.7 us  [the longest x35 36.8 us: row_send(): return lax.ppermute(x, 'row', pairs)]
    all_gather x3 -> x0, waiting for transfers between devices: 43.3 us -> none  [the longest x1 32.4 us: shards(): lax.all_gather(activate(gate_rows, up_rows), 'row', axis=0, tiled=True)]
    all_gather x1 -> x0, blocking collectives: 37.8 us -> none  [turned_gather(): result = lax.all_gather(both, axis, axis=0, tiled=True)]
    all_to_all x2 -> x0, waiting for transfers between devices: 21.3 us -> none  [sum_at_owner(): tiles = lax.all_to_all(cut_along(value, dim, size), axis, 0, 0, tiled=True)]
    unnamed x17 -> x46, local copies, waits for them, and re-layouts: 20.6 us -> 1.76 us
    dot_general x12 -> x24, matrix products: 45.5 us -> 63.1 us  [dot(): return lax.dot_general(a, b, (dims, ((), ())), preferred_element_type=F32)]
  transfers between devices with their start and end apart: 8 -> 47, of which waited for: 7 -> 18; matrix products, arithmetic and copies ran while one was open for 12% -> 39% of each run, Pallas kernels for 0% -> 0%
where the time goes in v1:
time: 201 us; the launch traced here: 200 us
  matrix products  63.1 us (31%)
  waiting for transfers between devices  57.7 us (29%)
  starting transfers between devices  55.7 us (28%)
  other arithmetic  14.5 us (7%)
  local copies, waits for them, and re-layouts  8.18 us (4%)
    dot_general x24, matrix products, dot(): return lax.dot_general(a, b, (dims, ((), ())), preferred_element_type=F32)  63.1 us
    ppermute x35, waiting for transfers between devices, row_send(): return lax.ppermute(x, 'row', pairs)  50.8 us
    ppermute x35, starting transfers between devices, row_send(): return lax.ppermute(x, 'row', pairs)  36.8 us
    ppermute x12, starting transfers between devices, col_send(): return lax.ppermute(x, 'col', pairs)  18.9 us
    ppermute x12, waiting for transfers between devices, col_send(): return lax.ppermute(x, 'col', pairs)  6.92 us
  transfers between devices with their start and end apart: 47, of which 18 were waited for; matrix products, arithmetic and copies ran while one was open for 39% of the time, Pallas kernels for 0%

profile of v1, /device:TPU:0, one launch (start us, length us, event | category | flops | bytes accessed | tf_op | source)
XLA Modules:
  0.0 200.5 jit_solution(657826099515666841)
XLA Ops:
  0.7 1.6 convolution_convert_fusion.9
  3.1 2.0 %convolution_convert_fusion.4 = bf16[192,2752]{1,0:T(8,128)(2,1)} fusion(bf16[512,2752]{0,1:T(8,128)(2,1)S(1)} %copy-done, bf16[384,512]{1,0:T(8,128)(2,1)S(1)} %convolution_convert_fusion.9), kind=kOutput, calls=%fused_computation.4 | convolution fusion | flops 541593600 | bytes 4071424 | tf_op jit(solution)/shard_map/dot_general | solution.py:12
  5.3 1.6 collective-permute-start.14
  7.6 2.7 %collective-permute-start.5 = (bf16[48,512]{1,0:T(8,128)(2,1)}, bf16[48,512]{1,0:T(8,128)(2,1)}, u32[]{:S(2)}, u32[]{:S(2)}) collective-permute-start(bf16[48,512]{1,0:T(8,128)(2,1)} %get-tuple-element.50), channel_id=1, source_target_pairs={{0,4},{1,5},{2,6},{3,7},{4,0},{5,1},{6,2},{7,3},{8,12},{9,13},{10,... | collective-permute-start | bytes 147464 | tf_op jit(solution)/shard_map/ppermute | solution.py:35
  11.7 3.8 %convolution_convert_fusion.6 = bf16[192,2752]{1,0:T(8,128)(2,1)} fusion(bf16[512,2752]{0,1:T(8,128)(2,1)} %param.13, bf16[384,512]{1,0:T(8,128)(2,1)S(1)} %convolution_convert_fusion.11), kind=kOutput, calls=%fused_computation.6 | convolution fusion | flops 541593600 | bytes 4071424 | tf_op jit(solution)/shard_map/dot_general | solution.py:12
  15.6 4.0 %convolution_convert_fusion.5 = bf16[192,2752]{1,0:T(8,128)(2,1)} fusion(bf16[512,2752]{0,1:T(8,128)(2,1)} %param.14, bf16[384,512]{1,0:T(8,128)(2,1)S(1)} %convolution_convert_fusion.11), kind=kOutput, calls=%fused_computation.5 | convolution fusion | flops 541593600 | bytes 4071424 | tf_op jit(solution)/shard_map/dot_general | solution.py:12
  19.6 2.4 %fusion.54 = f32[192,2752]{1,0:T(8,128)} fusion(bf16[512,2752]{0,1:T(8,128)(2,1)S(1)} %copy-done.2, bf16[384,512]{1,0:T(8,128)(2,1)S(1)} %convolution_convert_fusion.11), kind=kOutput, calls=%fused_computation.104 | convolution fusion | flops 541065216 | bytes 5128192 | tf_op jit(solution)/shard_map/dot_general | solution.py:12
  23.4 3.1 %collective-permute-start.8 = (bf16[2,48,512]{2,1,0:T(8,128)(2,1)S(1)}, bf16[2,48,512]{2,1,0:T(8,128)(2,1)S(1)}, u32[]{:S(2)}, u32[]{:S(2)}) collective-permute-start(bf16[2,48,512]{2,1,0:T(8,128)(2,1)S(1)} %get-tuple-element.48), channel_id=1, source_target_pairs={{0,3},{1,0},{2,1},{3,2},{4,7},{5,4},{6,5},{7,6},{8,11},{9,8},{10,9... | collective-permute-start | bytes 294920 | tf_op jit(solution)/shard_map/ppermute | solution.py:35
  28.9 2.4 %collective-permute-done.8 = bf16[2,48,512]{2,1,0:T(8,128)(2,1)S(1)} collective-permute-done((bf16[2,48,512]{2,1,0:T(8,128)(2,1)S(1)}, bf16[2,48,512]{2,1,0:T(8,128)(2,1)S(1)}, u32[]{:S(2)}, u32[]{:S(2)}) %collective-permute-start.8) | collective-permute-done | bytes 98336 | tf_op jit(solution)/shard_map/ppermute | solution.py:35
  31.3 1.9 collective-permute-start.17
  33.6 3.9 %collective-permute-start.16 = (bf16[2,8,8256]{2,1,0:T(8,128)(2,1)}, bf16[2,8,8256]{2,1,0:T(8,128)(2,1)}, u32[]{:S(2)}, u32[]{:S(2)}) collective-permute-start(bf16[2,8,8256]{2,1,0:T(8,128)(2,1)} %get-tuple-element.40), channel_id=1, source_target_pairs={{0,64},{8,72},{16,80},{24,88},{32,96},{40,104},{48,112},{56,120},{... | collective-permute-start | bytes 792584 | tf_op jit(solution)/shard_map/ppermute | solution.py:27
  42.9 2.4 %pad_maximum_fusion.3 = bf16[192,3136]{1,0:T(8,128)(2,1)} fusion(bf16[192,2752]{1,0:T(8,128)(2,1)} %convolution_convert_fusion.5, bf16[192,384]{1,0:T(8,128)(2,1)S(1)} %copy.23), kind=kLoop, calls=%fused_computation.27 | loop fusion | flops 2408448 | bytes 2408448 | tf_op jit(solution)/shard_map/concatenate | solution.py:137
  51.0 2.5 %convert_add_fusion = f32[192,2752]{1,0:T(8,128)S(1)} fusion(bf16[192,2752]{1,0:T(8,128)(2,1)} %collective-permute-done.28, bf16[512,2752]{0,1:T(8,128)(2,1)S(1)} %copy-done, bf16[384,512]{1,0:T(8,128)(2,1)S(1)} %copy-done.9), kind=kOutput, calls=%fused_computation.11 | convolution fusion | flops 542121984 | bytes 6184960 | tf_op jit(solution)/shard_map/dot_general | solution.py:12
  53.8 2.5 %convert_add_fusion.1 = f32[192,2752]{1,0:T(8,128)S(1)} fusion(bf16[192,2752]{1,0:T(8,128)(2,1)} %collective-permute-done, bf16[512,2752]{0,1:T(8,128)(2,1)S(1)} %copy-done.1, bf16[384,512]{1,0:T(8,128)(2,1)S(1)} %convolution_convert_fusion.11), kind=kOutput, calls=%fused_computation.12 | convolution fusion | flops 542121984 | bytes 6184960 | tf_op jit(solution)/shard_map/dot_general | solution.py:12
  56.4 1.7 collective-permute-start.1
  59.9 2.0 %collective-permute-start.11 = (bf16[2,24,3136]{2,1,0:T(8,128)(2,1)S(1)}, bf16[2,24,3136]{2,1,0:T(8,128)(2,1)S(1)}, u32[]{:S(2)}, u32[]{:S(2)}) collective-permute-start(bf16[2,24,3136]{2,1,0:T(8,128)(2,1)S(1)} %bitcast.175), channel_id=1, source_target_pairs={{0,96},{8,104},{16,112},{24,120},{32,0},{40,8},{48,16},{56,24},{64... | collective-permute-start | bytes 903176 | tf_op jit(solution)/shard_map/ppermute | solution.py:27
  63.3 5.4 %collective-permute-done.29 = bf16[4,24,2752]{2,1,0:T(8,128)(2,1)S(1)} collective-permute-done((bf16[4,24,2752]{2,1,0:T(8,128)(2,1)S(1)}, bf16[4,24,2752]{2,1,0:T(8,128)(2,1)S(1)}, u32[]{:S(2)}, u32[]{:S(2)}) %collective-permute-start.29) | collective-permute-done | bytes 528416 | tf_op jit(solution)/shard_map/ppermute | solution.py:27
  70.3 9.4 %collective-permute-done.1 = bf16[4,24,2752]{2,1,0:T(8,128)(2,1)S(1)} collective-permute-done((bf16[4,24,2752]{2,1,0:T(8,128)(2,1)S(1)}, bf16[4,24,2752]{2,1,0:T(8,128)(2,1)S(1)}, u32[]{:S(2)}, u32[]{:S(2)}) %collective-permute-start.1) | collective-permute-done | bytes 528416 | tf_op jit(solution)/shard_map/ppermute | solution.py:27
  79.7 2.9 %collective-permute-start.31 = (bf16[24,2752]{1,0:T(8,128)(2,1)S(1)}, bf16[24,2752]{1,0:T(8,128)(2,1)S(1)}, u32[]{:S(2)}, u32[]{:S(2)}) collective-permute-start(bf16[24,2752]{1,0:T(8,128)(2,1)S(1)} %get-tuple-element.23), channel_id=1, source_target_pairs={{0,96},{8,104},{16,112},{24,120},{32,0},{40,8},{48,16},{56,24},{64... | collective-permute-start | bytes 396296 | tf_op jit(solution)/shard_map/ppermute | solution.py:27
  85.0 3.6 %collective-permute-done.13 = bf16[24,3136]{1,0:T(8,128)(2,1)S(1)} collective-permute-done((bf16[24,3136]{1,0:T(8,128)(2,1)S(1)}, bf16[24,3136]{1,0:T(8,128)(2,1)S(1)}, u32[]{:S(2)}, u32[]{:S(2)}) %collective-permute-start.13) | collective-permute-done | bytes 150560 | tf_op jit(solution)/shard_map/ppermute | solution.py:27
  88.6 3.0 %collective-permute-start.3 = (bf16[24,2752]{1,0:T(8,128)(2,1)S(1)}, bf16[24,2752]{1,0:T(8,128)(2,1)S(1)}, u32[]{:S(2)}, u32[]{:S(2)}) collective-permute-start(bf16[24,2752]{1,0:T(8,128)(2,1)S(1)} %get-tuple-element.26), channel_id=1, source_target_pairs={{0,96},{8,104},{16,112},{24,120},{32,0},{40,8},{48,16},{56,24},{64... | collective-permute-start | bytes 396296 | tf_op jit(solution)/shard_map/ppermute | solution.py:27
  94.1 3.8 %collective-permute-done.2 = bf16[24,2752]{1,0:T(8,128)(2,1)S(1)} collective-permute-done((bf16[24,2752]{1,0:T(8,128)(2,1)S(1)}, bf16[24,2752]{1,0:T(8,128)(2,1)S(1)}, u32[]{:S(2)}, u32[]{:S(2)}) %collective-permute-start.2) | collective-permute-done | bytes 132128 | tf_op jit(solution)/shard_map/ppermute | solution.py:27
  100.2 1.7 collective-permute-start.38
  101.9 1.6 collective-permute-done.19
  105.4 2.2 %collective-permute-start.20 = (bf16[2,24,2752]{2,1,0:T(8,128)(2,1)S(1)}, bf16[2,24,2752]{2,1,0:T(8,128)(2,1)S(1)}, u32[]{:S(2)}, u32[]{:S(2)}) collective-permute-start(bf16[2,24,2752]{2,1,0:T(8,128)(2,1)S(1)} %get-tuple-element.38), channel_id=1, source_target_pairs={{0,96},{8,104},{16,112},{24,120},{32,0},{40,8},{48,16},{56,24},{64... | collective-permute-start | bytes 792584 | tf_op jit(solution)/shard_map/ppermute | solution.py:27
  107.6 10.0 %collective-permute-done.22 = bf16[2,24,2752]{2,1,0:T(8,128)(2,1)S(1)} collective-permute-done((bf16[2,24,2752]{2,1,0:T(8,128)(2,1)S(1)}, bf16[2,24,2752]{2,1,0:T(8,128)(2,1)S(1)}, u32[]{:S(2)}, u32[]{:S(2)}) %collective-permute-start.22) | collective-permute-done | bytes 264224 | tf_op jit(solution)/shard_map/ppermute | solution.py:27
  117.6 2.0 %collective-permute-start.41 = (bf16[2,24,2752]{2,1,0:T(8,128)(2,1)S(1)}, bf16[2,24,2752]{2,1,0:T(8,128)(2,1)S(1)}, u32[]{:S(2)}, u32[]{:S(2)}) collective-permute-start(bf16[2,24,2752]{2,1,0:T(8,128)(2,1)S(1)} %get-tuple-element.36), channel_id=1, source_target_pairs={{0,32},{8,40},{16,48},{24,56},{32,64},{40,72},{48,80},{56,88},{64,... | collective-permute-start | bytes 792584 | tf_op jit(solution)/shard_map/ppermute | solution.py:27
  119.8 2.8 %collective-permute-start.39 = (bf16[2,24,2752]{2,1,0:T(8,128)(2,1)S(1)}, bf16[2,24,2752]{2,1,0:T(8,128)(2,1)S(1)}, u32[]{:S(2)}, u32[]{:S(2)}) collective-permute-start(bf16[2,24,2752]{2,1,0:T(8,128)(2,1)S(1)} %get-tuple-element.36), channel_id=1, source_target_pairs={{0,96},{8,104},{16,112},{24,120},{32,0},{40,8},{48,16},{56,24},{64... | collective-permute-start | bytes 792584 | tf_op jit(solution)/shard_map/ppermute | solution.py:27
  122.6 1.9 collective-permute-done.33
  124.7 4.4 %collective-permute-done.41 = bf16[2,24,2752]{2,1,0:T(8,128)(2,1)S(1)} collective-permute-done((bf16[2,24,2752]{2,1,0:T(8,128)(2,1)S(1)}, bf16[2,24,2752]{2,1,0:T(8,128)(2,1)S(1)}, u32[]{:S(2)}, u32[]{:S(2)}) %collective-permute-start.41) | collective-permute-done | bytes 264224 | tf_op jit(solution)/shard_map/ppermute | solution.py:27
  129.1 3.2 %collective-permute-done.39 = bf16[2,24,2752]{2,1,0:T(8,128)(2,1)S(1)} collective-permute-done((bf16[2,24,2752]{2,1,0:T(8,128)(2,1)S(1)}, bf16[2,24,2752]{2,1,0:T(8,128)(2,1)S(1)}, u32[]{:S(2)}, u32[]{:S(2)}) %collective-permute-start.39) | collective-permute-done | bytes 264224 | tf_op jit(solution)/shard_map/ppermute | solution.py:27
  133.4 4.1 %collective-permute-done.36 = bf16[4,24,2752]{2,1,0:T(8,128)(2,1)S(1)} collective-permute-done((bf16[4,24,2752]{2,1,0:T(8,128)(2,1)S(1)}, bf16[4,24,2752]{2,1,0:T(8,128)(2,1)S(1)}, u32[]{:S(2)}, u32[]{:S(2)}) %collective-permute-start.36) | collective-permute-done | bytes 528416 | tf_op jit(solution)/shard_map/ppermute | solution.py:27
  138.6 3.7 %fusion.6 = f32[384,512]{1,0:T(8,128)} fusion(bf16[192,2752]{1,0:T(8,128)(2,1)} %collective-permute-done.23, bf16[192,2752]{1,0:T(8,128)(2,1)} %bitcast.166, bf16[128,8256]{0,1:T(8,128)(2,1)} %copy-done.4, bf16[384,512]{1,0:T(8,128)(2,1)} %copy-done.13), kind=kOutput, calls=%fused_computation.31 | convolution fusion | flops 325140480 | bytes 3784704 | tf_op jit(solution)/shard_map/dot_general | solution.py:12
  142.4 4.1 %convolution_convert_fusion.8 = bf16[384,512]{1,0:T(8,128)(2,1)} fusion(f32[384,512]{1,0:T(8,128)} %fusion.6, bf16[512,2752]{0,1:T(8,128)(2,1)S(1)} %copy-done, bf16[192,2752]{1,0:T(8,128)(2,1)} %collective-permute-done.23, bf16[192,2752]{1,0:T(8,128)(2,1)} %bitcast.167, s32[384]{0:T(512)S(1)} %copy-done.22, s32[384]{0:T(512)S(1)} %fusion.96), kind=kOutput, calls=%fused_computation.23 | convolution fusion | flops 1238089728 | bytes 6114304 | tf_op jit(solution)/shard_map/dot_general | solution.py:12
  146.5 1.7 fusion.176
  148.9 3.7 %fusion.8 = f32[384,512]{1,0:T(8,128)} fusion(bf16[192,2752]{1,0:T(8,128)(2,1)} %collective-permute-done.42, bf16[192,2752]{1,0:T(8,128)(2,1)} %bitcast.63, bf16[128,8256]{0,1:T(8,128)(2,1)} %copy-done.4, bf16[384,512]{1,0:T(8,128)(2,1)} %copy-done.13), kind=kOutput, calls=%fused_computation.33 | convolution fusion | flops 325140480 | bytes 3784704 | tf_op jit(solution)/shard_map/dot_general | solution.py:12
  152.6 4.8 %convolution_add_fusion = f32[384,512]{1,0:T(8,128)} fusion(f32[384,512]{1,0:T(8,128)} %fusion.8, bf16[512,2752]{0,1:T(8,128)(2,1)} %param.14, bf16[192,2752]{1,0:T(8,128)(2,1)} %collective-permute-done.42, bf16[192,2752]{1,0:T(8,128)(2,1)} %bitcast.63), kind=kOutput, calls=%fused_computation.16 | convolution fusion | flops 1086554112 | bytes 6504448 | tf_op jit(solution)/shard_map/dot_general | solution.py:12
  157.4 4.9 %convolution_convert_fusion.2 = bf16[512,2752]{0,1:T(8,128)(2,1)} fusion(bf16[384,512]{1,0:T(8,128)(2,1)S(1)} %convolution_convert_fusion.11, bf16[192,2752]{1,0:T(8,128)(2,1)} %collective-permute-done.42, bf16[192,2752]{1,0:T(8,128)(2,1)} %bitcast.63), kind=kOutput, calls=%fused_computation.2 | convolution fusion | flops 1087766528 | bytes 5324800 | tf_op jit(solution)/shard_map/dot_general | solution.py:12
  162.3 4.5 %convolution_convert_fusion.1 = bf16[512,2752]{0,1:T(8,128)(2,1)} fusion(bf16[384,512]{1,0:T(8,128)(2,1)S(1)} %copy-done.10, bf16[192,2752]{1,0:T(8,128)(2,1)} %collective-permute-done.23, bf16[192,2752]{1,0:T(8,128)(2,1)S(1)} %bitcast.168), kind=kOutput, calls=%fused_computation.1 | convolution fusion | flops 1087766528 | bytes 5324800 | tf_op jit(solution)/shard_map/dot_general | solution.py:12
  166.8 1.7 fusion.159
  169.3 2.8 %collective-permute-start.26 = (bf16[48,512]{1,0:T(8,128)(2,1)S(1)}, bf16[48,512]{1,0:T(8,128)(2,1)S(1)}, u32[]{:S(2)}, u32[]{:S(2)}) collective-permute-start(bf16[48,512]{1,0:T(8,128)(2,1)S(1)} %get-tuple-element.46), channel_id=1, source_target_pairs={{0,3},{1,0},{2,1},{3,2},{4,7},{5,4},{6,5},{7,6},{8,11},{9,8},{10,9... | collective-permute-start | bytes 147464 | tf_op jit(solution)/shard_map/ppermute | solution.py:35
  172.1 3.7 %fusion.7 = f32[384,512]{1,0:T(8,128)} fusion(bf16[192,2752]{1,0:T(8,128)(2,1)} %collective-permute-done.37, bf16[192,2752]{1,0:T(8,128)(2,1)} %bitcast.56, bf16[128,8256]{0,1:T(8,128)(2,1)} %copy-done.4, bf16[384,512]{1,0:T(8,128)(2,1)} %copy-done.13), kind=kOutput, calls=%fused_computation.32 | convolution fusion | flops 325140480 | bytes 3784704 | tf_op jit(solution)/shard_map/dot_general | solution.py:12
  175.8 5.2 %convolution_convert_fusion.7 = bf16[384,512]{1,0:T(8,128)(2,1)} fusion(f32[384,512]{1,0:T(8,128)} %convolution_add_fusion, f32[384,512]{1,0:T(8,128)} %fusion.7, bf16[512,2752]{0,1:T(8,128)(2,1)} %param.13, bf16[192,2752]{1,0:T(8,128)(2,1)} %collective-permute-done.37, bf16[192,2752]{1,0:T(8,128)(2,1)} %bitcast.56, s32[384]{0:T(512)S(1)} %copy-done.22, ...), kind=kOutput, calls=%fused_computation.22 | convolution fusion | flops 1238286336 | bytes 6900736 | tf_op jit(solution)/shard_map/dot_general | solution.py:12
  182.0 2.9 %collective-permute-start.43 = (bf16[4,48,512]{2,1,0:T(8,128)(2,1)S(1)}, bf16[4,48,512]{2,1,0:T(8,128)(2,1)S(1)}, u32[]{:S(2)}, u32[]{:S(2)}) collective-permute-start(bf16[4,48,512]{2,1,0:T(8,128)(2,1)S(1)} %bitcast.183), channel_id=1, source_target_pairs={{0,4},{1,5},{2,6},{3,7},{4,0},{5,1},{6,2},{7,3},{8,12},{9,13},{10,... | collective-permute-start | bytes 589832 | tf_op jit(solution)/shard_map/ppermute | solution.py:35
  186.5 3.6 %collective-permute-done.43 = bf16[4,48,512]{2,1,0:T(8,128)(2,1)S(1)} collective-permute-done((bf16[4,48,512]{2,1,0:T(8,128)(2,1)S(1)}, bf16[4,48,512]{2,1,0:T(8,128)(2,1)S(1)}, u32[]{:S(2)}, u32[]{:S(2)}) %collective-permute-start.43) | collective-permute-done | bytes 196640 | tf_op jit(solution)/shard_map/ppermute | solution.py:35
  190.2 2.0 collective-permute-start.46
  192.2 2.4 %collective-permute-start.45 = (bf16[48,512]{1,0:T(8,128)(2,1)S(1)}, bf16[48,512]{1,0:T(8,128)(2,1)S(1)}, u32[]{:S(2)}, u32[]{:S(2)}) collective-permute-start(bf16[48,512]{1,0:T(8,128)(2,1)S(1)} %get-tuple-element.43), channel_id=1, source_target_pairs={{0,3},{1,0},{2,1},{3,2},{4,7},{5,4},{6,5},{7,6},{8,11},{9,8},{10,9... | collective-permute-start | bytes 147464 | tf_op jit(solution)/shard_map/ppermute | solution.py:35
  194.5 4.8 %convolution_convert_fusion.3 = bf16[512,2752]{0,1:T(8,128)(2,1)} fusion(bf16[384,512]{1,0:T(8,128)(2,1)S(1)} %convolution_convert_fusion.11, bf16[192,2752]{1,0:T(8,128)(2,1)} %collective-permute-done.37, bf16[192,2752]{1,0:T(8,128)(2,1)} %bitcast.56), kind=kOutput, calls=%fused_computation.3 | convolution fusion | flops 1087766528 | bytes 5324800 | tf_op jit(solution)/shard_map/dot_general | solution.py:12
  (158 shorter events, 40.3 us)
Async XLA Ops:
  5.2 45.8 %collective-permute-start.28 = (bf16[192,2752]{1,0:T(8,128)(2,1)}, bf16[192,2752]{1,0:T(8,128)(2,1)}, u32[]{:S(2)}, u32[]{:S(2)}) collective-permute-start(bf16[192,2752]{1,0:T(8,128)(2,1)} %convolution_convert_fusion.4), channel_id=1, source_target_pairs={{0,8},{8,0},{16,24},{24,16},{32,40},{40,32},{48,56},{56,48},{64,72... | collective-permute-start | bytes 3170312 | tf_op jit(solution)/shard_map/ppermute | solution.py:27
  5.3 21.8 %collective-permute-start.14 = (bf16[8,8256]{1,0:T(8,128)(2,1)S(1)}, bf16[8,8256]{1,0:T(8,128)(2,1)S(1)}, u32[]{:S(2)}, u32[]{:S(2)}) collective-permute-start(bf16[8,8256]{1,0:T(8,128)(2,1)S(1)} %concatenate.31), channel_id=1, source_target_pairs={{0,16},{8,24},{16,0},{24,8},{32,48},{40,56},{48,32},{56,40},{64,80... | collective-permute-start | bytes 396296 | tf_op jit(solution)/shard_map/ppermute | solution.py:27
  7.6 15.0 %collective-permute-start.5 = (bf16[48,512]{1,0:T(8,128)(2,1)}, bf16[48,512]{1,0:T(8,128)(2,1)}, u32[]{:S(2)}, u32[]{:S(2)}) collective-permute-start(bf16[48,512]{1,0:T(8,128)(2,1)} %get-tuple-element.50), channel_id=1, source_target_pairs={{0,4},{1,5},{2,6},{3,7},{4,0},{5,1},{6,2},{7,3},{8,12},{9,13},{10,... | collective-permute-start | bytes 147464 | tf_op jit(solution)/shard_map/ppermute | solution.py:35
  15.6 38.3 %collective-permute-start = (bf16[192,2752]{1,0:T(8,128)(2,1)}, bf16[192,2752]{1,0:T(8,128)(2,1)}, u32[]{:S(2)}, u32[]{:S(2)}) collective-permute-start(bf16[192,2752]{1,0:T(8,128)(2,1)} %convolution_convert_fusion.6), channel_id=1, source_target_pairs={{0,8},{8,0},{16,24},{24,16},{32,40},{40,32},{48,56},{56,48},{64,72... | collective-permute-start | bytes 3170312 | tf_op jit(solution)/shard_map/ppermute | solution.py:27
  23.4 7.9 %collective-permute-start.8 = (bf16[2,48,512]{2,1,0:T(8,128)(2,1)S(1)}, bf16[2,48,512]{2,1,0:T(8,128)(2,1)S(1)}, u32[]{:S(2)}, u32[]{:S(2)}) collective-permute-start(bf16[2,48,512]{2,1,0:T(8,128)(2,1)S(1)} %get-tuple-element.48), channel_id=1, source_target_pairs={{0,3},{1,0},{2,1},{3,2},{4,7},{5,4},{6,5},{7,6},{8,11},{9,8},{10,9... | collective-permute-start | bytes 294920 | tf_op jit(solution)/shard_map/ppermute | solution.py:35
  26.5 7.1 %collective-permute-start.7 = (bf16[2,48,512]{2,1,0:T(8,128)(2,1)S(1)}, bf16[2,48,512]{2,1,0:T(8,128)(2,1)S(1)}, u32[]{:S(2)}, u32[]{:S(2)}) collective-permute-start(bf16[2,48,512]{2,1,0:T(8,128)(2,1)S(1)} %get-tuple-element.48), channel_id=1, source_target_pairs={{0,2},{1,3},{2,0},{3,1},{4,6},{5,7},{6,4},{7,5},{8,10},{9,11},{10,... | collective-permute-start | bytes 294920 | tf_op jit(solution)/shard_map/ppermute | solution.py:35
  27.1 10.4 %collective-permute-start.6 = (bf16[2,48,512]{2,1,0:T(8,128)(2,1)S(1)}, bf16[2,48,512]{2,1,0:T(8,128)(2,1)S(1)}, u32[]{:S(2)}, u32[]{:S(2)}) collective-permute-start(bf16[2,48,512]{2,1,0:T(8,128)(2,1)S(1)} %get-tuple-element.48), channel_id=1, source_target_pairs={{0,1},{1,2},{2,3},{3,0},{4,5},{5,6},{6,7},{7,4},{8,9},{9,10},{10,1... | collective-permute-start | bytes 294920 | tf_op jit(solution)/shard_map/ppermute | solution.py:35
  31.3 16.0 %collective-permute-start.17 = (bf16[2,8,8256]{2,1,0:T(8,128)(2,1)}, bf16[2,8,8256]{2,1,0:T(8,128)(2,1)}, u32[]{:S(2)}, u32[]{:S(2)}) collective-permute-start(bf16[2,8,8256]{2,1,0:T(8,128)(2,1)} %get-tuple-element.40), channel_id=1, source_target_pairs={{0,32},{8,40},{16,48},{24,56},{32,64},{40,72},{48,80},{56,88},{64,... | collective-permute-start | bytes 792584 | tf_op jit(solution)/shard_map/ppermute | solution.py:27
  33.6 15.1 %collective-permute-start.16 = (bf16[2,8,8256]{2,1,0:T(8,128)(2,1)}, bf16[2,8,8256]{2,1,0:T(8,128)(2,1)}, u32[]{:S(2)}, u32[]{:S(2)}) collective-permute-start(bf16[2,8,8256]{2,1,0:T(8,128)(2,1)} %get-tuple-element.40), channel_id=1, source_target_pairs={{0,64},{8,72},{16,80},{24,88},{32,96},{40,104},{48,112},{56,120},{... | collective-permute-start | bytes 792584 | tf_op jit(solution)/shard_map/ppermute | solution.py:27
  37.5 12.0 %collective-permute-start.15 = (bf16[2,8,8256]{2,1,0:T(8,128)(2,1)}, bf16[2,8,8256]{2,1,0:T(8,128)(2,1)}, u32[]{:S(2)}, u32[]{:S(2)}) collective-permute-start(bf16[2,8,8256]{2,1,0:T(8,128)(2,1)} %get-tuple-element.40), channel_id=1, source_target_pairs={{0,96},{8,104},{16,112},{24,120},{32,0},{40,8},{48,16},{56,24},{64... | collective-permute-start | bytes 792584 | tf_op jit(solution)/shard_map/ppermute | solution.py:27
  47.3 10.8 %collective-permute-start.9 = (bf16[192,3136]{1,0:T(8,128)(2,1)}, bf16[192,3136]{1,0:T(8,128)(2,1)S(1)}, u32[]{:S(2)}, u32[]{:S(2)}) collective-permute-start(bf16[192,3136]{1,0:T(8,128)(2,1)} %pad_maximum_fusion.3), channel_id=1, source_target_pairs={{0,8},{8,0},{16,24},{24,16},{32,40},{40,32},{48,56},{56,48},{64,72... | collective-permute-start | bytes 3612680 | tf_op jit(solution)/shard_map/ppermute | solution.py:27
  50.9 11.2 %collective-permute-start.18 = (bf16[64,8256]{1,0:T(8,128)(2,1)S(1)}, bf16[64,8256]{1,0:T(8,128)(2,1)S(1)}, u32[]{:S(2)}, u32[]{:S(2)}) collective-permute-start(bf16[64,8256]{1,0:T(8,128)(2,1)S(1)} %bitcast.162), channel_id=1, source_target_pairs={{0,8},{8,0},{16,24},{24,16},{32,40},{40,32},{48,56},{56,48},{64,72... | collective-permute-start | bytes 3170312 | tf_op jit(solution)/shard_map/ppermute | solution.py:27
  53.5 15.2 %collective-permute-start.29 = (bf16[4,24,2752]{2,1,0:T(8,128)(2,1)S(1)}, bf16[4,24,2752]{2,1,0:T(8,128)(2,1)S(1)}, u32[]{:S(2)}, u32[]{:S(2)}) collective-permute-start(bf16[4,24,2752]{2,1,0:T(8,128)(2,1)S(1)} %fusion.26), channel_id=1, source_target_pairs={{0,16},{8,24},{16,0},{24,8},{32,48},{40,56},{48,32},{56,40},{64,80... | collective-permute-start | bytes 1585160 | tf_op jit(solution)/shard_map/ppermute | solution.py:27
  56.4 23.3 %collective-permute-start.1 = (bf16[4,24,2752]{2,1,0:T(8,128)(2,1)S(1)}, bf16[4,24,2752]{2,1,0:T(8,128)(2,1)S(1)}, u32[]{:S(2)}, u32[]{:S(2)}) collective-permute-start(bf16[4,24,2752]{2,1,0:T(8,128)(2,1)S(1)} %fusion.25), channel_id=1, source_target_pairs={{0,16},{8,24},{16,0},{24,8},{32,48},{40,56},{48,32},{56,40},{64,80... | collective-permute-start | bytes 1585160 | tf_op jit(solution)/shard_map/ppermute | solution.py:27
  58.4 24.3 %collective-permute-start.12 = (bf16[2,24,3136]{2,1,0:T(8,128)(2,1)S(1)}, bf16[2,24,3136]{2,1,0:T(8,128)(2,1)S(1)}, u32[]{:S(2)}, u32[]{:S(2)}) collective-permute-start(bf16[2,24,3136]{2,1,0:T(8,128)(2,1)S(1)} %bitcast.176), channel_id=1, source_target_pairs={{0,64},{8,72},{16,80},{24,88},{32,96},{40,104},{48,112},{56,120},{... | collective-permute-start | bytes 903176 | tf_op jit(solution)/shard_map/ppermute | solution.py:27
  59.9 22.9 %collective-permute-start.11 = (bf16[2,24,3136]{2,1,0:T(8,128)(2,1)S(1)}, bf16[2,24,3136]{2,1,0:T(8,128)(2,1)S(1)}, u32[]{:S(2)}, u32[]{:S(2)}) collective-permute-start(bf16[2,24,3136]{2,1,0:T(8,128)(2,1)S(1)} %bitcast.175), channel_id=1, source_target_pairs={{0,96},{8,104},{16,112},{24,120},{32,0},{40,8},{48,16},{56,24},{64... | collective-permute-start | bytes 903176 | tf_op jit(solution)/shard_map/ppermute | solution.py:27
  62.0 20.8 %collective-permute-start.10 = (bf16[2,24,3136]{2,1,0:T(8,128)(2,1)S(1)}, bf16[2,24,3136]{2,1,0:T(8,128)(2,1)S(1)}, u32[]{:S(2)}, u32[]{:S(2)}) collective-permute-start(bf16[2,24,3136]{2,1,0:T(8,128)(2,1)S(1)} %bitcast.174), channel_id=1, source_target_pairs={{0,32},{8,40},{16,48},{24,56},{32,64},{40,72},{48,80},{56,88},{64,... | collective-permute-start | bytes 903176 | tf_op jit(solution)/shard_map/ppermute | solution.py:27
  63.3 34.6 %copy-start.4 = (bf16[128,8256]{0,1:T(8,128)(2,1)}, bf16[128,8256]{0,1:T(8,128)(2,1)S(1)}, u32[]{:S(2)}) copy-start(bf16[128,8256]{0,1:T(8,128)(2,1)S(1)} %convolution_convert_fusion) | copy-start | bytes 6340612
  68.9 22.7 %collective-permute-start.32 = (bf16[24,2752]{1,0:T(8,128)(2,1)S(1)}, bf16[24,2752]{1,0:T(8,128)(2,1)S(1)}, u32[]{:S(2)}, u32[]{:S(2)}) collective-permute-start(bf16[24,2752]{1,0:T(8,128)(2,1)S(1)} %get-tuple-element.22), channel_id=1, source_target_pairs={{0,64},{8,72},{16,80},{24,88},{32,96},{40,104},{48,112},{56,120},{... | collective-permute-start | bytes 396296 | tf_op jit(solution)/shard_map/ppermute | solution.py:27
  79.7 12.0 %collective-permute-start.31 = (bf16[24,2752]{1,0:T(8,128)(2,1)S(1)}, bf16[24,2752]{1,0:T(8,128)(2,1)S(1)}, u32[]{:S(2)}, u32[]{:S(2)}) collective-permute-start(bf16[24,2752]{1,0:T(8,128)(2,1)S(1)} %get-tuple-element.23), channel_id=1, source_target_pairs={{0,96},{8,104},{16,112},{24,120},{32,0},{40,8},{48,16},{56,24},{64... | collective-permute-start | bytes 396296 | tf_op jit(solution)/shard_map/ppermute | solution.py:27
  82.8 9.2 %collective-permute-start.30 = (bf16[24,2752]{1,0:T(8,128)(2,1)S(1)}, bf16[24,2752]{1,0:T(8,128)(2,1)S(1)}, u32[]{:S(2)}, u32[]{:S(2)}) collective-permute-start(bf16[24,2752]{1,0:T(8,128)(2,1)S(1)} %get-tuple-element.21), channel_id=1, source_target_pairs={{0,32},{8,40},{16,48},{24,56},{32,64},{40,72},{48,80},{56,88},{64,... | collective-permute-start | bytes 396296 | tf_op jit(solution)/shard_map/ppermute | solution.py:27
  83.1 5.5 %collective-permute-start.13 = (bf16[24,3136]{1,0:T(8,128)(2,1)S(1)}, bf16[24,3136]{1,0:T(8,128)(2,1)S(1)}, u32[]{:S(2)}, u32[]{:S(2)}) collective-permute-start(bf16[24,3136]{1,0:T(8,128)(2,1)S(1)} %fusion.60), channel_id=1, source_target_pairs={{0,16},{8,24},{16,0},{24,8},{32,48},{40,56},{48,32},{56,40},{64,80... | collective-permute-start | bytes 451592 | tf_op jit(solution)/shard_map/ppermute | solution.py:27
  83.4 9.5 %collective-permute-start.4 = (bf16[24,2752]{1,0:T(8,128)(2,1)S(1)}, bf16[24,2752]{1,0:T(8,128)(2,1)S(1)}, u32[]{:S(2)}, u32[]{:S(2)}) collective-permute-start(bf16[24,2752]{1,0:T(8,128)(2,1)S(1)} %get-tuple-element.25), channel_id=1, source_target_pairs={{0,64},{8,72},{16,80},{24,88},{32,96},{40,104},{48,112},{56,120},{... | collective-permute-start | bytes 396296 | tf_op jit(solution)/shard_map/ppermute | solution.py:27
  88.6 5.5 %collective-permute-start.3 = (bf16[24,2752]{1,0:T(8,128)(2,1)S(1)}, bf16[24,2752]{1,0:T(8,128)(2,1)S(1)}, u32[]{:S(2)}, u32[]{:S(2)}) collective-permute-start(bf16[24,2752]{1,0:T(8,128)(2,1)S(1)} %get-tuple-element.26), channel_id=1, source_target_pairs={{0,96},{8,104},{16,112},{24,120},{32,0},{40,8},{48,16},{56,24},{64... | collective-permute-start | bytes 396296 | tf_op jit(solution)/shard_map/ppermute | solution.py:27
  91.6 6.3 %collective-permute-start.2 = (bf16[24,2752]{1,0:T(8,128)(2,1)S(1)}, bf16[24,2752]{1,0:T(8,128)(2,1)S(1)}, u32[]{:S(2)}, u32[]{:S(2)}) collective-permute-start(bf16[24,2752]{1,0:T(8,128)(2,1)S(1)} %get-tuple-element.24), channel_id=1, source_target_pairs={{0,32},{8,40},{16,48},{24,56},{32,64},{40,72},{48,80},{56,88},{64,... | collective-permute-start | bytes 396296 | tf_op jit(solution)/shard_map/ppermute | solution.py:27
  98.4 5.1 %collective-permute-start.19 = (bf16[24,2752]{1,0:T(8,128)(2,1)S(1)}, bf16[24,2752]{1,0:T(8,128)(2,1)S(1)}, u32[]{:S(2)}, u32[]{:S(2)}) collective-permute-start(bf16[24,2752]{1,0:T(8,128)(2,1)S(1)} %get-tuple-element.17), channel_id=1, source_target_pairs={{0,16},{8,24},{16,0},{24,8},{32,48},{40,56},{48,32},{56,40},{64,80... | collective-permute-start | bytes 396296 | tf_op jit(solution)/shard_map/ppermute | solution.py:27
  98.8 21.0 %collective-permute-start.35 = (bf16[24,2752]{1,0:T(8,128)(2,1)S(1)}, bf16[24,2752]{1,0:T(8,128)(2,1)S(1)}, u32[]{:S(2)}, u32[]{:S(2)}) collective-permute-start(bf16[24,2752]{1,0:T(8,128)(2,1)S(1)} %get-tuple-element.16), channel_id=1, source_target_pairs={{0,32},{8,40},{16,48},{24,56},{32,64},{40,72},{48,80},{56,88},{64,... | collective-permute-start | bytes 396296 | tf_op jit(solution)/shard_map/ppermute | solution.py:27
  98.8 23.8 %collective-permute-start.34 = (bf16[24,2752]{1,0:T(8,128)(2,1)S(1)}, bf16[24,2752]{1,0:T(8,128)(2,1)S(1)}, u32[]{:S(2)}, u32[]{:S(2)}) collective-permute-start(bf16[24,2752]{1,0:T(8,128)(2,1)S(1)} %get-tuple-element.16), channel_id=1, source_target_pairs={{0,64},{8,72},{16,80},{24,88},{32,96},{40,104},{48,112},{56,120},{... | collective-permute-start | bytes 396296 | tf_op jit(solution)/shard_map/ppermute | solution.py:27
  100.2 5.2 %collective-permute-start.38 = (bf16[24,2752]{1,0:T(8,128)(2,1)S(1)}, bf16[24,2752]{1,0:T(8,128)(2,1)S(1)}, u32[]{:S(2)}, u32[]{:S(2)}) collective-permute-start(bf16[24,2752]{1,0:T(8,128)(2,1)S(1)} %get-tuple-element.20), channel_id=1, source_target_pairs={{0,16},{8,24},{16,0},{24,8},{32,48},{40,56},{48,32},{56,40},{64,80... | collective-permute-start | bytes 396296 | tf_op jit(solution)/shard_map/ppermute | solution.py:27
  103.6 14.0 %collective-permute-start.22 = (bf16[2,24,2752]{2,1,0:T(8,128)(2,1)S(1)}, bf16[2,24,2752]{2,1,0:T(8,128)(2,1)S(1)}, u32[]{:S(2)}, u32[]{:S(2)}) collective-permute-start(bf16[2,24,2752]{2,1,0:T(8,128)(2,1)S(1)} %get-tuple-element.38), channel_id=1, source_target_pairs={{0,32},{8,40},{16,48},{24,56},{32,64},{40,72},{48,80},{56,88},{64,... | collective-permute-start | bytes 792584 | tf_op jit(solution)/shard_map/ppermute | solution.py:27
  104.8 12.8 %collective-permute-start.21 = (bf16[2,24,2752]{2,1,0:T(8,128)(2,1)S(1)}, bf16[2,24,2752]{2,1,0:T(8,128)(2,1)S(1)}, u32[]{:S(2)}, u32[]{:S(2)}) collective-permute-start(bf16[2,24,2752]{2,1,0:T(8,128)(2,1)S(1)} %get-tuple-element.38), channel_id=1, source_target_pairs={{0,64},{8,72},{16,80},{24,88},{32,96},{40,104},{48,112},{56,120},{... | collective-permute-start | bytes 792584 | tf_op jit(solution)/shard_map/ppermute | solution.py:27
  105.4 14.2 %collective-permute-start.20 = (bf16[2,24,2752]{2,1,0:T(8,128)(2,1)S(1)}, bf16[2,24,2752]{2,1,0:T(8,128)(2,1)S(1)}, u32[]{:S(2)}, u32[]{:S(2)}) collective-permute-start(bf16[2,24,2752]{2,1,0:T(8,128)(2,1)S(1)} %get-tuple-element.38), channel_id=1, source_target_pairs={{0,96},{8,104},{16,112},{24,120},{32,0},{40,8},{48,16},{56,24},{64... | collective-permute-start | bytes 792584 | tf_op jit(solution)/shard_map/ppermute | solution.py:27
  117.6 6.9 %collective-permute-start.33 = (bf16[24,2752]{1,0:T(8,128)(2,1)S(1)}, bf16[24,2752]{1,0:T(8,128)(2,1)S(1)}, u32[]{:S(2)}, u32[]{:S(2)}) collective-permute-start(bf16[24,2752]{1,0:T(8,128)(2,1)S(1)} %get-tuple-element.16), channel_id=1, source_target_pairs={{0,96},{8,104},{16,112},{24,120},{32,0},{40,8},{48,16},{56,24},{64... | collective-permute-start | bytes 396296 | tf_op jit(solution)/shard_map/ppermute | solution.py:27
  117.6 11.5 %collective-permute-start.41 = (bf16[2,24,2752]{2,1,0:T(8,128)(2,1)S(1)}, bf16[2,24,2752]{2,1,0:T(8,128)(2,1)S(1)}, u32[]{:S(2)}, u32[]{:S(2)}) collective-permute-start(bf16[2,24,2752]{2,1,0:T(8,128)(2,1)S(1)} %get-tuple-element.36), channel_id=1, source_target_pairs={{0,32},{8,40},{16,48},{24,56},{32,64},{40,72},{48,80},{56,88},{64,... | collective-permute-start | bytes 792584 | tf_op jit(solution)/shard_map/ppermute | solution.py:27
  119.6 9.4 %collective-permute-start.40 = (bf16[2,24,2752]{2,1,0:T(8,128)(2,1)S(1)}, bf16[2,24,2752]{2,1,0:T(8,128)(2,1)S(1)}, u32[]{:S(2)}, u32[]{:S(2)}) collective-permute-start(bf16[2,24,2752]{2,1,0:T(8,128)(2,1)S(1)} %get-tuple-element.36), channel_id=1, source_target_pairs={{0,64},{8,72},{16,80},{24,88},{32,96},{40,104},{48,112},{56,120},{... | collective-permute-start | bytes 792584 | tf_op jit(solution)/shard_map/ppermute | solution.py:27
  119.8 12.5 %collective-permute-start.39 = (bf16[2,24,2752]{2,1,0:T(8,128)(2,1)S(1)}, bf16[2,24,2752]{2,1,0:T(8,128)(2,1)S(1)}, u32[]{:S(2)}, u32[]{:S(2)}) collective-permute-start(bf16[2,24,2752]{2,1,0:T(8,128)(2,1)S(1)} %get-tuple-element.36), channel_id=1, source_target_pairs={{0,96},{8,104},{16,112},{24,120},{32,0},{40,8},{48,16},{56,24},{64... | collective-permute-start | bytes 792584 | tf_op jit(solution)/shard_map/ppermute | solution.py:27
  122.6 16.0 %collective-permute-start.23 = (bf16[192,2752]{1,0:T(8,128)(2,1)S(1)}, bf16[192,2752]{1,0:T(8,128)(2,1)}, u32[]{:S(2)}, u32[]{:S(2)}) collective-permute-start(bf16[192,2752]{1,0:T(8,128)(2,1)S(1)} %bitcast.165), channel_id=1, source_target_pairs={{0,8},{8,0},{16,24},{24,16},{32,40},{40,32},{48,56},{56,48},{64,72... | collective-permute-start | bytes 3170312 | tf_op jit(solution)/shard_map/ppermute | solution.py:27
  124.6 12.9 %collective-permute-start.36 = (bf16[4,24,2752]{2,1,0:T(8,128)(2,1)S(1)}, bf16[4,24,2752]{2,1,0:T(8,128)(2,1)S(1)}, u32[]{:S(2)}, u32[]{:S(2)}) collective-permute-start(bf16[4,24,2752]{2,1,0:T(8,128)(2,1)S(1)} %get-tuple-element.19), channel_id=1, source_target_pairs={{0,16},{8,24},{16,0},{24,8},{32,48},{40,56},{48,32},{56,40},{64,80... | collective-permute-start | bytes 1585160 | tf_op jit(solution)/shard_map/ppermute | solution.py:27
  133.4 15.5 %collective-permute-start.42 = (bf16[192,2752]{1,0:T(8,128)(2,1)}, bf16[192,2752]{1,0:T(8,128)(2,1)}, u32[]{:S(2)}, u32[]{:S(2)}) collective-permute-start(bf16[192,2752]{1,0:T(8,128)(2,1)} %bitcast.63), channel_id=1, source_target_pairs={{0,8},{8,0},{16,24},{24,16},{32,40},{40,32},{48,56},{56,48},{64,72... | collective-permute-start | bytes 3170312 | tf_op jit(solution)/shard_map/ppermute | solution.py:27
  138.6 33.5 %collective-permute-start.37 = (bf16[192,2752]{1,0:T(8,128)(2,1)}, bf16[192,2752]{1,0:T(8,128)(2,1)}, u32[]{:S(2)}, u32[]{:S(2)}) collective-permute-start(bf16[192,2752]{1,0:T(8,128)(2,1)} %bitcast.56), channel_id=1, source_target_pairs={{0,8},{8,0},{16,24},{24,16},{32,40},{40,32},{48,56},{56,48},{64,72... | collective-permute-start | bytes 3170312 | tf_op jit(solution)/shard_map/ppermute | solution.py:27
  148.2 18.6 %collective-permute-start.24 = (bf16[4,48,512]{2,1,0:T(8,128)(2,1)}, bf16[4,48,512]{2,1,0:T(8,128)(2,1)}, u32[]{:S(2)}, u32[]{:S(2)}) collective-permute-start(bf16[4,48,512]{2,1,0:T(8,128)(2,1)} %bitcast.38), channel_id=1, source_target_pairs={{0,4},{1,5},{2,6},{3,7},{4,0},{5,1},{6,2},{7,3},{8,12},{9,13},{10,... | collective-permute-start | bytes 589832 | tf_op jit(solution)/shard_map/ppermute | solution.py:35
  168.6 16.3 %collective-permute-start.27 = (bf16[48,512]{1,0:T(8,128)(2,1)S(1)}, bf16[48,512]{1,0:T(8,128)(2,1)S(1)}, u32[]{:S(2)}, u32[]{:S(2)}) collective-permute-start(bf16[48,512]{1,0:T(8,128)(2,1)S(1)} %get-tuple-element.45), channel_id=1, source_target_pairs={{0,2},{1,3},{2,0},{3,1},{4,6},{5,7},{6,4},{7,5},{8,10},{9,11},{10,... | collective-permute-start | bytes 147464 | tf_op jit(solution)/shard_map/ppermute | solution.py:35
  169.3 15.6 %collective-permute-start.26 = (bf16[48,512]{1,0:T(8,128)(2,1)S(1)}, bf16[48,512]{1,0:T(8,128)(2,1)S(1)}, u32[]{:S(2)}, u32[]{:S(2)}) collective-permute-start(bf16[48,512]{1,0:T(8,128)(2,1)S(1)} %get-tuple-element.46), channel_id=1, source_target_pairs={{0,3},{1,0},{2,1},{3,2},{4,7},{5,4},{6,5},{7,6},{8,11},{9,8},{10,9... | collective-permute-start | bytes 147464 | tf_op jit(solution)/shard_map/ppermute | solution.py:35
  172.1 12.8 %collective-permute-start.25 = (bf16[48,512]{1,0:T(8,128)(2,1)S(1)}, bf16[48,512]{1,0:T(8,128)(2,1)S(1)}, u32[]{:S(2)}, u32[]{:S(2)}) collective-permute-start(bf16[48,512]{1,0:T(8,128)(2,1)S(1)} %get-tuple-element.44), channel_id=1, source_target_pairs={{0,1},{1,2},{2,3},{3,0},{4,5},{5,6},{6,7},{7,4},{8,9},{9,10},{10,1... | collective-permute-start | bytes 147464 | tf_op jit(solution)/shard_map/ppermute | solution.py:35
  182.0 8.0 %collective-permute-start.43 = (bf16[4,48,512]{2,1,0:T(8,128)(2,1)S(1)}, bf16[4,48,512]{2,1,0:T(8,128)(2,1)S(1)}, u32[]{:S(2)}, u32[]{:S(2)}) collective-permute-start(bf16[4,48,512]{2,1,0:T(8,128)(2,1)S(1)} %bitcast.183), channel_id=1, source_target_pairs={{0,4},{1,5},{2,6},{3,7},{4,0},{5,1},{6,2},{7,3},{8,12},{9,13},{10,... | collective-permute-start | bytes 589832 | tf_op jit(solution)/shard_map/ppermute | solution.py:35
  190.2 9.1 %collective-permute-start.46 = (bf16[48,512]{1,0:T(8,128)(2,1)S(1)}, bf16[48,512]{1,0:T(8,128)(2,1)S(1)}, u32[]{:S(2)}, u32[]{:S(2)}) collective-permute-start(bf16[48,512]{1,0:T(8,128)(2,1)S(1)} %get-tuple-element.42), channel_id=1, source_target_pairs={{0,2},{1,3},{2,0},{3,1},{4,6},{5,7},{6,4},{7,5},{8,10},{9,11},{10,... | collective-permute-start | bytes 147464 | tf_op jit(solution)/shard_map/ppermute | solution.py:35
  192.2 7.2 %collective-permute-start.45 = (bf16[48,512]{1,0:T(8,128)(2,1)S(1)}, bf16[48,512]{1,0:T(8,128)(2,1)S(1)}, u32[]{:S(2)}, u32[]{:S(2)}) collective-permute-start(bf16[48,512]{1,0:T(8,128)(2,1)S(1)} %get-tuple-element.43), channel_id=1, source_target_pairs={{0,3},{1,0},{2,1},{3,2},{4,7},{5,4},{6,5},{7,6},{8,11},{9,8},{10,9... | collective-permute-start | bytes 147464 | tf_op jit(solution)/shard_map/ppermute | solution.py:35
  194.5 5.3 %collective-permute-start.44 = (bf16[48,512]{1,0:T(8,128)(2,1)S(1)}, bf16[48,512]{1,0:T(8,128)(2,1)S(1)}, u32[]{:S(2)}, u32[]{:S(2)}) collective-permute-start(bf16[48,512]{1,0:T(8,128)(2,1)S(1)} %get-tuple-element.41), channel_id=1, source_target_pairs={{0,1},{1,2},{2,3},{3,0},{4,5},{5,6},{6,7},{7,4},{8,9},{9,10},{10,1... | collective-permute-start | bytes 147464 | tf_op jit(solution)/shard_map/ppermute | solution.py:35
  (22 other events, 102.7 us)

commit v2 on v1

v2 whole, which is shorter than its diff:
```python
import jax
import jax.numpy as jnp
from jax import lax
from jax.experimental import pallas as pl
from jax.experimental.pallas import tpu as pltpu
from jax.sharding import PartitionSpec as P

BF = jnp.bfloat16
F32 = jnp.float32
ROWS = 24
HALF = 192
CHUNK = 512
RANK = 128
LIMIT = 48 * 1024 * 1024

NN = ((1,), (0,))
NT = ((1,), (1,))
TN = ((0,), (0,))


def dot(a, b, dims):
    return lax.dot_general(a, b, (dims, ((), ())), preferred_element_type=F32)


def after(x, *others):
    return lax.optimization_barrier((x,) + others)[0]


def chunks(n):
    return [(at, min(CHUNK, n - at)) for at in range(0, n, CHUNK)]


def pick(index_ref, size):
    return (index_ref[...] == lax.broadcasted_iota(jnp.int32, (size, size), 1)).astype(BF)


VMEM = pl.BlockSpec(memory_space=pltpu.VMEM)
ANY = pl.BlockSpec(memory_space=pl.ANY)


def forward(x, weight, index=None, lefts=None):
    n = weight.shape[0]
    low = 0 if lefts is None else lefts.shape[0]
    size, depth = x.shape

    def body(*refs):
        refs = list(refs)
        x_ref = refs.pop(0)
        index_ref = None if index is None else refs.pop(0)
        left_ref = None if lefts is None else refs.pop(0)
        w_hbm = refs.pop(0)
        mine_ref, theirs_ref = refs.pop(0), refs.pop(0)
        turned_ref = None if index is None else refs.pop(0)
        w_ref, sems = refs
        copies = []
        for k, (at, wide) in enumerate(chunks(n)):
            part = pl.ds(at, wide)
            copies.append(pltpu.make_async_copy(w_hbm.at[part, :], w_ref.at[part, :], sems.at[k]))
            copies[-1].start()
        if index is None:
            value = x_ref[...]
        else:
            value = dot(pick(index_ref, size), x_ref[...], NN).astype(BF)
            turned_ref[...] = value
        if lefts is not None:
            got = dot(value, left_ref[...], NT)
            mine_ref[:, :low] = got[:HALF]
            theirs_ref[:, :low] = got[HALF:].astype(BF)
        for copy, (at, wide) in zip(copies, chunks(n)):
            copy.wait()
            got = dot(value, w_ref[at : at + wide, :], NT)
            mine_ref[:, low + at : low + at + wide] = got[:HALF]
            theirs_ref[:, low + at : low + at + wide] = got[HALF:].astype(BF)

    args, specs = [x], [VMEM]
    if index is not None:
        args.append(index)
        specs.append(VMEM)
    if lefts is not None:
        args.append(lefts)
        specs.append(VMEM)
    out = [jax.ShapeDtypeStruct((HALF, low + n), F32), jax.ShapeDtypeStruct((HALF, low + n), BF)]
    if index is not None:
        out.append(jax.ShapeDtypeStruct((size, depth), BF))
    return pl.pallas_call(
        body,
        out_shape=out,
        in_specs=specs + [ANY],
        out_specs=[VMEM] * len(out),
        scratch_shapes=[pltpu.VMEM((n, depth), BF), pltpu.SemaphoreType.DMA((len(chunks(n)),))],
        compiler_params=pltpu.CompilerParams(vmem_limit_bytes=LIMIT),
        name="forward",
    )(*args, weight)


def backward(mine, other, x, weight, rights, lefts, place, partial=None, index=None):
    n, depth = weight.shape
    size = 2 * HALF
    padded = rights.shape[1] // 3

    def body(*refs):
        refs = list(refs)
        mine_ref, other_ref, x_ref, right_ref, left_ref = refs[:5]
        refs = refs[5:]
        partial_ref = None if partial is None else refs.pop(0)
        index_ref = None if index is None else refs.pop(0)
        w_hbm, out_ref, grad_hbm, w_ref, grad_ref, w_sems, sems = refs
        copies = []
        for k, (at, wide) in enumerate(chunks(n)):
            part = pl.ds(at, wide)
            copies.append(pltpu.make_async_copy(w_hbm.at[part, :], w_ref.at[part, :], w_sems.at[k]))
            copies[-1].start()
        total = jnp.zeros((size, depth), F32) if partial is None else partial_ref[...]
        low = jnp.zeros((size, RANK), F32)
        x_all = x_ref[...]
        sent = []
        for k, (at, wide) in enumerate(chunks(n)):
            part = pl.ds(at, wide)
            value = jnp.concatenate([mine_ref[:, at : at + wide], other_ref[:, at : at + wide]], axis=0)
            grad_ref[at : at + wide, :] = dot(value, x_all, TN).astype(BF)
            sent.append(pltpu.make_async_copy(grad_ref.at[part, :], grad_hbm.at[part, :], sems.at[k]))
            sent[-1].start()
            low = low + dot(value, right_ref[:, at : at + wide], NT)
            copies[k].wait()
            total = total + dot(value, w_ref[at : at + wide, :], NN)
        total = total + dot(low.astype(BF), left_ref[...], NN)
        if index is None:
            out_ref[...] = total
        else:
            out_ref[...] = dot(pick(index_ref, size), total.astype(BF), NN).astype(BF)
        for copy in sent:
            copy.wait()

    args, specs = [mine, other, x, rights, lefts], [
        VMEM,
        VMEM,
        VMEM,
        pl.BlockSpec((RANK, padded), lambda i: (0, place)),
        pl.BlockSpec((RANK, depth), lambda i: (place, 0)),
    ]
    if partial is not None:
        args.append(partial)
        specs.append(VMEM)
    if index is not None:
        args.append(index)
        specs.append(VMEM)
    count = len(chunks(n))
    return pl.pallas_call(
        body,
        grid=(1,),
        out_shape=[
            jax.ShapeDtypeStruct((size, depth), F32 if index is None else BF),
            jax.ShapeDtypeStruct((n, depth), BF),
        ],
        in_specs=specs + [ANY],
        out_specs=[VMEM, ANY],
        scratch_shapes=[
            pltpu.VMEM((n, depth), BF),
            pltpu.VMEM((n, depth), BF),
            pltpu.SemaphoreType.DMA((count,)),
            pltpu.SemaphoreType.DMA((count,)),
        ],
        compiler_params=pltpu.CompilerParams(vmem_limit_bytes=LIMIT),
        name="backward",
    )(*args, weight)


def row_send(x, dz, da, dc):
    pairs = []
    for z in range(4):
        for a in range(2):
            for c in range(2):
                to = ((z + dz) % 4) * 4 + ((a + da) % 2) * 2 + (c + dc) % 2
                pairs.append((z * 4 + a * 2 + c, to))
    return lax.ppermute(x, "row", pairs)


def col_send(x, dh, dy):
    pairs = []
    for h in range(2):
        for y in range(4):
            pairs.append((h * 4 + y, ((h + dh) % 2) * 4 + (y + dy) % 4))
    return lax.ppermute(x, "col", pairs)


def pair_sum(mine, theirs):
    return (mine + row_send(theirs, 0, 0, 1).astype(F32)).reshape(4, 2, ROWS, -1)


def row_reduce(total, z_first):
    if z_first:
        own = total[0]
        parts = [row_send(total[d].astype(BF), d, 0, 0) for d in (1, 3, 2)]
        for p in parts:
            own = own + p.astype(F32)
        return own[0] + row_send(own[1].astype(BF), 0, 1, 0).astype(F32)
    own = total[:, 0] + row_send(total[:, 1].astype(BF), 0, 1, 0).astype(F32)
    parts = [row_send(own[d].astype(BF), d, 0, 0) for d in (1, 3, 2)]
    own = own[0]
    for p in parts:
        own = own + p.astype(F32)
    return own


def row_gather(x, z_last):
    rows, n = x.shape
    if z_last:
        pair = jnp.stack([x, row_send(x, 0, 1, 0)])
        got = {d: row_send(pair, d, 0, 0) for d in (1, 3, 2)}
        half = jnp.stack([pair, got[3], got[2], got[1]])
    else:
        got = {d: row_send(x, d, 0, 0) for d in (1, 3, 2)}
        four = jnp.stack([x, got[3], got[2], got[1]])
        half = jnp.stack([four, row_send(four, 0, 1, 0)], axis=1)
    half = half.reshape(8 * rows, n)
    return half, row_send(half, 0, 0, 1)


def col_reduce(spread):
    spread = spread.reshape(2, 4, 48, -1)
    own = spread[0].astype(F32) + col_send(spread[1], 1, 0).astype(F32)
    parts = [col_send(own[d].astype(BF), 0, d) for d in (1, 3, 2)]
    own = own[0]
    for p in parts:
        own = own + p.astype(F32)
    return own.astype(BF)


def shards(
    tokens,
    grad_out,
    gate_weight,
    up_weight,
    down_weight,
    gate_left,
    up_left,
    down_left,
    gate_right,
    up_right,
    down_right,
):
    n = gate_weight.shape[1]
    row, col = lax.axis_index("row"), lax.axis_index("col")
    z, a, c = row // 4, (row // 2) % 2, row % 2
    h, y = col // 4, col % 4

    k = jnp.arange(2 * HALF, dtype=jnp.int32)
    block = k // ROWS
    dc, dz, da = block // 8, (block // 2) % 4, block % 2
    held = ((((c + dc) % 2) * 4 + (z + dz) % 4) * 2 + (a + da) % 2) * ROWS + k % ROWS
    dest = (((h + k // 192) % 2) * 4 + (y + k // 48) % 4) * 48 + k % 48
    block = dest // ROWS
    dc, dz, da = (block // 8 - c) % 2, ((block // 2) % 4 - z) % 4, (block % 2 - a) % 2
    leave = ((dc * 4 + dz) * 2 + da) * ROWS + dest % ROWS
    held, leave = held[:, None], leave[:, None]
    my, mh, mt, mi = k // 96, (k // 48) % 2, (k // 16) % 3, k % 16
    rank = (((h - mh) % 2) * 4 + (y - my) % 4) * 16 + mi + RANK * mt
    match = (rank[None, :] == k[:, None]).astype(BF)

    edge = jnp.zeros((gate_right.shape[0], -n % 128), BF)
    rights = jnp.concatenate([gate_right, edge, up_right, edge, down_right, edge], axis=1)
    rights = lax.all_gather(rights, "row", axis=0, tiled=True)
    wide = rights.shape[1] // 3

    gate_w, up_w, down_w = gate_weight.T, up_weight.T, down_weight.T
    gate_mine, gate_theirs, tok = forward(tokens, gate_w, index=held)

    lefts = jnp.concatenate([gate_left.T, up_left.T, down_left.T], axis=0)
    lefts = jnp.stack([lefts, col_send(lefts, 1, 0)])
    gate_sum = pair_sum(gate_mine, gate_theirs)
    lefts = after(lefts, gate_sum)
    lefts = jnp.stack([lefts] + [col_send(lefts, 0, d) for d in (1, 2, 3)])
    lefts = dot(match, lefts.reshape(3 * RANK, -1), NN).astype(BF)

    gate_rows = row_reduce(gate_sum, False)
    up_mine, up_theirs = forward(tok, up_w, lefts=lefts[: 2 * RANK])
    back_mine, back_theirs, out = forward(
        after(grad_out, up_theirs), down_w, index=held, lefts=lefts[2 * RANK :]
    )
    up_rows = row_reduce(pair_sum(up_mine, up_theirs), True)
    back_rows = row_reduce(pair_sum(back_mine, back_theirs), False)

    low_g, low_u = up_rows[:, :RANK].astype(BF), up_rows[:, RANK : 2 * RANK].astype(BF)
    low_d = back_rows[:, :RANK].astype(BF)
    gate = gate_rows + dot(low_g, rights[:, :n], NN)
    up = up_rows[:, 2 * RANK :] + dot(low_u, rights[:, wide : wide + n], NN)
    hidden = (gate * jax.nn.sigmoid(gate) * up).astype(BF)
    gate, up, back_rows, _ = lax.optimization_barrier((gate, up, back_rows, hidden))
    hidden = row_gather(hidden, True)

    back = back_rows[:, RANK:] + dot(low_d, rights[:, 2 * wide : 2 * wide + n], NN)
    sigma = jax.nn.sigmoid(gate)
    gate_delta = (back * up * sigma * (1.0 + gate * (1.0 - sigma))).astype(BF)
    up_delta = (back * gate * sigma).astype(BF)
    gate_delta = row_gather(gate_delta, False)
    up_delta = row_gather(up_delta, True)

    mixed, down_grad = backward(*hidden, out, down_w, rights, lefts, 2, index=leave)
    mixed = col_reduce(mixed)
    partial, gate_grad = backward(*gate_delta, tok, gate_w, rights, lefts, 0)
    input_grad, up_grad = backward(*up_delta, tok, up_w, rights, lefts, 1, partial=partial, index=leave)
    input_grad = col_reduce(input_grad)
    return mixed, input_grad, gate_grad.T, up_grad.T, down_grad.T


def solution(mesh):
    arg = P("row", "col")
    in_specs = (P(None, "row"), P(None, "row")) + (arg,) * 9
    out_specs = (P("col", "row"), P("col", "row")) + (arg,) * 3
    return jax.shard_map(shards, mesh=mesh, in_specs=in_specs, out_specs=out_specs, check_vma=False)
```

time: 201 us -> 184 us (0.915)
  matrix products: 63.1 us -> 3.4 us
  Pallas kernels: 0 us -> 31.2 us
  between operations: 1.2 us -> 14.6 us
  other arithmetic: 14.5 us -> 6.46 us
  starting transfers between devices: 55.7 us -> 63.1 us
  local copies, waits for them, and re-layouts: 8.18 us -> 2.26 us
  waiting for transfers between devices: 57.7 us -> 61.2 us
    dot_general x24 -> x4, matrix products: 63.1 us -> 3.4 us  [dot(): return lax.dot_general(a, b, (dims, ((), ())), preferred_element_type=F32)]
    pallas_call x0 -> x6, Pallas kernels: none -> 31.2 us  [the longest x3 19.3 us: backward(): pl.pallas_call(body, grid=(1,), out_shape=[jax.ShapeDtypeStruct((size, de...]
    ppermute x12, waiting for transfers between devices: 6.92 us -> 14.4 us  [col_send(): return lax.ppermute(x, 'col', pairs)]
    ppermute x12, starting transfers between devices: 18.9 us -> 25.2 us  [col_send(): return lax.ppermute(x, 'col', pairs)]
    ppermute x35 -> x30, waiting for transfers between devices: 50.8 us -> 46.7 us  [row_send(): return lax.ppermute(x, 'row', pairs)]
    another operation x6 -> x4, other arithmetic: 3.59 us -> 0.36 us  [row_gather(): half = jnp.stack([pair, got[3], got[2], got[1]])]
    concatenate x2 -> x0, other arithmetic: 3.2 us -> none  [the longest x1 2.41 us: shards(): jnp.concatenate([low[192:].astype(BF), up_theirs], axis=1)]
    add x4 -> x5, other arithmetic: 0.61 us -> 3.39 us  [the longest x2 1.66 us: pair_sum(): mine + row_send(theirs, 0, 0, 1).astype(F32)]
  transfers between devices with their start and end apart: 47 -> 43, of which waited for: 18 -> 17; matrix products, arithmetic and copies ran while one was open for 39% -> 4% of each run, Pallas kernels for 0% -> 11%
where the time goes in v2:
time: 184 us; the launch traced here: 182 us
  starting transfers between devices  63.1 us (34%)
  waiting for transfers between devices  61.2 us (33%)
  Pallas kernels  31.2 us (17%)
  between operations  14.6 us (8%)
  other arithmetic  6.46 us (4%)
  matrix products  3.4 us (2%)
  local copies, waits for them, and re-layouts  2.26 us (1%)
    ppermute x30, waiting for transfers between devices, row_send(): return lax.ppermute(x, 'row', pairs)  46.7 us
    ppermute x30, starting transfers between devices, row_send(): return lax.ppermute(x, 'row', pairs)  37.9 us
    ppermute x12, starting transfers between devices, col_send(): return lax.ppermute(x, 'col', pairs)  25.2 us
    pallas_call x3, Pallas kernels, backward(): pl.pallas_call(body, grid=(1,), out_shape=[jax.ShapeDtypeStruct((size, de...  19.3 us
    ppermute x12, waiting for transfers between devices, col_send(): return lax.ppermute(x, 'col', pairs)  14.4 us
    pallas_call x3, Pallas kernels, forward(): pl.pallas_call(body, out_shape=out, in_specs=specs + [ANY], out_specs=[VM...  12 us
  transfers between devices with their start and end apart: 43, of which 17 were waited for; matrix products, arithmetic and copies ran while one was open for 4% of the time, Pallas kernels for 11%

profile of v2, /device:TPU:0, one launch (start us, length us, event | category | flops | bytes accessed | tf_op | source)
XLA Modules:
  0.0 182.1 jit_solution(5462503695548101681)
XLA Ops:
  9.0 4.5 %forward.3 = (f32[192,2752]{1,0:T(8,128)S(1)}, bf16[192,2752]{1,0:T(8,128)(2,1)}, bf16[384,512]{1,0:T(8,128)(2,1)S(1)}) custom-call(bf16[384,512]{1,0:T(8,128)(2,1)S(1)} %copy-done.2, s32[384,1]{1,0:T(8,128)S(1)} %fusion.38.refs_1_, bf16[2752,512]{1,0:T(8,128)(2,1)} %bitcast.147), custom_call_target="tpu_custom_call" | custom-call | tf_op jit(solution)/shard_map/forward/pallas_call | solution.py:85
  13.6 3.2 %collective-permute-start.5 = (bf16[48,512]{1,0:T(8,128)(2,1)S(1)}, bf16[48,512]{1,0:T(8,128)(2,1)S(1)}, u32[]{:S(2)}, u32[]{:S(2)}) collective-permute-start(bf16[48,512]{1,0:T(8,128)(2,1)S(1)} %get-tuple-element.83), channel_id=1, source_target_pairs={{0,4},{1,5},{2,6},{3,7},{4,0},{5,1},{6,2},{7,3},{8,12},{9,13},{10,... | collective-permute-start | bytes 147464 | tf_op jit(solution)/shard_map/ppermute | solution.py:183
  17.6 1.4 convert_add_fusion.2
  19.8 1.6 collective-permute-start.6
  21.5 2.9 %collective-permute-start.7 = (bf16[2,48,512]{2,1,0:T(8,128)(2,1)S(1)}, bf16[2,48,512]{2,1,0:T(8,128)(2,1)S(1)}, u32[]{:S(2)}, u32[]{:S(2)}) collective-permute-start(bf16[2,48,512]{2,1,0:T(8,128)(2,1)S(1)} %pad_maximum_fusion.7), channel_id=1, source_target_pairs={{0,2},{1,3},{2,0},{3,1},{4,6},{5,7},{6,4},{7,5},{8,10},{9,11},{10,... | collective-permute-start | bytes 294920 | tf_op jit(solution)/shard_map/ppermute | solution.py:183
  24.4 1.3 collective-permute-start.8
  25.8 3.3 %collective-permute-done.7 = bf16[2,48,512]{2,1,0:T(8,128)(2,1)S(1)} collective-permute-done((bf16[2,48,512]{2,1,0:T(8,128)(2,1)S(1)}, bf16[2,48,512]{2,1,0:T(8,128)(2,1)S(1)}, u32[]{:S(2)}, u32[]{:S(2)}) %collective-permute-start.7) | collective-permute-done | bytes 98336 | tf_op jit(solution)/shard_map/ppermute | solution.py:183
  29.5 3.5 %forward.4 = (f32[192,3008]{1,0:T(8,128)S(1)}, bf16[192,3008]{1,0:T(8,128)(2,1)S(1)}) custom-call(bf16[384,512]{1,0:T(8,128)(2,1)S(1)} %get-tuple-element.26.refs_0_.refs_2_, bf16[256,512]{1,0:T(8,128)(2,1)S(1)} %slice.195.refs_1_, bf16[2752,512]{1,0:T(8,128)(2,1)} %bitcast.145), custom_call_target="tpu_custom_call" | custom-call | tf_op jit(solution)/shard_map/forward/pallas_call | solution.py:85
  33.2 3.9 %forward.5 = (f32[192,2880]{1,0:T(8,128)S(1)}, bf16[192,2880]{1,0:T(8,128)(2,1)S(1)}, bf16[384,512]{1,0:T(8,128)(2,1)S(1)}) custom-call(bf16[384,512]{1,0:T(8,128)(2,1)S(1)} %copy-done.1, s32[384,1]{1,0:T(8,128)S(1)} %fusion.38.refs_1_, bf16[128,512]{1,0:T(8,128)(2,1)S(1)} %slice.207.refs_2_, bf16[2752,512]{1,0:T(8,128)(2,1)} %bitcast.143), custom_call_target="tpu_custom_call" | custom-call | tf_op jit(solution)/shard_map/forward/pallas_call | solution.py:85
  37.8 2.0 %collective-permute-start.2 = (bf16[24,2752]{1,0:T(8,128)(2,1)S(1)}, bf16[24,2752]{1,0:T(8,128)(2,1)S(1)}, u32[]{:S(2)}, u32[]{:S(2)}) collective-permute-start(bf16[24,2752]{1,0:T(8,128)(2,1)S(1)} %get-tuple-element.61), channel_id=1, source_target_pairs={{0,32},{8,40},{16,48},{24,56},{32,64},{40,72},{48,80},{56,88},{64,... | collective-permute-start | bytes 396296 | tf_op jit(solution)/shard_map/ppermute | solution.py:175
  39.8 3.2 %collective-permute-start.3 = (bf16[24,2752]{1,0:T(8,128)(2,1)S(1)}, bf16[24,2752]{1,0:T(8,128)(2,1)S(1)}, u32[]{:S(2)}, u32[]{:S(2)}) collective-permute-start(bf16[24,2752]{1,0:T(8,128)(2,1)S(1)} %get-tuple-element.63), channel_id=1, source_target_pairs={{0,96},{8,104},{16,112},{24,120},{32,0},{40,8},{48,16},{56,24},{64... | collective-permute-start | bytes 396296 | tf_op jit(solution)/shard_map/ppermute | solution.py:175
  43.8 3.2 %collective-permute-start.11 = (bf16[2,24,3008]{2,1,0:T(8,128)(2,1)S(1)}, bf16[2,24,3008]{2,1,0:T(8,128)(2,1)S(1)}, u32[]{:S(2)}, u32[]{:S(2)}) collective-permute-start(bf16[2,24,3008]{2,1,0:T(8,128)(2,1)S(1)} %bitcast.162), channel_id=1, source_target_pairs={{0,96},{8,104},{16,112},{24,120},{32,0},{40,8},{48,16},{56,24},{64... | collective-permute-start | bytes 866312 | tf_op jit(solution)/shard_map/ppermute | solution.py:175
  47.3 6.6 %collective-permute-done.10 = bf16[2,24,3008]{2,1,0:T(8,128)(2,1)S(1)} collective-permute-done((bf16[2,24,3008]{2,1,0:T(8,128)(2,1)S(1)}, bf16[2,24,3008]{2,1,0:T(8,128)(2,1)S(1)}, u32[]{:S(2)}, u32[]{:S(2)}) %collective-permute-start.10) | collective-permute-done | bytes 288800 | tf_op jit(solution)/shard_map/ppermute | solution.py:175
  53.9 1.1 collective-permute-start.24
  55.0 1.5 collective-permute-done.11
  56.6 7.3 %collective-permute-done.12 = bf16[2,24,3008]{2,1,0:T(8,128)(2,1)S(1)} collective-permute-done((bf16[2,24,3008]{2,1,0:T(8,128)(2,1)S(1)}, bf16[2,24,3008]{2,1,0:T(8,128)(2,1)S(1)}, u32[]{:S(2)}, u32[]{:S(2)}) %collective-permute-start.12) | collective-permute-done | bytes 288800 | tf_op jit(solution)/shard_map/ppermute | solution.py:175
  64.0 1.3 collective-permute-start.13
  65.2 4.2 %collective-permute-done.24 = bf16[4,24,2880]{2,1,0:T(8,128)(2,1)S(1)} collective-permute-done((bf16[4,24,2880]{2,1,0:T(8,128)(2,1)S(1)}, bf16[4,24,2880]{2,1,0:T(8,128)(2,1)S(1)}, u32[]{:S(2)}, u32[]{:S(2)}) %collective-permute-start.24) | collective-permute-done | bytes 552992 | tf_op jit(solution)/shard_map/ppermute | solution.py:175
  69.6 3.6 %collective-permute-start.25 = (bf16[24,2880]{1,0:T(8,128)(2,1)S(1)}, bf16[24,2880]{1,0:T(8,128)(2,1)S(1)}, u32[]{:S(2)}, u32[]{:S(2)}) collective-permute-start(bf16[24,2880]{1,0:T(8,128)(2,1)S(1)} %get-tuple-element.54), channel_id=1, source_target_pairs={{0,32},{8,40},{16,48},{24,56},{32,64},{40,72},{48,80},{56,88},{64,... | collective-permute-start | bytes 414728 | tf_op jit(solution)/shard_map/ppermute | solution.py:175
  74.1 2.4 %collective-permute-start.27 = (bf16[24,2880]{1,0:T(8,128)(2,1)S(1)}, bf16[24,2880]{1,0:T(8,128)(2,1)S(1)}, u32[]{:S(2)}, u32[]{:S(2)}) collective-permute-start(bf16[24,2880]{1,0:T(8,128)(2,1)S(1)} %get-tuple-element.55), channel_id=1, source_target_pairs={{0,64},{8,72},{16,80},{24,88},{32,96},{40,104},{48,112},{56,120},{... | collective-permute-start | bytes 414728 | tf_op jit(solution)/shard_map/ppermute | solution.py:175
  76.5 1.7 collective-permute-done.25
  78.2 2.4 %collective-permute-start.4 = (bf16[24,2752]{1,0:T(8,128)(2,1)S(1)}, bf16[24,2752]{1,0:T(8,128)(2,1)S(1)}, u32[]{:S(2)}, u32[]{:S(2)}) collective-permute-start(bf16[24,2752]{1,0:T(8,128)(2,1)S(1)} %get-tuple-element.62), channel_id=1, source_target_pairs={{0,64},{8,72},{16,80},{24,88},{32,96},{40,104},{48,112},{56,120},{... | collective-permute-start | bytes 396296 | tf_op jit(solution)/shard_map/ppermute | solution.py:175
  81.1 3.6 %collective-permute-done.4 = bf16[24,2752]{1,0:T(8,128)(2,1)S(1)} collective-permute-done((bf16[24,2752]{1,0:T(8,128)(2,1)S(1)}, bf16[24,2752]{1,0:T(8,128)(2,1)S(1)}, u32[]{:S(2)}, u32[]{:S(2)}) %collective-permute-start.4) | collective-permute-done | bytes 132128 | tf_op jit(solution)/shard_map/ppermute | solution.py:175
  84.7 1.5 fusion.23
  86.2 1.3 multiply_convert_fusion.2
  87.9 1.3 collective-permute-start.28
  89.3 2.1 %collective-permute-start.33 = (bf16[24,2752]{1,0:T(8,128)(2,1)S(1)}, bf16[24,2752]{1,0:T(8,128)(2,1)S(1)}, u32[]{:S(2)}, u32[]{:S(2)}) collective-permute-start(bf16[24,2752]{1,0:T(8,128)(2,1)S(1)} %get-tuple-element.59), channel_id=1, source_target_pairs={{0,96},{8,104},{16,112},{24,120},{32,0},{40,8},{48,16},{56,24},{64... | collective-permute-start | bytes 396296 | tf_op jit(solution)/shard_map/ppermute | solution.py:175
  93.9 2.4 %collective-permute-start.29 = (bf16[2,24,2752]{2,1,0:T(8,128)(2,1)S(1)}, bf16[2,24,2752]{2,1,0:T(8,128)(2,1)S(1)}, u32[]{:S(2)}, u32[]{:S(2)}) collective-permute-start(bf16[2,24,2752]{2,1,0:T(8,128)(2,1)S(1)} %get-tuple-element.73), channel_id=1, source_target_pairs={{0,96},{8,104},{16,112},{24,120},{32,0},{40,8},{48,16},{56,24},{64... | collective-permute-start | bytes 792584 | tf_op jit(solution)/shard_map/ppermute | solution.py:175
  96.3 2.0 %collective-permute-done.14 = bf16[24,2752]{1,0:T(8,128)(2,1)S(1)} collective-permute-done((bf16[24,2752]{1,0:T(8,128)(2,1)S(1)}, bf16[24,2752]{1,0:T(8,128)(2,1)S(1)}, u32[]{:S(2)}, u32[]{:S(2)}) %collective-permute-start.14) | collective-permute-done | bytes 132128 | tf_op jit(solution)/shard_map/ppermute | solution.py:175
  98.4 2.1 %collective-permute-start.30 = (bf16[2,24,2752]{2,1,0:T(8,128)(2,1)S(1)}, bf16[2,24,2752]{2,1,0:T(8,128)(2,1)S(1)}, u32[]{:S(2)}, u32[]{:S(2)}) collective-permute-start(bf16[2,24,2752]{2,1,0:T(8,128)(2,1)S(1)} %get-tuple-element.73), channel_id=1, source_target_pairs={{0,64},{8,72},{16,80},{24,88},{32,96},{40,104},{48,112},{56,120},{... | collective-permute-start | bytes 792584 | tf_op jit(solution)/shard_map/ppermute | solution.py:175
  100.5 2.2 %collective-permute-start.15 = (bf16[2,24,2752]{2,1,0:T(8,128)(2,1)S(1)}, bf16[2,24,2752]{2,1,0:T(8,128)(2,1)S(1)}, u32[]{:S(2)}, u32[]{:S(2)}) collective-permute-start(bf16[2,24,2752]{2,1,0:T(8,128)(2,1)S(1)} %get-tuple-element.75), channel_id=1, source_target_pairs={{0,96},{8,104},{16,112},{24,120},{32,0},{40,8},{48,16},{56,24},{64... | collective-permute-start | bytes 792584 | tf_op jit(solution)/shard_map/ppermute | solution.py:175
  102.7 1.0 collective-permute-start.16
  104.9 11.2 %collective-permute-done.15 = bf16[2,24,2752]{2,1,0:T(8,128)(2,1)S(1)} collective-permute-done((bf16[2,24,2752]{2,1,0:T(8,128)(2,1)S(1)}, bf16[2,24,2752]{2,1,0:T(8,128)(2,1)S(1)}, u32[]{:S(2)}, u32[]{:S(2)}) %collective-permute-start.15) | collective-permute-done | bytes 264224 | tf_op jit(solution)/shard_map/ppermute | solution.py:175
  116.1 1.7 collective-permute-start.36
  118.0 6.2 %collective-permute-done.31 = bf16[2,24,2752]{2,1,0:T(8,128)(2,1)S(1)} collective-permute-done((bf16[2,24,2752]{2,1,0:T(8,128)(2,1)S(1)}, bf16[2,24,2752]{2,1,0:T(8,128)(2,1)S(1)}, u32[]{:S(2)}, u32[]{:S(2)}) %collective-permute-start.31) | collective-permute-done | bytes 264224 | tf_op jit(solution)/shard_map/ppermute | solution.py:175
  124.3 1.1 collective-permute-done.36
  127.3 6.3 %backward.3 = (bf16[384,512]{1,0:T(8,128)(2,1)S(1)}, bf16[2752,512]{1,0:T(8,128)(2,1)}) custom-call(bf16[192,2752]{1,0:T(8,128)(2,1)S(1)} %bitcast.140, bf16[192,2752]{1,0:T(8,128)(2,1)S(1)} %collective-permute-done.18.refs_1_, bf16[384,512]{1,0:T(8,128)(2,1)S(1)} %get-tuple-element.31.refs_2_, bf16[128,8448]{1,0:T(8,128)(2,1)S(1)} %copy-done, ...), custom_call_target="tpu_custom_call" | custom-call | tf_op jit(solution)/shard_map/backward/pallas_call | solution.py:148
  133.6 5.4 %collective-permute-start.19 = (bf16[4,48,512]{2,1,0:T(8,128)(2,1)S(1)}, bf16[4,48,512]{2,1,0:T(8,128)(2,1)S(1)}, u32[]{:S(2)}, u32[]{:S(2)}) collective-permute-start(bf16[4,48,512]{2,1,0:T(8,128)(2,1)S(1)} %bitcast.171), channel_id=1, source_target_pairs={{0,4},{1,5},{2,6},{3,7},{4,0},{5,1},{6,2},{7,3},{8,12},{9,13},{10,... | collective-permute-start | bytes 589832 | tf_op jit(solution)/shard_map/ppermute | solution.py:183
  139.0 5.4 %collective-permute-done.19 = bf16[4,48,512]{2,1,0:T(8,128)(2,1)S(1)} collective-permute-done((bf16[4,48,512]{2,1,0:T(8,128)(2,1)S(1)}, bf16[4,48,512]{2,1,0:T(8,128)(2,1)S(1)}, u32[]{:S(2)}, u32[]{:S(2)}) %collective-permute-start.19) | collective-permute-done | bytes 196640 | tf_op jit(solution)/shard_map/ppermute | solution.py:183
  144.4 6.0 %backward.4 = (f32[384,512]{1,0:T(8,128)S(1)}, bf16[2752,512]{1,0:T(8,128)(2,1)}) custom-call(bf16[192,2752]{1,0:T(8,128)(2,1)S(1)} %bitcast.142, bf16[192,2752]{1,0:T(8,128)(2,1)S(1)} %collective-permute-done.37.refs_1_, bf16[384,512]{1,0:T(8,128)(2,1)S(1)} %get-tuple-element.26.refs_0_.refs_2_, bf16[128,8448]{1,0:T(8,128)(2,1)S(1)} %copy-done, ...), custom_call_target="tpu_custom_call" | custom-call | tf_op jit(solution)/shard_map/backward/pallas_call | solution.py:148
  150.4 7.0 %backward.5 = (bf16[384,512]{1,0:T(8,128)(2,1)S(1)}, bf16[2752,512]{1,0:T(8,128)(2,1)}) custom-call(bf16[192,2752]{1,0:T(8,128)(2,1)S(1)} %bitcast.138, bf16[192,2752]{1,0:T(8,128)(2,1)S(1)} %collective-permute-done.32.refs_1_, bf16[384,512]{1,0:T(8,128)(2,1)S(1)} %get-tuple-element.26.refs_0_.refs_2_, ...), custom_call_target="tpu_custom_call" | custom-call | tf_op jit(solution)/shard_map/backward/pallas_call | solution.py:148
  157.5 3.3 %collective-permute-start.38 = (bf16[4,48,512]{2,1,0:T(8,128)(2,1)S(1)}, bf16[4,48,512]{2,1,0:T(8,128)(2,1)S(1)}, u32[]{:S(2)}, u32[]{:S(2)}) collective-permute-start(bf16[4,48,512]{2,1,0:T(8,128)(2,1)S(1)} %bitcast.170), channel_id=1, source_target_pairs={{0,4},{1,5},{2,6},{3,7},{4,0},{5,1},{6,2},{7,3},{8,12},{9,13},{10,... | collective-permute-start | bytes 589832 | tf_op jit(solution)/shard_map/ppermute | solution.py:183
  160.8 1.2 collective-permute-start.20
  162.0 2.1 %collective-permute-start.21 = (bf16[48,512]{1,0:T(8,128)(2,1)S(1)}, bf16[48,512]{1,0:T(8,128)(2,1)S(1)}, u32[]{:S(2)}, u32[]{:S(2)}) collective-permute-start(bf16[48,512]{1,0:T(8,128)(2,1)S(1)} %get-tuple-element.81), channel_id=1, source_target_pairs={{0,3},{1,0},{2,1},{3,2},{4,7},{5,4},{6,5},{7,6},{8,11},{9,8},{10,9... | collective-permute-start | bytes 147464 | tf_op jit(solution)/shard_map/ppermute | solution.py:183
  164.1 1.5 collective-permute-done.38
  165.7 1.1 collective-permute-start.39
  166.9 2.2 %collective-permute-start.40 = (bf16[48,512]{1,0:T(8,128)(2,1)S(1)}, bf16[48,512]{1,0:T(8,128)(2,1)S(1)}, u32[]{:S(2)}, u32[]{:S(2)}) collective-permute-start(bf16[48,512]{1,0:T(8,128)(2,1)S(1)} %get-tuple-element.78), channel_id=1, source_target_pairs={{0,3},{1,0},{2,1},{3,2},{4,7},{5,4},{6,5},{7,6},{8,11},{9,8},{10,9... | collective-permute-start | bytes 147464 | tf_op jit(solution)/shard_map/ppermute | solution.py:183
  171.1 3.5 %collective-permute-done.41 = bf16[48,512]{1,0:T(8,128)(2,1)S(1)} collective-permute-done((bf16[48,512]{1,0:T(8,128)(2,1)S(1)}, bf16[48,512]{1,0:T(8,128)(2,1)S(1)}, u32[]{:S(2)}, u32[]{:S(2)}) %collective-permute-start.41) | collective-permute-done | bytes 49184 | tf_op jit(solution)/shard_map/ppermute | solution.py:183
  (108 shorter events, 16.6 us)
Async XLA Ops:
  7.2 77.6 %all-gather.2.cloned.1.call-start = ((), (), s32[]{:S(2)}) async-start(), calls=%async_computation | async-start | bytes 2297856 | tf_op jit(solution)/shard_map/all_gather | solution.py:262
  8.9 4.7 %copy-start.7 = (bf16[512,16]{0,1:T(8,128)(2,1)S(1)}, bf16[512,16]{0,1:T(8,128)(2,1)}, u32[]{:S(2)}) copy-start(bf16[512,16]{0,1:T(8,128)(2,1)} %param.17) | copy-start | bytes 49156
  8.9 4.7 %copy-start.8 = (bf16[512,16]{0,1:T(8,128)(2,1)S(1)}, bf16[512,16]{0,1:T(8,128)(2,1)}, u32[]{:S(2)}) copy-start(bf16[512,16]{0,1:T(8,128)(2,1)} %param.16) | copy-start | bytes 49156
  8.9 7.9 %copy-start.3 = (bf16[8,2752]{1,0:T(8,128)(2,1)S(1)}, bf16[8,2752]{1,0:T(8,128)(2,1)}, u32[]{:S(2)}) copy-start(bf16[8,2752]{1,0:T(8,128)(2,1)} %param.19) | copy-start | bytes 132100
  8.9 7.9 %copy-start.4 = (bf16[8,2752]{1,0:T(8,128)(2,1)S(1)}, bf16[8,2752]{1,0:T(8,128)(2,1)}, u32[]{:S(2)}) copy-start(bf16[8,2752]{1,0:T(8,128)(2,1)} %param.20) | copy-start | bytes 132100
  8.9 7.9 %copy-start.5 = (bf16[8,2752]{1,0:T(8,128)(2,1)S(1)}, bf16[8,2752]{1,0:T(8,128)(2,1)}, u32[]{:S(2)}) copy-start(bf16[8,2752]{1,0:T(8,128)(2,1)} %param.21) | copy-start | bytes 132100
  13.5 4.1 %collective-permute-start = (bf16[192,2752]{1,0:T(8,128)(2,1)}, bf16[192,2752]{1,0:T(8,128)(2,1)}, u32[]{:S(2)}, u32[]{:S(2)}) collective-permute-start(bf16[192,2752]{1,0:T(8,128)(2,1)} %get-tuple-element.25), channel_id=1, source_target_pairs={{0,8},{8,0},{16,24},{24,16},{32,40},{40,32},{48,56},{56,48},{64,72... | collective-permute-start | bytes 3170312 | tf_op jit(solution)/shard_map/ppermute | solution.py:175
  13.6 6.2 %collective-permute-start.5 = (bf16[48,512]{1,0:T(8,128)(2,1)S(1)}, bf16[48,512]{1,0:T(8,128)(2,1)S(1)}, u32[]{:S(2)}, u32[]{:S(2)}) collective-permute-start(bf16[48,512]{1,0:T(8,128)(2,1)S(1)} %get-tuple-element.83), channel_id=1, source_target_pairs={{0,4},{1,5},{2,6},{3,7},{4,0},{5,1},{6,2},{7,3},{8,12},{9,13},{10,... | collective-permute-start | bytes 147464 | tf_op jit(solution)/shard_map/ppermute | solution.py:183
  19.1 18.5 %collective-permute-start.1 = (bf16[4,24,2752]{2,1,0:T(8,128)(2,1)S(1)}, bf16[4,24,2752]{2,1,0:T(8,128)(2,1)S(1)}, u32[]{:S(2)}, u32[]{:S(2)}) collective-permute-start(bf16[4,24,2752]{2,1,0:T(8,128)(2,1)S(1)} %fusion.8), channel_id=1, source_target_pairs={{0,16},{8,24},{16,0},{24,8},{32,48},{40,56},{48,32},{56,40},{64,80... | collective-permute-start | bytes 1585160 | tf_op jit(solution)/shard_map/ppermute | solution.py:175
  19.8 5.9 %collective-permute-start.6 = (bf16[2,48,512]{2,1,0:T(8,128)(2,1)S(1)}, bf16[2,48,512]{2,1,0:T(8,128)(2,1)S(1)}, u32[]{:S(2)}, u32[]{:S(2)}) collective-permute-start(bf16[2,48,512]{2,1,0:T(8,128)(2,1)S(1)} %pad_maximum_fusion.7), channel_id=1, source_target_pairs={{0,1},{1,2},{2,3},{3,0},{4,5},{5,6},{6,7},{7,4},{8,9},{9,10},{10,1... | collective-permute-start | bytes 294920 | tf_op jit(solution)/shard_map/ppermute | solution.py:183
  21.5 7.6 %collective-permute-start.7 = (bf16[2,48,512]{2,1,0:T(8,128)(2,1)S(1)}, bf16[2,48,512]{2,1,0:T(8,128)(2,1)S(1)}, u32[]{:S(2)}, u32[]{:S(2)}) collective-permute-start(bf16[2,48,512]{2,1,0:T(8,128)(2,1)S(1)} %pad_maximum_fusion.7), channel_id=1, source_target_pairs={{0,2},{1,3},{2,0},{3,1},{4,6},{5,7},{6,4},{7,5},{8,10},{9,11},{10,... | collective-permute-start | bytes 294920 | tf_op jit(solution)/shard_map/ppermute | solution.py:183
  24.4 4.7 %collective-permute-start.8 = (bf16[2,48,512]{2,1,0:T(8,128)(2,1)S(1)}, bf16[2,48,512]{2,1,0:T(8,128)(2,1)S(1)}, u32[]{:S(2)}, u32[]{:S(2)}) collective-permute-start(bf16[2,48,512]{2,1,0:T(8,128)(2,1)S(1)} %pad_maximum_fusion.7), channel_id=1, source_target_pairs={{0,3},{1,0},{2,1},{3,2},{4,7},{5,4},{6,5},{7,6},{8,11},{9,8},{10,9... | collective-permute-start | bytes 294920 | tf_op jit(solution)/shard_map/ppermute | solution.py:183
  33.1 10.1 %collective-permute-start.9 = (bf16[192,3008]{1,0:T(8,128)(2,1)S(1)}, bf16[192,3008]{1,0:T(8,128)(2,1)S(1)}, u32[]{:S(2)}, u32[]{:S(2)}) collective-permute-start(bf16[192,3008]{1,0:T(8,128)(2,1)S(1)} %get-tuple-element.29), channel_id=1, source_target_pairs={{0,8},{8,0},{16,24},{24,16},{32,40},{40,32},{48,56},{56,48},{64,72... | collective-permute-start | bytes 3465224 | tf_op jit(solution)/shard_map/ppermute | solution.py:175
  37.1 5.9 %collective-permute-start.23 = (bf16[192,2880]{1,0:T(8,128)(2,1)S(1)}, bf16[192,2880]{1,0:T(8,128)(2,1)S(1)}, u32[]{:S(2)}, u32[]{:S(2)}) collective-permute-start(bf16[192,2880]{1,0:T(8,128)(2,1)S(1)} %get-tuple-element.34), channel_id=1, source_target_pairs={{0,8},{8,0},{16,24},{24,16},{32,40},{40,32},{48,56},{56,48},{64,72... | collective-permute-start | bytes 3317768 | tf_op jit(solution)/shard_map/ppermute | solution.py:175
  37.8 43.3 %collective-permute-start.2 = (bf16[24,2752]{1,0:T(8,128)(2,1)S(1)}, bf16[24,2752]{1,0:T(8,128)(2,1)S(1)}, u32[]{:S(2)}, u32[]{:S(2)}) collective-permute-start(bf16[24,2752]{1,0:T(8,128)(2,1)S(1)} %get-tuple-element.61), channel_id=1, source_target_pairs={{0,32},{8,40},{16,48},{24,56},{32,64},{40,72},{48,80},{56,88},{64,... | collective-permute-start | bytes 396296 | tf_op jit(solution)/shard_map/ppermute | solution.py:175
  39.8 41.4 %collective-permute-start.3 = (bf16[24,2752]{1,0:T(8,128)(2,1)S(1)}, bf16[24,2752]{1,0:T(8,128)(2,1)S(1)}, u32[]{:S(2)}, u32[]{:S(2)}) collective-permute-start(bf16[24,2752]{1,0:T(8,128)(2,1)S(1)} %get-tuple-element.63), channel_id=1, source_target_pairs={{0,96},{8,104},{16,112},{24,120},{32,0},{40,8},{48,16},{56,24},{64... | collective-permute-start | bytes 396296 | tf_op jit(solution)/shard_map/ppermute | solution.py:175
  43.7 10.2 %collective-permute-start.10 = (bf16[2,24,3008]{2,1,0:T(8,128)(2,1)S(1)}, bf16[2,24,3008]{2,1,0:T(8,128)(2,1)S(1)}, u32[]{:S(2)}, u32[]{:S(2)}) collective-permute-start(bf16[2,24,3008]{2,1,0:T(8,128)(2,1)S(1)} %bitcast.163), channel_id=1, source_target_pairs={{0,32},{8,40},{16,48},{24,56},{32,64},{40,72},{48,80},{56,88},{64,... | collective-permute-start | bytes 866312 | tf_op jit(solution)/shard_map/ppermute | solution.py:175
  43.8 12.7 %collective-permute-start.11 = (bf16[2,24,3008]{2,1,0:T(8,128)(2,1)S(1)}, bf16[2,24,3008]{2,1,0:T(8,128)(2,1)S(1)}, u32[]{:S(2)}, u32[]{:S(2)}) collective-permute-start(bf16[2,24,3008]{2,1,0:T(8,128)(2,1)S(1)} %bitcast.162), channel_id=1, source_target_pairs={{0,96},{8,104},{16,112},{24,120},{32,0},{40,8},{48,16},{56,24},{64... | collective-permute-start | bytes 866312 | tf_op jit(solution)/shard_map/ppermute | solution.py:175
  47.0 16.8 %collective-permute-start.12 = (bf16[2,24,3008]{2,1,0:T(8,128)(2,1)S(1)}, bf16[2,24,3008]{2,1,0:T(8,128)(2,1)S(1)}, u32[]{:S(2)}, u32[]{:S(2)}) collective-permute-start(bf16[2,24,3008]{2,1,0:T(8,128)(2,1)S(1)} %bitcast.161), channel_id=1, source_target_pairs={{0,64},{8,72},{16,80},{24,88},{32,96},{40,104},{48,112},{56,120},{... | collective-permute-start | bytes 866312 | tf_op jit(solution)/shard_map/ppermute | solution.py:175
  53.9 15.5 %collective-permute-start.24 = (bf16[4,24,2880]{2,1,0:T(8,128)(2,1)S(1)}, bf16[4,24,2880]{2,1,0:T(8,128)(2,1)S(1)}, u32[]{:S(2)}, u32[]{:S(2)}) collective-permute-start(bf16[4,24,2880]{2,1,0:T(8,128)(2,1)S(1)} %fusion.7), channel_id=1, source_target_pairs={{0,16},{8,24},{16,0},{24,8},{32,48},{40,56},{48,32},{56,40},{64,80... | collective-permute-start | bytes 1658888 | tf_op jit(solution)/shard_map/ppermute | solution.py:175
  64.0 10.1 %collective-permute-start.13 = (bf16[24,3008]{1,0:T(8,128)(2,1)S(1)}, bf16[24,3008]{1,0:T(8,128)(2,1)S(1)}, u32[]{:S(2)}, u32[]{:S(2)}) collective-permute-start(bf16[24,3008]{1,0:T(8,128)(2,1)S(1)} %fusion.70), channel_id=1, source_target_pairs={{0,16},{8,24},{16,0},{24,8},{32,48},{40,56},{48,32},{56,40},{64,80... | collective-permute-start | bytes 433160 | tf_op jit(solution)/shard_map/ppermute | solution.py:175
  69.6 8.6 %collective-permute-start.25 = (bf16[24,2880]{1,0:T(8,128)(2,1)S(1)}, bf16[24,2880]{1,0:T(8,128)(2,1)S(1)}, u32[]{:S(2)}, u32[]{:S(2)}) collective-permute-start(bf16[24,2880]{1,0:T(8,128)(2,1)S(1)} %get-tuple-element.54), channel_id=1, source_target_pairs={{0,32},{8,40},{16,48},{24,56},{32,64},{40,72},{48,80},{56,88},{64,... | collective-permute-start | bytes 414728 | tf_op jit(solution)/shard_map/ppermute | solution.py:175
  73.2 7.4 %collective-permute-start.26 = (bf16[24,2880]{1,0:T(8,128)(2,1)S(1)}, bf16[24,2880]{1,0:T(8,128)(2,1)S(1)}, u32[]{:S(2)}, u32[]{:S(2)}) collective-permute-start(bf16[24,2880]{1,0:T(8,128)(2,1)S(1)} %get-tuple-element.56), channel_id=1, source_target_pairs={{0,96},{8,104},{16,112},{24,120},{32,0},{40,8},{48,16},{56,24},{64... | collective-permute-start | bytes 414728 | tf_op jit(solution)/shard_map/ppermute | solution.py:175
  74.1 7.0 %collective-permute-start.27 = (bf16[24,2880]{1,0:T(8,128)(2,1)S(1)}, bf16[24,2880]{1,0:T(8,128)(2,1)S(1)}, u32[]{:S(2)}, u32[]{:S(2)}) collective-permute-start(bf16[24,2880]{1,0:T(8,128)(2,1)S(1)} %get-tuple-element.55), channel_id=1, source_target_pairs={{0,64},{8,72},{16,80},{24,88},{32,96},{40,104},{48,112},{56,120},{... | collective-permute-start | bytes 414728 | tf_op jit(solution)/shard_map/ppermute | solution.py:175
  78.2 6.5 %collective-permute-start.4 = (bf16[24,2752]{1,0:T(8,128)(2,1)S(1)}, bf16[24,2752]{1,0:T(8,128)(2,1)S(1)}, u32[]{:S(2)}, u32[]{:S(2)}) collective-permute-start(bf16[24,2752]{1,0:T(8,128)(2,1)S(1)} %get-tuple-element.62), channel_id=1, source_target_pairs={{0,64},{8,72},{16,80},{24,88},{32,96},{40,104},{48,112},{56,120},{... | collective-permute-start | bytes 396296 | tf_op jit(solution)/shard_map/ppermute | solution.py:175
  87.9 5.9 %collective-permute-start.28 = (bf16[24,2752]{1,0:T(8,128)(2,1)S(1)}, bf16[24,2752]{1,0:T(8,128)(2,1)S(1)}, u32[]{:S(2)}, u32[]{:S(2)}) collective-permute-start(bf16[24,2752]{1,0:T(8,128)(2,1)S(1)} %get-tuple-element.60), channel_id=1, source_target_pairs={{0,16},{8,24},{16,0},{24,8},{32,48},{40,56},{48,32},{56,40},{64,80... | collective-permute-start | bytes 396296 | tf_op jit(solution)/shard_map/ppermute | solution.py:175
  89.3 11.2 %collective-permute-start.33 = (bf16[24,2752]{1,0:T(8,128)(2,1)S(1)}, bf16[24,2752]{1,0:T(8,128)(2,1)S(1)}, u32[]{:S(2)}, u32[]{:S(2)}) collective-permute-start(bf16[24,2752]{1,0:T(8,128)(2,1)S(1)} %get-tuple-element.59), channel_id=1, source_target_pairs={{0,96},{8,104},{16,112},{24,120},{32,0},{40,8},{48,16},{56,24},{64... | collective-permute-start | bytes 396296 | tf_op jit(solution)/shard_map/ppermute | solution.py:175
  91.4 11.3 %collective-permute-start.34 = (bf16[24,2752]{1,0:T(8,128)(2,1)S(1)}, bf16[24,2752]{1,0:T(8,128)(2,1)S(1)}, u32[]{:S(2)}, u32[]{:S(2)}) collective-permute-start(bf16[24,2752]{1,0:T(8,128)(2,1)S(1)} %get-tuple-element.59), channel_id=1, source_target_pairs={{0,64},{8,72},{16,80},{24,88},{32,96},{40,104},{48,112},{56,120},{... | collective-permute-start | bytes 396296 | tf_op jit(solution)/shard_map/ppermute | solution.py:175
  92.5 12.1 %collective-permute-start.35 = (bf16[24,2752]{1,0:T(8,128)(2,1)S(1)}, bf16[24,2752]{1,0:T(8,128)(2,1)S(1)}, u32[]{:S(2)}, u32[]{:S(2)}) collective-permute-start(bf16[24,2752]{1,0:T(8,128)(2,1)S(1)} %get-tuple-element.59), channel_id=1, source_target_pairs={{0,32},{8,40},{16,48},{24,56},{32,64},{40,72},{48,80},{56,88},{64,... | collective-permute-start | bytes 396296 | tf_op jit(solution)/shard_map/ppermute | solution.py:175
  93.3 5.0 %collective-permute-start.14 = (bf16[24,2752]{1,0:T(8,128)(2,1)S(1)}, bf16[24,2752]{1,0:T(8,128)(2,1)S(1)}, u32[]{:S(2)}, u32[]{:S(2)}) collective-permute-start(bf16[24,2752]{1,0:T(8,128)(2,1)S(1)} %get-tuple-element.84), channel_id=1, source_target_pairs={{0,16},{8,24},{16,0},{24,8},{32,48},{40,56},{48,32},{56,40},{64,80... | collective-permute-start | bytes 396296 | tf_op jit(solution)/shard_map/ppermute | solution.py:175
  93.9 24.1 %collective-permute-start.29 = (bf16[2,24,2752]{2,1,0:T(8,128)(2,1)S(1)}, bf16[2,24,2752]{2,1,0:T(8,128)(2,1)S(1)}, u32[]{:S(2)}, u32[]{:S(2)}) collective-permute-start(bf16[2,24,2752]{2,1,0:T(8,128)(2,1)S(1)} %get-tuple-element.73), channel_id=1, source_target_pairs={{0,96},{8,104},{16,112},{24,120},{32,0},{40,8},{48,16},{56,24},{64... | collective-permute-start | bytes 792584 | tf_op jit(solution)/shard_map/ppermute | solution.py:175
  98.4 19.6 %collective-permute-start.30 = (bf16[2,24,2752]{2,1,0:T(8,128)(2,1)S(1)}, bf16[2,24,2752]{2,1,0:T(8,128)(2,1)S(1)}, u32[]{:S(2)}, u32[]{:S(2)}) collective-permute-start(bf16[2,24,2752]{2,1,0:T(8,128)(2,1)S(1)} %get-tuple-element.73), channel_id=1, source_target_pairs={{0,64},{8,72},{16,80},{24,88},{32,96},{40,104},{48,112},{56,120},{... | collective-permute-start | bytes 792584 | tf_op jit(solution)/shard_map/ppermute | solution.py:175
  100.5 15.6 %collective-permute-start.15 = (bf16[2,24,2752]{2,1,0:T(8,128)(2,1)S(1)}, bf16[2,24,2752]{2,1,0:T(8,128)(2,1)S(1)}, u32[]{:S(2)}, u32[]{:S(2)}) collective-permute-start(bf16[2,24,2752]{2,1,0:T(8,128)(2,1)S(1)} %get-tuple-element.75), channel_id=1, source_target_pairs={{0,96},{8,104},{16,112},{24,120},{32,0},{40,8},{48,16},{56,24},{64... | collective-permute-start | bytes 792584 | tf_op jit(solution)/shard_map/ppermute | solution.py:175
  102.7 13.4 %collective-permute-start.16 = (bf16[2,24,2752]{2,1,0:T(8,128)(2,1)S(1)}, bf16[2,24,2752]{2,1,0:T(8,128)(2,1)S(1)}, u32[]{:S(2)}, u32[]{:S(2)}) collective-permute-start(bf16[2,24,2752]{2,1,0:T(8,128)(2,1)S(1)} %get-tuple-element.75), channel_id=1, source_target_pairs={{0,64},{8,72},{16,80},{24,88},{32,96},{40,104},{48,112},{56,120},{... | collective-permute-start | bytes 792584 | tf_op jit(solution)/shard_map/ppermute | solution.py:175
  104.5 13.2 %collective-permute-start.17 = (bf16[2,24,2752]{2,1,0:T(8,128)(2,1)S(1)}, bf16[2,24,2752]{2,1,0:T(8,128)(2,1)S(1)}, u32[]{:S(2)}, u32[]{:S(2)}) collective-permute-start(bf16[2,24,2752]{2,1,0:T(8,128)(2,1)S(1)} %get-tuple-element.75), channel_id=1, source_target_pairs={{0,32},{8,40},{16,48},{24,56},{32,64},{40,72},{48,80},{56,88},{64,... | collective-permute-start | bytes 792584 | tf_op jit(solution)/shard_map/ppermute | solution.py:175
  116.1 8.1 %collective-permute-start.31 = (bf16[2,24,2752]{2,1,0:T(8,128)(2,1)S(1)}, bf16[2,24,2752]{2,1,0:T(8,128)(2,1)S(1)}, u32[]{:S(2)}, u32[]{:S(2)}) collective-permute-start(bf16[2,24,2752]{2,1,0:T(8,128)(2,1)S(1)} %get-tuple-element.73), channel_id=1, source_target_pairs={{0,32},{8,40},{16,48},{24,56},{32,64},{40,72},{48,80},{56,88},{64,... | collective-permute-start | bytes 792584 | tf_op jit(solution)/shard_map/ppermute | solution.py:175
  116.1 9.4 %collective-permute-start.36 = (bf16[4,24,2752]{2,1,0:T(8,128)(2,1)S(1)}, bf16[4,24,2752]{2,1,0:T(8,128)(2,1)S(1)}, u32[]{:S(2)}, u32[]{:S(2)}) collective-permute-start(bf16[4,24,2752]{2,1,0:T(8,128)(2,1)S(1)} %get-tuple-element.58), channel_id=1, source_target_pairs={{0,16},{8,24},{16,0},{24,8},{32,48},{40,56},{48,32},{56,40},{64,80... | collective-permute-start | bytes 1585160 | tf_op jit(solution)/shard_map/ppermute | solution.py:175
  117.9 9.4 %collective-permute-start.18 = (bf16[192,2752]{1,0:T(8,128)(2,1)S(1)}, bf16[192,2752]{1,0:T(8,128)(2,1)S(1)}, u32[]{:S(2)}, u32[]{:S(2)}) collective-permute-start(bf16[192,2752]{1,0:T(8,128)(2,1)S(1)} %bitcast.139), channel_id=1, source_target_pairs={{0,8},{8,0},{16,24},{24,16},{32,40},{40,32},{48,56},{56,48},{64,72... | collective-permute-start | bytes 3170312 | tf_op jit(solution)/shard_map/ppermute | solution.py:175
  125.6 18.8 %collective-permute-start.37 = (bf16[192,2752]{1,0:T(8,128)(2,1)S(1)}, bf16[192,2752]{1,0:T(8,128)(2,1)S(1)}, u32[]{:S(2)}, u32[]{:S(2)}) collective-permute-start(bf16[192,2752]{1,0:T(8,128)(2,1)S(1)} %bitcast.141), channel_id=1, source_target_pairs={{0,8},{8,0},{16,24},{24,16},{32,40},{40,32},{48,56},{56,48},{64,72... | collective-permute-start | bytes 3170312 | tf_op jit(solution)/shard_map/ppermute | solution.py:175
  125.7 24.7 %collective-permute-start.32 = (bf16[192,2752]{1,0:T(8,128)(2,1)S(1)}, bf16[192,2752]{1,0:T(8,128)(2,1)S(1)}, u32[]{:S(2)}, u32[]{:S(2)}) collective-permute-start(bf16[192,2752]{1,0:T(8,128)(2,1)S(1)} %bitcast.137), channel_id=1, source_target_pairs={{0,8},{8,0},{16,24},{24,16},{32,40},{40,32},{48,56},{56,48},{64,72... | collective-permute-start | bytes 3170312 | tf_op jit(solution)/shard_map/ppermute | solution.py:175
  133.6 10.8 %collective-permute-start.19 = (bf16[4,48,512]{2,1,0:T(8,128)(2,1)S(1)}, bf16[4,48,512]{2,1,0:T(8,128)(2,1)S(1)}, u32[]{:S(2)}, u32[]{:S(2)}) collective-permute-start(bf16[4,48,512]{2,1,0:T(8,128)(2,1)S(1)} %bitcast.171), channel_id=1, source_target_pairs={{0,4},{1,5},{2,6},{3,7},{4,0},{5,1},{6,2},{7,3},{8,12},{9,13},{10,... | collective-permute-start | bytes 589832 | tf_op jit(solution)/shard_map/ppermute | solution.py:183
  157.5 8.2 %collective-permute-start.38 = (bf16[4,48,512]{2,1,0:T(8,128)(2,1)S(1)}, bf16[4,48,512]{2,1,0:T(8,128)(2,1)S(1)}, u32[]{:S(2)}, u32[]{:S(2)}) collective-permute-start(bf16[4,48,512]{2,1,0:T(8,128)(2,1)S(1)} %bitcast.170), channel_id=1, source_target_pairs={{0,4},{1,5},{2,6},{3,7},{4,0},{5,1},{6,2},{7,3},{8,12},{9,13},{10,... | collective-permute-start | bytes 589832 | tf_op jit(solution)/shard_map/ppermute | solution.py:183
  160.8 8.3 %collective-permute-start.20 = (bf16[48,512]{1,0:T(8,128)(2,1)S(1)}, bf16[48,512]{1,0:T(8,128)(2,1)S(1)}, u32[]{:S(2)}, u32[]{:S(2)}) collective-permute-start(bf16[48,512]{1,0:T(8,128)(2,1)S(1)} %get-tuple-element.79), channel_id=1, source_target_pairs={{0,1},{1,2},{2,3},{3,0},{4,5},{5,6},{6,7},{7,4},{8,9},{9,10},{10,1... | collective-permute-start | bytes 147464 | tf_op jit(solution)/shard_map/ppermute | solution.py:183
  162.0 7.8 %collective-permute-start.21 = (bf16[48,512]{1,0:T(8,128)(2,1)S(1)}, bf16[48,512]{1,0:T(8,128)(2,1)S(1)}, u32[]{:S(2)}, u32[]{:S(2)}) collective-permute-start(bf16[48,512]{1,0:T(8,128)(2,1)S(1)} %get-tuple-element.81), channel_id=1, source_target_pairs={{0,3},{1,0},{2,1},{3,2},{4,7},{5,4},{6,5},{7,6},{8,11},{9,8},{10,9... | collective-permute-start | bytes 147464 | tf_op jit(solution)/shard_map/ppermute | solution.py:183
  164.1 5.7 %collective-permute-start.22 = (bf16[48,512]{1,0:T(8,128)(2,1)S(1)}, bf16[48,512]{1,0:T(8,128)(2,1)S(1)}, u32[]{:S(2)}, u32[]{:S(2)}) collective-permute-start(bf16[48,512]{1,0:T(8,128)(2,1)S(1)} %get-tuple-element.80), channel_id=1, source_target_pairs={{0,2},{1,3},{2,0},{3,1},{4,6},{5,7},{6,4},{7,5},{8,10},{9,11},{10,... | collective-permute-start | bytes 147464 | tf_op jit(solution)/shard_map/ppermute | solution.py:183
  165.7 5.4 %collective-permute-start.39 = (bf16[48,512]{1,0:T(8,128)(2,1)S(1)}, bf16[48,512]{1,0:T(8,128)(2,1)S(1)}, u32[]{:S(2)}, u32[]{:S(2)}) collective-permute-start(bf16[48,512]{1,0:T(8,128)(2,1)S(1)} %get-tuple-element.76), channel_id=1, source_target_pairs={{0,1},{1,2},{2,3},{3,0},{4,5},{5,6},{6,7},{7,4},{8,9},{9,10},{10,1... | collective-permute-start | bytes 147464 | tf_op jit(solution)/shard_map/ppermute | solution.py:183
  166.9 4.2 %collective-permute-start.40 = (bf16[48,512]{1,0:T(8,128)(2,1)S(1)}, bf16[48,512]{1,0:T(8,128)(2,1)S(1)}, u32[]{:S(2)}, u32[]{:S(2)}) collective-permute-start(bf16[48,512]{1,0:T(8,128)(2,1)S(1)} %get-tuple-element.78), channel_id=1, source_target_pairs={{0,3},{1,0},{2,1},{3,2},{4,7},{5,4},{6,5},{7,6},{8,11},{9,8},{10,9... | collective-permute-start | bytes 147464 | tf_op jit(solution)/shard_map/ppermute | solution.py:183
  169.1 5.6 %collective-permute-start.41 = (bf16[48,512]{1,0:T(8,128)(2,1)S(1)}, bf16[48,512]{1,0:T(8,128)(2,1)S(1)}, u32[]{:S(2)}, u32[]{:S(2)}) collective-permute-start(bf16[48,512]{1,0:T(8,128)(2,1)S(1)} %get-tuple-element.77), channel_id=1, source_target_pairs={{0,2},{1,3},{2,0},{3,1},{4,6},{5,7},{6,4},{7,5},{8,10},{9,11},{10,... | collective-permute-start | bytes 147464 | tf_op jit(solution)/shard_map/ppermute | solution.py:183
  (4 other events, 12.1 us)
Sparse Core Ops, SparseCore 0:
  17.7 37.8 all-gather.1

commit v3 on v1

v3 whole, which is shorter than its diff:
```python
import jax
import jax.numpy as jnp
from jax import lax
from jax.experimental import pallas as pl
from jax.experimental.pallas import tpu as pltpu
from jax.sharding import PartitionSpec as P

BF = jnp.bfloat16
F32 = jnp.float32
ROWS = 24
HALF = 192
CHUNK = 256
RANK = 128
LOW = 512
LIMIT = 48 * 1024 * 1024

NN = ((1,), (0,))
NT = ((1,), (1,))
TN = ((0,), (0,))


def dot(a, b, dims):
    return lax.dot_general(a, b, (dims, ((), ())), preferred_element_type=F32)


def after(x, *others):
    return lax.optimization_barrier((x,) + others)[0]


def pick(index_ref, size):
    return (index_ref[...] == lax.broadcasted_iota(jnp.int32, (size, size), 1)).astype(BF)


VMEM = pl.BlockSpec(memory_space=pltpu.VMEM)
ANY = pl.BlockSpec(memory_space=pl.ANY)
COST = pl.CostEstimate(flops=1024, bytes_accessed=1024, transcendentals=0)


def copy_in(src, dst, sems, k, at, wide):
    part = pl.ds(at, wide)
    return pltpu.make_async_copy(src.at[part, :], dst.at[part, :], sems.at[k])


def sweep(n, step):
    whole = n // CHUNK

    def body(k, _):
        step(k, pl.multiple_of(k * CHUNK, 128), CHUNK)
        return 0

    lax.fori_loop(0, whole, body, 0)
    if n % CHUNK:
        step(whole, whole * CHUNK, n % CHUNK)


def chunks(n):
    return -(-n // CHUNK)


def params():
    return pltpu.CompilerParams(vmem_limit_bytes=LIMIT)


def forward_first(tokens, grad_out, index, lefts, weight):
    n, depth = weight.shape
    size = tokens.shape[0]
    rank = lefts[0].shape[0]

    def body(t_ref, g_ref, i_ref, lg_ref, lu_ref, ld_ref, w_hbm, mine_ref, theirs_ref, tok_ref, out_ref, low_ref, w_ref, sems):
        for k in range(chunks(n)):
            copy_in(w_hbm, w_ref, sems, k, k * CHUNK, min(CHUNK, n - k * CHUNK)).start()
        turn = pick(i_ref, size)
        tok_ref[...] = dot(turn, t_ref[...], NN).astype(BF)

        def step(k, at, wide):
            copy_in(w_hbm, w_ref, sems, k, at, wide).wait()
            got = dot(tok_ref[...], w_ref[pl.ds(at, wide), :], NT)
            mine_ref[:, pl.ds(at, wide)] = got[:HALF]
            theirs_ref[:, pl.ds(at, wide)] = got[HALF:].astype(BF)

        sweep(n, step)
        out_ref[...] = dot(turn, g_ref[...], NN).astype(BF)
        none = jnp.zeros((RANK - 2 * rank, depth), BF)
        low = dot(t_ref[...], jnp.concatenate([lg_ref[...], lu_ref[...], none], axis=0), NT)
        none = jnp.zeros((rank, depth), BF)
        down = [none, none, ld_ref[...]] + [none] * (RANK // rank - 3)
        low = low + dot(g_ref[...], jnp.concatenate(down, axis=0), NT)
        low_ref[...] = low.astype(BF)

    return pl.pallas_call(
        body,
        out_shape=[
            jax.ShapeDtypeStruct((HALF, n), F32),
            jax.ShapeDtypeStruct((HALF, n), BF),
            jax.ShapeDtypeStruct((size, depth), BF),
            jax.ShapeDtypeStruct((size, depth), BF),
            jax.ShapeDtypeStruct((size, RANK), BF),
        ],
        in_specs=[VMEM] * 6 + [ANY],
        out_specs=[VMEM] * 5,
        scratch_shapes=[pltpu.VMEM((n, depth), BF), pltpu.SemaphoreType.DMA((chunks(n),))],
        compiler_params=params(),
        cost_estimate=COST,
        name="forward_first",
    )(tokens, grad_out, index, *lefts, weight)


def forward(x, weight):
    n, depth = weight.shape

    def body(x_ref, w_hbm, mine_ref, theirs_ref, w_ref, sems):
        for k in range(chunks(n)):
            copy_in(w_hbm, w_ref, sems, k, k * CHUNK, min(CHUNK, n - k * CHUNK)).start()

        def step(k, at, wide):
            copy_in(w_hbm, w_ref, sems, k, at, wide).wait()
            got = dot(x_ref[...], w_ref[pl.ds(at, wide), :], NT)
            mine_ref[:, pl.ds(at, wide)] = got[:HALF]
            theirs_ref[:, pl.ds(at, wide)] = got[HALF:].astype(BF)

        sweep(n, step)

    return pl.pallas_call(
        body,
        out_shape=[jax.ShapeDtypeStruct((HALF, n), F32), jax.ShapeDtypeStruct((HALF, n), BF)],
        in_specs=[VMEM, ANY],
        out_specs=[VMEM] * 2,
        scratch_shapes=[pltpu.VMEM((n, depth), BF), pltpu.SemaphoreType.DMA((chunks(n),))],
        compiler_params=params(),
        cost_estimate=COST,
        name="forward",
    )(x, weight)


def halves(mine_ref, other_ref, at, wide):
    part = pl.ds(at, wide)
    return jnp.concatenate([mine_ref[:, part], other_ref[:, part]], axis=0)


def product(mine, other, weight, rights, lefts, place, partial=None, index=None):
    n, depth = weight.shape
    size = 2 * HALF
    padded = rights.shape[1] // 3

    def body(*refs):
        refs = list(refs)
        mine_ref, other_ref, right_ref, left_ref = refs[:4]
        refs = refs[4:]
        partial_ref = None if partial is None else refs.pop(0)
        index_ref = None if index is None else refs.pop(0)
        w_hbm, out_ref, w_ref, total_ref, low_ref, sems = refs
        for k in range(chunks(n)):
            copy_in(w_hbm, w_ref, sems, k, k * CHUNK, min(CHUNK, n - k * CHUNK)).start()
        total_ref[...] = jnp.zeros((size, depth), F32) if partial is None else partial_ref[...]
        low_ref[...] = jnp.zeros((size, RANK), F32)

        def step(k, at, wide):
            value = halves(mine_ref, other_ref, at, wide)
            low_ref[...] += dot(value, right_ref[:, pl.ds(at, wide)], NT)
            copy_in(w_hbm, w_ref, sems, k, at, wide).wait()
            total_ref[...] += dot(value, w_ref[pl.ds(at, wide), :], NN)

        sweep(n, step)
        total = total_ref[...] + dot(low_ref[...].astype(BF), left_ref[...], NN)
        if index is None:
            out_ref[...] = total
        else:
            out_ref[...] = dot(pick(index_ref, size), total.astype(BF), NN).astype(BF)

    args = [mine, other, rights, lefts]
    specs = [
        VMEM,
        VMEM,
        pl.BlockSpec((RANK, padded), lambda i: (0, place)),
        pl.BlockSpec((RANK, depth), lambda i: (place, 0)),
    ]
    if partial is not None:
        args.append(partial)
        specs.append(VMEM)
    if index is not None:
        args.append(index)
        specs.append(VMEM)
    return pl.pallas_call(
        body,
        grid=(1,),
        out_shape=jax.ShapeDtypeStruct((size, depth), F32 if index is None else BF),
        in_specs=specs + [ANY],
        out_specs=VMEM,
        scratch_shapes=[
            pltpu.VMEM((n, depth), BF),
            pltpu.VMEM((size, depth), F32),
            pltpu.VMEM((size, RANK), F32),
            pltpu.SemaphoreType.DMA((chunks(n),)),
        ],
        compiler_params=params(),
        cost_estimate=COST,
        name="product",
    )(*args, weight)


def weight_grad(mine, other, x):
    n, depth = mine.shape[1], x.shape[1]

    def body(mine_ref, other_ref, x_ref, grad_hbm, grad_ref, sems):
        def step(k, at, wide):
            value = halves(mine_ref, other_ref, at, wide)
            grad_ref[pl.ds(at, wide), :] = dot(value, x_ref[...], TN).astype(BF)
            copy_in(grad_ref, grad_hbm, sems, k, at, wide).start()

        sweep(n, step)
        for k in range(chunks(n)):
            copy_in(grad_ref, grad_hbm, sems, k, k * CHUNK, min(CHUNK, n - k * CHUNK)).wait()

    return pl.pallas_call(
        body,
        out_shape=jax.ShapeDtypeStruct((n, depth), BF),
        in_specs=[VMEM] * 3,
        out_specs=ANY,
        scratch_shapes=[pltpu.VMEM((n, depth), BF), pltpu.SemaphoreType.DMA((chunks(n),))],
        compiler_params=params(),
        cost_estimate=COST,
        name="weight_grad",
    )(mine, other, x)


def act(gate, up, up_x, low, rights):
    rows, n = up.shape
    wide = rights.shape[1] // 3

    def body(g_ref, u_ref, x_ref, low_ref, right_ref, gate_ref, up_ref, hidden_ref):
        def step(k, at, size):
            part = pl.ds(at, size)
            lg = dot(low_ref[:RANK, LOW:], right_ref[:, part], TN)[:rows]
            lu = dot(low_ref[RANK : 2 * RANK, LOW:], right_ref[:, pl.ds(wide + at, size)], TN)[:rows]
            g = g_ref[:, part] + lg
            u = u_ref[:, part] + x_ref[:, part].astype(F32) + lu
            gate_ref[:, part] = g
            up_ref[:, part] = u
            hidden_ref[:, part] = (g * jax.nn.sigmoid(g) * u).astype(BF)

        sweep(n, step)

    return pl.pallas_call(
        body,
        out_shape=[jax.ShapeDtypeStruct((rows, n), t) for t in (F32, F32, BF)],
        in_specs=[VMEM] * 5,
        out_specs=[VMEM] * 3,
        compiler_params=params(),
        cost_estimate=COST,
        name="act",
    )(gate, up, up_x, low, rights)


def derive(gate, up, back, parts, low, rights):
    rows, n = up.shape
    wide = rights.shape[1] // 3

    def body(g_ref, u_ref, b_ref, p_ref, q_ref, r_ref, low_ref, right_ref, gd_ref, ud_ref):
        def step(k, at, size):
            part = pl.ds(at, size)
            b = dot(low_ref[2 * RANK :, LOW:], right_ref[:, pl.ds(2 * wide + at, size)], TN)[:rows]
            b = b + b_ref[:, part]
            for ref in (p_ref, q_ref, r_ref):
                b = b + ref[:, part].astype(F32)
            g, u = g_ref[:, part], u_ref[:, part]
            sigma = jax.nn.sigmoid(g)
            gd_ref[:, part] = (b * u * sigma * (1.0 + g * (1.0 - sigma))).astype(BF)
            ud_ref[:, part] = (b * g * sigma).astype(BF)

        sweep(n, step)

    return pl.pallas_call(
        body,
        out_shape=[jax.ShapeDtypeStruct((rows, n), BF)] * 2,
        in_specs=[VMEM] * 8,
        out_specs=[VMEM] * 2,
        compiler_params=params(),
        cost_estimate=COST,
        name="derive",
    )(gate, up, back, *parts, low, rights)


def row_send(x, dz, da, dc):
    pairs = []
    for z in range(4):
        for a in range(2):
            for c in range(2):
                to = ((z + dz) % 4) * 4 + ((a + da) % 2) * 2 + (c + dc) % 2
                pairs.append((z * 4 + a * 2 + c, to))
    return lax.ppermute(x, "row", pairs)


def pair_sum(mine, got):
    return (mine + got.astype(F32)).reshape(4, 2, ROWS, -1)


def z_send(blocks):
    return [row_send(blocks[d].astype(BF), d, 0, 0) for d in (1, 3, 2)]


def z_spread(x):
    return [row_send(x, d, 0, 0) for d in (3, 2, 1)]


def x_send(x):
    return row_send(x.astype(BF), 0, 1, 0)


def core_send(x):
    return row_send(x, 0, 0, 1)


def plus(own, parts):
    for p in parts:
        own = own + p.astype(F32)
    return own


def shards(
    tokens,
    grad_out,
    gate_weight,
    up_weight,
    down_weight,
    gate_left,
    up_left,
    down_left,
    gate_right,
    up_right,
    down_right,
):
    n = gate_weight.shape[1]
    row = lax.axis_index("row")
    z, a, c = row // 4, (row // 2) % 2, row % 2

    k = jnp.arange(2 * HALF, dtype=jnp.int32)
    block = k // ROWS
    dc, dz, da = block // 8, (block // 2) % 4, block % 2
    held = (((z + dz) % 4 * 4) + ((a + da) % 2) * 2 + (c + dc) % 2) * ROWS + k % ROWS
    block = k // ROWS
    dc, dz, da = (block % 2 - c) % 2, (block // 4 - z) % 4, ((block // 2) % 2 - a) % 2
    leave = ((dc * 4 + dz) * 2 + da) * ROWS + k % ROWS
    held, leave = held[:, None], leave[:, None]
    block = (k % RANK) // 8
    dc, dz, da = block // 8, (block // 2) % 4, block % 2
    right_rank = (((z + dz) % 4 * 4) + ((a + da) % 2) * 2 + (c + dc) % 2) * 8 + k % 8 + RANK * (k // RANK)
    left_rank = (k // 48) * 16 + k % 16 + RANK * ((k // 16) % 3)
    match = (left_rank[None, :] == right_rank[:, None]).astype(BF)

    gate_w, up_w, down_w = gate_weight.T, up_weight.T, down_weight.T
    lefts = (gate_left.T, up_left.T, down_left.T)
    edge = jnp.zeros((gate_right.shape[0], -n % 128), BF)
    rights = jnp.concatenate([gate_right, edge, up_right, edge, down_right, edge], axis=1)

    rights_x = x_send(rights)
    held, _ = lax.optimization_barrier((held, rights))
    gate_mine, gate_theirs, tok, out, low = forward_first(tokens, grad_out, held, lefts, gate_w)
    gate = pair_sum(gate_mine, core_send(gate_theirs))
    gate_send = gate[:, 1].astype(BF)
    gate_x = x_send(gate_send)
    rights, rights_x, tok, _, _ = lax.optimization_barrier((rights, rights_x, tok, gate, gate_send))
    rights_pair = jnp.stack([rights, rights_x])
    rights_z = z_spread(rights_pair)
    up_mine, up_theirs = forward(after(tok, rights_pair), up_w)
    up_got = core_send(up_theirs)
    back_mine, back_theirs = forward(after(out, up_theirs), down_w)
    back_got = core_send(back_theirs)
    gate_x, rights_z, _ = lax.optimization_barrier((gate_x, rights_z, back_theirs))
    up = pair_sum(up_mine, up_got)
    up, rights_z, _ = lax.optimization_barrier((up, rights_z, back_theirs))
    up_z = z_send(up)
    back_got, gate_x = lax.optimization_barrier((back_got, gate_x))
    back = pair_sum(back_mine, back_got)
    back_send = back[:, 1].astype(BF)
    back_x = x_send(back_send)

    low, _, _ = lax.optimization_barrier((low, back_send, up))
    low = lax.all_to_all(low, "row", 0, 0, tiled=True).reshape(16, ROWS, RANK)
    low = jnp.sum(low.astype(F32), axis=0)[:, :48].astype(BF).T
    low = jnp.pad(low, ((0, 0), (0, RANK - ROWS)))
    low = jnp.concatenate([jnp.concatenate(lefts, axis=0), low], axis=1)
    low = lax.all_to_all(jnp.broadcast_to(low, (8,) + low.shape), "col", 0, 0, tiled=True)

    gate = gate[:, 0] + gate_x.astype(F32)
    gate, up_z = lax.optimization_barrier((gate, up_z))
    gate_z = z_send(gate)
    up = plus(up[0], up_z)
    up_x = x_send(up[1])
    rights_half = jnp.stack([rights_pair] + rights_z).reshape(64, -1)
    rights_half, up_z = lax.optimization_barrier((rights_half, up_z))
    rights = jnp.concatenate([rights_half, core_send(rights_half)], axis=0)
    low = dot(match, low.reshape(3 * RANK, -1), NN).astype(BF)

    back = back[:, 0] + back_x.astype(F32)
    back, gate_z = lax.optimization_barrier((back, gate_z))
    back_z = z_send(back)
    gate, up, hidden = act(plus(gate[0], gate_z), up[0], up_x, low, rights)
    hidden_x = x_send(hidden)
    gate, hidden_x, back_z = lax.optimization_barrier((gate, hidden_x, back_z))
    hidden = jnp.stack([hidden, hidden_x])
    hidden_z = z_spread(hidden)
    gate_delta, up_delta = derive(gate, up, back[0], back_z, low, rights)
    up_x = x_send(up_delta)
    gate_delta, up_x, hidden_z = lax.optimization_barrier((gate_delta, up_x, hidden_z))
    gate_z = z_spread(gate_delta)

    hidden = jnp.stack([hidden] + hidden_z).reshape(HALF, n)
    hidden = (hidden, core_send(hidden))
    mixed = product(*hidden, down_w, rights, low, 2, index=leave)
    mixed_all = lax.all_to_all(mixed.reshape(8, 48, -1), "col", 0, 0, tiled=True)

    up_delta, gate_z = lax.optimization_barrier((up_delta, gate_z))
    gate_delta = jnp.stack([gate_delta] + gate_z)
    gate_x = x_send(gate_delta)
    up_delta = jnp.stack([up_delta, up_x])
    up_z = z_spread(up_delta)
    hidden, _ = lax.optimization_barrier((hidden, mixed))
    down_grad = weight_grad(*hidden, out)
    up_z, gate_x, mixed_all, _ = lax.optimization_barrier((up_z, gate_x, mixed_all, down_grad))

    up_delta = jnp.stack([up_delta] + up_z).reshape(HALF, n)
    up_delta = (up_delta, core_send(up_delta))
    gate_delta = jnp.stack([gate_delta, gate_x], axis=1).reshape(HALF, n)
    gate_delta = (gate_delta, core_send(gate_delta))
    partial = product(*up_delta, up_w, rights, low, 1)
    input_grad = product(*gate_delta, gate_w, rights, low, 0, partial=partial, index=leave)
    up_delta, gate_delta, _ = lax.optimization_barrier((up_delta, gate_delta, input_grad))
    input_all = lax.all_to_all(input_grad.reshape(8, 48, -1), "col", 0, 0, tiled=True)
    up_grad = weight_grad(*up_delta, tok)
    gate_grad = weight_grad(*gate_delta, tok)
    mixed = jnp.sum(mixed_all.astype(F32), axis=0).astype(BF)
    input_grad = jnp.sum(input_all.astype(F32), axis=0).astype(BF)
    return mixed, input_grad, gate_grad.T, up_grad.T, down_grad.T


def solution(mesh):
    arg = P("row", "col")
    in_specs = (P(None, "row"), P(None, "row")) + (arg,) * 9
    out_specs = (P("col", "row"), P("col", "row")) + (arg,) * 3
    return jax.shard_map(shards, mesh=mesh, in_specs=in_specs, out_specs=out_specs, check_vma=False)
```

time: 201 us -> 204 us (1.015)
  matrix products: 63.1 us -> 1.51 us
  Pallas kernels: 0 us -> 51.2 us
  local copies, waits for them, and re-layouts: 8.18 us -> 21 us
  waiting for transfers between devices: 57.7 us -> 46.7 us
  starting transfers between devices: 55.7 us -> 63.4 us
    dot_general x24 -> x1, matrix products: 63.1 us -> 1.51 us  [dot(): return lax.dot_general(a, b, (dims, ((), ())), preferred_element_type=F32)]
    pallas_call x0 -> x11, Pallas kernels: none -> 51.2 us  [the longest x3 19.8 us: product(): pl.pallas_call(body, grid=(1,), out_shape=jax.ShapeDtypeStruct((size, dep...]
    all_to_all x0 -> x4, starting transfers between devices: none -> 25.1 us  [the longest x1 7.09 us: shards(): lax.all_to_all(input_grad.reshape(8, 48, -1), 'col', 0, 0, tiled=True)]
    ppermute x12 -> x0, starting transfers between devices: 18.9 us -> none  [col_send(): return lax.ppermute(x, 'col', pairs)]
    ppermute x35, waiting for transfers between devices: 50.8 us -> 36.6 us  [row_send(): return lax.ppermute(x, 'row', pairs)]
    unnamed x46 -> x68, local copies, waits for them, and re-layouts: 1.76 us -> 14.6 us
    all_to_all x0 -> x4, waiting for transfers between devices: none -> 10.2 us  [the longest x1 7.26 us: shards(): low = lax.all_to_all(low, 'row', 0, 0, tiled=True).reshape(16, ROWS, RANK)]
    ppermute x12 -> x0, waiting for transfers between devices: 6.92 us -> none  [col_send(): return lax.ppermute(x, 'col', pairs)]
  transfers between devices with their start and end apart: 47 -> 39, of which waited for: 18 -> 13; matrix products, arithmetic and copies ran while one was open for 39% -> 10% of each run, Pallas kernels for 0% -> 17%
where the time goes in v3:
time: 204 us; the launch traced here: 202 us
  starting transfers between devices  63.4 us (31%)
  Pallas kernels  51.2 us (25%)
  waiting for transfers between devices  46.7 us (23%)
  local copies, waits for them, and re-layouts  21 us (10%)
  other arithmetic  16.4 us (8%)
    ppermute x35, starting transfers between devices, row_send(): return lax.ppermute(x, 'row', pairs)  38.3 us
    ppermute x35, waiting for transfers between devices, row_send(): return lax.ppermute(x, 'row', pairs)  36.6 us
    pallas_call x3, Pallas kernels, product(): pl.pallas_call(body, grid=(1,), out_shape=jax.ShapeDtypeStruct((size, dep...  19.8 us
    unnamed x68, local copies, waits for them, and re-layouts  14.6 us
    pallas_call x3, Pallas kernels, weight_grad(): pl.pallas_call(body, out_shape=jax.ShapeDtypeStruct((n, depth), BF), in_s...  12.9 us
    pallas_call x2, Pallas kernels, forward(): pl.pallas_call(body, out_shape=[jax.ShapeDtypeStruct((HALF, n), F32), jax...  8.62 us
    all_to_all x1, waiting for transfers between devices, shards(): low = lax.all_to_all(low, 'row', 0, 0, tiled=True).reshape(16, ROWS, RANK)  7.26 us
    all_to_all x1, starting transfers between devices, shards(): lax.all_to_all(input_grad.reshape(8, 48, -1), 'col', 0, 0, tiled=True)  7.09 us
  transfers between devices with their start and end apart: 39, of which 13 were waited for; matrix products, arithmetic and copies ran while one was open for 10% of the time, Pallas kernels for 17%

profile of v3, /device:TPU:0, one launch (start us, length us, event | category | flops | bytes accessed | tf_op | source)
XLA Modules:
  0.0 201.6 jit_solution(2265255946502375936)
XLA Ops:
  6.4 5.4 %forward_first.1 = (f32[192,2752]{1,0:T(8,128)S(1)}, bf16[192,2752]{1,0:T(8,128)(2,1)S(1)}, bf16[384,512]{1,0:T(8,128)(2,1)S(1)}, bf16[384,512]{1,0:T(8,128)(2,1)S(1)}, bf16[384,128]{1,0:T(8,128)(2,1)}) custom-call(bf16[384,512]{1,0:T(8,128)(2,1)S(1)} %copy-done.16, bf16[384,512]{1,0:T(8,128)(2,1)S(1)} %copy-done.17, s32[384,1]{1,0:T(8,128)S(1)} %fusion.23.i_ref, ...), custom_call_target="tpu_custom_call" | custom-call | flops 1024 | bytes 1024 | tf_op jit(solution)/shard_map/forward_first/pallas_call | solution.py:90
  11.9 1.6 collective-permute-start.1
  14.9 3.0 %collective-permute-done.1 = bf16[8,8448]{1,0:T(8,128)(2,1)S(1)} collective-permute-done((bf16[8,8448]{1,0:T(8,128)(2,1)S(1)}, bf16[8,8448]{1,0:T(8,128)(2,1)S(1)}, u32[]{:S(2)}, u32[]{:S(2)}) %collective-permute-start.1) | collective-permute-done | bytes 135200 | tf_op jit(solution)/shard_map/ppermute | solution.py:290
  18.0 4.3 %forward.2 = (f32[192,2752]{1,0:T(8,128)S(1)}, bf16[192,2752]{1,0:T(8,128)(2,1)S(1)}) custom-call(bf16[384,512]{1,0:T(8,128)(2,1)S(1)} %get-tuple-element.78.x_ref, bf16[2752,512]{1,0:T(8,128)(2,1)} %bitcast.123), custom_call_target="tpu_custom_call" | custom-call | flops 1024 | bytes 1024 | tf_op jit(solution)/shard_map/forward/pallas_call | solution.py:123
  22.4 1.6 collective-permute-start.3
  24.0 1.9 collective-permute-start.6
  26.0 3.6 %collective-permute-start.5 = (bf16[2,8,8448]{2,1,0:T(8,128)(2,1)S(1)}, bf16[2,8,8448]{2,1,0:T(8,128)(2,1)S(1)}, u32[]{:S(2)}, u32[]{:S(2)}) collective-permute-start(bf16[2,8,8448]{2,1,0:T(8,128)(2,1)S(1)} %get-tuple-element.151), channel_id=1, source_target_pairs={{0,64},{8,72},{16,80},{24,88},{32,96},{40,104},{48,112},{56,120},{... | collective-permute-start | bytes 811016 | tf_op jit(solution)/shard_map/ppermute | solution.py:290
  30.6 4.3 %forward.3 = (f32[192,2752]{1,0:T(8,128)S(1)}, bf16[192,2752]{1,0:T(8,128)(2,1)S(1)}) custom-call(bf16[384,512]{1,0:T(8,128)(2,1)S(1)} %get-tuple-element.80.x_ref, bf16[2752,512]{1,0:T(8,128)(2,1)} %bitcast.121), custom_call_target="tpu_custom_call" | custom-call | flops 1024 | bytes 1024 | tf_op jit(solution)/shard_map/forward/pallas_call | solution.py:123
  35.0 6.8 %collective-permute-done.5 = bf16[2,8,8448]{2,1,0:T(8,128)(2,1)S(1)} collective-permute-done((bf16[2,8,8448]{2,1,0:T(8,128)(2,1)S(1)}, bf16[2,8,8448]{2,1,0:T(8,128)(2,1)S(1)}, u32[]{:S(2)}, u32[]{:S(2)}) %collective-permute-start.5) | collective-permute-done | bytes 270368 | tf_op jit(solution)/shard_map/ppermute | solution.py:290
  43.8 2.1 %collective-permute-start.10 = (bf16[2,24,2752]{2,1,0:T(8,128)(2,1)}, bf16[2,24,2752]{2,1,0:T(8,128)(2,1)}, u32[]{:S(2)}, u32[]{:S(2)}) collective-permute-start(bf16[2,24,2752]{2,1,0:T(8,128)(2,1)} %get-tuple-element.135), channel_id=1, source_target_pairs={{0,64},{8,72},{16,80},{24,88},{32,96},{40,104},{48,112},{56,120},{... | collective-permute-start | bytes 792584 | tf_op jit(solution)/shard_map/ppermute | solution.py:290
  46.0 1.6 collective-permute-start.9
  48.2 1.3 copy-done.26
  50.9 5.1 %all-to-all-start = ((bf16[16,24,128]{2,1,0:T(8,128)(2,1)}), bf16[16,24,128]{2,1,0:T(8,128)(2,1)S(1)}, u32[]{:S(2)}, u32[]{:S(2)}) async-start(bf16[16,24,128]{2,1,0:T(8,128)(2,1)} %bitcast.25), calls=%async_computation | async-start | bytes 196608 | tf_op jit(solution)/shard_map/all_to_all | solution.py:378
  56.1 2.4 %pad_maximum_fusion = bf16[4,2,8,8448]{3,2,1,0:T(8,128)(2,1)} fusion(bf16[1,2,8,8448]{3,2,1,0:T(8,128)(2,1)} %bitcast.136, bf16[1,2,8,8448]{3,2,1,0:T(8,128)(2,1)} %bitcast.137, bf16[1,2,8,8448]{3,2,1,0:T(8,128)(2,1)} %bitcast.138, bf16[1,2,8,8448]{3,2,1,0:T(8,128)(2,1)S(1)} %get-tuple-element.150), kind=kLoop, calls=%fused_computation.10 | loop fusion | flops 1622016 | bytes 2162688 | tf_op jit(solution)/shard_map/stack | solution.py:389
  59.6 7.3 %all-to-all-done = bf16[16,24,128]{2,1,0:T(8,128)(2,1)S(1)} async-done(((bf16[16,24,128]{2,1,0:T(8,128)(2,1)}), bf16[16,24,128]{2,1,0:T(8,128)(2,1)S(1)}, u32[]{:S(2)}, u32[]{:S(2)}) %all-to-all-start) | async-done | bytes 98336 | tf_op jit(solution)/shard_map/all_to_all | solution.py:378
  67.8 6.6 %all-to-all-start.1 = ((bf16[8,48,640]{2,1,0:T(8,128)(2,1)}), bf16[8,48,640]{2,1,0:T(8,128)(2,1)S(1)}, u32[]{:S(2)}, u32[]{:S(2)}) async-start(bf16[8,48,640]{2,1,0:T(8,128)(2,1)} %broadcast_in_dim.5), calls=%async_computation.1 | async-start | bytes 983040 | tf_op jit(solution)/shard_map/all_to_all | solution.py:382
  76.5 1.4 constant_dynamic-update-slice_fusion.1
  78.8 1.3 collective-permute-start.14
  80.1 2.0 collective-permute-start.13
  82.1 2.9 %all-to-all-done.1 = bf16[8,48,640]{2,1,0:T(8,128)(2,1)S(1)} async-done(((bf16[8,48,640]{2,1,0:T(8,128)(2,1)}), bf16[8,48,640]{2,1,0:T(8,128)(2,1)S(1)}, u32[]{:S(2)}, u32[]{:S(2)}) %all-to-all-start.1) | async-done | bytes 491552 | tf_op jit(solution)/shard_map/all_to_all | solution.py:382
  85.8 1.5 convolution_convert_fusion.low_ref.refs_3_
  88.1 1.5 fusion
  89.6 4.3 %collective-permute-done.12 = bf16[24,2752]{1,0:T(8,128)(2,1)S(1)} collective-permute-done((bf16[24,2752]{1,0:T(8,128)(2,1)}, bf16[24,2752]{1,0:T(8,128)(2,1)S(1)}, u32[]{:S(2)}, u32[]{:S(2)}) %collective-permute-start.12) | collective-permute-done | bytes 132128 | tf_op jit(solution)/shard_map/ppermute | solution.py:290
  94.1 2.0 collective-permute-start.19
  98.6 2.3 %act.1 = (f32[24,2752]{1,0:T(8,128)S(1)}, f32[24,2752]{1,0:T(8,128)S(1)}, bf16[24,2752]{1,0:T(8,128)(2,1)S(1)}) custom-call(f32[24,2752]{1,0:T(8,128)S(1)} %fusion.14.g_ref, f32[24,2752]{1,0:T(8,128)S(1)} %slice_bitcast_fusion.u_ref, bf16[24,2752]{1,0:T(8,128)(2,1)S(1)} %collective-permute-done.15.x_ref, ...), custom_call_target="tpu_custom_call" | custom-call | flops 1024 | bytes 1024 | tf_op jit(solution)/shard_map/act/pallas_call | solution.py:243
  102.4 3.9 %collective-permute-done.17 = bf16[24,2752]{1,0:T(8,128)(2,1)S(1)} collective-permute-done((bf16[24,2752]{1,0:T(8,128)(2,1)S(1)}, bf16[24,2752]{1,0:T(8,128)(2,1)S(1)}, u32[]{:S(2)}, u32[]{:S(2)}) %collective-permute-start.17) | collective-permute-done | bytes 132128 | tf_op jit(solution)/shard_map/ppermute | solution.py:290
  106.3 1.4 collective-permute-start.24
  107.7 3.3 %collective-permute-start.23 = (bf16[2,24,2752]{2,1,0:T(8,128)(2,1)S(1)}, bf16[2,24,2752]{2,1,0:T(8,128)(2,1)S(1)}, u32[]{:S(2)}, u32[]{:S(2)}) collective-permute-start(bf16[2,24,2752]{2,1,0:T(8,128)(2,1)S(1)} %get-tuple-element.149), channel_id=1, source_target_pairs={{0,64},{8,72},{16,80},{24,88},{32,96},{40,104},{48,112},{56,120},{... | collective-permute-start | bytes 792584 | tf_op jit(solution)/shard_map/ppermute | solution.py:290
  111.0 1.4 collective-permute-start.22
  112.4 2.2 %derive.1 = (bf16[24,2752]{1,0:T(8,128)(2,1)S(1)}, bf16[24,2752]{1,0:T(8,128)(2,1)S(1)}) custom-call(f32[24,2752]{1,0:T(8,128)S(1)} %get-tuple-element.107.g_ref, f32[24,2752]{1,0:T(8,128)S(1)} %get-tuple-element.108.u_ref, f32[24,2752]{1,0:T(8,128)S(1)} %slice_bitcast_fusion.4.b_ref, bf16[24,2752]{1,0:T(8,128)(2,1)S(1)} %collective-permute-done.18.p_ref, ...), custom_call_target="tpu_custom_call" | custom-call | flops 1024 | bytes 1024 | tf_op jit(solution)/shard_map/derive/pallas_call | solution.py:272
  114.7 4.9 %collective-permute-done.21 = bf16[24,2752]{1,0:T(8,128)(2,1)S(1)} collective-permute-done((bf16[24,2752]{1,0:T(8,128)(2,1)S(1)}, bf16[24,2752]{1,0:T(8,128)(2,1)S(1)}, u32[]{:S(2)}, u32[]{:S(2)}) %collective-permute-start.21) | collective-permute-done | bytes 132128 | tf_op jit(solution)/shard_map/ppermute | solution.py:290
  120.7 1.9 collective-permute-start.26
  122.5 1.6 collective-permute-start.25
  124.8 5.2 %collective-permute-done.27 = bf16[24,2752]{1,0:T(8,128)(2,1)S(1)} collective-permute-done((bf16[24,2752]{1,0:T(8,128)(2,1)S(1)}, bf16[24,2752]{1,0:T(8,128)(2,1)S(1)}, u32[]{:S(2)}, u32[]{:S(2)}) %collective-permute-start.27) | collective-permute-done | bytes 132128 | tf_op jit(solution)/shard_map/ppermute | solution.py:290
  131.8 6.7 %product.3 = bf16[384,512]{1,0:T(8,128)(2,1)S(1)} custom-call(bf16[192,2752]{1,0:T(8,128)(2,1)S(1)} %bitcast.103, bf16[192,2752]{1,0:T(8,128)(2,1)S(1)} %collective-permute-done.32.refs_1_.other_ref, bf16[128,8448]{1,0:T(8,128)(2,1)S(1)} %constant_dynamic-update-slice_fusion.right_ref.refs_2_, bf16[384,640]{1,0:T(8,128)(2,1)S(1)} %convolution_convert_fusion.low_ref.refs_3_, ...), custom_call_target="tpu_custom_call" | custom-call | flops 1024 | bytes 1024 | tf_op jit(solution)/shard_map/product/pallas_call | solution.py:183
  139.3 6.3 %all-to-all-start.2 = ((bf16[8,48,512]{2,1,0:T(8,128)(2,1)}), bf16[8,48,512]{2,1,0:T(8,128)(2,1)}, u32[]{:S(2)}, u32[]{:S(2)}) async-start(bf16[8,48,512]{2,1,0:T(8,128)(2,1)} %bitcast.108), calls=%async_computation.2 | async-start | bytes 786432 | tf_op jit(solution)/shard_map/all_to_all | solution.py:410
  146.3 1.7 collective-permute-start.30
  148.1 2.4 %collective-permute-start.29 = (bf16[2,24,2752]{2,1,0:T(8,128)(2,1)S(1)}, bf16[2,24,2752]{2,1,0:T(8,128)(2,1)}, u32[]{:S(2)}, u32[]{:S(2)}) collective-permute-start(bf16[2,24,2752]{2,1,0:T(8,128)(2,1)S(1)} %get-tuple-element.147), channel_id=1, source_target_pairs={{0,64},{8,72},{16,80},{24,88},{32,96},{40,104},{48,112},{56,120},{... | collective-permute-start | bytes 792584 | tf_op jit(solution)/shard_map/ppermute | solution.py:290
  154.0 4.3 %weight_grad.3 = bf16[2752,512]{1,0:T(8,128)(2,1)} custom-call(bf16[192,2752]{1,0:T(8,128)(2,1)S(1)} %bitcast.104, bf16[192,2752]{1,0:T(8,128)(2,1)S(1)} %copy-done.9, bf16[384,512]{1,0:T(8,128)(2,1)S(1)} %copy-done.15), custom_call_target="tpu_custom_call" | custom-call | flops 1024 | bytes 1024 | tf_op jit(solution)/shard_map/weight_grad/pallas_call | solution.py:214
  158.3 3.7 %collective-permute-done.29 = bf16[2,24,2752]{2,1,0:T(8,128)(2,1)} collective-permute-done((bf16[2,24,2752]{2,1,0:T(8,128)(2,1)S(1)}, bf16[2,24,2752]{2,1,0:T(8,128)(2,1)}, u32[]{:S(2)}, u32[]{:S(2)}) %collective-permute-start.29) | collective-permute-done | bytes 264224 | tf_op jit(solution)/shard_map/ppermute | solution.py:290
  162.1 1.3 pad_maximum_fusion.2
  166.1 2.2 %collective-permute-done.34.refs_1_.other_ref = bf16[192,2752]{1,0:T(8,128)(2,1)S(1)} collective-permute-done((bf16[192,2752]{1,0:T(8,128)(2,1)S(1)}, bf16[192,2752]{1,0:T(8,128)(2,1)S(1)}, u32[]{:S(2)}, u32[]{:S(2)}) %collective-permute-start.34) | collective-permute-done | bytes 1056800 | tf_op jit(solution)/shard_map/ppermute | solution.py:290
  168.3 6.4 %product.4.refs_4_ = f32[384,512]{1,0:T(8,128)S(1)} custom-call(bf16[192,2752]{1,0:T(8,128)(2,1)S(1)} %bitcast.106, bf16[192,2752]{1,0:T(8,128)(2,1)S(1)} %collective-permute-done.34.refs_1_.other_ref, bf16[128,8448]{1,0:T(8,128)(2,1)S(1)} %constant_dynamic-update-slice_fusion.right_ref.refs_2_, ...), custom_call_target="tpu_custom_call" | custom-call | flops 1024 | bytes 1024 | tf_op jit(solution)/shard_map/product/pallas_call | solution.py:183
  174.8 6.7 %product.5 = bf16[384,512]{1,0:T(8,128)(2,1)S(1)} custom-call(bf16[192,2752]{1,0:T(8,128)(2,1)S(1)} %bitcast.100, bf16[192,2752]{1,0:T(8,128)(2,1)S(1)} %collective-permute-done.33.refs_1_.other_ref, bf16[128,8448]{1,0:T(8,128)(2,1)S(1)} %constant_dynamic-update-slice_fusion.right_ref.refs_2_, bf16[384,640]{1,0:T(8,128)(2,1)S(1)} %convolution_convert_fusion.low_ref.refs_3_, ...), custom_call_target="tpu_custom_call" | custom-call | flops 1024 | bytes 1024 | tf_op jit(solution)/shard_map/product/pallas_call | solution.py:183
  182.3 7.1 %all-to-all-start.3 = ((bf16[8,48,512]{2,1,0:T(8,128)(2,1)}), bf16[8,48,512]{2,1,0:T(8,128)(2,1)S(1)}, u32[]{:S(2)}, u32[]{:S(2)}) async-start(bf16[8,48,512]{2,1,0:T(8,128)(2,1)} %bitcast.109), calls=%async_computation.3 | async-start | bytes 786432 | tf_op jit(solution)/shard_map/all_to_all | solution.py:428
  189.3 1.7 reduce_sum.34
  192.3 4.3 %weight_grad.4 = bf16[2752,512]{1,0:T(8,128)(2,1)} custom-call(bf16[192,2752]{1,0:T(8,128)(2,1)S(1)} %bitcast.101, bf16[192,2752]{1,0:T(8,128)(2,1)S(1)} %copy-done.7, bf16[384,512]{1,0:T(8,128)(2,1)S(1)} %get-tuple-element.78.x_ref), custom_call_target="tpu_custom_call" | custom-call | flops 1024 | bytes 1024 | tf_op jit(solution)/shard_map/weight_grad/pallas_call | solution.py:214
  196.6 4.3 %weight_grad.5 = bf16[2752,512]{1,0:T(8,128)(2,1)} custom-call(bf16[192,2752]{1,0:T(8,128)(2,1)S(1)} %bitcast.107, bf16[192,2752]{1,0:T(8,128)(2,1)S(1)} %copy-done.11, bf16[384,512]{1,0:T(8,128)(2,1)S(1)} %get-tuple-element.78.x_ref), custom_call_target="tpu_custom_call" | custom-call | flops 1024 | bytes 1024 | tf_op jit(solution)/shard_map/weight_grad/pallas_call | solution.py:214
  (148 shorter events, 37.1 us)
Async XLA Ops:
  11.8 18.8 %copy-start.14 = (bf16[384,512]{1,0:T(8,128)(2,1)}, bf16[384,512]{1,0:T(8,128)(2,1)S(1)}, u32[]{:S(2)}) copy-start(bf16[384,512]{1,0:T(8,128)(2,1)S(1)} %get-tuple-element.80.x_ref) | copy-start | bytes 1179652
  11.8 2.8 %collective-permute-start = (bf16[192,2752]{1,0:T(8,128)(2,1)S(1)}, bf16[192,2752]{1,0:T(8,128)(2,1)S(1)}, u32[]{:S(2)}, u32[]{:S(2)}) collective-permute-start(bf16[192,2752]{1,0:T(8,128)(2,1)S(1)} %get-tuple-element.72), channel_id=1, source_target_pairs={{0,8},{8,0},{16,24},{24,16},{32,40},{40,32},{48,56},{56,48},{64,72... | collective-permute-start | bytes 3170312 | tf_op jit(solution)/shard_map/ppermute | solution.py:290
  11.9 6.0 %collective-permute-start.1 = (bf16[8,8448]{1,0:T(8,128)(2,1)S(1)}, bf16[8,8448]{1,0:T(8,128)(2,1)S(1)}, u32[]{:S(2)}, u32[]{:S(2)}) collective-permute-start(bf16[8,8448]{1,0:T(8,128)(2,1)S(1)} %concatenate.12), channel_id=1, source_target_pairs={{0,16},{8,24},{16,0},{24,8},{32,48},{40,56},{48,32},{56,40},{64,80... | collective-permute-start | bytes 405512 | tf_op jit(solution)/shard_map/ppermute | solution.py:290
  22.3 19.6 %collective-permute-start.7 = (bf16[192,2752]{1,0:T(8,128)(2,1)S(1)}, bf16[192,2752]{1,0:T(8,128)(2,1)S(1)}, u32[]{:S(2)}, u32[]{:S(2)}) collective-permute-start(bf16[192,2752]{1,0:T(8,128)(2,1)S(1)} %get-tuple-element.79), channel_id=1, source_target_pairs={{0,8},{8,0},{16,24},{24,16},{32,40},{40,32},{48,56},{56,48},{64,72... | collective-permute-start | bytes 3170312 | tf_op jit(solution)/shard_map/ppermute | solution.py:290
  22.4 19.5 %collective-permute-start.3 = (bf16[4,24,2752]{2,1,0:T(8,128)(2,1)S(1)}, bf16[4,24,2752]{2,1,0:T(8,128)(2,1)S(1)}, u32[]{:S(2)}, u32[]{:S(2)}) collective-permute-start(bf16[4,24,2752]{2,1,0:T(8,128)(2,1)S(1)} %fusion.3), channel_id=1, source_target_pairs={{0,16},{8,24},{16,0},{24,8},{32,48},{40,56},{48,32},{56,40},{64,80... | collective-permute-start | bytes 1585160 | tf_op jit(solution)/shard_map/ppermute | solution.py:290
  24.0 10.9 %collective-permute-start.6 = (bf16[2,8,8448]{2,1,0:T(8,128)(2,1)S(1)}, bf16[2,8,8448]{2,1,0:T(8,128)(2,1)S(1)}, u32[]{:S(2)}, u32[]{:S(2)}) collective-permute-start(bf16[2,8,8448]{2,1,0:T(8,128)(2,1)S(1)} %get-tuple-element.151), channel_id=1, source_target_pairs={{0,32},{8,40},{16,48},{24,56},{32,64},{40,72},{48,80},{56,88},{64,... | collective-permute-start | bytes 811016 | tf_op jit(solution)/shard_map/ppermute | solution.py:290
  26.0 15.9 %collective-permute-start.5 = (bf16[2,8,8448]{2,1,0:T(8,128)(2,1)S(1)}, bf16[2,8,8448]{2,1,0:T(8,128)(2,1)S(1)}, u32[]{:S(2)}, u32[]{:S(2)}) collective-permute-start(bf16[2,8,8448]{2,1,0:T(8,128)(2,1)S(1)} %get-tuple-element.151), channel_id=1, source_target_pairs={{0,64},{8,72},{16,80},{24,88},{32,96},{40,104},{48,112},{56,120},{... | collective-permute-start | bytes 811016 | tf_op jit(solution)/shard_map/ppermute | solution.py:290
  29.5 12.3 %collective-permute-start.4 = (bf16[2,8,8448]{2,1,0:T(8,128)(2,1)S(1)}, bf16[2,8,8448]{2,1,0:T(8,128)(2,1)S(1)}, u32[]{:S(2)}, u32[]{:S(2)}) collective-permute-start(bf16[2,8,8448]{2,1,0:T(8,128)(2,1)S(1)} %get-tuple-element.151), channel_id=1, source_target_pairs={{0,96},{8,104},{16,112},{24,120},{32,0},{40,8},{48,16},{56,24},{64... | collective-permute-start | bytes 811016 | tf_op jit(solution)/shard_map/ppermute | solution.py:290
  34.9 7.0 %copy-start.30 = (bf16[2,8,8448]{2,1,0:T(8,128)(2,1)}, bf16[2,8,8448]{2,1,0:T(8,128)(2,1)S(1)}, u32[]{:S(2)}) copy-start(bf16[2,8,8448]{2,1,0:T(8,128)(2,1)S(1)} %collective-permute-done.6) | copy-start | bytes 811012
  34.9 13.1 %collective-permute-start.2 = (bf16[192,2752]{1,0:T(8,128)(2,1)S(1)}, bf16[192,2752]{1,0:T(8,128)(2,1)S(1)}, u32[]{:S(2)}, u32[]{:S(2)}) collective-permute-start(bf16[192,2752]{1,0:T(8,128)(2,1)S(1)} %get-tuple-element.81), channel_id=1, source_target_pairs={{0,8},{8,0},{16,24},{24,16},{32,40},{40,32},{48,56},{56,48},{64,72... | collective-permute-start | bytes 3170312 | tf_op jit(solution)/shard_map/ppermute | solution.py:290
  43.8 30.6 %collective-permute-start.10 = (bf16[2,24,2752]{2,1,0:T(8,128)(2,1)}, bf16[2,24,2752]{2,1,0:T(8,128)(2,1)}, u32[]{:S(2)}, u32[]{:S(2)}) collective-permute-start(bf16[2,24,2752]{2,1,0:T(8,128)(2,1)} %get-tuple-element.135), channel_id=1, source_target_pairs={{0,64},{8,72},{16,80},{24,88},{32,96},{40,104},{48,112},{56,120},{... | collective-permute-start | bytes 792584 | tf_op jit(solution)/shard_map/ppermute | solution.py:290
  46.0 28.5 %collective-permute-start.9 = (bf16[2,24,2752]{2,1,0:T(8,128)(2,1)}, bf16[2,24,2752]{2,1,0:T(8,128)(2,1)}, u32[]{:S(2)}, u32[]{:S(2)}) collective-permute-start(bf16[2,24,2752]{2,1,0:T(8,128)(2,1)} %get-tuple-element.136), channel_id=1, source_target_pairs={{0,96},{8,104},{16,112},{24,120},{32,0},{40,8},{48,16},{56,24},{64... | collective-permute-start | bytes 792584 | tf_op jit(solution)/shard_map/ppermute | solution.py:290
  47.6 26.9 %collective-permute-start.8 = (bf16[2,24,2752]{2,1,0:T(8,128)(2,1)}, bf16[2,24,2752]{2,1,0:T(8,128)(2,1)}, u32[]{:S(2)}, u32[]{:S(2)}) collective-permute-start(bf16[2,24,2752]{2,1,0:T(8,128)(2,1)} %get-tuple-element.137), channel_id=1, source_target_pairs={{0,32},{8,40},{16,48},{24,56},{32,64},{40,72},{48,80},{56,88},{64,... | collective-permute-start | bytes 792584 | tf_op jit(solution)/shard_map/ppermute | solution.py:290
  50.4 36.9 %collective-permute-start.11 = (bf16[4,24,2752]{2,1,0:T(8,128)(2,1)}, bf16[4,24,2752]{2,1,0:T(8,128)(2,1)}, u32[]{:S(2)}, u32[]{:S(2)}) collective-permute-start(bf16[4,24,2752]{2,1,0:T(8,128)(2,1)} %fusion.4), channel_id=1, source_target_pairs={{0,16},{8,24},{16,0},{24,8},{32,48},{40,56},{48,32},{56,40},{64,80... | collective-permute-start | bytes 1585160 | tf_op jit(solution)/shard_map/ppermute | solution.py:290
  50.9 15.9 %all-to-all-start = ((bf16[16,24,128]{2,1,0:T(8,128)(2,1)}), bf16[16,24,128]{2,1,0:T(8,128)(2,1)S(1)}, u32[]{:S(2)}, u32[]{:S(2)}) async-start(bf16[16,24,128]{2,1,0:T(8,128)(2,1)} %bitcast.25), calls=%async_computation | async-start | bytes 196608 | tf_op jit(solution)/shard_map/all_to_all | solution.py:378
  58.4 8.5 %copy-start.19 = (bf16[512,16]{0,1:T(8,128)(2,1)S(1)}, bf16[512,16]{0,1:T(8,128)(2,1)}, u32[]{:S(2)}) copy-start(bf16[512,16]{0,1:T(8,128)(2,1)} %param.16) | copy-start | bytes 49156
  58.4 8.5 %copy-start.21 = (bf16[512,16]{0,1:T(8,128)(2,1)S(1)}, bf16[512,16]{0,1:T(8,128)(2,1)}, u32[]{:S(2)}) copy-start(bf16[512,16]{0,1:T(8,128)(2,1)} %param.17) | copy-start | bytes 49156
  58.4 8.5 %copy-start.23 = (bf16[512,16]{0,1:T(8,128)(2,1)S(1)}, bf16[512,16]{0,1:T(8,128)(2,1)}, u32[]{:S(2)}) copy-start(bf16[512,16]{0,1:T(8,128)(2,1)} %param.18) | copy-start | bytes 49156
  67.8 17.2 %all-to-all-start.1 = ((bf16[8,48,640]{2,1,0:T(8,128)(2,1)}), bf16[8,48,640]{2,1,0:T(8,128)(2,1)S(1)}, u32[]{:S(2)}, u32[]{:S(2)}) async-start(bf16[8,48,640]{2,1,0:T(8,128)(2,1)} %broadcast_in_dim.5), calls=%async_computation.1 | async-start | bytes 983040 | tf_op jit(solution)/shard_map/all_to_all | solution.py:382
  76.4 20.9 %collective-permute-start.16 = (bf16[64,8448]{1,0:T(8,128)(2,1)}, bf16[64,8448]{1,0:T(8,128)(2,1)}, u32[]{:S(2)}, u32[]{:S(2)}) collective-permute-start(bf16[64,8448]{1,0:T(8,128)(2,1)} %bitcast.32), channel_id=1, source_target_pairs={{0,8},{8,0},{16,24},{24,16},{32,40},{40,32},{48,56},{56,48},{64,72... | collective-permute-start | bytes 3244040 | tf_op jit(solution)/shard_map/ppermute | solution.py:290
  77.9 20.8 %collective-permute-start.15 = (bf16[24,2752]{1,0:T(8,128)(2,1)}, bf16[24,2752]{1,0:T(8,128)(2,1)S(1)}, u32[]{:S(2)}, u32[]{:S(2)}) collective-permute-start(bf16[24,2752]{1,0:T(8,128)(2,1)} %fusion.44), channel_id=1, source_target_pairs={{0,16},{8,24},{16,0},{24,8},{32,48},{40,56},{48,32},{56,40},{64,80... | collective-permute-start | bytes 396296 | tf_op jit(solution)/shard_map/ppermute | solution.py:290
  78.8 10.8 %collective-permute-start.14 = (bf16[24,2752]{1,0:T(8,128)(2,1)}, bf16[24,2752]{1,0:T(8,128)(2,1)}, u32[]{:S(2)}, u32[]{:S(2)}) collective-permute-start(bf16[24,2752]{1,0:T(8,128)(2,1)} %get-tuple-element.143), channel_id=1, source_target_pairs={{0,64},{8,72},{16,80},{24,88},{32,96},{40,104},{48,112},{56,120},{... | collective-permute-start | bytes 396296 | tf_op jit(solution)/shard_map/ppermute | solution.py:290
  80.1 9.4 %collective-permute-start.13 = (bf16[24,2752]{1,0:T(8,128)(2,1)}, bf16[24,2752]{1,0:T(8,128)(2,1)}, u32[]{:S(2)}, u32[]{:S(2)}) collective-permute-start(bf16[24,2752]{1,0:T(8,128)(2,1)} %get-tuple-element.144), channel_id=1, source_target_pairs={{0,96},{8,104},{16,112},{24,120},{32,0},{40,8},{48,16},{56,24},{64... | collective-permute-start | bytes 396296 | tf_op jit(solution)/shard_map/ppermute | solution.py:290
  87.3 6.5 %collective-permute-start.12 = (bf16[24,2752]{1,0:T(8,128)(2,1)}, bf16[24,2752]{1,0:T(8,128)(2,1)S(1)}, u32[]{:S(2)}, u32[]{:S(2)}) collective-permute-start(bf16[24,2752]{1,0:T(8,128)(2,1)} %get-tuple-element.145), channel_id=1, source_target_pairs={{0,32},{8,40},{16,48},{24,56},{32,64},{40,72},{48,80},{56,88},{64,... | collective-permute-start | bytes 396296 | tf_op jit(solution)/shard_map/ppermute | solution.py:290
  93.9 7.6 %collective-permute-start.20 = (bf16[24,2752]{1,0:T(8,128)(2,1)S(1)}, bf16[24,2752]{1,0:T(8,128)(2,1)S(1)}, u32[]{:S(2)}, u32[]{:S(2)}) collective-permute-start(bf16[24,2752]{1,0:T(8,128)(2,1)S(1)} %get-tuple-element.140), channel_id=1, source_target_pairs={{0,64},{8,72},{16,80},{24,88},{32,96},{40,104},{48,112},{56,120},{... | collective-permute-start | bytes 396296 | tf_op jit(solution)/shard_map/ppermute | solution.py:290
  94.1 7.4 %collective-permute-start.19 = (bf16[24,2752]{1,0:T(8,128)(2,1)S(1)}, bf16[24,2752]{1,0:T(8,128)(2,1)S(1)}, u32[]{:S(2)}, u32[]{:S(2)}) collective-permute-start(bf16[24,2752]{1,0:T(8,128)(2,1)S(1)} %get-tuple-element.141), channel_id=1, source_target_pairs={{0,96},{8,104},{16,112},{24,120},{32,0},{40,8},{48,16},{56,24},{64... | collective-permute-start | bytes 396296 | tf_op jit(solution)/shard_map/ppermute | solution.py:290
  96.1 6.2 %collective-permute-start.18 = (bf16[24,2752]{1,0:T(8,128)(2,1)S(1)}, bf16[24,2752]{1,0:T(8,128)(2,1)S(1)}, u32[]{:S(2)}, u32[]{:S(2)}) collective-permute-start(bf16[24,2752]{1,0:T(8,128)(2,1)S(1)} %get-tuple-element.142), channel_id=1, source_target_pairs={{0,32},{8,40},{16,48},{24,56},{32,64},{40,72},{48,80},{56,88},{64,... | collective-permute-start | bytes 396296 | tf_op jit(solution)/shard_map/ppermute | solution.py:290
  101.0 5.3 %collective-permute-start.17 = (bf16[24,2752]{1,0:T(8,128)(2,1)S(1)}, bf16[24,2752]{1,0:T(8,128)(2,1)S(1)}, u32[]{:S(2)}, u32[]{:S(2)}) collective-permute-start(bf16[24,2752]{1,0:T(8,128)(2,1)S(1)} %get-tuple-element.105), channel_id=1, source_target_pairs={{0,16},{8,24},{16,0},{24,8},{32,48},{40,56},{48,32},{56,40},{64,80... | collective-permute-start | bytes 396296 | tf_op jit(solution)/shard_map/ppermute | solution.py:290
  106.3 13.4 %collective-permute-start.24 = (bf16[2,24,2752]{2,1,0:T(8,128)(2,1)S(1)}, bf16[2,24,2752]{2,1,0:T(8,128)(2,1)S(1)}, u32[]{:S(2)}, u32[]{:S(2)}) collective-permute-start(bf16[2,24,2752]{2,1,0:T(8,128)(2,1)S(1)} %get-tuple-element.149), channel_id=1, source_target_pairs={{0,32},{8,40},{16,48},{24,56},{32,64},{40,72},{48,80},{56,88},{64,... | collective-permute-start | bytes 792584 | tf_op jit(solution)/shard_map/ppermute | solution.py:290
  107.7 12.0 %collective-permute-start.23 = (bf16[2,24,2752]{2,1,0:T(8,128)(2,1)S(1)}, bf16[2,24,2752]{2,1,0:T(8,128)(2,1)S(1)}, u32[]{:S(2)}, u32[]{:S(2)}) collective-permute-start(bf16[2,24,2752]{2,1,0:T(8,128)(2,1)S(1)} %get-tuple-element.149), channel_id=1, source_target_pairs={{0,64},{8,72},{16,80},{24,88},{32,96},{40,104},{48,112},{56,120},{... | collective-permute-start | bytes 792584 | tf_op jit(solution)/shard_map/ppermute | solution.py:290
  111.0 8.7 %collective-permute-start.22 = (bf16[2,24,2752]{2,1,0:T(8,128)(2,1)S(1)}, bf16[2,24,2752]{2,1,0:T(8,128)(2,1)S(1)}, u32[]{:S(2)}, u32[]{:S(2)}) collective-permute-start(bf16[2,24,2752]{2,1,0:T(8,128)(2,1)S(1)} %get-tuple-element.149), channel_id=1, source_target_pairs={{0,96},{8,104},{16,112},{24,120},{32,0},{40,8},{48,16},{56,24},{64... | collective-permute-start | bytes 792584 | tf_op jit(solution)/shard_map/ppermute | solution.py:290
  114.6 5.1 %collective-permute-start.21 = (bf16[24,2752]{1,0:T(8,128)(2,1)S(1)}, bf16[24,2752]{1,0:T(8,128)(2,1)S(1)}, u32[]{:S(2)}, u32[]{:S(2)}) collective-permute-start(bf16[24,2752]{1,0:T(8,128)(2,1)S(1)} %get-tuple-element.116), channel_id=1, source_target_pairs={{0,16},{8,24},{16,0},{24,8},{32,48},{40,56},{48,32},{56,40},{64,80... | collective-permute-start | bytes 396296 | tf_op jit(solution)/shard_map/ppermute | solution.py:290
  119.8 18.7 %copy-start.2 = (bf16[4,2,24,2752]{3,2,1,0:T(8,128)(2,1)}, bf16[4,2,24,2752]{3,2,1,0:T(8,128)(2,1)S(1)}, u32[]{:S(2)}) copy-start(bf16[4,2,24,2752]{3,2,1,0:T(8,128)(2,1)S(1)} %pad_maximum_fusion.1) | copy-start | bytes 3170308
  119.8 12.0 %collective-permute-start.32 = (bf16[192,2752]{1,0:T(8,128)(2,1)S(1)}, bf16[192,2752]{1,0:T(8,128)(2,1)S(1)}, u32[]{:S(2)}, u32[]{:S(2)}) collective-permute-start(bf16[192,2752]{1,0:T(8,128)(2,1)S(1)} %bitcast.102), channel_id=1, source_target_pairs={{0,8},{8,0},{16,24},{24,16},{32,40},{40,32},{48,56},{56,48},{64,72... | collective-permute-start | bytes 3170312 | tf_op jit(solution)/shard_map/ppermute | solution.py:290
  119.9 10.1 %collective-permute-start.27 = (bf16[24,2752]{1,0:T(8,128)(2,1)S(1)}, bf16[24,2752]{1,0:T(8,128)(2,1)S(1)}, u32[]{:S(2)}, u32[]{:S(2)}) collective-permute-start(bf16[24,2752]{1,0:T(8,128)(2,1)S(1)} %get-tuple-element.115), channel_id=1, source_target_pairs={{0,32},{8,40},{16,48},{24,56},{32,64},{40,72},{48,80},{56,88},{64,... | collective-permute-start | bytes 396296 | tf_op jit(solution)/shard_map/ppermute | solution.py:290
  120.7 9.4 %collective-permute-start.26 = (bf16[24,2752]{1,0:T(8,128)(2,1)S(1)}, bf16[24,2752]{1,0:T(8,128)(2,1)S(1)}, u32[]{:S(2)}, u32[]{:S(2)}) collective-permute-start(bf16[24,2752]{1,0:T(8,128)(2,1)S(1)} %get-tuple-element.115), channel_id=1, source_target_pairs={{0,64},{8,72},{16,80},{24,88},{32,96},{40,104},{48,112},{56,120},{... | collective-permute-start | bytes 396296 | tf_op jit(solution)/shard_map/ppermute | solution.py:290
  122.5 8.1 %collective-permute-start.25 = (bf16[24,2752]{1,0:T(8,128)(2,1)S(1)}, bf16[24,2752]{1,0:T(8,128)(2,1)S(1)}, u32[]{:S(2)}, u32[]{:S(2)}) collective-permute-start(bf16[24,2752]{1,0:T(8,128)(2,1)S(1)} %get-tuple-element.115), channel_id=1, source_target_pairs={{0,96},{8,104},{16,112},{24,120},{32,0},{40,8},{48,16},{56,24},{64... | collective-permute-start | bytes 396296 | tf_op jit(solution)/shard_map/ppermute | solution.py:290
  131.7 30.4 %collective-permute-start.31 = (bf16[4,24,2752]{2,1,0:T(8,128)(2,1)}, bf16[4,24,2752]{2,1,0:T(8,128)(2,1)}, u32[]{:S(2)}, u32[]{:S(2)}) collective-permute-start(bf16[4,24,2752]{2,1,0:T(8,128)(2,1)} %get-tuple-element.139), channel_id=1, source_target_pairs={{0,16},{8,24},{16,0},{24,8},{32,48},{40,56},{48,32},{56,40},{64,80... | collective-permute-start | bytes 1585160 | tf_op jit(solution)/shard_map/ppermute | solution.py:290
  139.3 22.8 %all-to-all-start.2 = ((bf16[8,48,512]{2,1,0:T(8,128)(2,1)}), bf16[8,48,512]{2,1,0:T(8,128)(2,1)}, u32[]{:S(2)}, u32[]{:S(2)}) async-start(bf16[8,48,512]{2,1,0:T(8,128)(2,1)} %bitcast.108), calls=%async_computation.2 | async-start | bytes 786432 | tf_op jit(solution)/shard_map/all_to_all | solution.py:410
  146.3 12.0 %collective-permute-start.30 = (bf16[2,24,2752]{2,1,0:T(8,128)(2,1)S(1)}, bf16[2,24,2752]{2,1,0:T(8,128)(2,1)S(1)}, u32[]{:S(2)}, u32[]{:S(2)}) collective-permute-start(bf16[2,24,2752]{2,1,0:T(8,128)(2,1)S(1)} %get-tuple-element.147), channel_id=1, source_target_pairs={{0,32},{8,40},{16,48},{24,56},{32,64},{40,72},{48,80},{56,88},{64,... | collective-permute-start | bytes 792584 | tf_op jit(solution)/shard_map/ppermute | solution.py:290
  148.1 14.0 %collective-permute-start.29 = (bf16[2,24,2752]{2,1,0:T(8,128)(2,1)S(1)}, bf16[2,24,2752]{2,1,0:T(8,128)(2,1)}, u32[]{:S(2)}, u32[]{:S(2)}) collective-permute-start(bf16[2,24,2752]{2,1,0:T(8,128)(2,1)S(1)} %get-tuple-element.147), channel_id=1, source_target_pairs={{0,64},{8,72},{16,80},{24,88},{32,96},{40,104},{48,112},{56,120},{... | collective-permute-start | bytes 792584 | tf_op jit(solution)/shard_map/ppermute | solution.py:290
  150.5 11.6 %collective-permute-start.28 = (bf16[2,24,2752]{2,1,0:T(8,128)(2,1)S(1)}, bf16[2,24,2752]{2,1,0:T(8,128)(2,1)}, u32[]{:S(2)}, u32[]{:S(2)}) collective-permute-start(bf16[2,24,2752]{2,1,0:T(8,128)(2,1)S(1)} %get-tuple-element.147), channel_id=1, source_target_pairs={{0,96},{8,104},{16,112},{24,120},{32,0},{40,8},{48,16},{56,24},{64... | collective-permute-start | bytes 792584 | tf_op jit(solution)/shard_map/ppermute | solution.py:290
  163.5 11.3 %copy-start = (bf16[4,2,24,2752]{3,2,1,0:T(8,128)(2,1)}, bf16[4,2,24,2752]{3,2,1,0:T(8,128)(2,1)S(1)}, u32[]{:S(2)}) copy-start(bf16[4,2,24,2752]{3,2,1,0:T(8,128)(2,1)S(1)} %copy.27) | copy-start | bytes 3170308
  165.5 9.2 %copy-start.4 = (bf16[4,2,24,2752]{3,2,1,0:T(8,128)(2,1)}, bf16[4,2,24,2752]{3,2,1,0:T(8,128)(2,1)S(1)}, u32[]{:S(2)}) copy-start(bf16[4,2,24,2752]{3,2,1,0:T(8,128)(2,1)S(1)} %pad_maximum_fusion.3) | copy-start | bytes 3170308
  165.6 2.8 %collective-permute-start.34 = (bf16[192,2752]{1,0:T(8,128)(2,1)S(1)}, bf16[192,2752]{1,0:T(8,128)(2,1)S(1)}, u32[]{:S(2)}, u32[]{:S(2)}) collective-permute-start(bf16[192,2752]{1,0:T(8,128)(2,1)S(1)} %bitcast.105), channel_id=1, source_target_pairs={{0,8},{8,0},{16,24},{24,16},{32,40},{40,32},{48,56},{56,48},{64,72... | collective-permute-start | bytes 3170312 | tf_op jit(solution)/shard_map/ppermute | solution.py:290
  165.6 9.1 %collective-permute-start.33 = (bf16[192,2752]{1,0:T(8,128)(2,1)S(1)}, bf16[192,2752]{1,0:T(8,128)(2,1)S(1)}, u32[]{:S(2)}, u32[]{:S(2)}) collective-permute-start(bf16[192,2752]{1,0:T(8,128)(2,1)S(1)} %bitcast.99), channel_id=1, source_target_pairs={{0,8},{8,0},{16,24},{24,16},{32,40},{40,32},{48,56},{56,48},{64,72... | collective-permute-start | bytes 3170312 | tf_op jit(solution)/shard_map/ppermute | solution.py:290
  182.2 8.8 %copy-start.1 = (bf16[4,2,24,2752]{3,2,1,0:T(8,128)(2,1)S(1)}, bf16[4,2,24,2752]{3,2,1,0:T(8,128)(2,1)}, u32[]{:S(2)}) copy-start(bf16[4,2,24,2752]{3,2,1,0:T(8,128)(2,1)} %copy-done) | copy-start | bytes 3170308
  182.3 18.7 %all-to-all-start.3 = ((bf16[8,48,512]{2,1,0:T(8,128)(2,1)}), bf16[8,48,512]{2,1,0:T(8,128)(2,1)S(1)}, u32[]{:S(2)}, u32[]{:S(2)}) async-start(bf16[8,48,512]{2,1,0:T(8,128)(2,1)} %bitcast.109), calls=%async_computation.3 | async-start | bytes 786432 | tf_op jit(solution)/shard_map/all_to_all | solution.py:428
  (24 other events, 55.5 us)

commit v4 on v1

v4 whole, which is shorter than its diff:
```python
import jax
import jax.numpy as jnp
from jax import lax
from jax.experimental import pallas as pl
from jax.experimental.pallas import tpu as pltpu
from jax.sharding import PartitionSpec as P

BF = jnp.bfloat16
F32 = jnp.float32
ROWS = 24
HALF = 192
SIZE = 384
CHUNK = 1408
STEP = 512
RANK = 128

NN = ((1,), (0,))
NT = ((1,), (1,))
TN = ((0,), (0,))

VMEM = pl.BlockSpec(memory_space=pltpu.VMEM)
HBM = pl.BlockSpec(memory_space=pltpu.HBM)


def dot(a, b, dims):
    return lax.dot_general(a, b, (dims, ((), ())), preferred_element_type=F32)


def tie(*arrays):
    return lax.optimization_barrier(arrays)


def cuts(n, step):
    return [(at, min(step, n - at)) for at in range(0, n, step)]


def padded(n):
    return -(-n // 128) * 128


def pick(index_ref, size):
    return (index_ref[...] == lax.broadcasted_iota(jnp.int32, (size, size), 1)).astype(BF)


def pallas(body, name, ins, outs, in_specs, out_specs, scratch):
    return pl.pallas_call(
        body,
        out_shape=outs,
        in_specs=in_specs,
        out_specs=out_specs,
        scratch_shapes=scratch,
        compiler_params=pltpu.CompilerParams(vmem_limit_bytes=16 * 1024 * 1024),
        name=name,
    )(*ins)


def forward_pair(tokens, grad_out, index, gate_w, down_w):
    n, depth = gate_w.shape
    wide = padded(n)

    def body(t_ref, g_ref, i_ref, gw_ref, dw_ref, mine_ref, theirs_ref, tok_ref, out_ref):
        mine_ref[:, n:wide] = jnp.zeros((HALF, wide - n), F32)
        theirs_ref[:, n:wide] = jnp.zeros((HALF, wide - n), BF)
        turn = pick(i_ref, SIZE)

        def product(x_ref, w_ref, first):
            for at, size in cuts(n, CHUNK):
                got = dot(x_ref[...], w_ref[at : at + size, :], NT)
                mine_ref[:, first + at : first + at + size] = got[:HALF]
                theirs_ref[:, first + at : first + at + size] = got[HALF:].astype(BF)

        tok_ref[...] = dot(turn, t_ref[...], NN).astype(BF)
        product(tok_ref, gw_ref, 0)
        out_ref[...] = dot(turn, g_ref[...], NN).astype(BF)
        product(out_ref, dw_ref, wide)

    cols = wide + n
    return pallas(
        body,
        "forward_pair",
        (tokens, grad_out, index, gate_w, down_w),
        [
            jax.ShapeDtypeStruct((HALF, cols), F32),
            jax.ShapeDtypeStruct((HALF, cols), BF),
            jax.ShapeDtypeStruct((SIZE, depth), BF),
            jax.ShapeDtypeStruct((SIZE, depth), BF),
        ],
        [VMEM] * 5,
        [VMEM] * 4,
        [],
    )


def forward_up(tok, out, lefts, up_w):
    n, depth = up_w.shape
    low = 3 * RANK

    def body(t_ref, o_ref, l_ref, w_ref, mine_ref, theirs_ref):
        def put(at, size, got):
            mine_ref[:, at : at + size] = got[:HALF]
            theirs_ref[:, at : at + size] = got[HALF:].astype(BF)

        put(0, 2 * RANK, dot(t_ref[...], l_ref[: 2 * RANK, :], NT))
        put(2 * RANK, RANK, dot(o_ref[...], l_ref[2 * RANK :, :], NT))
        for at, size in cuts(n, CHUNK):
            put(low + at, size, dot(t_ref[...], w_ref[at : at + size, :], NT))

    return pallas(
        body,
        "forward_up",
        (tok, out, lefts, up_w),
        [jax.ShapeDtypeStruct((HALF, low + n), F32), jax.ShapeDtypeStruct((HALF, low + n), BF)],
        [VMEM] * 4,
        [VMEM] * 2,
        [],
    )


def act(pair, pair_x, up, parts, near, far, sort, n):
    wide = padded(n)
    low_n = 3 * RANK

    def body(p_ref, px_ref, u_ref, a_ref, b_ref, c_ref, near_ref, far_ref, sort_ref, hidden_ref, delta_ref):
        def total(at, size):
            part = slice(at, at + size)
            return u_ref[:, part] + a_ref[:, part].astype(F32) + b_ref[:, part].astype(F32) + c_ref[:, part].astype(F32)

        low = total(0, low_n).astype(BF)
        low = [dot(low[:, RANK * t : RANK * (t + 1)], sort_ref[...], NN).astype(BF) for t in range(3)]
        delta_ref[:, n:wide] = jnp.zeros((ROWS, wide - n), BF)
        for at, size in cuts(n, CHUNK):

            def more(t):
                part = slice(wide * t + at, wide * t + at + size)
                return dot(low[t], jnp.concatenate([near_ref[:, part], far_ref[:, part]], axis=0), NN)

            def both(first):
                part = slice(first + at, first + at + size)
                return p_ref[:, part] + px_ref[:, part].astype(F32)

            gate = both(0) + more(0)
            up_value = total(low_n + at, size) + more(1)
            back = both(wide) + more(2)
            sigma = jax.nn.sigmoid(gate)
            hidden_ref[:, at : at + size] = (gate * sigma * up_value).astype(BF)
            slope = sigma * (1.0 + gate * (1.0 - sigma))
            delta_ref[:, at : at + size] = (back * up_value * slope).astype(BF)
            delta_ref[:, wide + at : wide + at + size] = (back * gate * sigma).astype(BF)

    return pallas(
        body,
        "act",
        (pair, pair_x, up, *parts, near, far, sort),
        [jax.ShapeDtypeStruct((ROWS, n), BF), jax.ShapeDtypeStruct((ROWS, wide + n), BF)],
        [VMEM] * 9,
        [VMEM] * 2,
        [],
    )


def through(mine_ref, other_ref, first, w_ref, near_ref, far_ref, left_ref, sort_ref, place):
    n = w_ref.shape[0]
    wide = padded(n)
    total = low = None
    for at, size in cuts(n, CHUNK):
        part = slice(first + at, first + at + size)
        value = jnp.concatenate([mine_ref[:, part], other_ref[:, part]], axis=0)
        part = slice(wide * place + at, wide * place + at + size)
        right = jnp.concatenate([near_ref[:, part], far_ref[:, part]], axis=0)
        more = dot(value, right, NT)
        low = more if low is None else low + more
        more = dot(value, w_ref[at : at + size, :], NN)
        total = more if total is None else total + more
    low = dot(low.astype(BF), sort_ref[...], NT).astype(BF)
    return total + dot(low, left_ref[RANK * place : RANK * (place + 1), :], NN)


def grads(mine_ref, other_ref, first, x_ref, grad_ref, grad_hbm, sems, slot=0):
    n = grad_ref.shape[0]
    sent = []
    for k, (at, size) in enumerate(cuts(n, STEP)):
        part = slice(first + at, first + at + size)
        value = jnp.concatenate([mine_ref[:, part], other_ref[:, part]], axis=0)
        grad_ref[at : at + size, :] = dot(value, x_ref[...], TN).astype(BF)
        part = pl.ds(at, size)
        sent.append(pltpu.make_async_copy(grad_ref.at[part, :], grad_hbm.at[part, :], sems.at[slot + k]))
        sent[-1].start()
    return sent


def backward_hidden(mine, other, x, weight, near, far, lefts, sort, index):
    n, depth = weight.shape

    def body(m_ref, o_ref, x_ref, near_ref, far_ref, l_ref, s_ref, i_ref, w_ref, out_ref, grad_hbm, grad_ref, sems):
        sent = grads(m_ref, o_ref, 0, x_ref, grad_ref, grad_hbm, sems)
        total = through(m_ref, o_ref, 0, w_ref, near_ref, far_ref, l_ref, s_ref, 2)
        out_ref[...] = dot(pick(i_ref, SIZE), total.astype(BF), NN).astype(BF)
        for copy in sent:
            copy.wait()

    return pallas(
        body,
        "backward_hidden",
        (mine, other, x, near, far, lefts, sort, index, weight),
        [jax.ShapeDtypeStruct((SIZE, depth), BF), jax.ShapeDtypeStruct((n, depth), BF)],
        [VMEM] * 9,
        [VMEM, HBM],
        [pltpu.VMEM((n, depth), BF), pltpu.SemaphoreType.DMA((len(cuts(n, STEP)),))],
    )


def backward_pair(mine, other, gate_w, up_w, near, far, lefts, sort, index):
    n, depth = gate_w.shape
    wide = padded(n)

    def body(m_ref, o_ref, near_ref, far_ref, l_ref, s_ref, i_ref, gw_ref, uw_ref, out_ref):
        total = through(m_ref, o_ref, 0, gw_ref, near_ref, far_ref, l_ref, s_ref, 0)
        total = total + through(m_ref, o_ref, wide, uw_ref, near_ref, far_ref, l_ref, s_ref, 1)
        out_ref[...] = dot(pick(i_ref, SIZE), total.astype(BF), NN).astype(BF)

    return pallas(
        body,
        "backward_pair",
        (mine, other, near, far, lefts, sort, index, gate_w, up_w),
        jax.ShapeDtypeStruct((SIZE, depth), BF),
        [VMEM] * 9,
        VMEM,
        [],
    )


def weight_grad(mine, other, x, first, n):
    depth = x.shape[1]

    def body(m_ref, o_ref, x_ref, grad_hbm, grad_ref, sems):
        for copy in grads(m_ref, o_ref, first, x_ref, grad_ref, grad_hbm, sems):
            copy.wait()

    return pallas(
        body,
        "weight_grad",
        (mine, other, x),
        jax.ShapeDtypeStruct((n, depth), BF),
        [VMEM] * 3,
        HBM,
        [pltpu.VMEM((n, depth), BF), pltpu.SemaphoreType.DMA((len(cuts(n, STEP)),))],
    )


def row_send(x, dz, da, dc):
    pairs = []
    for z in range(4):
        for a in range(2):
            for c in range(2):
                to = ((z + dz) % 4) * 4 + ((a + da) % 2) * 2 + (c + dc) % 2
                pairs.append((z * 4 + a * 2 + c, to))
    return lax.ppermute(x, "row", pairs)


def col_send(x, dh, dy):
    pairs = []
    for h in range(2):
        for y in range(4):
            pairs.append((h * 4 + y, ((h + dh) % 2) * 4 + (y + dy) % 4))
    return lax.ppermute(x, "col", pairs)


def z_send(blocks):
    return [row_send(blocks[d].astype(BF), d, 0, 0) for d in (1, 3, 2)]


def z_spread(x):
    return [row_send(x, d, 0, 0) for d in (3, 2, 1)]


def x_send(x):
    return row_send(x, 0, 1, 0)


def core_send(x):
    return row_send(x, 0, 0, 1)


def pair_sum(mine, got):
    return (mine + got.astype(F32)).reshape(4, 2, ROWS, -1)


def plus(own, parts):
    for p in parts:
        own = own + p.astype(F32)
    return own


def shards(
    tokens,
    grad_out,
    gate_weight,
    up_weight,
    down_weight,
    gate_left,
    up_left,
    down_left,
    gate_right,
    up_right,
    down_right,
):
    n = gate_weight.shape[1]
    row, col = lax.axis_index("row"), lax.axis_index("col")
    z, a, c = row // 4, (row // 2) % 2, row % 2
    h, y = col // 4, col % 4

    k = jnp.arange(SIZE, dtype=jnp.int32)

    def owner(block):
        dc, dz, da = block // 8, (block // 2) % 4, block % 2
        return (z + dz) % 4 * 4 + (a + da) % 2 * 2 + (c + dc) % 2

    held = owner(k // ROWS) * ROWS + k % ROWS
    dest = (((h + k // 192) % 2) * 4 + (y + k // 48) % 4) * 48 + k % 48
    block = dest // ROWS
    dc, dz, da = (block % 2 - c) % 2, (block // 4 - z) % 4, ((block // 2) % 2 - a) % 2
    leave = ((dc * 4 + dz) * 2 + da) * ROWS + dest % ROWS
    held, leave = held[:, None], leave[:, None]
    j = jnp.arange(RANK, dtype=jnp.int32)
    sort = (j[:, None] == (owner(j // 8) * 8 + j % 8)[None, :]).astype(BF)
    my, mh, mt, mi = k // 96, (k // 48) % 2, (k // 16) % 3, k % 16
    rank = (((h - mh) % 2) * 4 + (y - my) % 4) * 16 + mi + RANK * mt
    match = (rank[None, :] == k[:, None]).astype(BF)

    gate_w, up_w, down_w = gate_weight.T, up_weight.T, down_weight.T
    edge = jnp.zeros((gate_right.shape[0], padded(n) - n), BF)
    rights = jnp.concatenate([gate_right, edge, up_right, edge, down_right, edge], axis=1)
    lefts = jnp.concatenate([gate_left.T, up_left.T, down_left.T], axis=0)
    lefts_h = col_send(lefts, 1, 0)
    rights_z = z_spread(rights)
    held, rights, lefts = tie(held, rights, lefts)

    mine, theirs, tok, out = forward_pair(tokens, grad_out, held, gate_w, down_w)
    got = core_send(theirs)
    lefts_h, tok = tie(lefts_h, tok)
    lefts = jnp.stack([lefts, lefts_h])
    lefts_y = [col_send(lefts, 0, d) for d in (1, 2, 3)]
    rights = jnp.stack([rights] + rights_z)
    rights_x = x_send(rights)

    tok, pair = tie(tok, pair_sum(mine, got))
    pair_z = z_send(pair)
    lefts = jnp.stack([lefts] + lefts_y).reshape(SIZE, -1)
    lefts = dot(match, lefts, NN).astype(BF)
    mine, theirs = forward_up(tok, out, lefts, up_w)
    got, rights_x = tie(core_send(theirs), rights_x)
    up = pair_sum(mine, got)
    up_x = x_send(up[:, 1].astype(BF))
    near = jnp.stack([rights, rights_x], axis=1).reshape(64, -1)
    far = core_send(near)

    *pair_z, up_x = tie(*pair_z, up_x)
    pair = plus(pair[0], pair_z)
    pair_x = x_send(pair[1].astype(BF))
    up = up[:, 0] + up_x.astype(F32)
    up_z = z_send(up)
    hidden, delta = act(pair[0], pair_x, up[0], up_z, near, far, sort, n)

    delta_x = x_send(delta)
    hidden_z = z_spread(hidden)
    delta_x, hidden_z = tie(delta_x, hidden_z)
    delta = jnp.stack([delta, delta_x])
    delta_z = z_spread(delta)
    hidden = jnp.stack([hidden] + hidden_z)
    hidden_x, delta_z = tie(x_send(hidden), delta_z)
    hidden = jnp.stack([hidden, hidden_x], axis=1).reshape(HALF, n)
    hidden_far = core_send(hidden)
    mixed, down_grad = backward_hidden(hidden, hidden_far, out, down_w, near, far, lefts, sort, leave)
    delta = jnp.stack([delta] + delta_z).reshape(HALF, -1)
    delta_far, mixed = tie(core_send(delta), mixed)
    input_grad = backward_pair(delta, delta_far, gate_w, up_w, near, far, lefts, sort, leave)

    both = jnp.stack([mixed, input_grad]).reshape(2, 2, 4, 48, -1)
    leaving = both[:, 1]
    delta, leaving = tie(delta, leaving)
    both_h = col_send(leaving, 1, 0)
    up_grad = weight_grad(delta, delta_far, tok, padded(n), n)
    both_h, delta, up_grad = tie(both_h, delta, up_grad)
    both = both[:, 0].astype(F32) + both_h.astype(F32)
    delta, leaving = tie(delta, both[:, 1:].astype(BF))
    both_y = [col_send(leaving[:, d - 1], 0, d) for d in (1, 3, 2)]
    gate_grad = weight_grad(delta, delta_far, tok, 0, n)
    both = plus(both[:, 0], both_y).astype(BF)
    return both[0], both[1], gate_grad.T, up_grad.T, down_grad.T


def solution(mesh):
    arg = P("row", "col")
    in_specs = (P(None, "row"), P(None, "row")) + (arg,) * 9
    out_specs = (P("col", "row"), P("col", "row")) + (arg,) * 3
    return jax.shard_map(shards, mesh=mesh, in_specs=in_specs, out_specs=out_specs, check_vma=False)
```

time: 201 us -> 156 us (0.78)
  matrix products: 63.1 us -> 0.37 us
  Pallas kernels: 0 us -> 19 us
  waiting for transfers between devices: 57.7 us -> 74.7 us
  starting transfers between devices: 55.7 us -> 42.3 us
  other arithmetic: 14.5 us -> 8.76 us
    dot_general x24 -> x1, matrix products: 63.1 us -> 0.37 us  [dot(): return lax.dot_general(a, b, (dims, ((), ())), preferred_element_type=F32)]
    pallas_call x0 -> x7, Pallas kernels: none -> 19 us  [pallas(): pl.pallas_call(body, out_shape=outs, in_specs=in_specs, out_specs=out_spe...]
    ppermute x35 -> x25, waiting for transfers between devices: 50.8 us -> 62.2 us  [row_send(): return lax.ppermute(x, 'row', pairs)]
    ppermute x35 -> x25, starting transfers between devices: 36.8 us -> 26 us  [row_send(): return lax.ppermute(x, 'row', pairs)]
    another operation x18 -> x10, other arithmetic: 8.39 us -> 2.14 us  [the longest x2 1.16 us: shards(): near = jnp.stack([rights, rights_x], axis=1).reshape(64, -1)]
    unnamed x46 -> x16, local copies, waits for them, and re-layouts: 1.76 us -> 7.83 us
    ppermute x12 -> x8, waiting for transfers between devices: 6.92 us -> 12.5 us  [col_send(): return lax.ppermute(x, 'col', pairs)]
    slice x6 -> x1, local copies, waits for them, and re-layouts: 5.07 us -> 0.04 us  [shards(): delta, leaving = tie(delta, both[:, 1:].astype(BF))]
  transfers between devices with their start and end apart: 47 -> 33, of which waited for: 18 -> 20; matrix products, arithmetic and copies ran while one was open for 39% -> 5% of each run, Pallas kernels for 0% -> 7%
where the time goes in v4:
time: 156 us
  waiting for transfers between devices  74.7 us (48%)
  starting transfers between devices  42.3 us (27%)
  Pallas kernels  19 us (12%)
  local copies, waits for them, and re-layouts  9.9 us (6%)
  other arithmetic  8.76 us (6%)
    ppermute x25, waiting for transfers between devices, row_send(): return lax.ppermute(x, 'row', pairs)  62.2 us
    ppermute x25, starting transfers between devices, row_send(): return lax.ppermute(x, 'row', pairs)  26 us
    pallas_call x7, Pallas kernels, pallas(): pl.pallas_call(body, out_shape=outs, in_specs=in_specs, out_specs=out_spe...  19 us
    ppermute x8, starting transfers between devices, col_send(): return lax.ppermute(x, 'col', pairs)  16.2 us
    ppermute x8, waiting for transfers between devices, col_send(): return lax.ppermute(x, 'col', pairs)  12.5 us
    unnamed x16, local copies, waits for them, and re-layouts  7.83 us
    add x2, other arithmetic, pair_sum(): return (mine + got.astype(F32)).reshape(4, 2, ROWS, -1)  3.69 us
  transfers between devices with their start and end apart: 33, of which 20 were waited for; matrix products, arithmetic and copies ran while one was open for 5% of the time, Pallas kernels for 7%

profile of v4, /device:TPU:0, one launch (start us, length us, event | category | flops | bytes accessed | tf_op | source)
XLA Modules:
  0.0 156.0 jit_solution(3426673405007421311)
XLA Ops:
  3.0 1.8 %copy-done = bf16[512,2752]{0,1:T(8,128)(2,1)S(1)} copy-done((bf16[512,2752]{0,1:T(8,128)(2,1)S(1)}, bf16[512,2752]{0,1:T(8,128)(2,1)}, u32[]{:S(2)}) %copy-start) | copy-done | bytes 2818072
  4.8 1.8 %copy-done.2 = bf16[512,2752]{0,1:T(8,128)(2,1)S(1)} copy-done((bf16[512,2752]{0,1:T(8,128)(2,1)S(1)}, bf16[512,2752]{0,1:T(8,128)(2,1)}, u32[]{:S(2)}) %copy-start.2) | copy-done | bytes 2818072
  6.6 1.0 copy-done.6
  7.6 1.0 copy-done.7
  8.6 3.2 %forward_pair.1 = (f32[192,5568]{1,0:T(8,128)S(1)}, bf16[192,5568]{1,0:T(8,128)(2,1)S(1)}, bf16[384,512]{1,0:T(8,128)(2,1)S(1)}, bf16[384,512]{1,0:T(8,128)(2,1)S(1)}) custom-call(bf16[384,512]{1,0:T(8,128)(2,1)S(1)} %copy-done.6, bf16[384,512]{1,0:T(8,128)(2,1)S(1)} %copy-done.7, s32[384,1]{1,0:T(8,128)S(1)} %fusion.28.i_ref, ...), custom_call_target="tpu_custom_call" | custom-call | tf_op jit(solution)/shard_map/forward_pair/pallas_call | solution.py:46
  11.8 2.0 %copy-done.5 = f32[192,5568]{1,0:T(8,128)} copy-done((f32[192,5568]{1,0:T(8,128)}, f32[192,5568]{1,0:T(8,128)S(1)}, u32[]{:S(2)}) %copy-start.5) | copy-done | bytes 4276248
  13.8 3.1 %collective-permute-start = (bf16[48,512]{1,0:T(8,128)(2,1)S(1)}, bf16[48,512]{1,0:T(8,128)(2,1)S(1)}, u32[]{:S(2)}, u32[]{:S(2)}) collective-permute-start(bf16[48,512]{1,0:T(8,128)(2,1)S(1)} %pad_maximum_fusion.9), channel_id=1, source_target_pairs={{0,4},{1,5},{2,6},{3,7},{4,0},{5,1},{6,2},{7,3},{8,12},{9,13},{10,... | collective-permute-start | bytes 147464 | tf_op jit(solution)/shard_map/ppermute | solution.py:265
  16.9 4.0 %collective-permute-start.9 = (bf16[8,8448]{1,0:T(8,128)(2,1)S(1)}, bf16[8,8448]{1,0:T(8,128)(2,1)S(1)}, u32[]{:S(2)}, u32[]{:S(2)}) collective-permute-start(bf16[8,8448]{1,0:T(8,128)(2,1)S(1)} %concatenate.8), channel_id=1, source_target_pairs={{0,96},{8,104},{16,112},{24,120},{32,0},{40,8},{48,16},{56,24},{64... | collective-permute-start | bytes 405512 | tf_op jit(solution)/shard_map/ppermute | solution.py:257
  20.9 1.3 collective-permute-start.11
  22.3 1.6 %collective-permute-start.5 = (bf16[2,48,512]{2,1,0:T(8,128)(2,1)S(1)}, bf16[2,48,512]{2,1,0:T(8,128)(2,1)S(1)}, u32[]{:S(2)}, u32[]{:S(2)}) collective-permute-start(bf16[2,48,512]{2,1,0:T(8,128)(2,1)S(1)} %get-tuple-element.105), channel_id=1, source_target_pairs={{0,1},{1,2},{2,3},{3,0},{4,5},{5,6},{6,7},{7,4},{8,9},{9,10},{10,1... | collective-permute-start | bytes 294920 | tf_op jit(solution)/shard_map/ppermute | solution.py:265
  24.0 3.1 %collective-permute-done.9 = bf16[8,8448]{1,0:T(8,128)(2,1)S(1)} collective-permute-done((bf16[8,8448]{1,0:T(8,128)(2,1)S(1)}, bf16[8,8448]{1,0:T(8,128)(2,1)S(1)}, u32[]{:S(2)}, u32[]{:S(2)}) %collective-permute-start.9) | collective-permute-done | bytes 135200 | tf_op jit(solution)/shard_map/ppermute | solution.py:257
  27.1 3.2 %collective-permute-start.6 = (bf16[2,48,512]{2,1,0:T(8,128)(2,1)S(1)}, bf16[2,48,512]{2,1,0:T(8,128)(2,1)S(1)}, u32[]{:S(2)}, u32[]{:S(2)}) collective-permute-start(bf16[2,48,512]{2,1,0:T(8,128)(2,1)S(1)} %get-tuple-element.105), channel_id=1, source_target_pairs={{0,2},{1,3},{2,0},{3,1},{4,6},{5,7},{6,4},{7,5},{8,10},{9,11},{10,... | collective-permute-start | bytes 294920 | tf_op jit(solution)/shard_map/ppermute | solution.py:265
  30.3 1.8 %collective-permute-start.7 = (bf16[2,48,512]{2,1,0:T(8,128)(2,1)S(1)}, bf16[2,48,512]{2,1,0:T(8,128)(2,1)S(1)}, u32[]{:S(2)}, u32[]{:S(2)}) collective-permute-start(bf16[2,48,512]{2,1,0:T(8,128)(2,1)S(1)} %get-tuple-element.105), channel_id=1, source_target_pairs={{0,3},{1,0},{2,1},{3,2},{4,7},{5,4},{6,5},{7,6},{8,11},{9,8},{10,9... | collective-permute-start | bytes 294920 | tf_op jit(solution)/shard_map/ppermute | solution.py:265
  32.0 1.1 fusion.102
  33.8 1.5 collective-permute-done.7
  35.8 3.5 %convert_add_fusion = f32[192,5568]{1,0:T(8,128)S(1)} fusion(f32[192,5568]{1,0:T(8,128)} %copy-done.5, bf16[192,5568]{1,0:T(8,128)(2,1)} %collective-permute-done.1), kind=kLoop, calls=%fused_computation | loop fusion | flops 2138112 | bytes 10690560 | tf_op jit(solution)/shard_map/add | solution.py:285
  39.5 1.6 %forward_up.1 = (f32[192,3136]{1,0:T(8,128)S(1)}, bf16[192,3136]{1,0:T(8,128)(2,1)S(1)}) custom-call(bf16[384,512]{1,0:T(8,128)(2,1)S(1)} %get-tuple-element.51.t_ref.x_ref, bf16[384,512]{1,0:T(8,128)(2,1)S(1)} %get-tuple-element.52.o_ref.x_ref, bf16[384,512]{1,0:T(8,128)(2,1)S(1)} %convolution_convert_fusion.l_ref, bf16[2752,512]{1,0:T(8,128)(2,1)S(1)} %bitcast.120), custom_call_target="tpu_custom_call" | custom-call | tf_op jit(solution)/shard_map/forward_up/pallas_call | solution.py:46
  41.6 3.8 %collective-permute-start.3 = (bf16[2,24,5568]{2,1,0:T(8,128)(2,1)S(1)}, bf16[2,24,5568]{2,1,0:T(8,128)(2,1)S(1)}, u32[]{:S(2)}, u32[]{:S(2)}) collective-permute-start(bf16[2,24,5568]{2,1,0:T(8,128)(2,1)S(1)} %get-tuple-element.88), channel_id=1, source_target_pairs={{0,96},{8,104},{16,112},{24,120},{32,0},{40,8},{48,16},{56,24},{64... | collective-permute-start | bytes 1603592 | tf_op jit(solution)/shard_map/ppermute | solution.py:257
  45.4 1.4 collective-permute-start.4
  48.0 10.2 %collective-permute-done.2 = bf16[2,24,5568]{2,1,0:T(8,128)(2,1)S(1)} collective-permute-done((bf16[2,24,5568]{2,1,0:T(8,128)(2,1)S(1)}, bf16[2,24,5568]{2,1,0:T(8,128)(2,1)S(1)}, u32[]{:S(2)}, u32[]{:S(2)}) %collective-permute-start.2) | collective-permute-done | bytes 534560 | tf_op jit(solution)/shard_map/ppermute | solution.py:257
  58.2 10.9 %collective-permute-done.3 = bf16[2,24,5568]{2,1,0:T(8,128)(2,1)S(1)} collective-permute-done((bf16[2,24,5568]{2,1,0:T(8,128)(2,1)S(1)}, bf16[2,24,5568]{2,1,0:T(8,128)(2,1)S(1)}, u32[]{:S(2)}, u32[]{:S(2)}) %collective-permute-start.3) | collective-permute-done | bytes 534560 | tf_op jit(solution)/shard_map/ppermute | solution.py:257
  69.2 1.8 %collective-permute-done.4 = bf16[2,24,5568]{2,1,0:T(8,128)(2,1)S(1)} collective-permute-done((bf16[2,24,5568]{2,1,0:T(8,128)(2,1)S(1)}, bf16[2,24,5568]{2,1,0:T(8,128)(2,1)S(1)}, u32[]{:S(2)}, u32[]{:S(2)}) %collective-permute-start.4) | collective-permute-done | bytes 534560 | tf_op jit(solution)/shard_map/ppermute | solution.py:257
  71.5 1.2 collective-permute-start.15
  72.7 2.1 %collective-permute-start.16 = (bf16[24,3136]{1,0:T(8,128)(2,1)S(1)}, bf16[24,3136]{1,0:T(8,128)(2,1)S(1)}, u32[]{:S(2)}, u32[]{:S(2)}) collective-permute-start(bf16[24,3136]{1,0:T(8,128)(2,1)S(1)} %get-tuple-element.91), channel_id=1, source_target_pairs={{0,96},{8,104},{16,112},{24,120},{32,0},{40,8},{48,16},{56,24},{64... | collective-permute-start | bytes 451592 | tf_op jit(solution)/shard_map/ppermute | solution.py:257
  75.6 3.0 %collective-permute-done.15.a_ref = bf16[24,3136]{1,0:T(8,128)(2,1)S(1)} collective-permute-done((bf16[24,3136]{1,0:T(8,128)(2,1)S(1)}, bf16[24,3136]{1,0:T(8,128)(2,1)S(1)}, u32[]{:S(2)}, u32[]{:S(2)}) %collective-permute-start.15) | collective-permute-done | bytes 150560 | tf_op jit(solution)/shard_map/ppermute | solution.py:257
  78.6 2.3 %collective-permute-done.16.b_ref = bf16[24,3136]{1,0:T(8,128)(2,1)S(1)} collective-permute-done((bf16[24,3136]{1,0:T(8,128)(2,1)S(1)}, bf16[24,3136]{1,0:T(8,128)(2,1)S(1)}, u32[]{:S(2)}, u32[]{:S(2)}) %collective-permute-start.16) | collective-permute-done | bytes 150560 | tf_op jit(solution)/shard_map/ppermute | solution.py:257
  83.7 2.2 %collective-permute-start.20 = (bf16[24,2752]{1,0:T(8,128)(2,1)S(1)}, bf16[24,2752]{1,0:T(8,128)(2,1)S(1)}, u32[]{:S(2)}, u32[]{:S(2)}) collective-permute-start(bf16[24,2752]{1,0:T(8,128)(2,1)S(1)} %get-tuple-element.65), channel_id=1, source_target_pairs={{0,96},{8,104},{16,112},{24,120},{32,0},{40,8},{48,16},{56,24},{64... | collective-permute-start | bytes 396296 | tf_op jit(solution)/shard_map/ppermute | solution.py:257
  85.9 1.0 collective-permute-start.21
  86.9 1.4 collective-permute-start.22
  89.2 3.4 %collective-permute-done.21 = bf16[24,2752]{1,0:T(8,128)(2,1)S(1)} collective-permute-done((bf16[24,2752]{1,0:T(8,128)(2,1)S(1)}, bf16[24,2752]{1,0:T(8,128)(2,1)S(1)}, u32[]{:S(2)}, u32[]{:S(2)}) %collective-permute-start.21) | collective-permute-done | bytes 132128 | tf_op jit(solution)/shard_map/ppermute | solution.py:257
  92.5 1.4 collective-permute-done.22
  94.6 1.0 collective-permute-start.25
  96.6 1.5 collective-permute-start.23
  98.1 8.6 %collective-permute-done.23 = bf16[4,24,2752]{2,1,0:T(8,128)(2,1)S(1)} collective-permute-done((bf16[4,24,2752]{2,1,0:T(8,128)(2,1)S(1)}, bf16[4,24,2752]{2,1,0:T(8,128)(2,1)S(1)}, u32[]{:S(2)}, u32[]{:S(2)}) %collective-permute-start.23) | collective-permute-done | bytes 528416 | tf_op jit(solution)/shard_map/ppermute | solution.py:257
  106.8 2.5 %collective-permute-done.24 = bf16[2,24,5568]{2,1,0:T(8,128)(2,1)S(1)} collective-permute-done((bf16[2,24,5568]{2,1,0:T(8,128)(2,1)S(1)}, bf16[2,24,5568]{2,1,0:T(8,128)(2,1)S(1)}, u32[]{:S(2)}, u32[]{:S(2)}) %collective-permute-start.24) | collective-permute-done | bytes 534560 | tf_op jit(solution)/shard_map/ppermute | solution.py:257
  109.3 2.1 %collective-permute-done.25 = bf16[2,24,5568]{2,1,0:T(8,128)(2,1)S(1)} collective-permute-done((bf16[2,24,5568]{2,1,0:T(8,128)(2,1)S(1)}, bf16[2,24,5568]{2,1,0:T(8,128)(2,1)S(1)}, u32[]{:S(2)}, u32[]{:S(2)}) %collective-permute-start.25) | collective-permute-done | bytes 534560 | tf_op jit(solution)/shard_map/ppermute | solution.py:257
  111.3 6.5 %collective-permute-done.26 = bf16[2,24,5568]{2,1,0:T(8,128)(2,1)S(1)} collective-permute-done((bf16[2,24,5568]{2,1,0:T(8,128)(2,1)S(1)}, bf16[2,24,5568]{2,1,0:T(8,128)(2,1)S(1)}, u32[]{:S(2)}, u32[]{:S(2)}) %collective-permute-start.26) | collective-permute-done | bytes 534560 | tf_op jit(solution)/shard_map/ppermute | solution.py:257
  118.9 1.0 fusion.49.i_ref
  120.0 4.0 %collective-permute-done.28.o_ref = bf16[192,2752]{1,0:T(8,128)(2,1)S(1)} collective-permute-done((bf16[192,2752]{1,0:T(8,128)(2,1)S(1)}, bf16[192,2752]{1,0:T(8,128)(2,1)S(1)}, u32[]{:S(2)}, u32[]{:S(2)}) %collective-permute-start.28) | collective-permute-done | bytes 1056800 | tf_op jit(solution)/shard_map/ppermute | solution.py:257
  124.0 4.2 %backward_hidden.1 = (bf16[384,512]{1,0:T(8,128)(2,1)S(1)}, bf16[2752,512]{1,0:T(8,128)(2,1)}) custom-call(bf16[192,2752]{1,0:T(8,128)(2,1)S(1)} %bitcast.123, bf16[192,2752]{1,0:T(8,128)(2,1)S(1)} %collective-permute-done.28.o_ref, bf16[384,512]{1,0:T(8,128)(2,1)S(1)} %get-tuple-element.52.o_ref.x_ref, bf16[64,8448]{1,0:T(8,128)(2,1)S(1)} %bitcast.114, ...), custom_call_target="tpu_custom_call" | custom-call | tf_op jit(solution)/shard_map/backward_hidden/pallas_call | solution.py:46
  128.2 4.5 %backward_pair.1 = bf16[384,512]{1,0:T(8,128)(2,1)S(1)} custom-call(bf16[192,5568]{1,0:T(8,128)(2,1)S(1)} %bitcast.109, bf16[192,5568]{1,0:T(8,128)(2,1)S(1)} %collective-permute-done.27.o_ref, bf16[64,8448]{1,0:T(8,128)(2,1)S(1)} %bitcast.115, bf16[64,8448]{1,0:T(8,128)(2,1)S(1)} %collective-permute-done.18.far_ref, ...), custom_call_target="tpu_custom_call" | custom-call | tf_op jit(solution)/shard_map/backward_pair/pallas_call | solution.py:46
  132.7 2.3 %collective-permute-start.29 = (bf16[2,4,48,512]{3,2,0,1:T(8,128)(2,1)S(1)}, bf16[2,4,48,512]{3,2,0,1:T(8,128)(2,1)S(1)}, u32[]{:S(2)}, u32[]{:S(2)}) collective-permute-start(bf16[2,4,48,512]{3,2,0,1:T(8,128)(2,1)S(1)} %fusion.6), channel_id=1, source_target_pairs={{0,4},{1,5},{2,6},{3,7},{4,0},{5,1},{6,2},{7,3},{8,12},{9,13},{10,... | collective-permute-start | bytes 1179656 | tf_op jit(solution)/shard_map/ppermute | solution.py:265
  135.0 2.5 %weight_grad.2 = bf16[2752,512]{1,0:T(8,128)(2,1)} custom-call(bf16[192,5568]{1,0:T(8,128)(2,1)S(1)} %bitcast.110, bf16[192,5568]{1,0:T(8,128)(2,1)S(1)} %collective-permute-done.27.o_ref, bf16[384,512]{1,0:T(8,128)(2,1)S(1)} %get-tuple-element.51.t_ref.x_ref), custom_call_target="tpu_custom_call" | custom-call | tf_op jit(solution)/shard_map/weight_grad/pallas_call | solution.py:46
  137.5 8.2 %collective-permute-done.29 = bf16[2,4,48,512]{3,2,0,1:T(8,128)(2,1)S(1)} collective-permute-done((bf16[2,4,48,512]{3,2,0,1:T(8,128)(2,1)S(1)}, bf16[2,4,48,512]{3,2,0,1:T(8,128)(2,1)S(1)}, u32[]{:S(2)}, u32[]{:S(2)}) %collective-permute-start.29) | collective-permute-done | bytes 393248 | tf_op jit(solution)/shard_map/ppermute | solution.py:265
  145.9 1.3 collective-permute-start.30
  147.2 2.0 %collective-permute-start.31 = (bf16[2,48,512]{2,1,0:T(8,128)(2,1)S(1)}, bf16[2,48,512]{2,1,0:T(8,128)(2,1)S(1)}, u32[]{:S(2)}, u32[]{:S(2)}) collective-permute-start(bf16[2,48,512]{2,1,0:T(8,128)(2,1)S(1)} %get-tuple-element.101), channel_id=1, source_target_pairs={{0,3},{1,0},{2,1},{3,2},{4,7},{5,4},{6,5},{7,6},{8,11},{9,8},{10,9... | collective-permute-start | bytes 294920 | tf_op jit(solution)/shard_map/ppermute | solution.py:265
  150.1 2.5 %weight_grad.3 = bf16[2752,512]{1,0:T(8,128)(2,1)} custom-call(bf16[192,5568]{1,0:T(8,128)(2,1)S(1)} %bitcast.111, bf16[192,5568]{1,0:T(8,128)(2,1)S(1)} %collective-permute-done.27.o_ref, bf16[384,512]{1,0:T(8,128)(2,1)S(1)} %get-tuple-element.51.t_ref.x_ref), custom_call_target="tpu_custom_call" | custom-call | tf_op jit(solution)/shard_map/weight_grad/pallas_call | solution.py:46
  152.8 2.6 %collective-permute-done.32 = bf16[2,48,512]{2,1,0:T(8,128)(2,1)S(1)} collective-permute-done((bf16[2,48,512]{2,1,0:T(8,128)(2,1)S(1)}, bf16[2,48,512]{2,1,0:T(8,128)(2,1)S(1)}, u32[]{:S(2)}, u32[]{:S(2)}) %collective-permute-start.32) | collective-permute-done | bytes 98336 | tf_op jit(solution)/shard_map/ppermute | solution.py:265
  (77 shorter events, 15.2 us)
Async XLA Ops:
  3.0 1.8 %copy-start = (bf16[512,2752]{0,1:T(8,128)(2,1)S(1)}, bf16[512,2752]{0,1:T(8,128)(2,1)}, u32[]{:S(2)}) copy-start(bf16[512,2752]{0,1:T(8,128)(2,1)} %param.15) | copy-start | bytes 8454148
  4.8 1.8 %copy-start.2 = (bf16[512,2752]{0,1:T(8,128)(2,1)S(1)}, bf16[512,2752]{0,1:T(8,128)(2,1)}, u32[]{:S(2)}) copy-start(bf16[512,2752]{0,1:T(8,128)(2,1)} %param.13) | copy-start | bytes 8454148
  6.6 1.0 copy-start.6
  7.6 1.0 copy-start.7
  11.8 2.0 %copy-start.5 = (f32[192,5568]{1,0:T(8,128)}, f32[192,5568]{1,0:T(8,128)S(1)}, u32[]{:S(2)}) copy-start(f32[192,5568]{1,0:T(8,128)S(1)} %get-tuple-element.48) | copy-start | bytes 12828676
  13.8 22.0 %collective-permute-start.1 = (bf16[192,5568]{1,0:T(8,128)(2,1)S(1)}, bf16[192,5568]{1,0:T(8,128)(2,1)}, u32[]{:S(2)}, u32[]{:S(2)}) collective-permute-start(bf16[192,5568]{1,0:T(8,128)(2,1)S(1)} %get-tuple-element.49), channel_id=1, source_target_pairs={{0,8},{8,0},{16,24},{24,16},{32,40},{40,32},{48,56},{56,48},{64,72... | collective-permute-start | bytes 6414344 | tf_op jit(solution)/shard_map/ppermute | solution.py:257
  13.8 8.5 %collective-permute-start = (bf16[48,512]{1,0:T(8,128)(2,1)S(1)}, bf16[48,512]{1,0:T(8,128)(2,1)S(1)}, u32[]{:S(2)}, u32[]{:S(2)}) collective-permute-start(bf16[48,512]{1,0:T(8,128)(2,1)S(1)} %pad_maximum_fusion.9), channel_id=1, source_target_pairs={{0,4},{1,5},{2,6},{3,7},{4,0},{5,1},{6,2},{7,3},{8,12},{9,13},{10,... | collective-permute-start | bytes 147464 | tf_op jit(solution)/shard_map/ppermute | solution.py:265
  16.9 10.2 %collective-permute-start.9 = (bf16[8,8448]{1,0:T(8,128)(2,1)S(1)}, bf16[8,8448]{1,0:T(8,128)(2,1)S(1)}, u32[]{:S(2)}, u32[]{:S(2)}) collective-permute-start(bf16[8,8448]{1,0:T(8,128)(2,1)S(1)} %concatenate.8), channel_id=1, source_target_pairs={{0,96},{8,104},{16,112},{24,120},{32,0},{40,8},{48,16},{56,24},{64... | collective-permute-start | bytes 405512 | tf_op jit(solution)/shard_map/ppermute | solution.py:257
  20.9 9.3 %collective-permute-start.10 = (bf16[8,8448]{1,0:T(8,128)(2,1)S(1)}, bf16[8,8448]{1,0:T(8,128)(2,1)}, u32[]{:S(2)}, u32[]{:S(2)}) collective-permute-start(bf16[8,8448]{1,0:T(8,128)(2,1)S(1)} %concatenate.8), channel_id=1, source_target_pairs={{0,64},{8,72},{16,80},{24,88},{32,96},{40,104},{48,112},{56,120},{... | collective-permute-start | bytes 405512 | tf_op jit(solution)/shard_map/ppermute | solution.py:257
  20.9 11.1 %collective-permute-start.11 = (bf16[8,8448]{1,0:T(8,128)(2,1)S(1)}, bf16[8,8448]{1,0:T(8,128)(2,1)}, u32[]{:S(2)}, u32[]{:S(2)}) collective-permute-start(bf16[8,8448]{1,0:T(8,128)(2,1)S(1)} %concatenate.8), channel_id=1, source_target_pairs={{0,32},{8,40},{16,48},{24,56},{32,64},{40,72},{48,80},{56,88},{64,... | collective-permute-start | bytes 405512 | tf_op jit(solution)/shard_map/ppermute | solution.py:257
  22.3 11.4 %collective-permute-start.5 = (bf16[2,48,512]{2,1,0:T(8,128)(2,1)S(1)}, bf16[2,48,512]{2,1,0:T(8,128)(2,1)S(1)}, u32[]{:S(2)}, u32[]{:S(2)}) collective-permute-start(bf16[2,48,512]{2,1,0:T(8,128)(2,1)S(1)} %get-tuple-element.105), channel_id=1, source_target_pairs={{0,1},{1,2},{2,3},{3,0},{4,5},{5,6},{6,7},{7,4},{8,9},{9,10},{10,1... | collective-permute-start | bytes 294920 | tf_op jit(solution)/shard_map/ppermute | solution.py:265
  27.1 6.7 %collective-permute-start.6 = (bf16[2,48,512]{2,1,0:T(8,128)(2,1)S(1)}, bf16[2,48,512]{2,1,0:T(8,128)(2,1)S(1)}, u32[]{:S(2)}, u32[]{:S(2)}) collective-permute-start(bf16[2,48,512]{2,1,0:T(8,128)(2,1)S(1)} %get-tuple-element.105), channel_id=1, source_target_pairs={{0,2},{1,3},{2,0},{3,1},{4,6},{5,7},{6,4},{7,5},{8,10},{9,11},{10,... | collective-permute-start | bytes 294920 | tf_op jit(solution)/shard_map/ppermute | solution.py:265
  30.3 5.0 %collective-permute-start.7 = (bf16[2,48,512]{2,1,0:T(8,128)(2,1)S(1)}, bf16[2,48,512]{2,1,0:T(8,128)(2,1)S(1)}, u32[]{:S(2)}, u32[]{:S(2)}) collective-permute-start(bf16[2,48,512]{2,1,0:T(8,128)(2,1)S(1)} %get-tuple-element.105), channel_id=1, source_target_pairs={{0,3},{1,0},{2,1},{3,2},{4,7},{5,4},{6,5},{7,6},{8,11},{9,8},{10,9... | collective-permute-start | bytes 294920 | tf_op jit(solution)/shard_map/ppermute | solution.py:265
  33.1 13.7 %collective-permute-start.12 = (bf16[4,8,8448]{2,1,0:T(8,128)(2,1)S(1)}, bf16[4,8,8448]{2,1,0:T(8,128)(2,1)S(1)}, u32[]{:S(2)}, u32[]{:S(2)}) collective-permute-start(bf16[4,8,8448]{2,1,0:T(8,128)(2,1)S(1)} %get-tuple-element.98), channel_id=1, source_target_pairs={{0,16},{8,24},{16,0},{24,8},{32,48},{40,56},{48,32},{56,40},{64,80... | collective-permute-start | bytes 1622024 | tf_op jit(solution)/shard_map/ppermute | solution.py:257
  35.8 3.7 %copy-start.4 = (bf16[512,2752]{0,1:T(8,128)(2,1)S(1)}, bf16[512,2752]{0,1:T(8,128)(2,1)}, u32[]{:S(2)}) copy-start(bf16[512,2752]{0,1:T(8,128)(2,1)} %param.14) | copy-start | bytes 8454148
  41.1 5.7 %collective-permute-start.8 = (bf16[192,3136]{1,0:T(8,128)(2,1)S(1)}, bf16[192,3136]{1,0:T(8,128)(2,1)S(1)}, u32[]{:S(2)}, u32[]{:S(2)}) collective-permute-start(bf16[192,3136]{1,0:T(8,128)(2,1)S(1)} %get-tuple-element.56), channel_id=1, source_target_pairs={{0,8},{8,0},{16,24},{24,16},{32,40},{40,32},{48,56},{56,48},{64,72... | collective-permute-start | bytes 3612680 | tf_op jit(solution)/shard_map/ppermute | solution.py:257
  41.5 16.7 %collective-permute-start.2 = (bf16[2,24,5568]{2,1,0:T(8,128)(2,1)S(1)}, bf16[2,24,5568]{2,1,0:T(8,128)(2,1)S(1)}, u32[]{:S(2)}, u32[]{:S(2)}) collective-permute-start(bf16[2,24,5568]{2,1,0:T(8,128)(2,1)S(1)} %get-tuple-element.89), channel_id=1, source_target_pairs={{0,32},{8,40},{16,48},{24,56},{32,64},{40,72},{48,80},{56,88},{64,... | collective-permute-start | bytes 1603592 | tf_op jit(solution)/shard_map/ppermute | solution.py:257
  41.6 27.5 %collective-permute-start.3 = (bf16[2,24,5568]{2,1,0:T(8,128)(2,1)S(1)}, bf16[2,24,5568]{2,1,0:T(8,128)(2,1)S(1)}, u32[]{:S(2)}, u32[]{:S(2)}) collective-permute-start(bf16[2,24,5568]{2,1,0:T(8,128)(2,1)S(1)} %get-tuple-element.88), channel_id=1, source_target_pairs={{0,96},{8,104},{16,112},{24,120},{32,0},{40,8},{48,16},{56,24},{64... | collective-permute-start | bytes 1603592 | tf_op jit(solution)/shard_map/ppermute | solution.py:257
  45.4 25.6 %collective-permute-start.4 = (bf16[2,24,5568]{2,1,0:T(8,128)(2,1)S(1)}, bf16[2,24,5568]{2,1,0:T(8,128)(2,1)S(1)}, u32[]{:S(2)}, u32[]{:S(2)}) collective-permute-start(bf16[2,24,5568]{2,1,0:T(8,128)(2,1)S(1)} %get-tuple-element.87), channel_id=1, source_target_pairs={{0,64},{8,72},{16,80},{24,88},{32,96},{40,104},{48,112},{56,120},{... | collective-permute-start | bytes 1603592 | tf_op jit(solution)/shard_map/ppermute | solution.py:257
  47.0 23.9 %collective-permute-start.13 = (bf16[4,24,3136]{2,1,0:T(8,128)(2,1)S(1)}, bf16[4,24,3136]{2,1,0:T(8,128)(2,1)S(1)}, u32[]{:S(2)}, u32[]{:S(2)}) collective-permute-start(bf16[4,24,3136]{2,1,0:T(8,128)(2,1)S(1)} %fusion.3), channel_id=1, source_target_pairs={{0,16},{8,24},{16,0},{24,8},{32,48},{40,56},{48,32},{56,40},{64,80... | collective-permute-start | bytes 1806344 | tf_op jit(solution)/shard_map/ppermute | solution.py:257
  47.9 34.5 %collective-permute-start.18 = (bf16[64,8448]{1,0:T(8,128)(2,1)S(1)}, bf16[64,8448]{1,0:T(8,128)(2,1)S(1)}, u32[]{:S(2)}, u32[]{:S(2)}) collective-permute-start(bf16[64,8448]{1,0:T(8,128)(2,1)S(1)} %bitcast.112), channel_id=1, source_target_pairs={{0,8},{8,0},{16,24},{24,16},{32,40},{40,32},{48,56},{56,48},{64,72... | collective-permute-start | bytes 3244040 | tf_op jit(solution)/shard_map/ppermute | solution.py:257
  71.5 7.1 %collective-permute-start.15 = (bf16[24,3136]{1,0:T(8,128)(2,1)S(1)}, bf16[24,3136]{1,0:T(8,128)(2,1)S(1)}, u32[]{:S(2)}, u32[]{:S(2)}) collective-permute-start(bf16[24,3136]{1,0:T(8,128)(2,1)S(1)} %get-tuple-element.92), channel_id=1, source_target_pairs={{0,32},{8,40},{16,48},{24,56},{32,64},{40,72},{48,80},{56,88},{64,... | collective-permute-start | bytes 451592 | tf_op jit(solution)/shard_map/ppermute | solution.py:257
  72.7 8.3 %collective-permute-start.16 = (bf16[24,3136]{1,0:T(8,128)(2,1)S(1)}, bf16[24,3136]{1,0:T(8,128)(2,1)S(1)}, u32[]{:S(2)}, u32[]{:S(2)}) collective-permute-start(bf16[24,3136]{1,0:T(8,128)(2,1)S(1)} %get-tuple-element.91), channel_id=1, source_target_pairs={{0,96},{8,104},{16,112},{24,120},{32,0},{40,8},{48,16},{56,24},{64... | collective-permute-start | bytes 451592 | tf_op jit(solution)/shard_map/ppermute | solution.py:257
  74.8 6.9 %collective-permute-start.17 = (bf16[24,3136]{1,0:T(8,128)(2,1)S(1)}, bf16[24,3136]{1,0:T(8,128)(2,1)S(1)}, u32[]{:S(2)}, u32[]{:S(2)}) collective-permute-start(bf16[24,3136]{1,0:T(8,128)(2,1)S(1)} %get-tuple-element.90), channel_id=1, source_target_pairs={{0,64},{8,72},{16,80},{24,88},{32,96},{40,104},{48,112},{56,120},{... | collective-permute-start | bytes 451592 | tf_op jit(solution)/shard_map/ppermute | solution.py:257
  75.0 7.4 %collective-permute-start.14 = (bf16[24,5568]{1,0:T(8,128)(2,1)S(1)}, bf16[24,5568]{1,0:T(8,128)(2,1)S(1)}, u32[]{:S(2)}, u32[]{:S(2)}) collective-permute-start(bf16[24,5568]{1,0:T(8,128)(2,1)S(1)} %fusion.14), channel_id=1, source_target_pairs={{0,16},{8,24},{16,0},{24,8},{32,48},{40,56},{48,32},{56,40},{64,80... | collective-permute-start | bytes 801800 | tf_op jit(solution)/shard_map/ppermute | solution.py:257
  83.1 10.8 %collective-permute-start.19 = (bf16[24,5568]{1,0:T(8,128)(2,1)S(1)}, bf16[24,5568]{1,0:T(8,128)(2,1)S(1)}, u32[]{:S(2)}, u32[]{:S(2)}) collective-permute-start(bf16[24,5568]{1,0:T(8,128)(2,1)S(1)} %get-tuple-element.64), channel_id=1, source_target_pairs={{0,16},{8,24},{16,0},{24,8},{32,48},{40,56},{48,32},{56,40},{64,80... | collective-permute-start | bytes 801800 | tf_op jit(solution)/shard_map/ppermute | solution.py:257
  83.7 5.4 %collective-permute-start.20 = (bf16[24,2752]{1,0:T(8,128)(2,1)S(1)}, bf16[24,2752]{1,0:T(8,128)(2,1)S(1)}, u32[]{:S(2)}, u32[]{:S(2)}) collective-permute-start(bf16[24,2752]{1,0:T(8,128)(2,1)S(1)} %get-tuple-element.65), channel_id=1, source_target_pairs={{0,96},{8,104},{16,112},{24,120},{32,0},{40,8},{48,16},{56,24},{64... | collective-permute-start | bytes 396296 | tf_op jit(solution)/shard_map/ppermute | solution.py:257
  85.9 6.6 %collective-permute-start.21 = (bf16[24,2752]{1,0:T(8,128)(2,1)S(1)}, bf16[24,2752]{1,0:T(8,128)(2,1)S(1)}, u32[]{:S(2)}, u32[]{:S(2)}) collective-permute-start(bf16[24,2752]{1,0:T(8,128)(2,1)S(1)} %get-tuple-element.65), channel_id=1, source_target_pairs={{0,64},{8,72},{16,80},{24,88},{32,96},{40,104},{48,112},{56,120},{... | collective-permute-start | bytes 396296 | tf_op jit(solution)/shard_map/ppermute | solution.py:257
  86.9 7.0 %collective-permute-start.22 = (bf16[24,2752]{1,0:T(8,128)(2,1)S(1)}, bf16[24,2752]{1,0:T(8,128)(2,1)S(1)}, u32[]{:S(2)}, u32[]{:S(2)}) collective-permute-start(bf16[24,2752]{1,0:T(8,128)(2,1)S(1)} %get-tuple-element.65), channel_id=1, source_target_pairs={{0,32},{8,40},{16,48},{24,56},{32,64},{40,72},{48,80},{56,88},{64,... | collective-permute-start | bytes 396296 | tf_op jit(solution)/shard_map/ppermute | solution.py:257
  94.0 15.3 %collective-permute-start.24 = (bf16[2,24,5568]{2,1,0:T(8,128)(2,1)S(1)}, bf16[2,24,5568]{2,1,0:T(8,128)(2,1)S(1)}, u32[]{:S(2)}, u32[]{:S(2)}) collective-permute-start(bf16[2,24,5568]{2,1,0:T(8,128)(2,1)S(1)} %get-tuple-element.96), channel_id=1, source_target_pairs={{0,96},{8,104},{16,112},{24,120},{32,0},{40,8},{48,16},{56,24},{64... | collective-permute-start | bytes 1603592 | tf_op jit(solution)/shard_map/ppermute | solution.py:257
  94.6 16.7 %collective-permute-start.25 = (bf16[2,24,5568]{2,1,0:T(8,128)(2,1)S(1)}, bf16[2,24,5568]{2,1,0:T(8,128)(2,1)S(1)}, u32[]{:S(2)}, u32[]{:S(2)}) collective-permute-start(bf16[2,24,5568]{2,1,0:T(8,128)(2,1)S(1)} %get-tuple-element.96), channel_id=1, source_target_pairs={{0,64},{8,72},{16,80},{24,88},{32,96},{40,104},{48,112},{56,120},{... | collective-permute-start | bytes 1603592 | tf_op jit(solution)/shard_map/ppermute | solution.py:257
  95.6 22.2 %collective-permute-start.26 = (bf16[2,24,5568]{2,1,0:T(8,128)(2,1)S(1)}, bf16[2,24,5568]{2,1,0:T(8,128)(2,1)S(1)}, u32[]{:S(2)}, u32[]{:S(2)}) collective-permute-start(bf16[2,24,5568]{2,1,0:T(8,128)(2,1)S(1)} %get-tuple-element.96), channel_id=1, source_target_pairs={{0,32},{8,40},{16,48},{24,56},{32,64},{40,72},{48,80},{56,88},{64,... | collective-permute-start | bytes 1603592 | tf_op jit(solution)/shard_map/ppermute | solution.py:257
  96.6 10.2 %collective-permute-start.23 = (bf16[4,24,2752]{2,1,0:T(8,128)(2,1)S(1)}, bf16[4,24,2752]{2,1,0:T(8,128)(2,1)S(1)}, u32[]{:S(2)}, u32[]{:S(2)}) collective-permute-start(bf16[4,24,2752]{2,1,0:T(8,128)(2,1)S(1)} %get-tuple-element.94), channel_id=1, source_target_pairs={{0,16},{8,24},{16,0},{24,8},{32,48},{40,56},{48,32},{56,40},{64,80... | collective-permute-start | bytes 1585160 | tf_op jit(solution)/shard_map/ppermute | solution.py:257
  118.1 10.1 %collective-permute-start.27 = (bf16[192,5568]{1,0:T(8,128)(2,1)S(1)}, bf16[192,5568]{1,0:T(8,128)(2,1)S(1)}, u32[]{:S(2)}, u32[]{:S(2)}) collective-permute-start(bf16[192,5568]{1,0:T(8,128)(2,1)S(1)} %bitcast.108), channel_id=1, source_target_pairs={{0,8},{8,0},{16,24},{24,16},{32,40},{40,32},{48,56},{56,48},{64,72... | collective-permute-start | bytes 6414344 | tf_op jit(solution)/shard_map/ppermute | solution.py:257
  118.2 5.8 %copy-start.1 = (bf16[512,2752]{0,1:T(8,128)(2,1)S(1)}, bf16[512,2752]{0,1:T(8,128)(2,1)}, u32[]{:S(2)}) copy-start(bf16[512,2752]{0,1:T(8,128)(2,1)} %param.15) | copy-start | bytes 8454148
  118.4 5.6 %collective-permute-start.28 = (bf16[192,2752]{1,0:T(8,128)(2,1)S(1)}, bf16[192,2752]{1,0:T(8,128)(2,1)S(1)}, u32[]{:S(2)}, u32[]{:S(2)}) collective-permute-start(bf16[192,2752]{1,0:T(8,128)(2,1)S(1)} %bitcast.122), channel_id=1, source_target_pairs={{0,8},{8,0},{16,24},{24,16},{32,40},{40,32},{48,56},{56,48},{64,72... | collective-permute-start | bytes 3170312 | tf_op jit(solution)/shard_map/ppermute | solution.py:257
  120.0 8.2 %copy-start.3 = (bf16[512,2752]{0,1:T(8,128)(2,1)S(1)}, bf16[512,2752]{0,1:T(8,128)(2,1)}, u32[]{:S(2)}) copy-start(bf16[512,2752]{0,1:T(8,128)(2,1)} %param.13) | copy-start | bytes 8454148
  132.7 13.0 %collective-permute-start.29 = (bf16[2,4,48,512]{3,2,0,1:T(8,128)(2,1)S(1)}, bf16[2,4,48,512]{3,2,0,1:T(8,128)(2,1)S(1)}, u32[]{:S(2)}, u32[]{:S(2)}) collective-permute-start(bf16[2,4,48,512]{3,2,0,1:T(8,128)(2,1)S(1)} %fusion.6), channel_id=1, source_target_pairs={{0,4},{1,5},{2,6},{3,7},{4,0},{5,1},{6,2},{7,3},{8,12},{9,13},{10,... | collective-permute-start | bytes 1179656 | tf_op jit(solution)/shard_map/ppermute | solution.py:265
  145.9 6.7 %collective-permute-start.30 = (bf16[2,48,512]{2,1,0:T(8,128)(2,1)S(1)}, bf16[2,48,512]{2,1,0:T(8,128)(2,1)S(1)}, u32[]{:S(2)}, u32[]{:S(2)}) collective-permute-start(bf16[2,48,512]{2,1,0:T(8,128)(2,1)S(1)} %get-tuple-element.99), channel_id=1, source_target_pairs={{0,1},{1,2},{2,3},{3,0},{4,5},{5,6},{6,7},{7,4},{8,9},{9,10},{10,1... | collective-permute-start | bytes 294920 | tf_op jit(solution)/shard_map/ppermute | solution.py:265
  147.2 5.6 %collective-permute-start.31 = (bf16[2,48,512]{2,1,0:T(8,128)(2,1)S(1)}, bf16[2,48,512]{2,1,0:T(8,128)(2,1)S(1)}, u32[]{:S(2)}, u32[]{:S(2)}) collective-permute-start(bf16[2,48,512]{2,1,0:T(8,128)(2,1)S(1)} %get-tuple-element.101), channel_id=1, source_target_pairs={{0,3},{1,0},{2,1},{3,2},{4,7},{5,4},{6,5},{7,6},{8,11},{9,8},{10,9... | collective-permute-start | bytes 294920 | tf_op jit(solution)/shard_map/ppermute | solution.py:265
  149.2 6.1 %collective-permute-start.32 = (bf16[2,48,512]{2,1,0:T(8,128)(2,1)S(1)}, bf16[2,48,512]{2,1,0:T(8,128)(2,1)S(1)}, u32[]{:S(2)}, u32[]{:S(2)}) collective-permute-start(bf16[2,48,512]{2,1,0:T(8,128)(2,1)S(1)} %get-tuple-element.100), channel_id=1, source_target_pairs={{0,2},{1,3},{2,0},{3,1},{4,6},{5,7},{6,4},{7,5},{8,10},{9,11},{10,... | collective-permute-start | bytes 294920 | tf_op jit(solution)/shard_map/ppermute | solution.py:265

commit v5 on v4

--- a/solution.py
+++ b/solution.py
@@ -54,37 +54,52 @@
     )(*ins)
 
 
-def forward_pair(tokens, grad_out, index, gate_w, down_w):
+def forward_theirs(tokens, grad_out, index, gate_w, down_w):
     n, depth = gate_w.shape
     wide = padded(n)
 
-    def body(t_ref, g_ref, i_ref, gw_ref, dw_ref, mine_ref, theirs_ref, tok_ref, out_ref):
-        mine_ref[:, n:wide] = jnp.zeros((HALF, wide - n), F32)
+    def body(t_ref, g_ref, i_ref, gw_ref, dw_ref, theirs_ref, tok_ref, out_ref):
         theirs_ref[:, n:wide] = jnp.zeros((HALF, wide - n), BF)
         turn = pick(i_ref, SIZE)
-
-        def product(x_ref, w_ref, first):
+        for in_ref, turned_ref, w_ref, first in ((t_ref, tok_ref, gw_ref, 0), (g_ref, out_ref, dw_ref, wide)):
+            turned_ref[...] = dot(turn, in_ref[...], NN).astype(BF)
             for at, size in cuts(n, CHUNK):
-                got = dot(x_ref[...], w_ref[at : at + size, :], NT)
-                mine_ref[:, first + at : first + at + size] = got[:HALF]
-                theirs_ref[:, first + at : first + at + size] = got[HALF:].astype(BF)
-
-        tok_ref[...] = dot(turn, t_ref[...], NN).astype(BF)
-        product(tok_ref, gw_ref, 0)
-        out_ref[...] = dot(turn, g_ref[...], NN).astype(BF)
-        product(out_ref, dw_ref, wide)
-
-    cols = wide + n
-    return pallas(
-        body,
-        "forward_pair",
+                got = dot(turned_ref[HALF:, :], w_ref[at : at + size, :], NT)
+                theirs_ref[:, first + at : first + at + size] = got.astype(BF)
+
+    return pallas(
+        body,
+        "forward_theirs",
         (tokens, grad_out, index, gate_w, down_w),
-        [
-            jax.ShapeDtypeStruct((HALF, cols), F32),
-            jax.ShapeDtypeStruct((HALF, cols), BF),
-            jax.ShapeDtypeStruct((SIZE, depth), BF),
-            jax.ShapeDtypeStruct((SIZE, depth), BF),
-        ],
+        [jax.ShapeDtypeStruct((HALF, wide + n), BF)] + [jax.ShapeDtypeStruct((SIZE, depth), BF)] * 2,
+        [VMEM] * 5,
+        [VMEM] * 3,
+        [],
+    )
+
+
+def forward_mine(tok, out, gate_w, down_w, got):
+    n, depth = gate_w.shape
+    wide = padded(n)
+    quarter = HALF // 4
+
+    def body(t_ref, o_ref, gw_ref, dw_ref, got_ref, own_ref, *send_refs):
+        own_ref[:, n:wide] = jnp.zeros((quarter, wide - n), F32)
+        for ref in send_refs:
+            ref[:, n:wide] = jnp.zeros((quarter, wide - n), BF)
+        for x_ref, w_ref, first in ((t_ref, gw_ref, 0), (o_ref, dw_ref, wide)):
+            for at, size in cuts(n, CHUNK):
+                part = slice(first + at, first + at + size)
+                total = dot(x_ref[:HALF, :], w_ref[at : at + size, :], NT) + got_ref[:, part].astype(F32)
+                own_ref[:, part] = total[:quarter]
+                for d, ref in enumerate(send_refs, 1):
+                    ref[:, part] = total[quarter * d : quarter * (d + 1)].astype(BF)
+
+    return pallas(
+        body,
+        "forward_mine",
+        (tok, out, gate_w, down_w, got),
+        [jax.ShapeDtypeStruct((quarter, wide + n), F32)] + [jax.ShapeDtypeStruct((quarter, wide + n), BF)] * 3,
         [VMEM] * 5,
         [VMEM] * 4,
         [],
@@ -308,6 +323,11 @@
     row, col = lax.axis_index("row"), lax.axis_index("col")
     z, a, c = row // 4, (row // 2) % 2, row % 2
     h, y = col // 4, col % 4
+    z, a, c, h, y, tokens, grad_out, gate_weight, down_weight, *small = tie(
+        *(z, a, c, h, y, tokens, grad_out, gate_weight, down_weight),
+        *(gate_left, up_left, down_left, gate_right, up_right, down_right),
+    )
+    gate_left, up_left, down_left, gate_right, up_right, down_right = small
 
     k = jnp.arange(SIZE, dtype=jnp.int32)
 
@@ -333,18 +353,20 @@
     lefts = jnp.concatenate([gate_left.T, up_left.T, down_left.T], axis=0)
     lefts_h = col_send(lefts, 1, 0)
     rights_z = z_spread(rights)
-    held, rights, lefts = tie(held, rights, lefts)
-
-    mine, theirs, tok, out = forward_pair(tokens, grad_out, held, gate_w, down_w)
+    held, leave, sort, match, rights, lefts, lefts_h, *rights_z = tie(
+        held, leave, sort, match, rights, lefts, lefts_h, *rights_z
+    )
+
+    theirs, tok, out = forward_theirs(tokens, grad_out, held, gate_w, down_w)
     got = core_send(theirs)
-    lefts_h, tok = tie(lefts_h, tok)
     lefts = jnp.stack([lefts, lefts_h])
     lefts_y = [col_send(lefts, 0, d) for d in (1, 2, 3)]
     rights = jnp.stack([rights] + rights_z)
     rights_x = x_send(rights)
 
-    tok, pair = tie(tok, pair_sum(mine, got))
-    pair_z = z_send(pair)
+    pair, *sends = forward_mine(tok, out, gate_w, down_w, got)
+    tok, pair = tie(tok, pair)
+    pair_z = [row_send(sends[d - 1], d, 0, 0) for d in (1, 3, 2)]
     lefts = jnp.stack([lefts] + lefts_y).reshape(SIZE, -1)
     lefts = dot(match, lefts, NN).astype(BF)
     mine, theirs = forward_up(tok, out, lefts, up_w)
@@ -355,7 +377,7 @@
     far = core_send(near)
 
     *pair_z, up_x = tie(*pair_z, up_x)
-    pair = plus(pair[0], pair_z)
+    pair = plus(pair, pair_z).reshape(2, ROWS, -1)
     pair_x = x_send(pair[1].astype(BF))
     up = up[:, 0] + up_x.astype(F32)
     up_z = z_send(up)
@@ -369,23 +391,25 @@
     hidden = jnp.stack([hidden] + hidden_z)
     hidden_x, delta_z = tie(x_send(hidden), delta_z)
     hidden = jnp.stack([hidden, hidden_x], axis=1).reshape(HALF, n)
-    hidden_far = core_send(hidden)
+    delta = jnp.stack([delta] + delta_z).reshape(HALF, -1)
+    hidden_far, delta = tie(core_send(hidden), delta)
+    delta_far = core_send(delta)
     mixed, down_grad = backward_hidden(hidden, hidden_far, out, down_w, near, far, lefts, sort, leave)
-    delta = jnp.stack([delta] + delta_z).reshape(HALF, -1)
-    delta_far, mixed = tie(core_send(delta), mixed)
+    mixed = mixed.reshape(2, 4, 48, -1)
+    mixed_h = col_send(mixed[1], 1, 0)
+    delta_far, mixed = tie(delta_far, mixed)
     input_grad = backward_pair(delta, delta_far, gate_w, up_w, near, far, lefts, sort, leave)
-
-    both = jnp.stack([mixed, input_grad]).reshape(2, 2, 4, 48, -1)
-    leaving = both[:, 1]
-    delta, leaving = tie(delta, leaving)
-    both_h = col_send(leaving, 1, 0)
+    input_grad = input_grad.reshape(2, 4, 48, -1)
+    delta, leaving = tie(delta, input_grad[1])
+    input_h = col_send(leaving, 1, 0)
     up_grad = weight_grad(delta, delta_far, tok, padded(n), n)
-    both_h, delta, up_grad = tie(both_h, delta, up_grad)
-    both = both[:, 0].astype(F32) + both_h.astype(F32)
-    delta, leaving = tie(delta, both[:, 1:].astype(BF))
-    both_y = [col_send(leaving[:, d - 1], 0, d) for d in (1, 3, 2)]
+    input_h, delta, up_grad = tie(input_h, delta, up_grad)
+    both = [mixed[0].astype(F32) + mixed_h.astype(F32), input_grad[0].astype(F32) + input_h.astype(F32)]
+    leaving = [jnp.stack([part[d] for part in both]).astype(BF) for d in (1, 3, 2)]
+    delta, *leaving = tie(delta, *leaving)
+    both_y = [col_send(part, 0, d) for part, d in zip(leaving, (1, 3, 2))]
     gate_grad = weight_grad(delta, delta_far, tok, 0, n)
-    both = plus(both[:, 0], both_y).astype(BF)
+    both = [plus(both[t][0], [part[t] for part in both_y]).astype(BF) for t in range(2)]
     return both[0], both[1], gate_grad.T, up_grad.T, down_grad.T
 
 

time: 156 us -> 146 us (0.936)
  waiting for transfers between devices: 74.7 us -> 64.9 us
  starting transfers between devices: 42.3 us -> 48.9 us
  local copies, waits for them, and re-layouts: 9.9 us -> 4.98 us
  other arithmetic: 8.76 us -> 4.84 us
    ppermute x25, waiting for transfers between devices: 62.2 us -> 53.7 us  [row_send(): return lax.ppermute(x, 'row', pairs)]
    ppermute x25, starting transfers between devices: 26 us -> 30.9 us  [row_send(): return lax.ppermute(x, 'row', pairs)]
    unnamed x16 -> x14, local copies, waits for them, and re-layouts: 7.83 us -> 3.61 us
    add x2 -> x1, other arithmetic: 3.69 us -> 0.27 us  [pair_sum(): return (mine + got.astype(F32)).reshape(4, 2, ROWS, -1)]
    ppermute x8 -> x9, starting transfers between devices: 16.2 us -> 17.9 us  [col_send(): return lax.ppermute(x, 'col', pairs)]
    ppermute x8 -> x9, waiting for transfers between devices: 12.5 us -> 11.1 us  [col_send(): return lax.ppermute(x, 'col', pairs)]
    pallas_call x7 -> x8, Pallas kernels: 19 us -> 20.3 us  [pallas(): pl.pallas_call(body, out_shape=outs, in_specs=in_specs, out_specs=out_spe...]
  transfers between devices with their start and end apart: 33 -> 34, of which waited for: 20 -> 19; matrix products, arithmetic and copies ran while one was open for 5% -> 3% of each run, Pallas kernels for 7% -> 9%
where the time goes in v5:
time: 146 us; the launch traced here: 145 us
  waiting for transfers between devices  64.9 us (44%)
  starting transfers between devices  48.9 us (33%)
  Pallas kernels  20.3 us (14%)
  local copies, waits for them, and re-layouts  4.98 us (3%)
  other arithmetic  4.84 us (3%)
    ppermute x25, waiting for transfers between devices, row_send(): return lax.ppermute(x, 'row', pairs)  53.7 us
    ppermute x25, starting transfers between devices, row_send(): return lax.ppermute(x, 'row', pairs)  30.9 us
    pallas_call x8, Pallas kernels, pallas(): pl.pallas_call(body, out_shape=outs, in_specs=in_specs, out_specs=out_spe...  20.3 us
    ppermute x9, starting transfers between devices, col_send(): return lax.ppermute(x, 'col', pairs)  17.9 us
    ppermute x9, waiting for transfers between devices, col_send(): return lax.ppermute(x, 'col', pairs)  11.1 us
    unnamed x14, local copies, waits for them, and re-layouts  3.61 us
  transfers between devices with their start and end apart: 34, of which 19 were waited for; matrix products, arithmetic and copies ran while one was open for 3% of the time, Pallas kernels for 9%

profile of v5, /device:TPU:0, one launch (start us, length us, event | category | flops | bytes accessed | tf_op | source)
XLA Modules:
  0.0 145.3 jit_solution(10361552984953652341)
XLA Ops:
  0.7 1.0 concatenate.6
  1.7 2.0 %collective-permute-start.3 = (bf16[8,8448]{1,0:T(8,128)(2,1)S(1)}, bf16[8,8448]{1,0:T(8,128)(2,1)S(1)}, u32[]{:S(2)}, u32[]{:S(2)}) collective-permute-start(bf16[8,8448]{1,0:T(8,128)(2,1)S(1)} %concatenate.6), channel_id=1, source_target_pairs={{0,32},{8,40},{16,48},{24,56},{32,64},{40,72},{48,80},{56,88},{64,... | collective-permute-start | bytes 405512 | tf_op jit(solution)/shard_map/ppermute | solution.py:272
  3.7 3.6 %collective-permute-start.2 = (bf16[8,8448]{1,0:T(8,128)(2,1)S(1)}, bf16[8,8448]{1,0:T(8,128)(2,1)S(1)}, u32[]{:S(2)}, u32[]{:S(2)}) collective-permute-start(bf16[8,8448]{1,0:T(8,128)(2,1)S(1)} %concatenate.6), channel_id=1, source_target_pairs={{0,64},{8,72},{16,80},{24,88},{32,96},{40,104},{48,112},{56,120},{... | collective-permute-start | bytes 405512 | tf_op jit(solution)/shard_map/ppermute | solution.py:272
  7.3 1.0 collective-permute-start.1
  8.3 0.8 pad_maximum_fusion.11
  9.0 3.0 %collective-permute-start = (bf16[48,512]{1,0:T(8,128)(2,1)S(1)}, bf16[48,512]{1,0:T(8,128)(2,1)S(1)}, u32[]{:S(2)}, u32[]{:S(2)}) collective-permute-start(bf16[48,512]{1,0:T(8,128)(2,1)S(1)} %pad_maximum_fusion.11), channel_id=1, source_target_pairs={{0,4},{1,5},{2,6},{3,7},{4,0},{5,1},{6,2},{7,3},{8,12},{9,13},{10,... | collective-permute-start | bytes 147464 | tf_op jit(solution)/shard_map/ppermute | solution.py:280
  12.1 1.7 %fusion.22 = (s32[384,1]{1,0:T(8,128)S(1)}, s32[384,1]{1,0:T(8,128)S(1)}) fusion(s32[]{:T(128)S(6)} %select_n.419, s32[]{:T(128)S(6)} %select_n.418, s32[]{:T(128)S(6)} %select_n.416, s32[]{:T(128)S(6)} %select_n.421, s32[]{:T(128)S(6)} %select_n.420), kind=kLoop, calls=%fused_computation.98 | loop fusion | flops 89088 | bytes 3092 | tf_op jit(solution)/shard_map/add | solution.py:338
  14.7 1.8 %copy-done = bf16[512,2752]{0,1:T(8,128)(2,1)S(1)} copy-done((bf16[512,2752]{0,1:T(8,128)(2,1)S(1)}, bf16[512,2752]{0,1:T(8,128)(2,1)}, u32[]{:S(2)}) %copy-start) | copy-done | bytes 2818072
  16.5 1.8 %copy-done.2 = bf16[512,2752]{0,1:T(8,128)(2,1)S(1)} copy-done((bf16[512,2752]{0,1:T(8,128)(2,1)S(1)}, bf16[512,2752]{0,1:T(8,128)(2,1)}, u32[]{:S(2)}) %copy-start.2) | copy-done | bytes 2818072
  18.3 2.5 %forward_theirs.1 = (bf16[192,5568]{1,0:T(8,128)(2,1)S(1)}, bf16[384,512]{1,0:T(8,128)(2,1)S(1)}, bf16[384,512]{1,0:T(8,128)(2,1)S(1)}) custom-call(bf16[384,512]{1,0:T(8,128)(2,1)S(1)} %copy-done.5, bf16[384,512]{1,0:T(8,128)(2,1)S(1)} %copy-done.6, s32[384,1]{1,0:T(8,128)S(1)} %get-tuple-element.85.i_ref, bf16[2752,512]{1,0:T(8,128)(2,1)S(1)} %bitcast.80, ...), custom_call_target="tpu_custom_call" | custom-call | tf_op jit(solution)/shard_map/forward_theirs/pallas_call | solution.py:46
  20.9 3.3 %collective-permute-start.9 = (bf16[2,48,512]{2,1,0:T(8,128)(2,1)S(1)}, bf16[2,48,512]{2,1,0:T(8,128)(2,1)S(1)}, u32[]{:S(2)}, u32[]{:S(2)}) collective-permute-start(bf16[2,48,512]{2,1,0:T(8,128)(2,1)S(1)} %get-tuple-element.165), channel_id=1, source_target_pairs={{0,2},{1,3},{2,0},{3,1},{4,6},{5,7},{6,4},{7,5},{8,10},{9,11},{10,... | collective-permute-start | bytes 294920 | tf_op jit(solution)/shard_map/ppermute | solution.py:280
  24.9 2.6 %collective-permute-start.10 = (bf16[2,48,512]{2,1,0:T(8,128)(2,1)S(1)}, bf16[2,48,512]{2,1,0:T(8,128)(2,1)S(1)}, u32[]{:S(2)}, u32[]{:S(2)}) collective-permute-start(bf16[2,48,512]{2,1,0:T(8,128)(2,1)S(1)} %get-tuple-element.165), channel_id=1, source_target_pairs={{0,3},{1,0},{2,1},{3,2},{4,7},{5,4},{6,5},{7,6},{8,11},{9,8},{10,9... | collective-permute-start | bytes 294920 | tf_op jit(solution)/shard_map/ppermute | solution.py:280
  27.8 2.5 %collective-permute-done.8 = bf16[2,48,512]{2,1,0:T(8,128)(2,1)S(1)} collective-permute-done((bf16[2,48,512]{2,1,0:T(8,128)(2,1)S(1)}, bf16[2,48,512]{2,1,0:T(8,128)(2,1)S(1)}, u32[]{:S(2)}, u32[]{:S(2)}) %collective-permute-start.8) | collective-permute-done | bytes 98336 | tf_op jit(solution)/shard_map/ppermute | solution.py:280
  30.8 2.0 %forward_mine.1 = (f32[48,5568]{1,0:T(8,128)S(1)}, bf16[48,5568]{1,0:T(8,128)(2,1)S(1)}, bf16[48,5568]{1,0:T(8,128)(2,1)S(1)}, bf16[48,5568]{1,0:T(8,128)(2,1)S(1)}) custom-call(bf16[384,512]{1,0:T(8,128)(2,1)S(1)} %get-tuple-element.96.t_ref.x_ref, bf16[384,512]{1,0:T(8,128)(2,1)S(1)} %get-tuple-element.89.o_ref.x_ref, bf16[2752,512]{1,0:T(8,128)(2,1)S(1)} %bitcast.81, ...), custom_call_target="tpu_custom_call" | custom-call | tf_op jit(solution)/shard_map/forward_mine/pallas_call | solution.py:46
  32.8 1.6 %forward_up.1 = (f32[192,3136]{1,0:T(8,128)S(1)}, bf16[192,3136]{1,0:T(8,128)(2,1)S(1)}) custom-call(bf16[384,512]{1,0:T(8,128)(2,1)S(1)} %get-tuple-element.96.t_ref.x_ref, bf16[384,512]{1,0:T(8,128)(2,1)S(1)} %get-tuple-element.89.o_ref.x_ref, bf16[384,512]{1,0:T(8,128)(2,1)S(1)} %convolution_convert_fusion.l_ref, bf16[2752,512]{1,0:T(8,128)(2,1)S(1)} %bitcast.87), custom_call_target="tpu_custom_call" | custom-call | tf_op jit(solution)/shard_map/forward_up/pallas_call | solution.py:46
  34.6 1.6 %collective-permute-start.12 = (bf16[4,8,8448]{2,1,0:T(8,128)(2,1)S(1)}, bf16[4,8,8448]{2,1,0:T(8,128)(2,1)S(1)}, u32[]{:S(2)}, u32[]{:S(2)}) collective-permute-start(bf16[4,8,8448]{2,1,0:T(8,128)(2,1)S(1)} %get-tuple-element.151), channel_id=1, source_target_pairs={{0,16},{8,24},{16,0},{24,8},{32,48},{40,56},{48,32},{56,40},{64,80... | collective-permute-start | bytes 1622024 | tf_op jit(solution)/shard_map/ppermute | solution.py:272
  36.1 1.0 collective-permute-start.5
  37.2 2.2 %collective-permute-start.6 = (bf16[48,5568]{1,0:T(8,128)(2,1)S(1)}, bf16[48,5568]{1,0:T(8,128)(2,1)S(1)}, u32[]{:S(2)}, u32[]{:S(2)}) collective-permute-start(bf16[48,5568]{1,0:T(8,128)(2,1)S(1)} %get-tuple-element.94), channel_id=1, source_target_pairs={{0,96},{8,104},{16,112},{24,120},{32,0},{40,8},{48,16},{56,24},{64... | collective-permute-start | bytes 1603592 | tf_op jit(solution)/shard_map/ppermute | solution.py:272
  39.4 9.9 %collective-permute-done.12 = bf16[4,8,8448]{2,1,0:T(8,128)(2,1)S(1)} collective-permute-done((bf16[4,8,8448]{2,1,0:T(8,128)(2,1)S(1)}, bf16[4,8,8448]{2,1,0:T(8,128)(2,1)S(1)}, u32[]{:S(2)}, u32[]{:S(2)}) %collective-permute-start.12) | collective-permute-done | bytes 540704 | tf_op jit(solution)/shard_map/ppermute | solution.py:272
  49.7 1.6 %collective-permute-start.13 = (bf16[4,24,3136]{2,1,0:T(8,128)(2,1)S(1)}, bf16[4,24,3136]{2,1,0:T(8,128)(2,1)S(1)}, u32[]{:S(2)}, u32[]{:S(2)}) collective-permute-start(bf16[4,24,3136]{2,1,0:T(8,128)(2,1)S(1)} %fusion.1), channel_id=1, source_target_pairs={{0,16},{8,24},{16,0},{24,8},{32,48},{40,56},{48,32},{56,40},{64,80... | collective-permute-start | bytes 1806344 | tf_op jit(solution)/shard_map/ppermute | solution.py:272
  51.7 11.6 %collective-permute-done.5 = bf16[48,5568]{1,0:T(8,128)(2,1)S(1)} collective-permute-done((bf16[48,5568]{1,0:T(8,128)(2,1)S(1)}, bf16[48,5568]{1,0:T(8,128)(2,1)S(1)}, u32[]{:S(2)}, u32[]{:S(2)}) %collective-permute-start.5) | collective-permute-done | bytes 534560 | tf_op jit(solution)/shard_map/ppermute | solution.py:272
  63.3 1.9 %collective-permute-done.13 = bf16[4,24,3136]{2,1,0:T(8,128)(2,1)S(1)} collective-permute-done((bf16[4,24,3136]{2,1,0:T(8,128)(2,1)S(1)}, bf16[4,24,3136]{2,1,0:T(8,128)(2,1)S(1)}, u32[]{:S(2)}, u32[]{:S(2)}) %collective-permute-start.13) | collective-permute-done | bytes 602144 | tf_op jit(solution)/shard_map/ppermute | solution.py:272
  65.4 1.1 collective-permute-start.17
  66.5 2.6 %collective-permute-start.16 = (bf16[24,3136]{1,0:T(8,128)(2,1)S(1)}, bf16[24,3136]{1,0:T(8,128)(2,1)S(1)}, u32[]{:S(2)}, u32[]{:S(2)}) collective-permute-start(bf16[24,3136]{1,0:T(8,128)(2,1)S(1)} %get-tuple-element.142), channel_id=1, source_target_pairs={{0,96},{8,104},{16,112},{24,120},{32,0},{40,8},{48,16},{56,24},{64... | collective-permute-start | bytes 451592 | tf_op jit(solution)/shard_map/ppermute | solution.py:272
  69.4 1.6 %collective-permute-start.14 = (bf16[24,5568]{1,0:T(8,128)(2,1)S(1)}, bf16[24,5568]{1,0:T(8,128)(2,1)S(1)}, u32[]{:S(2)}, u32[]{:S(2)}) collective-permute-start(bf16[24,5568]{1,0:T(8,128)(2,1)S(1)} %slice.176), channel_id=1, source_target_pairs={{0,16},{8,24},{16,0},{24,8},{32,48},{40,56},{48,32},{56,40},{64,80... | collective-permute-start | bytes 801800 | tf_op jit(solution)/shard_map/ppermute | solution.py:272
  71.1 2.4 %collective-permute-done.17.c_ref = bf16[24,3136]{1,0:T(8,128)(2,1)S(1)} collective-permute-done((bf16[24,3136]{1,0:T(8,128)(2,1)S(1)}, bf16[24,3136]{1,0:T(8,128)(2,1)S(1)}, u32[]{:S(2)}, u32[]{:S(2)}) %collective-permute-start.17) | collective-permute-done | bytes 150560 | tf_op jit(solution)/shard_map/ppermute | solution.py:272
  73.5 2.4 %collective-permute-done.15.a_ref = bf16[24,3136]{1,0:T(8,128)(2,1)S(1)} collective-permute-done((bf16[24,3136]{1,0:T(8,128)(2,1)S(1)}, bf16[24,3136]{1,0:T(8,128)(2,1)S(1)}, u32[]{:S(2)}, u32[]{:S(2)}) %collective-permute-start.15) | collective-permute-done | bytes 150560 | tf_op jit(solution)/shard_map/ppermute | solution.py:272
  76.8 1.6 %collective-permute-start.19 = (bf16[24,5568]{1,0:T(8,128)(2,1)S(1)}, bf16[24,5568]{1,0:T(8,128)(2,1)S(1)}, u32[]{:S(2)}, u32[]{:S(2)}) collective-permute-start(bf16[24,5568]{1,0:T(8,128)(2,1)S(1)} %get-tuple-element.114), channel_id=1, source_target_pairs={{0,16},{8,24},{16,0},{24,8},{32,48},{40,56},{48,32},{56,40},{64,80... | collective-permute-start | bytes 801800 | tf_op jit(solution)/shard_map/ppermute | solution.py:272
  78.4 4.5 %collective-permute-start.21 = (bf16[24,2752]{1,0:T(8,128)(2,1)S(1)}, bf16[24,2752]{1,0:T(8,128)(2,1)S(1)}, u32[]{:S(2)}, u32[]{:S(2)}) collective-permute-start(bf16[24,2752]{1,0:T(8,128)(2,1)S(1)} %get-tuple-element.113), channel_id=1, source_target_pairs={{0,64},{8,72},{16,80},{24,88},{32,96},{40,104},{48,112},{56,120},{... | collective-permute-start | bytes 396296 | tf_op jit(solution)/shard_map/ppermute | solution.py:272
  82.9 1.8 %collective-permute-done.22 = bf16[24,2752]{1,0:T(8,128)(2,1)S(1)} collective-permute-done((bf16[24,2752]{1,0:T(8,128)(2,1)S(1)}, bf16[24,2752]{1,0:T(8,128)(2,1)S(1)}, u32[]{:S(2)}, u32[]{:S(2)}) %collective-permute-start.22) | collective-permute-done | bytes 132128 | tf_op jit(solution)/shard_map/ppermute | solution.py:272
  84.7 2.7 %collective-permute-done.21 = bf16[24,2752]{1,0:T(8,128)(2,1)S(1)} collective-permute-done((bf16[24,2752]{1,0:T(8,128)(2,1)S(1)}, bf16[24,2752]{1,0:T(8,128)(2,1)S(1)}, u32[]{:S(2)}, u32[]{:S(2)}) %collective-permute-start.21) | collective-permute-done | bytes 132128 | tf_op jit(solution)/shard_map/ppermute | solution.py:272
  88.1 3.1 %collective-permute-start.25 = (bf16[2,24,5568]{2,1,0:T(8,128)(2,1)S(1)}, bf16[2,24,5568]{2,1,0:T(8,128)(2,1)S(1)}, u32[]{:S(2)}, u32[]{:S(2)}) collective-permute-start(bf16[2,24,5568]{2,1,0:T(8,128)(2,1)S(1)} %get-tuple-element.147), channel_id=1, source_target_pairs={{0,64},{8,72},{16,80},{24,88},{32,96},{40,104},{48,112},{56,120},{... | collective-permute-start | bytes 1603592 | tf_op jit(solution)/shard_map/ppermute | solution.py:272
  91.2 2.0 %collective-permute-start.24 = (bf16[2,24,5568]{2,1,0:T(8,128)(2,1)S(1)}, bf16[2,24,5568]{2,1,0:T(8,128)(2,1)S(1)}, u32[]{:S(2)}, u32[]{:S(2)}) collective-permute-start(bf16[2,24,5568]{2,1,0:T(8,128)(2,1)S(1)} %get-tuple-element.147), channel_id=1, source_target_pairs={{0,96},{8,104},{16,112},{24,120},{32,0},{40,8},{48,16},{56,24},{64... | collective-permute-start | bytes 1603592 | tf_op jit(solution)/shard_map/ppermute | solution.py:272
  93.9 8.8 %collective-permute-done.23 = bf16[4,24,2752]{2,1,0:T(8,128)(2,1)S(1)} collective-permute-done((bf16[4,24,2752]{2,1,0:T(8,128)(2,1)S(1)}, bf16[4,24,2752]{2,1,0:T(8,128)(2,1)S(1)}, u32[]{:S(2)}, u32[]{:S(2)}) %collective-permute-start.23) | collective-permute-done | bytes 528416 | tf_op jit(solution)/shard_map/ppermute | solution.py:272
  102.7 1.1 collective-permute-done.26
  103.8 7.5 %collective-permute-done.25 = bf16[2,24,5568]{2,1,0:T(8,128)(2,1)S(1)} collective-permute-done((bf16[2,24,5568]{2,1,0:T(8,128)(2,1)S(1)}, bf16[2,24,5568]{2,1,0:T(8,128)(2,1)S(1)}, u32[]{:S(2)}, u32[]{:S(2)}) %collective-permute-start.25) | collective-permute-done | bytes 534560 | tf_op jit(solution)/shard_map/ppermute | solution.py:272
  112.2 2.4 %collective-permute-done.27.o_ref = bf16[192,2752]{1,0:T(8,128)(2,1)S(1)} collective-permute-done((bf16[192,2752]{1,0:T(8,128)(2,1)S(1)}, bf16[192,2752]{1,0:T(8,128)(2,1)S(1)}, u32[]{:S(2)}, u32[]{:S(2)}) %collective-permute-start.27) | collective-permute-done | bytes 1056800 | tf_op jit(solution)/shard_map/ppermute | solution.py:272
  114.8 4.2 %backward_hidden.1 = (bf16[384,512]{1,0:T(8,128)(2,1)S(1)}, bf16[2752,512]{1,0:T(8,128)(2,1)}) custom-call(bf16[192,2752]{1,0:T(8,128)(2,1)S(1)} %bitcast.90, bf16[192,2752]{1,0:T(8,128)(2,1)S(1)} %collective-permute-done.27.o_ref, bf16[384,512]{1,0:T(8,128)(2,1)S(1)} %get-tuple-element.89.o_ref.x_ref, bf16[64,8448]{1,0:T(8,128)(2,1)S(1)} %bitcast.85, ...), custom_call_target="tpu_custom_call" | custom-call | tf_op jit(solution)/shard_map/backward_hidden/pallas_call | solution.py:46
  119.0 3.0 %collective-permute-start.29 = (bf16[4,48,512]{2,1,0:T(8,128)(2,1)S(1)}, bf16[4,48,512]{2,1,0:T(8,128)(2,1)S(1)}, u32[]{:S(2)}, u32[]{:S(2)}) collective-permute-start(bf16[4,48,512]{2,1,0:T(8,128)(2,1)S(1)} %bitcast.108), channel_id=1, source_target_pairs={{0,4},{1,5},{2,6},{3,7},{4,0},{5,1},{6,2},{7,3},{8,12},{9,13},{10,... | collective-permute-start | bytes 589832 | tf_op jit(solution)/shard_map/ppermute | solution.py:280
  122.0 4.5 %backward_pair.1 = bf16[384,512]{1,0:T(8,128)(2,1)S(1)} custom-call(bf16[192,5568]{1,0:T(8,128)(2,1)S(1)} %bitcast.74, bf16[192,5568]{1,0:T(8,128)(2,1)S(1)} %collective-permute-done.28.o_ref, bf16[64,8448]{1,0:T(8,128)(2,1)S(1)} %bitcast.86, bf16[64,8448]{1,0:T(8,128)(2,1)S(1)} %collective-permute-done.18.far_ref, ...), custom_call_target="tpu_custom_call" | custom-call | tf_op jit(solution)/shard_map/backward_pair/pallas_call | solution.py:46
  126.6 0.9 collective-permute-start.30
  127.5 2.5 %weight_grad.2 = bf16[2752,512]{1,0:T(8,128)(2,1)} custom-call(bf16[192,5568]{1,0:T(8,128)(2,1)S(1)} %bitcast.75, bf16[192,5568]{1,0:T(8,128)(2,1)S(1)} %collective-permute-done.28.o_ref, bf16[384,512]{1,0:T(8,128)(2,1)S(1)} %get-tuple-element.96.t_ref.x_ref), custom_call_target="tpu_custom_call" | custom-call | tf_op jit(solution)/shard_map/weight_grad/pallas_call | solution.py:46
  130.0 5.0 %collective-permute-done.30 = bf16[4,48,512]{2,1,0:T(8,128)(2,1)S(1)} collective-permute-done((bf16[4,48,512]{2,1,0:T(8,128)(2,1)S(1)}, bf16[4,48,512]{2,1,0:T(8,128)(2,1)S(1)}, u32[]{:S(2)}, u32[]{:S(2)}) %collective-permute-start.30) | collective-permute-done | bytes 196640 | tf_op jit(solution)/shard_map/ppermute | solution.py:280
  135.2 1.3 collective-permute-start.31
  136.5 2.0 %collective-permute-start.32 = (bf16[2,48,512]{2,1,0:T(8,128)(2,1)S(1)}, bf16[2,48,512]{2,1,0:T(8,128)(2,1)S(1)}, u32[]{:S(2)}, u32[]{:S(2)}) collective-permute-start(bf16[2,48,512]{2,1,0:T(8,128)(2,1)S(1)} %pad_maximum_fusion.9), channel_id=1, source_target_pairs={{0,3},{1,0},{2,1},{3,2},{4,7},{5,4},{6,5},{7,6},{8,11},{9,8},{10,9... | collective-permute-start | bytes 294920 | tf_op jit(solution)/shard_map/ppermute | solution.py:280
  138.5 1.2 collective-permute-start.33
  139.7 2.5 %weight_grad.3 = bf16[2752,512]{1,0:T(8,128)(2,1)} custom-call(bf16[192,5568]{1,0:T(8,128)(2,1)S(1)} %bitcast.76, bf16[192,5568]{1,0:T(8,128)(2,1)S(1)} %collective-permute-done.28.o_ref, bf16[384,512]{1,0:T(8,128)(2,1)S(1)} %get-tuple-element.96.t_ref.x_ref), custom_call_target="tpu_custom_call" | custom-call | tf_op jit(solution)/shard_map/weight_grad/pallas_call | solution.py:46
  142.2 2.5 %collective-permute-done.33 = bf16[2,48,512]{2,1,0:T(8,128)(2,1)S(1)} collective-permute-done((bf16[2,48,512]{2,1,0:T(8,128)(2,1)S(1)}, bf16[2,48,512]{2,1,0:T(8,128)(2,1)S(1)}, u32[]{:S(2)}, u32[]{:S(2)}) %collective-permute-start.33) | collective-permute-done | bytes 98336 | tf_op jit(solution)/shard_map/ppermute | solution.py:280
  (79 shorter events, 8.3 us)
Async XLA Ops:
  0.6 14.0 %copy-start.6 = (bf16[384,512]{1,0:T(8,128)(2,1)S(1)}, bf16[384,512]{1,0:T(8,128)(2,1)}, u32[]{:S(2)}) copy-start(bf16[384,512]{1,0:T(8,128)(2,1)} %g_ref) | copy-start | bytes 1179652
  0.6 14.0 %copy-start.5 = (bf16[384,512]{1,0:T(8,128)(2,1)S(1)}, bf16[384,512]{1,0:T(8,128)(2,1)}, u32[]{:S(2)}) copy-start(bf16[384,512]{1,0:T(8,128)(2,1)} %t_ref) | copy-start | bytes 1179652
  1.7 13.0 %collective-permute-start.3 = (bf16[8,8448]{1,0:T(8,128)(2,1)S(1)}, bf16[8,8448]{1,0:T(8,128)(2,1)S(1)}, u32[]{:S(2)}, u32[]{:S(2)}) collective-permute-start(bf16[8,8448]{1,0:T(8,128)(2,1)S(1)} %concatenate.6), channel_id=1, source_target_pairs={{0,32},{8,40},{16,48},{24,56},{32,64},{40,72},{48,80},{56,88},{64,... | collective-permute-start | bytes 405512 | tf_op jit(solution)/shard_map/ppermute | solution.py:272
  3.7 10.9 %collective-permute-start.2 = (bf16[8,8448]{1,0:T(8,128)(2,1)S(1)}, bf16[8,8448]{1,0:T(8,128)(2,1)S(1)}, u32[]{:S(2)}, u32[]{:S(2)}) collective-permute-start(bf16[8,8448]{1,0:T(8,128)(2,1)S(1)} %concatenate.6), channel_id=1, source_target_pairs={{0,64},{8,72},{16,80},{24,88},{32,96},{40,104},{48,112},{56,120},{... | collective-permute-start | bytes 405512 | tf_op jit(solution)/shard_map/ppermute | solution.py:272
  7.3 7.4 %collective-permute-start.1 = (bf16[8,8448]{1,0:T(8,128)(2,1)S(1)}, bf16[8,8448]{1,0:T(8,128)(2,1)S(1)}, u32[]{:S(2)}, u32[]{:S(2)}) collective-permute-start(bf16[8,8448]{1,0:T(8,128)(2,1)S(1)} %concatenate.6), channel_id=1, source_target_pairs={{0,96},{8,104},{16,112},{24,120},{32,0},{40,8},{48,16},{56,24},{64... | collective-permute-start | bytes 405512 | tf_op jit(solution)/shard_map/ppermute | solution.py:272
  9.0 5.6 %collective-permute-start = (bf16[48,512]{1,0:T(8,128)(2,1)S(1)}, bf16[48,512]{1,0:T(8,128)(2,1)S(1)}, u32[]{:S(2)}, u32[]{:S(2)}) collective-permute-start(bf16[48,512]{1,0:T(8,128)(2,1)S(1)} %pad_maximum_fusion.11), channel_id=1, source_target_pairs={{0,4},{1,5},{2,6},{3,7},{4,0},{5,1},{6,2},{7,3},{8,12},{9,13},{10,... | collective-permute-start | bytes 147464 | tf_op jit(solution)/shard_map/ppermute | solution.py:280
  14.7 1.8 %copy-start = (bf16[512,2752]{0,1:T(8,128)(2,1)S(1)}, bf16[512,2752]{0,1:T(8,128)(2,1)}, u32[]{:S(2)}) copy-start(bf16[512,2752]{0,1:T(8,128)(2,1)} %param.15) | copy-start | bytes 8454148
  16.5 1.8 %copy-start.2 = (bf16[512,2752]{0,1:T(8,128)(2,1)S(1)}, bf16[512,2752]{0,1:T(8,128)(2,1)}, u32[]{:S(2)}) copy-start(bf16[512,2752]{0,1:T(8,128)(2,1)} %param.13) | copy-start | bytes 8454148
  18.3 12.5 %copy-start.1 = (bf16[512,2752]{0,1:T(8,128)(2,1)S(1)}, bf16[512,2752]{0,1:T(8,128)(2,1)}, u32[]{:S(2)}) copy-start(bf16[512,2752]{0,1:T(8,128)(2,1)} %param.15) | copy-start | bytes 8454148
  20.8 9.9 %collective-permute-start.4 = (bf16[192,5568]{1,0:T(8,128)(2,1)S(1)}, bf16[192,5568]{1,0:T(8,128)(2,1)S(1)}, u32[]{:S(2)}, u32[]{:S(2)}) collective-permute-start(bf16[192,5568]{1,0:T(8,128)(2,1)S(1)} %get-tuple-element.90), channel_id=1, source_target_pairs={{0,8},{8,0},{16,24},{24,16},{32,40},{40,32},{48,56},{56,48},{64,72... | collective-permute-start | bytes 6414344 | tf_op jit(solution)/shard_map/ppermute | solution.py:272
  20.9 6.9 %collective-permute-start.9 = (bf16[2,48,512]{2,1,0:T(8,128)(2,1)S(1)}, bf16[2,48,512]{2,1,0:T(8,128)(2,1)S(1)}, u32[]{:S(2)}, u32[]{:S(2)}) collective-permute-start(bf16[2,48,512]{2,1,0:T(8,128)(2,1)S(1)} %get-tuple-element.165), channel_id=1, source_target_pairs={{0,2},{1,3},{2,0},{3,1},{4,6},{5,7},{6,4},{7,5},{8,10},{9,11},{10,... | collective-permute-start | bytes 294920 | tf_op jit(solution)/shard_map/ppermute | solution.py:280
  24.2 6.1 %collective-permute-start.8 = (bf16[2,48,512]{2,1,0:T(8,128)(2,1)S(1)}, bf16[2,48,512]{2,1,0:T(8,128)(2,1)S(1)}, u32[]{:S(2)}, u32[]{:S(2)}) collective-permute-start(bf16[2,48,512]{2,1,0:T(8,128)(2,1)S(1)} %get-tuple-element.165), channel_id=1, source_target_pairs={{0,1},{1,2},{2,3},{3,0},{4,5},{5,6},{6,7},{7,4},{8,9},{9,10},{10,1... | collective-permute-start | bytes 294920 | tf_op jit(solution)/shard_map/ppermute | solution.py:280
  24.9 5.4 %collective-permute-start.10 = (bf16[2,48,512]{2,1,0:T(8,128)(2,1)S(1)}, bf16[2,48,512]{2,1,0:T(8,128)(2,1)S(1)}, u32[]{:S(2)}, u32[]{:S(2)}) collective-permute-start(bf16[2,48,512]{2,1,0:T(8,128)(2,1)S(1)} %get-tuple-element.165), channel_id=1, source_target_pairs={{0,3},{1,0},{2,1},{3,2},{4,7},{5,4},{6,5},{7,6},{8,11},{9,8},{10,9... | collective-permute-start | bytes 294920 | tf_op jit(solution)/shard_map/ppermute | solution.py:280
  30.8 2.0 %copy-start.4 = (bf16[512,2752]{0,1:T(8,128)(2,1)S(1)}, bf16[512,2752]{0,1:T(8,128)(2,1)}, u32[]{:S(2)}) copy-start(bf16[512,2752]{0,1:T(8,128)(2,1)} %param.14) | copy-start | bytes 8454148
  34.4 14.9 %collective-permute-start.11 = (bf16[192,3136]{1,0:T(8,128)(2,1)S(1)}, bf16[192,3136]{1,0:T(8,128)(2,1)S(1)}, u32[]{:S(2)}, u32[]{:S(2)}) collective-permute-start(bf16[192,3136]{1,0:T(8,128)(2,1)S(1)} %get-tuple-element.101), channel_id=1, source_target_pairs={{0,8},{8,0},{16,24},{24,16},{32,40},{40,32},{48,56},{56,48},{64,72... | collective-permute-start | bytes 3612680 | tf_op jit(solution)/shard_map/ppermute | solution.py:272
  34.6 14.8 %collective-permute-start.12 = (bf16[4,8,8448]{2,1,0:T(8,128)(2,1)S(1)}, bf16[4,8,8448]{2,1,0:T(8,128)(2,1)S(1)}, u32[]{:S(2)}, u32[]{:S(2)}) collective-permute-start(bf16[4,8,8448]{2,1,0:T(8,128)(2,1)S(1)} %get-tuple-element.151), channel_id=1, source_target_pairs={{0,16},{8,24},{16,0},{24,8},{32,48},{40,56},{48,32},{56,40},{64,80... | collective-permute-start | bytes 1622024 | tf_op jit(solution)/shard_map/ppermute | solution.py:272
  36.1 27.2 %collective-permute-start.5 = (bf16[48,5568]{1,0:T(8,128)(2,1)S(1)}, bf16[48,5568]{1,0:T(8,128)(2,1)S(1)}, u32[]{:S(2)}, u32[]{:S(2)}) collective-permute-start(bf16[48,5568]{1,0:T(8,128)(2,1)S(1)} %get-tuple-element.93), channel_id=1, source_target_pairs={{0,32},{8,40},{16,48},{24,56},{32,64},{40,72},{48,80},{56,88},{64,... | collective-permute-start | bytes 1603592 | tf_op jit(solution)/shard_map/ppermute | solution.py:272
  37.2 26.2 %collective-permute-start.6 = (bf16[48,5568]{1,0:T(8,128)(2,1)S(1)}, bf16[48,5568]{1,0:T(8,128)(2,1)S(1)}, u32[]{:S(2)}, u32[]{:S(2)}) collective-permute-start(bf16[48,5568]{1,0:T(8,128)(2,1)S(1)} %get-tuple-element.94), channel_id=1, source_target_pairs={{0,96},{8,104},{16,112},{24,120},{32,0},{40,8},{48,16},{56,24},{64... | collective-permute-start | bytes 1603592 | tf_op jit(solution)/shard_map/ppermute | solution.py:272
  39.4 24.0 %collective-permute-start.7 = (bf16[48,5568]{1,0:T(8,128)(2,1)S(1)}, bf16[48,5568]{1,0:T(8,128)(2,1)S(1)}, u32[]{:S(2)}, u32[]{:S(2)}) collective-permute-start(bf16[48,5568]{1,0:T(8,128)(2,1)S(1)} %get-tuple-element.95), channel_id=1, source_target_pairs={{0,64},{8,72},{16,80},{24,88},{32,96},{40,104},{48,112},{56,120},{... | collective-permute-start | bytes 1603592 | tf_op jit(solution)/shard_map/ppermute | solution.py:272
  49.7 15.5 %collective-permute-start.13 = (bf16[4,24,3136]{2,1,0:T(8,128)(2,1)S(1)}, bf16[4,24,3136]{2,1,0:T(8,128)(2,1)S(1)}, u32[]{:S(2)}, u32[]{:S(2)}) collective-permute-start(bf16[4,24,3136]{2,1,0:T(8,128)(2,1)S(1)} %fusion.1), channel_id=1, source_target_pairs={{0,16},{8,24},{16,0},{24,8},{32,48},{40,56},{48,32},{56,40},{64,80... | collective-permute-start | bytes 1806344 | tf_op jit(solution)/shard_map/ppermute | solution.py:272
  51.4 24.7 %collective-permute-start.18 = (bf16[64,8448]{1,0:T(8,128)(2,1)S(1)}, bf16[64,8448]{1,0:T(8,128)(2,1)S(1)}, u32[]{:S(2)}, u32[]{:S(2)}) collective-permute-start(bf16[64,8448]{1,0:T(8,128)(2,1)S(1)} %bitcast.83), channel_id=1, source_target_pairs={{0,8},{8,0},{16,24},{24,16},{32,40},{40,32},{48,56},{56,48},{64,72... | collective-permute-start | bytes 3244040 | tf_op jit(solution)/shard_map/ppermute | solution.py:272
  65.4 8.0 %collective-permute-start.17 = (bf16[24,3136]{1,0:T(8,128)(2,1)S(1)}, bf16[24,3136]{1,0:T(8,128)(2,1)S(1)}, u32[]{:S(2)}, u32[]{:S(2)}) collective-permute-start(bf16[24,3136]{1,0:T(8,128)(2,1)S(1)} %get-tuple-element.141), channel_id=1, source_target_pairs={{0,64},{8,72},{16,80},{24,88},{32,96},{40,104},{48,112},{56,120},{... | collective-permute-start | bytes 451592 | tf_op jit(solution)/shard_map/ppermute | solution.py:272
  66.5 6.9 %collective-permute-start.16 = (bf16[24,3136]{1,0:T(8,128)(2,1)S(1)}, bf16[24,3136]{1,0:T(8,128)(2,1)S(1)}, u32[]{:S(2)}, u32[]{:S(2)}) collective-permute-start(bf16[24,3136]{1,0:T(8,128)(2,1)S(1)} %get-tuple-element.142), channel_id=1, source_target_pairs={{0,96},{8,104},{16,112},{24,120},{32,0},{40,8},{48,16},{56,24},{64... | collective-permute-start | bytes 451592 | tf_op jit(solution)/shard_map/ppermute | solution.py:272
  69.2 6.7 %collective-permute-start.15 = (bf16[24,3136]{1,0:T(8,128)(2,1)S(1)}, bf16[24,3136]{1,0:T(8,128)(2,1)S(1)}, u32[]{:S(2)}, u32[]{:S(2)}) collective-permute-start(bf16[24,3136]{1,0:T(8,128)(2,1)S(1)} %get-tuple-element.143), channel_id=1, source_target_pairs={{0,32},{8,40},{16,48},{24,56},{32,64},{40,72},{48,80},{56,88},{64,... | collective-permute-start | bytes 451592 | tf_op jit(solution)/shard_map/ppermute | solution.py:272
  69.4 6.7 %collective-permute-start.14 = (bf16[24,5568]{1,0:T(8,128)(2,1)S(1)}, bf16[24,5568]{1,0:T(8,128)(2,1)S(1)}, u32[]{:S(2)}, u32[]{:S(2)}) collective-permute-start(bf16[24,5568]{1,0:T(8,128)(2,1)S(1)} %slice.176), channel_id=1, source_target_pairs={{0,16},{8,24},{16,0},{24,8},{32,48},{40,56},{48,32},{56,40},{64,80... | collective-permute-start | bytes 801800 | tf_op jit(solution)/shard_map/ppermute | solution.py:272
  76.8 11.1 %collective-permute-start.19 = (bf16[24,5568]{1,0:T(8,128)(2,1)S(1)}, bf16[24,5568]{1,0:T(8,128)(2,1)S(1)}, u32[]{:S(2)}, u32[]{:S(2)}) collective-permute-start(bf16[24,5568]{1,0:T(8,128)(2,1)S(1)} %get-tuple-element.114), channel_id=1, source_target_pairs={{0,16},{8,24},{16,0},{24,8},{32,48},{40,56},{48,32},{56,40},{64,80... | collective-permute-start | bytes 801800 | tf_op jit(solution)/shard_map/ppermute | solution.py:272
  78.4 6.3 %collective-permute-start.22 = (bf16[24,2752]{1,0:T(8,128)(2,1)S(1)}, bf16[24,2752]{1,0:T(8,128)(2,1)S(1)}, u32[]{:S(2)}, u32[]{:S(2)}) collective-permute-start(bf16[24,2752]{1,0:T(8,128)(2,1)S(1)} %get-tuple-element.113), channel_id=1, source_target_pairs={{0,32},{8,40},{16,48},{24,56},{32,64},{40,72},{48,80},{56,88},{64,... | collective-permute-start | bytes 396296 | tf_op jit(solution)/shard_map/ppermute | solution.py:272
  78.4 8.9 %collective-permute-start.21 = (bf16[24,2752]{1,0:T(8,128)(2,1)S(1)}, bf16[24,2752]{1,0:T(8,128)(2,1)S(1)}, u32[]{:S(2)}, u32[]{:S(2)}) collective-permute-start(bf16[24,2752]{1,0:T(8,128)(2,1)S(1)} %get-tuple-element.113), channel_id=1, source_target_pairs={{0,64},{8,72},{16,80},{24,88},{32,96},{40,104},{48,112},{56,120},{... | collective-permute-start | bytes 396296 | tf_op jit(solution)/shard_map/ppermute | solution.py:272
  82.9 5.0 %collective-permute-start.20 = (bf16[24,2752]{1,0:T(8,128)(2,1)S(1)}, bf16[24,2752]{1,0:T(8,128)(2,1)S(1)}, u32[]{:S(2)}, u32[]{:S(2)}) collective-permute-start(bf16[24,2752]{1,0:T(8,128)(2,1)S(1)} %get-tuple-element.113), channel_id=1, source_target_pairs={{0,96},{8,104},{16,112},{24,120},{32,0},{40,8},{48,16},{56,24},{64... | collective-permute-start | bytes 396296 | tf_op jit(solution)/shard_map/ppermute | solution.py:272
  88.0 15.8 %collective-permute-start.26 = (bf16[2,24,5568]{2,1,0:T(8,128)(2,1)S(1)}, bf16[2,24,5568]{2,1,0:T(8,128)(2,1)S(1)}, u32[]{:S(2)}, u32[]{:S(2)}) collective-permute-start(bf16[2,24,5568]{2,1,0:T(8,128)(2,1)S(1)} %get-tuple-element.147), channel_id=1, source_target_pairs={{0,32},{8,40},{16,48},{24,56},{32,64},{40,72},{48,80},{56,88},{64,... | collective-permute-start | bytes 1603592 | tf_op jit(solution)/shard_map/ppermute | solution.py:272
  88.1 23.2 %collective-permute-start.25 = (bf16[2,24,5568]{2,1,0:T(8,128)(2,1)S(1)}, bf16[2,24,5568]{2,1,0:T(8,128)(2,1)S(1)}, u32[]{:S(2)}, u32[]{:S(2)}) collective-permute-start(bf16[2,24,5568]{2,1,0:T(8,128)(2,1)S(1)} %get-tuple-element.147), channel_id=1, source_target_pairs={{0,64},{8,72},{16,80},{24,88},{32,96},{40,104},{48,112},{56,120},{... | collective-permute-start | bytes 1603592 | tf_op jit(solution)/shard_map/ppermute | solution.py:272
  91.2 20.5 %collective-permute-start.24 = (bf16[2,24,5568]{2,1,0:T(8,128)(2,1)S(1)}, bf16[2,24,5568]{2,1,0:T(8,128)(2,1)S(1)}, u32[]{:S(2)}, u32[]{:S(2)}) collective-permute-start(bf16[2,24,5568]{2,1,0:T(8,128)(2,1)S(1)} %get-tuple-element.147), channel_id=1, source_target_pairs={{0,96},{8,104},{16,112},{24,120},{32,0},{40,8},{48,16},{56,24},{64... | collective-permute-start | bytes 1603592 | tf_op jit(solution)/shard_map/ppermute | solution.py:272
  93.3 9.4 %collective-permute-start.23 = (bf16[4,24,2752]{2,1,0:T(8,128)(2,1)S(1)}, bf16[4,24,2752]{2,1,0:T(8,128)(2,1)S(1)}, u32[]{:S(2)}, u32[]{:S(2)}) collective-permute-start(bf16[4,24,2752]{2,1,0:T(8,128)(2,1)S(1)} %get-tuple-element.149), channel_id=1, source_target_pairs={{0,16},{8,24},{16,0},{24,8},{32,48},{40,56},{48,32},{56,40},{64,80... | collective-permute-start | bytes 1585160 | tf_op jit(solution)/shard_map/ppermute | solution.py:272
  111.9 2.8 %collective-permute-start.27 = (bf16[192,2752]{1,0:T(8,128)(2,1)S(1)}, bf16[192,2752]{1,0:T(8,128)(2,1)S(1)}, u32[]{:S(2)}, u32[]{:S(2)}) collective-permute-start(bf16[192,2752]{1,0:T(8,128)(2,1)S(1)} %bitcast.89), channel_id=1, source_target_pairs={{0,8},{8,0},{16,24},{24,16},{32,40},{40,32},{48,56},{56,48},{64,72... | collective-permute-start | bytes 3170312 | tf_op jit(solution)/shard_map/ppermute | solution.py:272
  114.6 7.4 %collective-permute-start.28 = (bf16[192,5568]{1,0:T(8,128)(2,1)S(1)}, bf16[192,5568]{1,0:T(8,128)(2,1)S(1)}, u32[]{:S(2)}, u32[]{:S(2)}) collective-permute-start(bf16[192,5568]{1,0:T(8,128)(2,1)S(1)} %bitcast.73), channel_id=1, source_target_pairs={{0,8},{8,0},{16,24},{24,16},{32,40},{40,32},{48,56},{56,48},{64,72... | collective-permute-start | bytes 6414344 | tf_op jit(solution)/shard_map/ppermute | solution.py:272
  114.8 7.3 %copy-start.3 = (bf16[512,2752]{0,1:T(8,128)(2,1)S(1)}, bf16[512,2752]{0,1:T(8,128)(2,1)}, u32[]{:S(2)}) copy-start(bf16[512,2752]{0,1:T(8,128)(2,1)} %param.13) | copy-start | bytes 8454148
  119.0 10.9 %collective-permute-start.29 = (bf16[4,48,512]{2,1,0:T(8,128)(2,1)S(1)}, bf16[4,48,512]{2,1,0:T(8,128)(2,1)S(1)}, u32[]{:S(2)}, u32[]{:S(2)}) collective-permute-start(bf16[4,48,512]{2,1,0:T(8,128)(2,1)S(1)} %bitcast.108), channel_id=1, source_target_pairs={{0,4},{1,5},{2,6},{3,7},{4,0},{5,1},{6,2},{7,3},{8,12},{9,13},{10,... | collective-permute-start | bytes 589832 | tf_op jit(solution)/shard_map/ppermute | solution.py:280
  126.6 8.5 %collective-permute-start.30 = (bf16[4,48,512]{2,1,0:T(8,128)(2,1)S(1)}, bf16[4,48,512]{2,1,0:T(8,128)(2,1)S(1)}, u32[]{:S(2)}, u32[]{:S(2)}) collective-permute-start(bf16[4,48,512]{2,1,0:T(8,128)(2,1)S(1)} %bitcast.109), channel_id=1, source_target_pairs={{0,4},{1,5},{2,6},{3,7},{4,0},{5,1},{6,2},{7,3},{8,12},{9,13},{10,... | collective-permute-start | bytes 589832 | tf_op jit(solution)/shard_map/ppermute | solution.py:280
  135.2 7.0 %collective-permute-start.31 = (bf16[2,48,512]{2,1,0:T(8,128)(2,1)S(1)}, bf16[2,48,512]{2,1,0:T(8,128)(2,1)S(1)}, u32[]{:S(2)}, u32[]{:S(2)}) collective-permute-start(bf16[2,48,512]{2,1,0:T(8,128)(2,1)S(1)} %pad_maximum_fusion.8), channel_id=1, source_target_pairs={{0,1},{1,2},{2,3},{3,0},{4,5},{5,6},{6,7},{7,4},{8,9},{9,10},{10,1... | collective-permute-start | bytes 294920 | tf_op jit(solution)/shard_map/ppermute | solution.py:280
  136.5 5.7 %collective-permute-start.32 = (bf16[2,48,512]{2,1,0:T(8,128)(2,1)S(1)}, bf16[2,48,512]{2,1,0:T(8,128)(2,1)S(1)}, u32[]{:S(2)}, u32[]{:S(2)}) collective-permute-start(bf16[2,48,512]{2,1,0:T(8,128)(2,1)S(1)} %pad_maximum_fusion.9), channel_id=1, source_target_pairs={{0,3},{1,0},{2,1},{3,2},{4,7},{5,4},{6,5},{7,6},{8,11},{9,8},{10,9... | collective-permute-start | bytes 294920 | tf_op jit(solution)/shard_map/ppermute | solution.py:280
  138.5 6.1 %collective-permute-start.33 = (bf16[2,48,512]{2,1,0:T(8,128)(2,1)S(1)}, bf16[2,48,512]{2,1,0:T(8,128)(2,1)S(1)}, u32[]{:S(2)}, u32[]{:S(2)}) collective-permute-start(bf16[2,48,512]{2,1,0:T(8,128)(2,1)S(1)} %pad_maximum_fusion.10), channel_id=1, source_target_pairs={{0,2},{1,3},{2,0},{3,1},{4,6},{5,7},{6,4},{7,5},{8,10},{9,11},{10,... | collective-permute-start | bytes 294920 | tf_op jit(solution)/shard_map/ppermute | solution.py:280

commit v6 on v5

--- a/solution.py
+++ b/solution.py
@@ -352,13 +352,12 @@
     rights = jnp.concatenate([gate_right, edge, up_right, edge, down_right, edge], axis=1)
     lefts = jnp.concatenate([gate_left.T, up_left.T, down_left.T], axis=0)
     lefts_h = col_send(lefts, 1, 0)
-    rights_z = z_spread(rights)
-    held, leave, sort, match, rights, lefts, lefts_h, *rights_z = tie(
-        held, leave, sort, match, rights, lefts, lefts_h, *rights_z
-    )
+    held, sort, match, rights, lefts, lefts_h = tie(held, sort, match, rights, lefts, lefts_h)
 
     theirs, tok, out = forward_theirs(tokens, grad_out, held, gate_w, down_w)
     got = core_send(theirs)
+    tok, rights = tie(tok, rights)
+    rights_z = z_spread(rights)
     lefts = jnp.stack([lefts, lefts_h])
     lefts_y = [col_send(lefts, 0, d) for d in (1, 2, 3)]
     rights = jnp.stack([rights] + rights_z)
@@ -376,7 +375,7 @@
     near = jnp.stack([rights, rights_x], axis=1).reshape(64, -1)
     far = core_send(near)
 
-    *pair_z, up_x = tie(*pair_z, up_x)
+    *pair_z, up_x, leave = tie(*pair_z, up_x, leave)
     pair = plus(pair, pair_z).reshape(2, ROWS, -1)
     pair_x = x_send(pair[1].astype(BF))
     up = up[:, 0] + up_x.astype(F32)

time: 146 us -> 141 us (0.966)
  waiting for transfers between devices: 64.9 us -> 58.8 us
  starting transfers between devices: 48.9 us -> 50.7 us
    ppermute x25, waiting for transfers between devices: 53.7 us -> 50.6 us  [row_send(): return lax.ppermute(x, 'row', pairs)]
    ppermute x9, waiting for transfers between devices: 11.1 us -> 8.15 us  [col_send(): return lax.ppermute(x, 'col', pairs)]
    ppermute x25, starting transfers between devices: 30.9 us -> 32.5 us  [row_send(): return lax.ppermute(x, 'row', pairs)]
  transfers between devices with their start and end apart: 34 -> 34, of which waited for: 19 -> 20; matrix products, arithmetic and copies ran while one was open for 3% -> 3% of each run, Pallas kernels for 9% -> 12%
where the time goes in v6:
time: 141 us
  waiting for transfers between devices  58.8 us (42%)
  starting transfers between devices  50.7 us (36%)
  Pallas kernels  20.3 us (14%)
  local copies, waits for them, and re-layouts  4.93 us (3%)
  other arithmetic  4.92 us (3%)
    ppermute x25, waiting for transfers between devices, row_send(): return lax.ppermute(x, 'row', pairs)  50.6 us
    ppermute x25, starting transfers between devices, row_send(): return lax.ppermute(x, 'row', pairs)  32.5 us
    pallas_call x8, Pallas kernels, pallas(): pl.pallas_call(body, out_shape=outs, in_specs=in_specs, out_specs=out_spe...  20.3 us
    ppermute x9, starting transfers between devices, col_send(): return lax.ppermute(x, 'col', pairs)  18.2 us
    ppermute x9, waiting for transfers between devices, col_send(): return lax.ppermute(x, 'col', pairs)  8.15 us
    unnamed x14, local copies, waits for them, and re-layouts  3.61 us
  transfers between devices with their start and end apart: 34, of which 20 were waited for; matrix products, arithmetic and copies ran while one was open for 3% of the time, Pallas kernels for 12%

profile of v6, /device:TPU:0, one launch (start us, length us, event | category | flops | bytes accessed | tf_op | source)
XLA Modules:
  0.0 141.1 jit_solution(6339108766801174434)
XLA Ops:
  1.5 3.1 %collective-permute-start = (bf16[48,512]{1,0:T(8,128)(2,1)S(1)}, bf16[48,512]{1,0:T(8,128)(2,1)S(1)}, u32[]{:S(2)}, u32[]{:S(2)}) collective-permute-start(bf16[48,512]{1,0:T(8,128)(2,1)S(1)} %pad_maximum_fusion.11), channel_id=1, source_target_pairs={{0,4},{1,5},{2,6},{3,7},{4,0},{5,1},{6,2},{7,3},{8,12},{9,13},{10,... | collective-permute-start | bytes 147464 | tf_op jit(solution)/shard_map/ppermute | solution.py:280
  5.5 0.9 concatenate.6
  7.1 1.8 %copy-done = bf16[512,2752]{0,1:T(8,128)(2,1)S(1)} copy-done((bf16[512,2752]{0,1:T(8,128)(2,1)S(1)}, bf16[512,2752]{0,1:T(8,128)(2,1)}, u32[]{:S(2)}) %copy-start) | copy-done | bytes 2818072
  8.9 1.8 %copy-done.2 = bf16[512,2752]{0,1:T(8,128)(2,1)S(1)} copy-done((bf16[512,2752]{0,1:T(8,128)(2,1)S(1)}, bf16[512,2752]{0,1:T(8,128)(2,1)}, u32[]{:S(2)}) %copy-start.2) | copy-done | bytes 2818072
  10.7 2.5 %forward_theirs.1 = (bf16[192,5568]{1,0:T(8,128)(2,1)S(1)}, bf16[384,512]{1,0:T(8,128)(2,1)S(1)}, bf16[384,512]{1,0:T(8,128)(2,1)S(1)}) custom-call(bf16[384,512]{1,0:T(8,128)(2,1)S(1)} %copy-done.5, bf16[384,512]{1,0:T(8,128)(2,1)S(1)} %copy-done.6, s32[384,1]{1,0:T(8,128)S(1)} %fusion.22.i_ref, bf16[2752,512]{1,0:T(8,128)(2,1)S(1)} %bitcast.80, ...), custom_call_target="tpu_custom_call" | custom-call | tf_op jit(solution)/shard_map/forward_theirs/pallas_call | solution.py:46
  13.4 3.4 %collective-permute-start.6 = (bf16[2,48,512]{2,1,0:T(8,128)(2,1)S(1)}, bf16[2,48,512]{2,1,0:T(8,128)(2,1)S(1)}, u32[]{:S(2)}, u32[]{:S(2)}) collective-permute-start(bf16[2,48,512]{2,1,0:T(8,128)(2,1)S(1)} %get-tuple-element.163), channel_id=1, source_target_pairs={{0,2},{1,3},{2,0},{3,1},{4,6},{5,7},{6,4},{7,5},{8,10},{9,11},{10,... | collective-permute-start | bytes 294920 | tf_op jit(solution)/shard_map/ppermute | solution.py:280
  17.4 2.6 %collective-permute-start.7 = (bf16[2,48,512]{2,1,0:T(8,128)(2,1)S(1)}, bf16[2,48,512]{2,1,0:T(8,128)(2,1)S(1)}, u32[]{:S(2)}, u32[]{:S(2)}) collective-permute-start(bf16[2,48,512]{2,1,0:T(8,128)(2,1)S(1)} %get-tuple-element.163), channel_id=1, source_target_pairs={{0,3},{1,0},{2,1},{3,2},{4,7},{5,4},{6,5},{7,6},{8,11},{9,8},{10,9... | collective-permute-start | bytes 294920 | tf_op jit(solution)/shard_map/ppermute | solution.py:280
  20.0 1.9 %collective-permute-start.11 = (bf16[8,8448]{1,0:T(8,128)(2,1)S(1)}, bf16[8,8448]{1,0:T(8,128)(2,1)S(1)}, u32[]{:S(2)}, u32[]{:S(2)}) collective-permute-start(bf16[8,8448]{1,0:T(8,128)(2,1)S(1)} %concatenate.6), channel_id=1, source_target_pairs={{0,32},{8,40},{16,48},{24,56},{32,64},{40,72},{48,80},{56,88},{64,... | collective-permute-start | bytes 405512 | tf_op jit(solution)/shard_map/ppermute | solution.py:272
  21.9 3.6 %collective-permute-start.10 = (bf16[8,8448]{1,0:T(8,128)(2,1)S(1)}, bf16[8,8448]{1,0:T(8,128)(2,1)S(1)}, u32[]{:S(2)}, u32[]{:S(2)}) collective-permute-start(bf16[8,8448]{1,0:T(8,128)(2,1)S(1)} %concatenate.6), channel_id=1, source_target_pairs={{0,64},{8,72},{16,80},{24,88},{32,96},{40,104},{48,112},{56,120},{... | collective-permute-start | bytes 405512 | tf_op jit(solution)/shard_map/ppermute | solution.py:272
  25.5 1.4 %collective-permute-start.9 = (bf16[8,8448]{1,0:T(8,128)(2,1)S(1)}, bf16[8,8448]{1,0:T(8,128)(2,1)S(1)}, u32[]{:S(2)}, u32[]{:S(2)}) collective-permute-start(bf16[8,8448]{1,0:T(8,128)(2,1)S(1)} %concatenate.6), channel_id=1, source_target_pairs={{0,96},{8,104},{16,112},{24,120},{32,0},{40,8},{48,16},{56,24},{64... | collective-permute-start | bytes 405512 | tf_op jit(solution)/shard_map/ppermute | solution.py:272
  27.3 2.0 %forward_mine.1 = (f32[48,5568]{1,0:T(8,128)S(1)}, bf16[48,5568]{1,0:T(8,128)(2,1)S(1)}, bf16[48,5568]{1,0:T(8,128)(2,1)S(1)}, bf16[48,5568]{1,0:T(8,128)(2,1)S(1)}) custom-call(bf16[384,512]{1,0:T(8,128)(2,1)S(1)} %get-tuple-element.97.t_ref.x_ref, bf16[384,512]{1,0:T(8,128)(2,1)S(1)} %get-tuple-element.90.o_ref.x_ref, bf16[2752,512]{1,0:T(8,128)(2,1)S(1)} %bitcast.81, ...), custom_call_target="tpu_custom_call" | custom-call | tf_op jit(solution)/shard_map/forward_mine/pallas_call | solution.py:46
  29.3 1.6 %forward_up.1 = (f32[192,3136]{1,0:T(8,128)S(1)}, bf16[192,3136]{1,0:T(8,128)(2,1)S(1)}) custom-call(bf16[384,512]{1,0:T(8,128)(2,1)S(1)} %get-tuple-element.97.t_ref.x_ref, bf16[384,512]{1,0:T(8,128)(2,1)S(1)} %get-tuple-element.90.o_ref.x_ref, bf16[384,512]{1,0:T(8,128)(2,1)S(1)} %convolution_convert_fusion.l_ref, bf16[2752,512]{1,0:T(8,128)(2,1)S(1)} %bitcast.87), custom_call_target="tpu_custom_call" | custom-call | tf_op jit(solution)/shard_map/forward_up/pallas_call | solution.py:46
  31.6 1.6 %collective-permute-start.12 = (bf16[4,8,8448]{2,1,0:T(8,128)(2,1)S(1)}, bf16[4,8,8448]{2,1,0:T(8,128)(2,1)S(1)}, u32[]{:S(2)}, u32[]{:S(2)}) collective-permute-start(bf16[4,8,8448]{2,1,0:T(8,128)(2,1)S(1)} %get-tuple-element.149), channel_id=1, source_target_pairs={{0,16},{8,24},{16,0},{24,8},{32,48},{40,56},{48,32},{56,40},{64,80... | collective-permute-start | bytes 1622024 | tf_op jit(solution)/shard_map/ppermute | solution.py:272
  33.1 1.0 fusion.43.i_ref
  34.2 1.5 %collective-permute-start.2 = (bf16[48,5568]{1,0:T(8,128)(2,1)S(1)}, bf16[48,5568]{1,0:T(8,128)(2,1)S(1)}, u32[]{:S(2)}, u32[]{:S(2)}) collective-permute-start(bf16[48,5568]{1,0:T(8,128)(2,1)S(1)} %get-tuple-element.94), channel_id=1, source_target_pairs={{0,32},{8,40},{16,48},{24,56},{32,64},{40,72},{48,80},{56,88},{64,... | collective-permute-start | bytes 1603592 | tf_op jit(solution)/shard_map/ppermute | solution.py:272
  35.7 1.8 %collective-permute-start.3 = (bf16[48,5568]{1,0:T(8,128)(2,1)S(1)}, bf16[48,5568]{1,0:T(8,128)(2,1)S(1)}, u32[]{:S(2)}, u32[]{:S(2)}) collective-permute-start(bf16[48,5568]{1,0:T(8,128)(2,1)S(1)} %get-tuple-element.95), channel_id=1, source_target_pairs={{0,96},{8,104},{16,112},{24,120},{32,0},{40,8},{48,16},{56,24},{64... | collective-permute-start | bytes 1603592 | tf_op jit(solution)/shard_map/ppermute | solution.py:272
  37.5 1.0 collective-permute-start.4
  38.5 7.4 %collective-permute-done.12 = bf16[4,8,8448]{2,1,0:T(8,128)(2,1)S(1)} collective-permute-done((bf16[4,8,8448]{2,1,0:T(8,128)(2,1)S(1)}, bf16[4,8,8448]{2,1,0:T(8,128)(2,1)S(1)}, u32[]{:S(2)}, u32[]{:S(2)}) %collective-permute-start.12) | collective-permute-done | bytes 540704 | tf_op jit(solution)/shard_map/ppermute | solution.py:272
  46.3 1.6 %collective-permute-start.13 = (bf16[4,24,3136]{2,1,0:T(8,128)(2,1)S(1)}, bf16[4,24,3136]{2,1,0:T(8,128)(2,1)S(1)}, u32[]{:S(2)}, u32[]{:S(2)}) collective-permute-start(bf16[4,24,3136]{2,1,0:T(8,128)(2,1)S(1)} %fusion.1), channel_id=1, source_target_pairs={{0,16},{8,24},{16,0},{24,8},{32,48},{40,56},{48,32},{56,40},{64,80... | collective-permute-start | bytes 1806344 | tf_op jit(solution)/shard_map/ppermute | solution.py:272
  48.3 3.2 %collective-permute-done.2 = bf16[48,5568]{1,0:T(8,128)(2,1)S(1)} collective-permute-done((bf16[48,5568]{1,0:T(8,128)(2,1)S(1)}, bf16[48,5568]{1,0:T(8,128)(2,1)S(1)}, u32[]{:S(2)}, u32[]{:S(2)}) %collective-permute-start.2) | collective-permute-done | bytes 534560 | tf_op jit(solution)/shard_map/ppermute | solution.py:272
  51.5 8.8 %collective-permute-done.3 = bf16[48,5568]{1,0:T(8,128)(2,1)S(1)} collective-permute-done((bf16[48,5568]{1,0:T(8,128)(2,1)S(1)}, bf16[48,5568]{1,0:T(8,128)(2,1)S(1)}, u32[]{:S(2)}, u32[]{:S(2)}) %collective-permute-start.3) | collective-permute-done | bytes 534560 | tf_op jit(solution)/shard_map/ppermute | solution.py:272
  61.5 1.3 collective-permute-start.17
  62.9 2.5 %collective-permute-start.16 = (bf16[24,3136]{1,0:T(8,128)(2,1)S(1)}, bf16[24,3136]{1,0:T(8,128)(2,1)S(1)}, u32[]{:S(2)}, u32[]{:S(2)}) collective-permute-start(bf16[24,3136]{1,0:T(8,128)(2,1)S(1)} %get-tuple-element.140), channel_id=1, source_target_pairs={{0,96},{8,104},{16,112},{24,120},{32,0},{40,8},{48,16},{56,24},{64... | collective-permute-start | bytes 451592 | tf_op jit(solution)/shard_map/ppermute | solution.py:272
  65.6 1.6 %collective-permute-start.14 = (bf16[24,5568]{1,0:T(8,128)(2,1)S(1)}, bf16[24,5568]{1,0:T(8,128)(2,1)S(1)}, u32[]{:S(2)}, u32[]{:S(2)}) collective-permute-start(bf16[24,5568]{1,0:T(8,128)(2,1)S(1)} %slice.176), channel_id=1, source_target_pairs={{0,16},{8,24},{16,0},{24,8},{32,48},{40,56},{48,32},{56,40},{64,80... | collective-permute-start | bytes 801800 | tf_op jit(solution)/shard_map/ppermute | solution.py:272
  67.2 1.8 %collective-permute-done.17.c_ref = bf16[24,3136]{1,0:T(8,128)(2,1)S(1)} collective-permute-done((bf16[24,3136]{1,0:T(8,128)(2,1)S(1)}, bf16[24,3136]{1,0:T(8,128)(2,1)S(1)}, u32[]{:S(2)}, u32[]{:S(2)}) %collective-permute-start.17) | collective-permute-done | bytes 150560 | tf_op jit(solution)/shard_map/ppermute | solution.py:272
  69.0 1.2 collective-permute-done.16.b_ref
  70.2 1.5 %collective-permute-done.15.a_ref = bf16[24,3136]{1,0:T(8,128)(2,1)S(1)} collective-permute-done((bf16[24,3136]{1,0:T(8,128)(2,1)S(1)}, bf16[24,3136]{1,0:T(8,128)(2,1)S(1)}, u32[]{:S(2)}, u32[]{:S(2)}) %collective-permute-start.15) | collective-permute-done | bytes 150560 | tf_op jit(solution)/shard_map/ppermute | solution.py:272
  72.8 1.6 %collective-permute-start.19 = (bf16[24,5568]{1,0:T(8,128)(2,1)S(1)}, bf16[24,5568]{1,0:T(8,128)(2,1)S(1)}, u32[]{:S(2)}, u32[]{:S(2)}) collective-permute-start(bf16[24,5568]{1,0:T(8,128)(2,1)S(1)} %get-tuple-element.112), channel_id=1, source_target_pairs={{0,16},{8,24},{16,0},{24,8},{32,48},{40,56},{48,32},{56,40},{64,80... | collective-permute-start | bytes 801800 | tf_op jit(solution)/shard_map/ppermute | solution.py:272
  74.3 1.2 collective-permute-start.22
  75.6 3.7 %collective-permute-start.21 = (bf16[24,2752]{1,0:T(8,128)(2,1)S(1)}, bf16[24,2752]{1,0:T(8,128)(2,1)S(1)}, u32[]{:S(2)}, u32[]{:S(2)}) collective-permute-start(bf16[24,2752]{1,0:T(8,128)(2,1)S(1)} %get-tuple-element.111), channel_id=1, source_target_pairs={{0,64},{8,72},{16,80},{24,88},{32,96},{40,104},{48,112},{56,120},{... | collective-permute-start | bytes 396296 | tf_op jit(solution)/shard_map/ppermute | solution.py:272
  79.3 1.5 %collective-permute-done.22 = bf16[24,2752]{1,0:T(8,128)(2,1)S(1)} collective-permute-done((bf16[24,2752]{1,0:T(8,128)(2,1)S(1)}, bf16[24,2752]{1,0:T(8,128)(2,1)S(1)}, u32[]{:S(2)}, u32[]{:S(2)}) %collective-permute-start.22) | collective-permute-done | bytes 132128 | tf_op jit(solution)/shard_map/ppermute | solution.py:272
  80.8 3.0 %collective-permute-done.21 = bf16[24,2752]{1,0:T(8,128)(2,1)S(1)} collective-permute-done((bf16[24,2752]{1,0:T(8,128)(2,1)S(1)}, bf16[24,2752]{1,0:T(8,128)(2,1)S(1)}, u32[]{:S(2)}, u32[]{:S(2)}) %collective-permute-start.21) | collective-permute-done | bytes 132128 | tf_op jit(solution)/shard_map/ppermute | solution.py:272
  83.8 1.1 collective-permute-done.20
  85.0 2.4 %collective-permute-start.25 = (bf16[2,24,5568]{2,1,0:T(8,128)(2,1)S(1)}, bf16[2,24,5568]{2,1,0:T(8,128)(2,1)S(1)}, u32[]{:S(2)}, u32[]{:S(2)}) collective-permute-start(bf16[2,24,5568]{2,1,0:T(8,128)(2,1)S(1)} %get-tuple-element.145), channel_id=1, source_target_pairs={{0,64},{8,72},{16,80},{24,88},{32,96},{40,104},{48,112},{56,120},{... | collective-permute-start | bytes 1603592 | tf_op jit(solution)/shard_map/ppermute | solution.py:272
  87.4 2.5 %collective-permute-start.24 = (bf16[2,24,5568]{2,1,0:T(8,128)(2,1)S(1)}, bf16[2,24,5568]{2,1,0:T(8,128)(2,1)S(1)}, u32[]{:S(2)}, u32[]{:S(2)}) collective-permute-start(bf16[2,24,5568]{2,1,0:T(8,128)(2,1)S(1)} %get-tuple-element.145), channel_id=1, source_target_pairs={{0,96},{8,104},{16,112},{24,120},{32,0},{40,8},{48,16},{56,24},{64... | collective-permute-start | bytes 1603592 | tf_op jit(solution)/shard_map/ppermute | solution.py:272
  90.7 8.8 %collective-permute-done.23 = bf16[4,24,2752]{2,1,0:T(8,128)(2,1)S(1)} collective-permute-done((bf16[4,24,2752]{2,1,0:T(8,128)(2,1)S(1)}, bf16[4,24,2752]{2,1,0:T(8,128)(2,1)S(1)}, u32[]{:S(2)}, u32[]{:S(2)}) %collective-permute-start.23) | collective-permute-done | bytes 528416 | tf_op jit(solution)/shard_map/ppermute | solution.py:272
  99.5 7.7 %collective-permute-done.26 = bf16[2,24,5568]{2,1,0:T(8,128)(2,1)S(1)} collective-permute-done((bf16[2,24,5568]{2,1,0:T(8,128)(2,1)S(1)}, bf16[2,24,5568]{2,1,0:T(8,128)(2,1)S(1)}, u32[]{:S(2)}, u32[]{:S(2)}) %collective-permute-start.26) | collective-permute-done | bytes 534560 | tf_op jit(solution)/shard_map/ppermute | solution.py:272
  108.0 2.4 %collective-permute-done.27.o_ref = bf16[192,2752]{1,0:T(8,128)(2,1)S(1)} collective-permute-done((bf16[192,2752]{1,0:T(8,128)(2,1)S(1)}, bf16[192,2752]{1,0:T(8,128)(2,1)S(1)}, u32[]{:S(2)}, u32[]{:S(2)}) %collective-permute-start.27) | collective-permute-done | bytes 1056800 | tf_op jit(solution)/shard_map/ppermute | solution.py:272
  110.6 4.2 %backward_hidden.1 = (bf16[384,512]{1,0:T(8,128)(2,1)S(1)}, bf16[2752,512]{1,0:T(8,128)(2,1)}) custom-call(bf16[192,2752]{1,0:T(8,128)(2,1)S(1)} %bitcast.90, bf16[192,2752]{1,0:T(8,128)(2,1)S(1)} %collective-permute-done.27.o_ref, bf16[384,512]{1,0:T(8,128)(2,1)S(1)} %get-tuple-element.90.o_ref.x_ref, bf16[64,8448]{1,0:T(8,128)(2,1)S(1)} %bitcast.85, ...), custom_call_target="tpu_custom_call" | custom-call | tf_op jit(solution)/shard_map/backward_hidden/pallas_call | solution.py:46
  114.8 3.0 %collective-permute-start.29 = (bf16[4,48,512]{2,1,0:T(8,128)(2,1)S(1)}, bf16[4,48,512]{2,1,0:T(8,128)(2,1)S(1)}, u32[]{:S(2)}, u32[]{:S(2)}) collective-permute-start(bf16[4,48,512]{2,1,0:T(8,128)(2,1)S(1)} %bitcast.108), channel_id=1, source_target_pairs={{0,4},{1,5},{2,6},{3,7},{4,0},{5,1},{6,2},{7,3},{8,12},{9,13},{10,... | collective-permute-start | bytes 589832 | tf_op jit(solution)/shard_map/ppermute | solution.py:280
  117.9 4.5 %backward_pair.1 = bf16[384,512]{1,0:T(8,128)(2,1)S(1)} custom-call(bf16[192,5568]{1,0:T(8,128)(2,1)S(1)} %bitcast.74, bf16[192,5568]{1,0:T(8,128)(2,1)S(1)} %collective-permute-done.28.o_ref, bf16[64,8448]{1,0:T(8,128)(2,1)S(1)} %bitcast.86, bf16[64,8448]{1,0:T(8,128)(2,1)S(1)} %collective-permute-done.18.far_ref, ...), custom_call_target="tpu_custom_call" | custom-call | tf_op jit(solution)/shard_map/backward_pair/pallas_call | solution.py:46
  123.3 2.5 %weight_grad.2 = bf16[2752,512]{1,0:T(8,128)(2,1)} custom-call(bf16[192,5568]{1,0:T(8,128)(2,1)S(1)} %bitcast.75, bf16[192,5568]{1,0:T(8,128)(2,1)S(1)} %collective-permute-done.28.o_ref, bf16[384,512]{1,0:T(8,128)(2,1)S(1)} %get-tuple-element.97.t_ref.x_ref), custom_call_target="tpu_custom_call" | custom-call | tf_op jit(solution)/shard_map/weight_grad/pallas_call | solution.py:46
  125.8 5.0 %collective-permute-done.30 = bf16[4,48,512]{2,1,0:T(8,128)(2,1)S(1)} collective-permute-done((bf16[4,48,512]{2,1,0:T(8,128)(2,1)S(1)}, bf16[4,48,512]{2,1,0:T(8,128)(2,1)S(1)}, u32[]{:S(2)}, u32[]{:S(2)}) %collective-permute-start.30) | collective-permute-done | bytes 196640 | tf_op jit(solution)/shard_map/ppermute | solution.py:280
  131.0 1.2 collective-permute-start.31
  132.1 2.2 %collective-permute-start.32 = (bf16[2,48,512]{2,1,0:T(8,128)(2,1)S(1)}, bf16[2,48,512]{2,1,0:T(8,128)(2,1)S(1)}, u32[]{:S(2)}, u32[]{:S(2)}) collective-permute-start(bf16[2,48,512]{2,1,0:T(8,128)(2,1)S(1)} %get-tuple-element.132), channel_id=1, source_target_pairs={{0,3},{1,0},{2,1},{3,2},{4,7},{5,4},{6,5},{7,6},{8,11},{9,8},{10,9... | collective-permute-start | bytes 294920 | tf_op jit(solution)/shard_map/ppermute | solution.py:280
  134.3 1.3 collective-permute-start.33
  135.6 2.5 %weight_grad.3 = bf16[2752,512]{1,0:T(8,128)(2,1)} custom-call(bf16[192,5568]{1,0:T(8,128)(2,1)S(1)} %bitcast.76, bf16[192,5568]{1,0:T(8,128)(2,1)S(1)} %collective-permute-done.28.o_ref, bf16[384,512]{1,0:T(8,128)(2,1)S(1)} %get-tuple-element.97.t_ref.x_ref), custom_call_target="tpu_custom_call" | custom-call | tf_op jit(solution)/shard_map/weight_grad/pallas_call | solution.py:46
  138.0 2.4 %collective-permute-done.33 = bf16[2,48,512]{2,1,0:T(8,128)(2,1)S(1)} collective-permute-done((bf16[2,48,512]{2,1,0:T(8,128)(2,1)S(1)}, bf16[2,48,512]{2,1,0:T(8,128)(2,1)S(1)}, u32[]{:S(2)}, u32[]{:S(2)}) %collective-permute-start.33) | collective-permute-done | bytes 98336 | tf_op jit(solution)/shard_map/ppermute | solution.py:280
  (79 shorter events, 11.1 us)
Async XLA Ops:
  0.6 6.5 %copy-start.6 = (bf16[384,512]{1,0:T(8,128)(2,1)S(1)}, bf16[384,512]{1,0:T(8,128)(2,1)}, u32[]{:S(2)}) copy-start(bf16[384,512]{1,0:T(8,128)(2,1)} %g_ref) | copy-start | bytes 1179652
  0.6 6.5 %copy-start.5 = (bf16[384,512]{1,0:T(8,128)(2,1)S(1)}, bf16[384,512]{1,0:T(8,128)(2,1)}, u32[]{:S(2)}) copy-start(bf16[384,512]{1,0:T(8,128)(2,1)} %t_ref) | copy-start | bytes 1179652
  1.5 5.6 %collective-permute-start = (bf16[48,512]{1,0:T(8,128)(2,1)S(1)}, bf16[48,512]{1,0:T(8,128)(2,1)S(1)}, u32[]{:S(2)}, u32[]{:S(2)}) collective-permute-start(bf16[48,512]{1,0:T(8,128)(2,1)S(1)} %pad_maximum_fusion.11), channel_id=1, source_target_pairs={{0,4},{1,5},{2,6},{3,7},{4,0},{5,1},{6,2},{7,3},{8,12},{9,13},{10,... | collective-permute-start | bytes 147464 | tf_op jit(solution)/shard_map/ppermute | solution.py:280
  7.1 1.8 %copy-start = (bf16[512,2752]{0,1:T(8,128)(2,1)S(1)}, bf16[512,2752]{0,1:T(8,128)(2,1)}, u32[]{:S(2)}) copy-start(bf16[512,2752]{0,1:T(8,128)(2,1)} %param.15) | copy-start | bytes 8454148
  8.9 1.8 %copy-start.2 = (bf16[512,2752]{0,1:T(8,128)(2,1)S(1)}, bf16[512,2752]{0,1:T(8,128)(2,1)}, u32[]{:S(2)}) copy-start(bf16[512,2752]{0,1:T(8,128)(2,1)} %param.13) | copy-start | bytes 8454148
  10.7 16.6 %copy-start.1 = (bf16[512,2752]{0,1:T(8,128)(2,1)S(1)}, bf16[512,2752]{0,1:T(8,128)(2,1)}, u32[]{:S(2)}) copy-start(bf16[512,2752]{0,1:T(8,128)(2,1)} %param.15) | copy-start | bytes 8454148
  13.3 14.1 %collective-permute-start.1 = (bf16[192,5568]{1,0:T(8,128)(2,1)S(1)}, bf16[192,5568]{1,0:T(8,128)(2,1)S(1)}, u32[]{:S(2)}, u32[]{:S(2)}) collective-permute-start(bf16[192,5568]{1,0:T(8,128)(2,1)S(1)} %get-tuple-element.91), channel_id=1, source_target_pairs={{0,8},{8,0},{16,24},{24,16},{32,40},{40,32},{48,56},{56,48},{64,72... | collective-permute-start | bytes 6414344 | tf_op jit(solution)/shard_map/ppermute | solution.py:272
  13.4 8.5 %collective-permute-start.6 = (bf16[2,48,512]{2,1,0:T(8,128)(2,1)S(1)}, bf16[2,48,512]{2,1,0:T(8,128)(2,1)S(1)}, u32[]{:S(2)}, u32[]{:S(2)}) collective-permute-start(bf16[2,48,512]{2,1,0:T(8,128)(2,1)S(1)} %get-tuple-element.163), channel_id=1, source_target_pairs={{0,2},{1,3},{2,0},{3,1},{4,6},{5,7},{6,4},{7,5},{8,10},{9,11},{10,... | collective-permute-start | bytes 294920 | tf_op jit(solution)/shard_map/ppermute | solution.py:280
  16.7 8.7 %collective-permute-start.5 = (bf16[2,48,512]{2,1,0:T(8,128)(2,1)S(1)}, bf16[2,48,512]{2,1,0:T(8,128)(2,1)S(1)}, u32[]{:S(2)}, u32[]{:S(2)}) collective-permute-start(bf16[2,48,512]{2,1,0:T(8,128)(2,1)S(1)} %get-tuple-element.163), channel_id=1, source_target_pairs={{0,1},{1,2},{2,3},{3,0},{4,5},{5,6},{6,7},{7,4},{8,9},{9,10},{10,1... | collective-permute-start | bytes 294920 | tf_op jit(solution)/shard_map/ppermute | solution.py:280
  17.4 9.5 %collective-permute-start.7 = (bf16[2,48,512]{2,1,0:T(8,128)(2,1)S(1)}, bf16[2,48,512]{2,1,0:T(8,128)(2,1)S(1)}, u32[]{:S(2)}, u32[]{:S(2)}) collective-permute-start(bf16[2,48,512]{2,1,0:T(8,128)(2,1)S(1)} %get-tuple-element.163), channel_id=1, source_target_pairs={{0,3},{1,0},{2,1},{3,2},{4,7},{5,4},{6,5},{7,6},{8,11},{9,8},{10,9... | collective-permute-start | bytes 294920 | tf_op jit(solution)/shard_map/ppermute | solution.py:280
  20.0 11.1 %collective-permute-start.11 = (bf16[8,8448]{1,0:T(8,128)(2,1)S(1)}, bf16[8,8448]{1,0:T(8,128)(2,1)S(1)}, u32[]{:S(2)}, u32[]{:S(2)}) collective-permute-start(bf16[8,8448]{1,0:T(8,128)(2,1)S(1)} %concatenate.6), channel_id=1, source_target_pairs={{0,32},{8,40},{16,48},{24,56},{32,64},{40,72},{48,80},{56,88},{64,... | collective-permute-start | bytes 405512 | tf_op jit(solution)/shard_map/ppermute | solution.py:272
  21.9 9.6 %collective-permute-start.10 = (bf16[8,8448]{1,0:T(8,128)(2,1)S(1)}, bf16[8,8448]{1,0:T(8,128)(2,1)S(1)}, u32[]{:S(2)}, u32[]{:S(2)}) collective-permute-start(bf16[8,8448]{1,0:T(8,128)(2,1)S(1)} %concatenate.6), channel_id=1, source_target_pairs={{0,64},{8,72},{16,80},{24,88},{32,96},{40,104},{48,112},{56,120},{... | collective-permute-start | bytes 405512 | tf_op jit(solution)/shard_map/ppermute | solution.py:272
  25.5 6.0 %collective-permute-start.9 = (bf16[8,8448]{1,0:T(8,128)(2,1)S(1)}, bf16[8,8448]{1,0:T(8,128)(2,1)S(1)}, u32[]{:S(2)}, u32[]{:S(2)}) collective-permute-start(bf16[8,8448]{1,0:T(8,128)(2,1)S(1)} %concatenate.6), channel_id=1, source_target_pairs={{0,96},{8,104},{16,112},{24,120},{32,0},{40,8},{48,16},{56,24},{64... | collective-permute-start | bytes 405512 | tf_op jit(solution)/shard_map/ppermute | solution.py:272
  27.3 2.0 %copy-start.4 = (bf16[512,2752]{0,1:T(8,128)(2,1)S(1)}, bf16[512,2752]{0,1:T(8,128)(2,1)}, u32[]{:S(2)}) copy-start(bf16[512,2752]{0,1:T(8,128)(2,1)} %param.14) | copy-start | bytes 8454148
  30.9 15.0 %collective-permute-start.8 = (bf16[192,3136]{1,0:T(8,128)(2,1)S(1)}, bf16[192,3136]{1,0:T(8,128)(2,1)S(1)}, u32[]{:S(2)}, u32[]{:S(2)}) collective-permute-start(bf16[192,3136]{1,0:T(8,128)(2,1)S(1)} %get-tuple-element.102), channel_id=1, source_target_pairs={{0,8},{8,0},{16,24},{24,16},{32,40},{40,32},{48,56},{56,48},{64,72... | collective-permute-start | bytes 3612680 | tf_op jit(solution)/shard_map/ppermute | solution.py:272
  31.6 14.3 %collective-permute-start.12 = (bf16[4,8,8448]{2,1,0:T(8,128)(2,1)S(1)}, bf16[4,8,8448]{2,1,0:T(8,128)(2,1)S(1)}, u32[]{:S(2)}, u32[]{:S(2)}) collective-permute-start(bf16[4,8,8448]{2,1,0:T(8,128)(2,1)S(1)} %get-tuple-element.149), channel_id=1, source_target_pairs={{0,16},{8,24},{16,0},{24,8},{32,48},{40,56},{48,32},{56,40},{64,80... | collective-permute-start | bytes 1622024 | tf_op jit(solution)/shard_map/ppermute | solution.py:272
  34.2 17.3 %collective-permute-start.2 = (bf16[48,5568]{1,0:T(8,128)(2,1)S(1)}, bf16[48,5568]{1,0:T(8,128)(2,1)S(1)}, u32[]{:S(2)}, u32[]{:S(2)}) collective-permute-start(bf16[48,5568]{1,0:T(8,128)(2,1)S(1)} %get-tuple-element.94), channel_id=1, source_target_pairs={{0,32},{8,40},{16,48},{24,56},{32,64},{40,72},{48,80},{56,88},{64,... | collective-permute-start | bytes 1603592 | tf_op jit(solution)/shard_map/ppermute | solution.py:272
  35.7 24.6 %collective-permute-start.3 = (bf16[48,5568]{1,0:T(8,128)(2,1)S(1)}, bf16[48,5568]{1,0:T(8,128)(2,1)S(1)}, u32[]{:S(2)}, u32[]{:S(2)}) collective-permute-start(bf16[48,5568]{1,0:T(8,128)(2,1)S(1)} %get-tuple-element.95), channel_id=1, source_target_pairs={{0,96},{8,104},{16,112},{24,120},{32,0},{40,8},{48,16},{56,24},{64... | collective-permute-start | bytes 1603592 | tf_op jit(solution)/shard_map/ppermute | solution.py:272
  37.5 23.5 %collective-permute-start.4 = (bf16[48,5568]{1,0:T(8,128)(2,1)S(1)}, bf16[48,5568]{1,0:T(8,128)(2,1)S(1)}, u32[]{:S(2)}, u32[]{:S(2)}) collective-permute-start(bf16[48,5568]{1,0:T(8,128)(2,1)S(1)} %get-tuple-element.96), channel_id=1, source_target_pairs={{0,64},{8,72},{16,80},{24,88},{32,96},{40,104},{48,112},{56,120},{... | collective-permute-start | bytes 1603592 | tf_op jit(solution)/shard_map/ppermute | solution.py:272
  46.3 15.1 %collective-permute-start.13 = (bf16[4,24,3136]{2,1,0:T(8,128)(2,1)S(1)}, bf16[4,24,3136]{2,1,0:T(8,128)(2,1)S(1)}, u32[]{:S(2)}, u32[]{:S(2)}) collective-permute-start(bf16[4,24,3136]{2,1,0:T(8,128)(2,1)S(1)} %fusion.1), channel_id=1, source_target_pairs={{0,16},{8,24},{16,0},{24,8},{32,48},{40,56},{48,32},{56,40},{64,80... | collective-permute-start | bytes 1806344 | tf_op jit(solution)/shard_map/ppermute | solution.py:272
  48.0 24.1 %collective-permute-start.18 = (bf16[64,8448]{1,0:T(8,128)(2,1)S(1)}, bf16[64,8448]{1,0:T(8,128)(2,1)S(1)}, u32[]{:S(2)}, u32[]{:S(2)}) collective-permute-start(bf16[64,8448]{1,0:T(8,128)(2,1)S(1)} %bitcast.83), channel_id=1, source_target_pairs={{0,8},{8,0},{16,24},{24,16},{32,40},{40,32},{48,56},{56,48},{64,72... | collective-permute-start | bytes 3244040 | tf_op jit(solution)/shard_map/ppermute | solution.py:272
  61.5 7.5 %collective-permute-start.17 = (bf16[24,3136]{1,0:T(8,128)(2,1)S(1)}, bf16[24,3136]{1,0:T(8,128)(2,1)S(1)}, u32[]{:S(2)}, u32[]{:S(2)}) collective-permute-start(bf16[24,3136]{1,0:T(8,128)(2,1)S(1)} %get-tuple-element.139), channel_id=1, source_target_pairs={{0,64},{8,72},{16,80},{24,88},{32,96},{40,104},{48,112},{56,120},{... | collective-permute-start | bytes 451592 | tf_op jit(solution)/shard_map/ppermute | solution.py:272
  62.9 7.3 %collective-permute-start.16 = (bf16[24,3136]{1,0:T(8,128)(2,1)S(1)}, bf16[24,3136]{1,0:T(8,128)(2,1)S(1)}, u32[]{:S(2)}, u32[]{:S(2)}) collective-permute-start(bf16[24,3136]{1,0:T(8,128)(2,1)S(1)} %get-tuple-element.140), channel_id=1, source_target_pairs={{0,96},{8,104},{16,112},{24,120},{32,0},{40,8},{48,16},{56,24},{64... | collective-permute-start | bytes 451592 | tf_op jit(solution)/shard_map/ppermute | solution.py:272
  65.3 6.4 %collective-permute-start.15 = (bf16[24,3136]{1,0:T(8,128)(2,1)S(1)}, bf16[24,3136]{1,0:T(8,128)(2,1)S(1)}, u32[]{:S(2)}, u32[]{:S(2)}) collective-permute-start(bf16[24,3136]{1,0:T(8,128)(2,1)S(1)} %get-tuple-element.141), channel_id=1, source_target_pairs={{0,32},{8,40},{16,48},{24,56},{32,64},{40,72},{48,80},{56,88},{64,... | collective-permute-start | bytes 451592 | tf_op jit(solution)/shard_map/ppermute | solution.py:272
  65.6 6.5 %collective-permute-start.14 = (bf16[24,5568]{1,0:T(8,128)(2,1)S(1)}, bf16[24,5568]{1,0:T(8,128)(2,1)S(1)}, u32[]{:S(2)}, u32[]{:S(2)}) collective-permute-start(bf16[24,5568]{1,0:T(8,128)(2,1)S(1)} %slice.176), channel_id=1, source_target_pairs={{0,16},{8,24},{16,0},{24,8},{32,48},{40,56},{48,32},{56,40},{64,80... | collective-permute-start | bytes 801800 | tf_op jit(solution)/shard_map/ppermute | solution.py:272
  72.8 12.1 %collective-permute-start.19 = (bf16[24,5568]{1,0:T(8,128)(2,1)S(1)}, bf16[24,5568]{1,0:T(8,128)(2,1)S(1)}, u32[]{:S(2)}, u32[]{:S(2)}) collective-permute-start(bf16[24,5568]{1,0:T(8,128)(2,1)S(1)} %get-tuple-element.112), channel_id=1, source_target_pairs={{0,16},{8,24},{16,0},{24,8},{32,48},{40,56},{48,32},{56,40},{64,80... | collective-permute-start | bytes 801800 | tf_op jit(solution)/shard_map/ppermute | solution.py:272
  74.3 6.5 %collective-permute-start.22 = (bf16[24,2752]{1,0:T(8,128)(2,1)S(1)}, bf16[24,2752]{1,0:T(8,128)(2,1)S(1)}, u32[]{:S(2)}, u32[]{:S(2)}) collective-permute-start(bf16[24,2752]{1,0:T(8,128)(2,1)S(1)} %get-tuple-element.111), channel_id=1, source_target_pairs={{0,32},{8,40},{16,48},{24,56},{32,64},{40,72},{48,80},{56,88},{64,... | collective-permute-start | bytes 396296 | tf_op jit(solution)/shard_map/ppermute | solution.py:272
  75.6 8.2 %collective-permute-start.21 = (bf16[24,2752]{1,0:T(8,128)(2,1)S(1)}, bf16[24,2752]{1,0:T(8,128)(2,1)S(1)}, u32[]{:S(2)}, u32[]{:S(2)}) collective-permute-start(bf16[24,2752]{1,0:T(8,128)(2,1)S(1)} %get-tuple-element.111), channel_id=1, source_target_pairs={{0,64},{8,72},{16,80},{24,88},{32,96},{40,104},{48,112},{56,120},{... | collective-permute-start | bytes 396296 | tf_op jit(solution)/shard_map/ppermute | solution.py:272
  79.3 5.6 %collective-permute-start.20 = (bf16[24,2752]{1,0:T(8,128)(2,1)S(1)}, bf16[24,2752]{1,0:T(8,128)(2,1)S(1)}, u32[]{:S(2)}, u32[]{:S(2)}) collective-permute-start(bf16[24,2752]{1,0:T(8,128)(2,1)S(1)} %get-tuple-element.111), channel_id=1, source_target_pairs={{0,96},{8,104},{16,112},{24,120},{32,0},{40,8},{48,16},{56,24},{64... | collective-permute-start | bytes 396296 | tf_op jit(solution)/shard_map/ppermute | solution.py:272
  85.0 22.2 %collective-permute-start.26 = (bf16[2,24,5568]{2,1,0:T(8,128)(2,1)S(1)}, bf16[2,24,5568]{2,1,0:T(8,128)(2,1)S(1)}, u32[]{:S(2)}, u32[]{:S(2)}) collective-permute-start(bf16[2,24,5568]{2,1,0:T(8,128)(2,1)S(1)} %get-tuple-element.145), channel_id=1, source_target_pairs={{0,32},{8,40},{16,48},{24,56},{32,64},{40,72},{48,80},{56,88},{64,... | collective-permute-start | bytes 1603592 | tf_op jit(solution)/shard_map/ppermute | solution.py:272
  85.0 22.1 %collective-permute-start.25 = (bf16[2,24,5568]{2,1,0:T(8,128)(2,1)S(1)}, bf16[2,24,5568]{2,1,0:T(8,128)(2,1)S(1)}, u32[]{:S(2)}, u32[]{:S(2)}) collective-permute-start(bf16[2,24,5568]{2,1,0:T(8,128)(2,1)S(1)} %get-tuple-element.145), channel_id=1, source_target_pairs={{0,64},{8,72},{16,80},{24,88},{32,96},{40,104},{48,112},{56,120},{... | collective-permute-start | bytes 1603592 | tf_op jit(solution)/shard_map/ppermute | solution.py:272
  87.4 20.1 %collective-permute-start.24 = (bf16[2,24,5568]{2,1,0:T(8,128)(2,1)S(1)}, bf16[2,24,5568]{2,1,0:T(8,128)(2,1)S(1)}, u32[]{:S(2)}, u32[]{:S(2)}) collective-permute-start(bf16[2,24,5568]{2,1,0:T(8,128)(2,1)S(1)} %get-tuple-element.145), channel_id=1, source_target_pairs={{0,96},{8,104},{16,112},{24,120},{32,0},{40,8},{48,16},{56,24},{64... | collective-permute-start | bytes 1603592 | tf_op jit(solution)/shard_map/ppermute | solution.py:272
  90.1 9.4 %collective-permute-start.23 = (bf16[4,24,2752]{2,1,0:T(8,128)(2,1)S(1)}, bf16[4,24,2752]{2,1,0:T(8,128)(2,1)S(1)}, u32[]{:S(2)}, u32[]{:S(2)}) collective-permute-start(bf16[4,24,2752]{2,1,0:T(8,128)(2,1)S(1)} %get-tuple-element.147), channel_id=1, source_target_pairs={{0,16},{8,24},{16,0},{24,8},{32,48},{40,56},{48,32},{56,40},{64,80... | collective-permute-start | bytes 1585160 | tf_op jit(solution)/shard_map/ppermute | solution.py:272
  107.7 2.8 %collective-permute-start.27 = (bf16[192,2752]{1,0:T(8,128)(2,1)S(1)}, bf16[192,2752]{1,0:T(8,128)(2,1)S(1)}, u32[]{:S(2)}, u32[]{:S(2)}) collective-permute-start(bf16[192,2752]{1,0:T(8,128)(2,1)S(1)} %bitcast.89), channel_id=1, source_target_pairs={{0,8},{8,0},{16,24},{24,16},{32,40},{40,32},{48,56},{56,48},{64,72... | collective-permute-start | bytes 3170312 | tf_op jit(solution)/shard_map/ppermute | solution.py:272
  110.5 7.4 %collective-permute-start.28 = (bf16[192,5568]{1,0:T(8,128)(2,1)S(1)}, bf16[192,5568]{1,0:T(8,128)(2,1)S(1)}, u32[]{:S(2)}, u32[]{:S(2)}) collective-permute-start(bf16[192,5568]{1,0:T(8,128)(2,1)S(1)} %bitcast.73), channel_id=1, source_target_pairs={{0,8},{8,0},{16,24},{24,16},{32,40},{40,32},{48,56},{56,48},{64,72... | collective-permute-start | bytes 6414344 | tf_op jit(solution)/shard_map/ppermute | solution.py:272
  110.6 7.3 %copy-start.3 = (bf16[512,2752]{0,1:T(8,128)(2,1)S(1)}, bf16[512,2752]{0,1:T(8,128)(2,1)}, u32[]{:S(2)}) copy-start(bf16[512,2752]{0,1:T(8,128)(2,1)} %param.13) | copy-start | bytes 8454148
  114.8 10.9 %collective-permute-start.29 = (bf16[4,48,512]{2,1,0:T(8,128)(2,1)S(1)}, bf16[4,48,512]{2,1,0:T(8,128)(2,1)S(1)}, u32[]{:S(2)}, u32[]{:S(2)}) collective-permute-start(bf16[4,48,512]{2,1,0:T(8,128)(2,1)S(1)} %bitcast.108), channel_id=1, source_target_pairs={{0,4},{1,5},{2,6},{3,7},{4,0},{5,1},{6,2},{7,3},{8,12},{9,13},{10,... | collective-permute-start | bytes 589832 | tf_op jit(solution)/shard_map/ppermute | solution.py:280
  122.4 8.5 %collective-permute-start.30 = (bf16[4,48,512]{2,1,0:T(8,128)(2,1)S(1)}, bf16[4,48,512]{2,1,0:T(8,128)(2,1)S(1)}, u32[]{:S(2)}, u32[]{:S(2)}) collective-permute-start(bf16[4,48,512]{2,1,0:T(8,128)(2,1)S(1)} %bitcast.109), channel_id=1, source_target_pairs={{0,4},{1,5},{2,6},{3,7},{4,0},{5,1},{6,2},{7,3},{8,12},{9,13},{10,... | collective-permute-start | bytes 589832 | tf_op jit(solution)/shard_map/ppermute | solution.py:280
  131.0 7.0 %collective-permute-start.31 = (bf16[2,48,512]{2,1,0:T(8,128)(2,1)S(1)}, bf16[2,48,512]{2,1,0:T(8,128)(2,1)S(1)}, u32[]{:S(2)}, u32[]{:S(2)}) collective-permute-start(bf16[2,48,512]{2,1,0:T(8,128)(2,1)S(1)} %get-tuple-element.131), channel_id=1, source_target_pairs={{0,1},{1,2},{2,3},{3,0},{4,5},{5,6},{6,7},{7,4},{8,9},{9,10},{10,1... | collective-permute-start | bytes 294920 | tf_op jit(solution)/shard_map/ppermute | solution.py:280
  132.1 5.9 %collective-permute-start.32 = (bf16[2,48,512]{2,1,0:T(8,128)(2,1)S(1)}, bf16[2,48,512]{2,1,0:T(8,128)(2,1)S(1)}, u32[]{:S(2)}, u32[]{:S(2)}) collective-permute-start(bf16[2,48,512]{2,1,0:T(8,128)(2,1)S(1)} %get-tuple-element.132), channel_id=1, source_target_pairs={{0,3},{1,0},{2,1},{3,2},{4,7},{5,4},{6,5},{7,6},{8,11},{9,8},{10,9... | collective-permute-start | bytes 294920 | tf_op jit(solution)/shard_map/ppermute | solution.py:280
  134.3 6.1 %collective-permute-start.33 = (bf16[2,48,512]{2,1,0:T(8,128)(2,1)S(1)}, bf16[2,48,512]{2,1,0:T(8,128)(2,1)S(1)}, u32[]{:S(2)}, u32[]{:S(2)}) collective-permute-start(bf16[2,48,512]{2,1,0:T(8,128)(2,1)S(1)} %pad_maximum_fusion.10), channel_id=1, source_target_pairs={{0,2},{1,3},{2,0},{3,1},{4,6},{5,7},{6,4},{7,5},{8,10},{9,11},{10,... | collective-permute-start | bytes 294920 | tf_op jit(solution)/shard_map/ppermute | solution.py:280

commit v7 on v6

--- a/solution.py
+++ b/solution.py
@@ -282,6 +282,11 @@
 
 def z_send(blocks):
     return [row_send(blocks[d].astype(BF), d, 0, 0) for d in (1, 3, 2)]
+
+
+def swap(x, axis, bit):
+    step = 4 * bit if axis == "row" else bit
+    return lax.ppermute(x, axis, [(i, i ^ step) for i in range(16 if axis == "row" else 8)])
 
 
 def z_spread(x):
@@ -342,9 +347,12 @@
     leave = ((dc * 4 + dz) * 2 + da) * ROWS + dest % ROWS
     held, leave = held[:, None], leave[:, None]
     j = jnp.arange(RANK, dtype=jnp.int32)
-    sort = (j[:, None] == (owner(j // 8) * 8 + j % 8)[None, :]).astype(BF)
+    block = j // 8
+    dc, ez, da = block // 8, (block // 2) % 4, block % 2
+    source = (z ^ ez) * 4 + (a + da) % 2 * 2 + (c + dc) % 2
+    sort = (j[:, None] == (source * 8 + j % 8)[None, :]).astype(BF)
     my, mh, mt, mi = k // 96, (k // 48) % 2, (k // 16) % 3, k % 16
-    rank = (((h - mh) % 2) * 4 + (y - my) % 4) * 16 + mi + RANK * mt
+    rank = (((h - mh) % 2) * 4 + (y ^ my)) * 16 + mi + RANK * mt
     match = (rank[None, :] == k[:, None]).astype(BF)
 
     gate_w, up_w, down_w = gate_weight.T, up_weight.T, down_weight.T
@@ -357,16 +365,17 @@
     theirs, tok, out = forward_theirs(tokens, grad_out, held, gate_w, down_w)
     got = core_send(theirs)
     tok, rights = tie(tok, rights)
-    rights_z = z_spread(rights)
     lefts = jnp.stack([lefts, lefts_h])
-    lefts_y = [col_send(lefts, 0, d) for d in (1, 2, 3)]
-    rights = jnp.stack([rights] + rights_z)
+    lefts = jnp.stack([lefts, swap(lefts, "col", 1)])
+    rights = jnp.stack([rights, swap(rights, "row", 1)])
+    lefts = jnp.stack([lefts, swap(lefts, "col", 2)])
+    rights = jnp.stack([rights, swap(rights, "row", 2)]).reshape(4, *rights.shape[1:])
     rights_x = x_send(rights)
 
     pair, *sends = forward_mine(tok, out, gate_w, down_w, got)
     tok, pair = tie(tok, pair)
     pair_z = [row_send(sends[d - 1], d, 0, 0) for d in (1, 3, 2)]
-    lefts = jnp.stack([lefts] + lefts_y).reshape(SIZE, -1)
+    lefts = lefts.reshape(SIZE, -1)
     lefts = dot(match, lefts, NN).astype(BF)
     mine, theirs = forward_up(tok, out, lefts, up_w)
     got, rights_x = tie(core_send(theirs), rights_x)

time: 141 us -> 143 us (1.014)
  waiting for transfers between devices: 58.8 us -> 60.3 us
    ppermute x0 -> x4, starting transfers between devices: none -> 11 us  [swap(): lax.ppermute(x, axis, [(i, i ^ step) for i in range(16 if axis == 'row' e...]
    ppermute x25 -> x22, starting transfers between devices: 32.5 us -> 26.9 us  [row_send(): return lax.ppermute(x, 'row', pairs)]
    ppermute x9 -> x6, starting transfers between devices: 18.2 us -> 13.4 us  [col_send(): return lax.ppermute(x, 'col', pairs)]
    ppermute x0 -> x4, waiting for transfers between devices: none -> 3.55 us  [swap(): lax.ppermute(x, axis, [(i, i ^ step) for i in range(16 if axis == 'row' e...]
    ppermute x25 -> x22, waiting for transfers between devices: 50.6 us -> 49.1 us  [row_send(): return lax.ppermute(x, 'row', pairs)]
    ppermute x9 -> x6, waiting for transfers between devices: 8.15 us -> 7.6 us  [col_send(): return lax.ppermute(x, 'col', pairs)]
  transfers between devices with their start and end apart: 34 -> 32, of which waited for: 20 -> 22; matrix products, arithmetic and copies ran while one was open for 3% -> 3% of each run, Pallas kernels for 12% -> 12%
where the time goes in v7:
time: 143 us
  waiting for transfers between devices  60.3 us (42%)
  starting transfers between devices  51.3 us (36%)
  Pallas kernels  20.3 us (14%)
  other arithmetic  4.93 us (3%)
  local copies, waits for them, and re-layouts  4.86 us (3%)
    ppermute x22, waiting for transfers between devices, row_send(): return lax.ppermute(x, 'row', pairs)  49.1 us
    ppermute x22, starting transfers between devices, row_send(): return lax.ppermute(x, 'row', pairs)  26.9 us
    pallas_call x8, Pallas kernels, pallas(): pl.pallas_call(body, out_shape=outs, in_specs=in_specs, out_specs=out_spe...  20.3 us
    ppermute x6, starting transfers between devices, col_send(): return lax.ppermute(x, 'col', pairs)  13.4 us
    ppermute x4, starting transfers between devices, swap(): lax.ppermute(x, axis, [(i, i ^ step) for i in range(16 if axis == 'row' e...  11 us
    ppermute x6, waiting for transfers between devices, col_send(): return lax.ppermute(x, 'col', pairs)  7.6 us
    unnamed x14, local copies, waits for them, and re-layouts  3.61 us
    ppermute x4, waiting for transfers between devices, swap(): lax.ppermute(x, axis, [(i, i ^ step) for i in range(16 if axis == 'row' e...  3.55 us
  transfers between devices with their start and end apart: 32, of which 22 were waited for; matrix products, arithmetic and copies ran while one was open for 3% of the time, Pallas kernels for 12%

profile of v7, /device:TPU:0, one launch (start us, length us, event | category | flops | bytes accessed | tf_op | source)
XLA Modules:
  0.0 143.1 jit_solution(15299804172961278602)
XLA Ops:
  1.5 3.1 %collective-permute-start = (bf16[48,512]{1,0:T(8,128)(2,1)S(1)}, bf16[48,512]{1,0:T(8,128)(2,1)S(1)}, u32[]{:S(2)}, u32[]{:S(2)}) collective-permute-start(bf16[48,512]{1,0:T(8,128)(2,1)S(1)} %pad_maximum_fusion.13), channel_id=1, source_target_pairs={{0,4},{1,5},{2,6},{3,7},{4,0},{5,1},{6,2},{7,3},{8,12},{9,13},{10,... | collective-permute-start | bytes 147464 | tf_op jit(solution)/shard_map/ppermute | solution.py:280
  7.1 1.8 %copy-done = bf16[512,2752]{0,1:T(8,128)(2,1)S(1)} copy-done((bf16[512,2752]{0,1:T(8,128)(2,1)S(1)}, bf16[512,2752]{0,1:T(8,128)(2,1)}, u32[]{:S(2)}) %copy-start) | copy-done | bytes 2818072
  8.9 1.8 %copy-done.2 = bf16[512,2752]{0,1:T(8,128)(2,1)S(1)} copy-done((bf16[512,2752]{0,1:T(8,128)(2,1)S(1)}, bf16[512,2752]{0,1:T(8,128)(2,1)}, u32[]{:S(2)}) %copy-start.2) | copy-done | bytes 2818072
  10.7 2.5 %forward_theirs.1 = (bf16[192,5568]{1,0:T(8,128)(2,1)S(1)}, bf16[384,512]{1,0:T(8,128)(2,1)S(1)}, bf16[384,512]{1,0:T(8,128)(2,1)S(1)}) custom-call(bf16[384,512]{1,0:T(8,128)(2,1)S(1)} %copy-done.5, bf16[384,512]{1,0:T(8,128)(2,1)S(1)} %copy-done.6, s32[384,1]{1,0:T(8,128)S(1)} %fusion.22.i_ref, bf16[2752,512]{1,0:T(8,128)(2,1)S(1)} %bitcast.84, ...), custom_call_target="tpu_custom_call" | custom-call | tf_op jit(solution)/shard_map/forward_theirs/pallas_call | solution.py:46
  13.4 1.7 %collective-permute-start.5 = (bf16[2,48,512]{2,1,0:T(8,128)(2,1)S(1)}, bf16[2,48,512]{2,1,0:T(8,128)(2,1)S(1)}, u32[]{:S(2)}, u32[]{:S(2)}) collective-permute-start(bf16[2,48,512]{2,1,0:T(8,128)(2,1)S(1)} %get-tuple-element.165), channel_id=1, source_target_pairs={{0,1},{1,0},{2,3},{3,2},{4,5},{5,4},{6,7},{7,6},{8,9},{9,8},{10,11... | collective-permute-start | bytes 294920 | tf_op jit(solution)/shard_map/ppermute | solution.py:289
  15.1 1.9 %collective-permute-start.8 = (bf16[8,8448]{1,0:T(8,128)(2,1)S(1)}, bf16[8,8448]{1,0:T(8,128)(2,1)S(1)}, u32[]{:S(2)}, u32[]{:S(2)}) collective-permute-start(bf16[8,8448]{1,0:T(8,128)(2,1)S(1)} %concatenate.6), channel_id=1, source_target_pairs={{0,32},{8,40},{16,48},{24,56},{32,0},{40,8},{48,16},{56,24},{64,96... | collective-permute-start | bytes 405512 | tf_op jit(solution)/shard_map/ppermute | solution.py:289
  17.0 1.6 %collective-permute-done.5 = bf16[2,48,512]{2,1,0:T(8,128)(2,1)S(1)} collective-permute-done((bf16[2,48,512]{2,1,0:T(8,128)(2,1)S(1)}, bf16[2,48,512]{2,1,0:T(8,128)(2,1)S(1)}, u32[]{:S(2)}, u32[]{:S(2)}) %collective-permute-start.5) | collective-permute-done | bytes 98336 | tf_op jit(solution)/shard_map/ppermute | solution.py:289
  18.7 3.4 %collective-permute-start.6 = (bf16[2,2,48,512]{3,2,1,0:T(8,128)(2,1)S(1)}, bf16[2,2,48,512]{3,2,1,0:T(8,128)(2,1)S(1)}, u32[]{:S(2)}, u32[]{:S(2)}) collective-permute-start(bf16[2,2,48,512]{3,2,1,0:T(8,128)(2,1)S(1)} %get-tuple-element.163), channel_id=1, source_target_pairs={{0,2},{1,3},{2,0},{3,1},{4,6},{5,7},{6,4},{7,5},{8,10},{9,11},{10,... | collective-permute-start | bytes 589832 | tf_op jit(solution)/shard_map/ppermute | solution.py:289
  22.1 4.0 %collective-permute-start.9 = (bf16[2,8,8448]{2,1,0:T(8,128)(2,1)S(1)}, bf16[2,8,8448]{2,1,0:T(8,128)(2,1)S(1)}, u32[]{:S(2)}, u32[]{:S(2)}) collective-permute-start(bf16[2,8,8448]{2,1,0:T(8,128)(2,1)S(1)} %get-tuple-element.155), channel_id=1, source_target_pairs={{0,64},{8,72},{16,80},{24,88},{32,96},{40,104},{48,112},{56,120},{... | collective-permute-start | bytes 811016 | tf_op jit(solution)/shard_map/ppermute | solution.py:289
  27.3 2.0 %forward_mine.1 = (f32[48,5568]{1,0:T(8,128)S(1)}, bf16[48,5568]{1,0:T(8,128)(2,1)S(1)}, bf16[48,5568]{1,0:T(8,128)(2,1)S(1)}, bf16[48,5568]{1,0:T(8,128)(2,1)S(1)}) custom-call(bf16[384,512]{1,0:T(8,128)(2,1)S(1)} %get-tuple-element.97.t_ref.x_ref, bf16[384,512]{1,0:T(8,128)(2,1)S(1)} %get-tuple-element.90.o_ref.x_ref, bf16[2752,512]{1,0:T(8,128)(2,1)S(1)} %bitcast.85, ...), custom_call_target="tpu_custom_call" | custom-call | tf_op jit(solution)/shard_map/forward_mine/pallas_call | solution.py:46
  29.3 1.6 %forward_up.1 = (f32[192,3136]{1,0:T(8,128)S(1)}, bf16[192,3136]{1,0:T(8,128)(2,1)S(1)}) custom-call(bf16[384,512]{1,0:T(8,128)(2,1)S(1)} %get-tuple-element.97.t_ref.x_ref, bf16[384,512]{1,0:T(8,128)(2,1)S(1)} %get-tuple-element.90.o_ref.x_ref, bf16[384,512]{1,0:T(8,128)(2,1)S(1)} %convolution_convert_fusion.l_ref, bf16[2752,512]{1,0:T(8,128)(2,1)S(1)} %bitcast.91), custom_call_target="tpu_custom_call" | custom-call | tf_op jit(solution)/shard_map/forward_up/pallas_call | solution.py:46
  31.0 1.2 collective-permute-done.9
  32.2 1.6 %collective-permute-start.10 = (bf16[4,8,8448]{2,1,0:T(8,128)(2,1)S(1)}, bf16[4,8,8448]{2,1,0:T(8,128)(2,1)S(1)}, u32[]{:S(2)}, u32[]{:S(2)}) collective-permute-start(bf16[4,8,8448]{2,1,0:T(8,128)(2,1)S(1)} %bitcast.102), channel_id=1, source_target_pairs={{0,16},{8,24},{16,0},{24,8},{32,48},{40,56},{48,32},{56,40},{64,80... | collective-permute-start | bytes 1622024 | tf_op jit(solution)/shard_map/ppermute | solution.py:272
  34.8 1.3 collective-permute-start.2
  36.1 2.2 %collective-permute-start.3 = (bf16[48,5568]{1,0:T(8,128)(2,1)S(1)}, bf16[48,5568]{1,0:T(8,128)(2,1)S(1)}, u32[]{:S(2)}, u32[]{:S(2)}) collective-permute-start(bf16[48,5568]{1,0:T(8,128)(2,1)S(1)} %get-tuple-element.95), channel_id=1, source_target_pairs={{0,96},{8,104},{16,112},{24,120},{32,0},{40,8},{48,16},{56,24},{64... | collective-permute-start | bytes 1603592 | tf_op jit(solution)/shard_map/ppermute | solution.py:272
  38.3 1.8 %collective-permute-start.4 = (bf16[48,5568]{1,0:T(8,128)(2,1)S(1)}, bf16[48,5568]{1,0:T(8,128)(2,1)S(1)}, u32[]{:S(2)}, u32[]{:S(2)}) collective-permute-start(bf16[48,5568]{1,0:T(8,128)(2,1)S(1)} %get-tuple-element.96), channel_id=1, source_target_pairs={{0,64},{8,72},{16,80},{24,88},{32,96},{40,104},{48,112},{56,120},{... | collective-permute-start | bytes 1603592 | tf_op jit(solution)/shard_map/ppermute | solution.py:272
  40.1 5.7 %collective-permute-done.10 = bf16[4,8,8448]{2,1,0:T(8,128)(2,1)S(1)} collective-permute-done((bf16[4,8,8448]{2,1,0:T(8,128)(2,1)S(1)}, bf16[4,8,8448]{2,1,0:T(8,128)(2,1)S(1)}, u32[]{:S(2)}, u32[]{:S(2)}) %collective-permute-start.10) | collective-permute-done | bytes 540704 | tf_op jit(solution)/shard_map/ppermute | solution.py:272
  46.1 1.6 %collective-permute-start.11 = (bf16[4,24,3136]{2,1,0:T(8,128)(2,1)S(1)}, bf16[4,24,3136]{2,1,0:T(8,128)(2,1)S(1)}, u32[]{:S(2)}, u32[]{:S(2)}) collective-permute-start(bf16[4,24,3136]{2,1,0:T(8,128)(2,1)S(1)} %fusion.1), channel_id=1, source_target_pairs={{0,16},{8,24},{16,0},{24,8},{32,48},{40,56},{48,32},{56,40},{64,80... | collective-permute-start | bytes 1806344 | tf_op jit(solution)/shard_map/ppermute | solution.py:272
  47.9 2.6 %collective-permute-done.2 = bf16[48,5568]{1,0:T(8,128)(2,1)S(1)} collective-permute-done((bf16[48,5568]{1,0:T(8,128)(2,1)S(1)}, bf16[48,5568]{1,0:T(8,128)(2,1)S(1)}, u32[]{:S(2)}, u32[]{:S(2)}) %collective-permute-start.2) | collective-permute-done | bytes 534560 | tf_op jit(solution)/shard_map/ppermute | solution.py:272
  50.5 10.9 %collective-permute-done.3 = bf16[48,5568]{1,0:T(8,128)(2,1)S(1)} collective-permute-done((bf16[48,5568]{1,0:T(8,128)(2,1)S(1)}, bf16[48,5568]{1,0:T(8,128)(2,1)S(1)}, u32[]{:S(2)}, u32[]{:S(2)}) %collective-permute-start.3) | collective-permute-done | bytes 534560 | tf_op jit(solution)/shard_map/ppermute | solution.py:272
  61.4 1.8 %collective-permute-done.4 = bf16[48,5568]{1,0:T(8,128)(2,1)S(1)} collective-permute-done((bf16[48,5568]{1,0:T(8,128)(2,1)S(1)}, bf16[48,5568]{1,0:T(8,128)(2,1)S(1)}, u32[]{:S(2)}, u32[]{:S(2)}) %collective-permute-start.4) | collective-permute-done | bytes 534560 | tf_op jit(solution)/shard_map/ppermute | solution.py:272
  63.4 2.0 %collective-permute-start.15 = (bf16[24,3136]{1,0:T(8,128)(2,1)S(1)}, bf16[24,3136]{1,0:T(8,128)(2,1)S(1)}, u32[]{:S(2)}, u32[]{:S(2)}) collective-permute-start(bf16[24,3136]{1,0:T(8,128)(2,1)S(1)} %get-tuple-element.139), channel_id=1, source_target_pairs={{0,64},{8,72},{16,80},{24,88},{32,96},{40,104},{48,112},{56,120},{... | collective-permute-start | bytes 451592 | tf_op jit(solution)/shard_map/ppermute | solution.py:272
  65.3 1.9 %collective-permute-start.14 = (bf16[24,3136]{1,0:T(8,128)(2,1)S(1)}, bf16[24,3136]{1,0:T(8,128)(2,1)S(1)}, u32[]{:S(2)}, u32[]{:S(2)}) collective-permute-start(bf16[24,3136]{1,0:T(8,128)(2,1)S(1)} %get-tuple-element.140), channel_id=1, source_target_pairs={{0,96},{8,104},{16,112},{24,120},{32,0},{40,8},{48,16},{56,24},{64... | collective-permute-start | bytes 451592 | tf_op jit(solution)/shard_map/ppermute | solution.py:272
  67.6 1.5 %collective-permute-start.12 = (bf16[24,5568]{1,0:T(8,128)(2,1)S(1)}, bf16[24,5568]{1,0:T(8,128)(2,1)S(1)}, u32[]{:S(2)}, u32[]{:S(2)}) collective-permute-start(bf16[24,5568]{1,0:T(8,128)(2,1)S(1)} %slice.176), channel_id=1, source_target_pairs={{0,16},{8,24},{16,0},{24,8},{32,48},{40,56},{48,32},{56,40},{64,80... | collective-permute-start | bytes 801800 | tf_op jit(solution)/shard_map/ppermute | solution.py:272
  69.2 2.2 %collective-permute-done.15.c_ref = bf16[24,3136]{1,0:T(8,128)(2,1)S(1)} collective-permute-done((bf16[24,3136]{1,0:T(8,128)(2,1)S(1)}, bf16[24,3136]{1,0:T(8,128)(2,1)S(1)}, u32[]{:S(2)}, u32[]{:S(2)}) %collective-permute-start.15) | collective-permute-done | bytes 150560 | tf_op jit(solution)/shard_map/ppermute | solution.py:272
  71.7 2.0 %collective-permute-done.13.a_ref = bf16[24,3136]{1,0:T(8,128)(2,1)S(1)} collective-permute-done((bf16[24,3136]{1,0:T(8,128)(2,1)S(1)}, bf16[24,3136]{1,0:T(8,128)(2,1)S(1)}, u32[]{:S(2)}, u32[]{:S(2)}) %collective-permute-start.13) | collective-permute-done | bytes 150560 | tf_op jit(solution)/shard_map/ppermute | solution.py:272
  74.8 1.5 %collective-permute-start.17 = (bf16[24,5568]{1,0:T(8,128)(2,1)S(1)}, bf16[24,5568]{1,0:T(8,128)(2,1)S(1)}, u32[]{:S(2)}, u32[]{:S(2)}) collective-permute-start(bf16[24,5568]{1,0:T(8,128)(2,1)S(1)} %get-tuple-element.112), channel_id=1, source_target_pairs={{0,16},{8,24},{16,0},{24,8},{32,48},{40,56},{48,32},{56,40},{64,80... | collective-permute-start | bytes 801800 | tf_op jit(solution)/shard_map/ppermute | solution.py:272
  76.3 1.1 collective-permute-start.20
  77.4 2.6 %collective-permute-start.19 = (bf16[24,2752]{1,0:T(8,128)(2,1)S(1)}, bf16[24,2752]{1,0:T(8,128)(2,1)S(1)}, u32[]{:S(2)}, u32[]{:S(2)}) collective-permute-start(bf16[24,2752]{1,0:T(8,128)(2,1)S(1)} %get-tuple-element.111), channel_id=1, source_target_pairs={{0,64},{8,72},{16,80},{24,88},{32,96},{40,104},{48,112},{56,120},{... | collective-permute-start | bytes 396296 | tf_op jit(solution)/shard_map/ppermute | solution.py:272
  80.1 2.5 %collective-permute-done.20 = bf16[24,2752]{1,0:T(8,128)(2,1)S(1)} collective-permute-done((bf16[24,2752]{1,0:T(8,128)(2,1)S(1)}, bf16[24,2752]{1,0:T(8,128)(2,1)S(1)}, u32[]{:S(2)}, u32[]{:S(2)}) %collective-permute-start.20) | collective-permute-done | bytes 132128 | tf_op jit(solution)/shard_map/ppermute | solution.py:272
  82.6 1.9 %collective-permute-done.19 = bf16[24,2752]{1,0:T(8,128)(2,1)S(1)} collective-permute-done((bf16[24,2752]{1,0:T(8,128)(2,1)S(1)}, bf16[24,2752]{1,0:T(8,128)(2,1)S(1)}, u32[]{:S(2)}, u32[]{:S(2)}) %collective-permute-start.19) | collective-permute-done | bytes 132128 | tf_op jit(solution)/shard_map/ppermute | solution.py:272
  85.6 3.6 %collective-permute-start.23 = (bf16[2,24,5568]{2,1,0:T(8,128)(2,1)S(1)}, bf16[2,24,5568]{2,1,0:T(8,128)(2,1)S(1)}, u32[]{:S(2)}, u32[]{:S(2)}) collective-permute-start(bf16[2,24,5568]{2,1,0:T(8,128)(2,1)S(1)} %get-tuple-element.145), channel_id=1, source_target_pairs={{0,64},{8,72},{16,80},{24,88},{32,96},{40,104},{48,112},{56,120},{... | collective-permute-start | bytes 1603592 | tf_op jit(solution)/shard_map/ppermute | solution.py:272
  89.2 1.6 %collective-permute-start.22 = (bf16[2,24,5568]{2,1,0:T(8,128)(2,1)S(1)}, bf16[2,24,5568]{2,1,0:T(8,128)(2,1)S(1)}, u32[]{:S(2)}, u32[]{:S(2)}) collective-permute-start(bf16[2,24,5568]{2,1,0:T(8,128)(2,1)S(1)} %get-tuple-element.145), channel_id=1, source_target_pairs={{0,96},{8,104},{16,112},{24,120},{32,0},{40,8},{48,16},{56,24},{64... | collective-permute-start | bytes 1603592 | tf_op jit(solution)/shard_map/ppermute | solution.py:272
  90.8 1.6 %collective-permute-start.21 = (bf16[4,24,2752]{2,1,0:T(8,128)(2,1)S(1)}, bf16[4,24,2752]{2,1,0:T(8,128)(2,1)S(1)}, u32[]{:S(2)}, u32[]{:S(2)}) collective-permute-start(bf16[4,24,2752]{2,1,0:T(8,128)(2,1)S(1)} %get-tuple-element.147), channel_id=1, source_target_pairs={{0,16},{8,24},{16,0},{24,8},{32,48},{40,56},{48,32},{56,40},{64,80... | collective-permute-start | bytes 1585160 | tf_op jit(solution)/shard_map/ppermute | solution.py:272
  92.4 7.9 %collective-permute-done.21 = bf16[4,24,2752]{2,1,0:T(8,128)(2,1)S(1)} collective-permute-done((bf16[4,24,2752]{2,1,0:T(8,128)(2,1)S(1)}, bf16[4,24,2752]{2,1,0:T(8,128)(2,1)S(1)}, u32[]{:S(2)}, u32[]{:S(2)}) %collective-permute-start.21) | collective-permute-done | bytes 528416 | tf_op jit(solution)/shard_map/ppermute | solution.py:272
  100.3 1.3 collective-permute-done.24
  101.6 6.5 %collective-permute-done.23 = bf16[2,24,5568]{2,1,0:T(8,128)(2,1)S(1)} collective-permute-done((bf16[2,24,5568]{2,1,0:T(8,128)(2,1)S(1)}, bf16[2,24,5568]{2,1,0:T(8,128)(2,1)S(1)}, u32[]{:S(2)}, u32[]{:S(2)}) %collective-permute-start.23) | collective-permute-done | bytes 534560 | tf_op jit(solution)/shard_map/ppermute | solution.py:272
  108.8 2.4 %collective-permute-done.25.o_ref = bf16[192,2752]{1,0:T(8,128)(2,1)S(1)} collective-permute-done((bf16[192,2752]{1,0:T(8,128)(2,1)S(1)}, bf16[192,2752]{1,0:T(8,128)(2,1)S(1)}, u32[]{:S(2)}, u32[]{:S(2)}) %collective-permute-start.25) | collective-permute-done | bytes 1056800 | tf_op jit(solution)/shard_map/ppermute | solution.py:272
  111.3 4.2 %backward_hidden.1 = (bf16[384,512]{1,0:T(8,128)(2,1)S(1)}, bf16[2752,512]{1,0:T(8,128)(2,1)}) custom-call(bf16[192,2752]{1,0:T(8,128)(2,1)S(1)} %bitcast.94, bf16[192,2752]{1,0:T(8,128)(2,1)S(1)} %collective-permute-done.25.o_ref, bf16[384,512]{1,0:T(8,128)(2,1)S(1)} %get-tuple-element.90.o_ref.x_ref, bf16[64,8448]{1,0:T(8,128)(2,1)S(1)} %bitcast.89, ...), custom_call_target="tpu_custom_call" | custom-call | tf_op jit(solution)/shard_map/backward_hidden/pallas_call | solution.py:46
  115.6 3.1 %collective-permute-start.27 = (bf16[4,48,512]{2,1,0:T(8,128)(2,1)S(1)}, bf16[4,48,512]{2,1,0:T(8,128)(2,1)S(1)}, u32[]{:S(2)}, u32[]{:S(2)}) collective-permute-start(bf16[4,48,512]{2,1,0:T(8,128)(2,1)S(1)} %bitcast.115), channel_id=1, source_target_pairs={{0,4},{1,5},{2,6},{3,7},{4,0},{5,1},{6,2},{7,3},{8,12},{9,13},{10,... | collective-permute-start | bytes 589832 | tf_op jit(solution)/shard_map/ppermute | solution.py:280
  118.7 4.5 %backward_pair.1 = bf16[384,512]{1,0:T(8,128)(2,1)S(1)} custom-call(bf16[192,5568]{1,0:T(8,128)(2,1)S(1)} %bitcast.78, bf16[192,5568]{1,0:T(8,128)(2,1)S(1)} %collective-permute-done.26.o_ref, bf16[64,8448]{1,0:T(8,128)(2,1)S(1)} %bitcast.90, bf16[64,8448]{1,0:T(8,128)(2,1)S(1)} %collective-permute-done.16.far_ref, ...), custom_call_target="tpu_custom_call" | custom-call | tf_op jit(solution)/shard_map/backward_pair/pallas_call | solution.py:46
  124.0 2.5 %weight_grad.2 = bf16[2752,512]{1,0:T(8,128)(2,1)} custom-call(bf16[192,5568]{1,0:T(8,128)(2,1)S(1)} %bitcast.79, bf16[192,5568]{1,0:T(8,128)(2,1)S(1)} %collective-permute-done.26.o_ref, bf16[384,512]{1,0:T(8,128)(2,1)S(1)} %get-tuple-element.97.t_ref.x_ref), custom_call_target="tpu_custom_call" | custom-call | tf_op jit(solution)/shard_map/weight_grad/pallas_call | solution.py:46
  126.6 5.3 %collective-permute-done.28 = bf16[4,48,512]{2,1,0:T(8,128)(2,1)S(1)} collective-permute-done((bf16[4,48,512]{2,1,0:T(8,128)(2,1)S(1)}, bf16[4,48,512]{2,1,0:T(8,128)(2,1)S(1)}, u32[]{:S(2)}, u32[]{:S(2)}) %collective-permute-start.28) | collective-permute-done | bytes 196640 | tf_op jit(solution)/shard_map/ppermute | solution.py:280
  132.0 2.7 %collective-permute-start.29 = (bf16[2,48,512]{2,1,0:T(8,128)(2,1)S(1)}, bf16[2,48,512]{2,1,0:T(8,128)(2,1)S(1)}, u32[]{:S(2)}, u32[]{:S(2)}) collective-permute-start(bf16[2,48,512]{2,1,0:T(8,128)(2,1)S(1)} %get-tuple-element.131), channel_id=1, source_target_pairs={{0,1},{1,2},{2,3},{3,0},{4,5},{5,6},{6,7},{7,4},{8,9},{9,10},{10,1... | collective-permute-start | bytes 294920 | tf_op jit(solution)/shard_map/ppermute | solution.py:280
  134.8 1.5 %collective-permute-start.30 = (bf16[2,48,512]{2,1,0:T(8,128)(2,1)S(1)}, bf16[2,48,512]{2,1,0:T(8,128)(2,1)S(1)}, u32[]{:S(2)}, u32[]{:S(2)}) collective-permute-start(bf16[2,48,512]{2,1,0:T(8,128)(2,1)S(1)} %get-tuple-element.132), channel_id=1, source_target_pairs={{0,3},{1,0},{2,1},{3,2},{4,7},{5,4},{6,5},{7,6},{8,11},{9,8},{10,9... | collective-permute-start | bytes 294920 | tf_op jit(solution)/shard_map/ppermute | solution.py:280
  136.3 2.1 %collective-permute-start.31 = (bf16[2,48,512]{2,1,0:T(8,128)(2,1)S(1)}, bf16[2,48,512]{2,1,0:T(8,128)(2,1)S(1)}, u32[]{:S(2)}, u32[]{:S(2)}) collective-permute-start(bf16[2,48,512]{2,1,0:T(8,128)(2,1)S(1)} %pad_maximum_fusion.12), channel_id=1, source_target_pairs={{0,2},{1,3},{2,0},{3,1},{4,6},{5,7},{6,4},{7,5},{8,10},{9,11},{10,... | collective-permute-start | bytes 294920 | tf_op jit(solution)/shard_map/ppermute | solution.py:280
  138.4 2.5 %weight_grad.3 = bf16[2752,512]{1,0:T(8,128)(2,1)} custom-call(bf16[192,5568]{1,0:T(8,128)(2,1)S(1)} %bitcast.80, bf16[192,5568]{1,0:T(8,128)(2,1)S(1)} %collective-permute-done.26.o_ref, bf16[384,512]{1,0:T(8,128)(2,1)S(1)} %get-tuple-element.97.t_ref.x_ref), custom_call_target="tpu_custom_call" | custom-call | tf_op jit(solution)/shard_map/weight_grad/pallas_call | solution.py:46
  140.9 1.5 %collective-permute-done.31 = bf16[2,48,512]{2,1,0:T(8,128)(2,1)S(1)} collective-permute-done((bf16[2,48,512]{2,1,0:T(8,128)(2,1)S(1)}, bf16[2,48,512]{2,1,0:T(8,128)(2,1)S(1)}, u32[]{:S(2)}, u32[]{:S(2)}) %collective-permute-start.31) | collective-permute-done | bytes 98336 | tf_op jit(solution)/shard_map/ppermute | solution.py:280
  (76 shorter events, 12.2 us)
Async XLA Ops:
  0.6 6.5 %copy-start.6 = (bf16[384,512]{1,0:T(8,128)(2,1)S(1)}, bf16[384,512]{1,0:T(8,128)(2,1)}, u32[]{:S(2)}) copy-start(bf16[384,512]{1,0:T(8,128)(2,1)} %g_ref) | copy-start | bytes 1179652
  0.6 6.5 %copy-start.5 = (bf16[384,512]{1,0:T(8,128)(2,1)S(1)}, bf16[384,512]{1,0:T(8,128)(2,1)}, u32[]{:S(2)}) copy-start(bf16[384,512]{1,0:T(8,128)(2,1)} %t_ref) | copy-start | bytes 1179652
  1.5 5.6 %collective-permute-start = (bf16[48,512]{1,0:T(8,128)(2,1)S(1)}, bf16[48,512]{1,0:T(8,128)(2,1)S(1)}, u32[]{:S(2)}, u32[]{:S(2)}) collective-permute-start(bf16[48,512]{1,0:T(8,128)(2,1)S(1)} %pad_maximum_fusion.13), channel_id=1, source_target_pairs={{0,4},{1,5},{2,6},{3,7},{4,0},{5,1},{6,2},{7,3},{8,12},{9,13},{10,... | collective-permute-start | bytes 147464 | tf_op jit(solution)/shard_map/ppermute | solution.py:280
  7.1 1.8 %copy-start = (bf16[512,2752]{0,1:T(8,128)(2,1)S(1)}, bf16[512,2752]{0,1:T(8,128)(2,1)}, u32[]{:S(2)}) copy-start(bf16[512,2752]{0,1:T(8,128)(2,1)} %param.15) | copy-start | bytes 8454148
  8.9 1.8 %copy-start.2 = (bf16[512,2752]{0,1:T(8,128)(2,1)S(1)}, bf16[512,2752]{0,1:T(8,128)(2,1)}, u32[]{:S(2)}) copy-start(bf16[512,2752]{0,1:T(8,128)(2,1)} %param.13) | copy-start | bytes 8454148
  13.3 14.0 %collective-permute-start.1 = (bf16[192,5568]{1,0:T(8,128)(2,1)S(1)}, bf16[192,5568]{1,0:T(8,128)(2,1)S(1)}, u32[]{:S(2)}, u32[]{:S(2)}) collective-permute-start(bf16[192,5568]{1,0:T(8,128)(2,1)S(1)} %get-tuple-element.91), channel_id=1, source_target_pairs={{0,8},{8,0},{16,24},{24,16},{32,40},{40,32},{48,56},{56,48},{64,72... | collective-permute-start | bytes 6414344 | tf_op jit(solution)/shard_map/ppermute | solution.py:272
  13.4 5.3 %collective-permute-start.5 = (bf16[2,48,512]{2,1,0:T(8,128)(2,1)S(1)}, bf16[2,48,512]{2,1,0:T(8,128)(2,1)S(1)}, u32[]{:S(2)}, u32[]{:S(2)}) collective-permute-start(bf16[2,48,512]{2,1,0:T(8,128)(2,1)S(1)} %get-tuple-element.165), channel_id=1, source_target_pairs={{0,1},{1,0},{2,3},{3,2},{4,5},{5,4},{6,7},{7,6},{8,9},{9,8},{10,11... | collective-permute-start | bytes 294920 | tf_op jit(solution)/shard_map/ppermute | solution.py:289
  15.1 6.9 %collective-permute-start.8 = (bf16[8,8448]{1,0:T(8,128)(2,1)S(1)}, bf16[8,8448]{1,0:T(8,128)(2,1)S(1)}, u32[]{:S(2)}, u32[]{:S(2)}) collective-permute-start(bf16[8,8448]{1,0:T(8,128)(2,1)S(1)} %concatenate.6), channel_id=1, source_target_pairs={{0,32},{8,40},{16,48},{24,56},{32,0},{40,8},{48,16},{56,24},{64,96... | collective-permute-start | bytes 405512 | tf_op jit(solution)/shard_map/ppermute | solution.py:289
  18.6 8.6 %copy-start.1 = (bf16[512,2752]{0,1:T(8,128)(2,1)S(1)}, bf16[512,2752]{0,1:T(8,128)(2,1)}, u32[]{:S(2)}) copy-start(bf16[512,2752]{0,1:T(8,128)(2,1)} %param.15) | copy-start | bytes 8454148
  18.7 8.1 %collective-permute-start.6 = (bf16[2,2,48,512]{3,2,1,0:T(8,128)(2,1)S(1)}, bf16[2,2,48,512]{3,2,1,0:T(8,128)(2,1)S(1)}, u32[]{:S(2)}, u32[]{:S(2)}) collective-permute-start(bf16[2,2,48,512]{3,2,1,0:T(8,128)(2,1)S(1)} %get-tuple-element.163), channel_id=1, source_target_pairs={{0,2},{1,3},{2,0},{3,1},{4,6},{5,7},{6,4},{7,5},{8,10},{9,11},{10,... | collective-permute-start | bytes 589832 | tf_op jit(solution)/shard_map/ppermute | solution.py:289
  22.1 10.0 %collective-permute-start.9 = (bf16[2,8,8448]{2,1,0:T(8,128)(2,1)S(1)}, bf16[2,8,8448]{2,1,0:T(8,128)(2,1)S(1)}, u32[]{:S(2)}, u32[]{:S(2)}) collective-permute-start(bf16[2,8,8448]{2,1,0:T(8,128)(2,1)S(1)} %get-tuple-element.155), channel_id=1, source_target_pairs={{0,64},{8,72},{16,80},{24,88},{32,96},{40,104},{48,112},{56,120},{... | collective-permute-start | bytes 811016 | tf_op jit(solution)/shard_map/ppermute | solution.py:289
  27.2 2.0 %copy-start.4 = (bf16[512,2752]{0,1:T(8,128)(2,1)S(1)}, bf16[512,2752]{0,1:T(8,128)(2,1)}, u32[]{:S(2)}) copy-start(bf16[512,2752]{0,1:T(8,128)(2,1)} %param.14) | copy-start | bytes 8454148
  30.9 14.9 %collective-permute-start.7 = (bf16[192,3136]{1,0:T(8,128)(2,1)S(1)}, bf16[192,3136]{1,0:T(8,128)(2,1)S(1)}, u32[]{:S(2)}, u32[]{:S(2)}) collective-permute-start(bf16[192,3136]{1,0:T(8,128)(2,1)S(1)} %get-tuple-element.102), channel_id=1, source_target_pairs={{0,8},{8,0},{16,24},{24,16},{32,40},{40,32},{48,56},{56,48},{64,72... | collective-permute-start | bytes 3612680 | tf_op jit(solution)/shard_map/ppermute | solution.py:272
  32.2 13.6 %collective-permute-start.10 = (bf16[4,8,8448]{2,1,0:T(8,128)(2,1)S(1)}, bf16[4,8,8448]{2,1,0:T(8,128)(2,1)S(1)}, u32[]{:S(2)}, u32[]{:S(2)}) collective-permute-start(bf16[4,8,8448]{2,1,0:T(8,128)(2,1)S(1)} %bitcast.102), channel_id=1, source_target_pairs={{0,16},{8,24},{16,0},{24,8},{32,48},{40,56},{48,32},{56,40},{64,80... | collective-permute-start | bytes 1622024 | tf_op jit(solution)/shard_map/ppermute | solution.py:272
  34.8 15.7 %collective-permute-start.2 = (bf16[48,5568]{1,0:T(8,128)(2,1)S(1)}, bf16[48,5568]{1,0:T(8,128)(2,1)S(1)}, u32[]{:S(2)}, u32[]{:S(2)}) collective-permute-start(bf16[48,5568]{1,0:T(8,128)(2,1)S(1)} %get-tuple-element.94), channel_id=1, source_target_pairs={{0,32},{8,40},{16,48},{24,56},{32,64},{40,72},{48,80},{56,88},{64,... | collective-permute-start | bytes 1603592 | tf_op jit(solution)/shard_map/ppermute | solution.py:272
  36.1 25.2 %collective-permute-start.3 = (bf16[48,5568]{1,0:T(8,128)(2,1)S(1)}, bf16[48,5568]{1,0:T(8,128)(2,1)S(1)}, u32[]{:S(2)}, u32[]{:S(2)}) collective-permute-start(bf16[48,5568]{1,0:T(8,128)(2,1)S(1)} %get-tuple-element.95), channel_id=1, source_target_pairs={{0,96},{8,104},{16,112},{24,120},{32,0},{40,8},{48,16},{56,24},{64... | collective-permute-start | bytes 1603592 | tf_op jit(solution)/shard_map/ppermute | solution.py:272
  38.3 24.8 %collective-permute-start.4 = (bf16[48,5568]{1,0:T(8,128)(2,1)S(1)}, bf16[48,5568]{1,0:T(8,128)(2,1)S(1)}, u32[]{:S(2)}, u32[]{:S(2)}) collective-permute-start(bf16[48,5568]{1,0:T(8,128)(2,1)S(1)} %get-tuple-element.96), channel_id=1, source_target_pairs={{0,64},{8,72},{16,80},{24,88},{32,96},{40,104},{48,112},{56,120},{... | collective-permute-start | bytes 1603592 | tf_op jit(solution)/shard_map/ppermute | solution.py:272
  46.1 17.1 %collective-permute-start.11 = (bf16[4,24,3136]{2,1,0:T(8,128)(2,1)S(1)}, bf16[4,24,3136]{2,1,0:T(8,128)(2,1)S(1)}, u32[]{:S(2)}, u32[]{:S(2)}) collective-permute-start(bf16[4,24,3136]{2,1,0:T(8,128)(2,1)S(1)} %fusion.1), channel_id=1, source_target_pairs={{0,16},{8,24},{16,0},{24,8},{32,48},{40,56},{48,32},{56,40},{64,80... | collective-permute-start | bytes 1806344 | tf_op jit(solution)/shard_map/ppermute | solution.py:272
  47.8 26.3 %collective-permute-start.16 = (bf16[64,8448]{1,0:T(8,128)(2,1)S(1)}, bf16[64,8448]{1,0:T(8,128)(2,1)S(1)}, u32[]{:S(2)}, u32[]{:S(2)}) collective-permute-start(bf16[64,8448]{1,0:T(8,128)(2,1)S(1)} %bitcast.87), channel_id=1, source_target_pairs={{0,8},{8,0},{16,24},{24,16},{32,40},{40,32},{48,56},{56,48},{64,72... | collective-permute-start | bytes 3244040 | tf_op jit(solution)/shard_map/ppermute | solution.py:272
  63.4 8.1 %collective-permute-start.15 = (bf16[24,3136]{1,0:T(8,128)(2,1)S(1)}, bf16[24,3136]{1,0:T(8,128)(2,1)S(1)}, u32[]{:S(2)}, u32[]{:S(2)}) collective-permute-start(bf16[24,3136]{1,0:T(8,128)(2,1)S(1)} %get-tuple-element.139), channel_id=1, source_target_pairs={{0,64},{8,72},{16,80},{24,88},{32,96},{40,104},{48,112},{56,120},{... | collective-permute-start | bytes 451592 | tf_op jit(solution)/shard_map/ppermute | solution.py:272
  65.3 6.4 %collective-permute-start.14 = (bf16[24,3136]{1,0:T(8,128)(2,1)S(1)}, bf16[24,3136]{1,0:T(8,128)(2,1)S(1)}, u32[]{:S(2)}, u32[]{:S(2)}) collective-permute-start(bf16[24,3136]{1,0:T(8,128)(2,1)S(1)} %get-tuple-element.140), channel_id=1, source_target_pairs={{0,96},{8,104},{16,112},{24,120},{32,0},{40,8},{48,16},{56,24},{64... | collective-permute-start | bytes 451592 | tf_op jit(solution)/shard_map/ppermute | solution.py:272
  67.3 6.5 %collective-permute-start.13 = (bf16[24,3136]{1,0:T(8,128)(2,1)S(1)}, bf16[24,3136]{1,0:T(8,128)(2,1)S(1)}, u32[]{:S(2)}, u32[]{:S(2)}) collective-permute-start(bf16[24,3136]{1,0:T(8,128)(2,1)S(1)} %get-tuple-element.141), channel_id=1, source_target_pairs={{0,32},{8,40},{16,48},{24,56},{32,64},{40,72},{48,80},{56,88},{64,... | collective-permute-start | bytes 451592 | tf_op jit(solution)/shard_map/ppermute | solution.py:272
  67.6 6.5 %collective-permute-start.12 = (bf16[24,5568]{1,0:T(8,128)(2,1)S(1)}, bf16[24,5568]{1,0:T(8,128)(2,1)S(1)}, u32[]{:S(2)}, u32[]{:S(2)}) collective-permute-start(bf16[24,5568]{1,0:T(8,128)(2,1)S(1)} %slice.176), channel_id=1, source_target_pairs={{0,16},{8,24},{16,0},{24,8},{32,48},{40,56},{48,32},{56,40},{64,80... | collective-permute-start | bytes 801800 | tf_op jit(solution)/shard_map/ppermute | solution.py:272
  74.8 10.4 %collective-permute-start.17 = (bf16[24,5568]{1,0:T(8,128)(2,1)S(1)}, bf16[24,5568]{1,0:T(8,128)(2,1)S(1)}, u32[]{:S(2)}, u32[]{:S(2)}) collective-permute-start(bf16[24,5568]{1,0:T(8,128)(2,1)S(1)} %get-tuple-element.112), channel_id=1, source_target_pairs={{0,16},{8,24},{16,0},{24,8},{32,48},{40,56},{48,32},{56,40},{64,80... | collective-permute-start | bytes 801800 | tf_op jit(solution)/shard_map/ppermute | solution.py:272
  76.3 6.2 %collective-permute-start.20 = (bf16[24,2752]{1,0:T(8,128)(2,1)S(1)}, bf16[24,2752]{1,0:T(8,128)(2,1)S(1)}, u32[]{:S(2)}, u32[]{:S(2)}) collective-permute-start(bf16[24,2752]{1,0:T(8,128)(2,1)S(1)} %get-tuple-element.111), channel_id=1, source_target_pairs={{0,32},{8,40},{16,48},{24,56},{32,64},{40,72},{48,80},{56,88},{64,... | collective-permute-start | bytes 396296 | tf_op jit(solution)/shard_map/ppermute | solution.py:272
  77.4 7.0 %collective-permute-start.19 = (bf16[24,2752]{1,0:T(8,128)(2,1)S(1)}, bf16[24,2752]{1,0:T(8,128)(2,1)S(1)}, u32[]{:S(2)}, u32[]{:S(2)}) collective-permute-start(bf16[24,2752]{1,0:T(8,128)(2,1)S(1)} %get-tuple-element.111), channel_id=1, source_target_pairs={{0,64},{8,72},{16,80},{24,88},{32,96},{40,104},{48,112},{56,120},{... | collective-permute-start | bytes 396296 | tf_op jit(solution)/shard_map/ppermute | solution.py:272
  80.0 5.2 %collective-permute-start.18 = (bf16[24,2752]{1,0:T(8,128)(2,1)S(1)}, bf16[24,2752]{1,0:T(8,128)(2,1)S(1)}, u32[]{:S(2)}, u32[]{:S(2)}) collective-permute-start(bf16[24,2752]{1,0:T(8,128)(2,1)S(1)} %get-tuple-element.111), channel_id=1, source_target_pairs={{0,96},{8,104},{16,112},{24,120},{32,0},{40,8},{48,16},{56,24},{64... | collective-permute-start | bytes 396296 | tf_op jit(solution)/shard_map/ppermute | solution.py:272
  85.3 16.3 %collective-permute-start.24 = (bf16[2,24,5568]{2,1,0:T(8,128)(2,1)S(1)}, bf16[2,24,5568]{2,1,0:T(8,128)(2,1)S(1)}, u32[]{:S(2)}, u32[]{:S(2)}) collective-permute-start(bf16[2,24,5568]{2,1,0:T(8,128)(2,1)S(1)} %get-tuple-element.145), channel_id=1, source_target_pairs={{0,32},{8,40},{16,48},{24,56},{32,64},{40,72},{48,80},{56,88},{64,... | collective-permute-start | bytes 1603592 | tf_op jit(solution)/shard_map/ppermute | solution.py:272
  85.6 22.4 %collective-permute-start.23 = (bf16[2,24,5568]{2,1,0:T(8,128)(2,1)S(1)}, bf16[2,24,5568]{2,1,0:T(8,128)(2,1)S(1)}, u32[]{:S(2)}, u32[]{:S(2)}) collective-permute-start(bf16[2,24,5568]{2,1,0:T(8,128)(2,1)S(1)} %get-tuple-element.145), channel_id=1, source_target_pairs={{0,64},{8,72},{16,80},{24,88},{32,96},{40,104},{48,112},{56,120},{... | collective-permute-start | bytes 1603592 | tf_op jit(solution)/shard_map/ppermute | solution.py:272
  89.2 19.0 %collective-permute-start.22 = (bf16[2,24,5568]{2,1,0:T(8,128)(2,1)S(1)}, bf16[2,24,5568]{2,1,0:T(8,128)(2,1)S(1)}, u32[]{:S(2)}, u32[]{:S(2)}) collective-permute-start(bf16[2,24,5568]{2,1,0:T(8,128)(2,1)S(1)} %get-tuple-element.145), channel_id=1, source_target_pairs={{0,96},{8,104},{16,112},{24,120},{32,0},{40,8},{48,16},{56,24},{64... | collective-permute-start | bytes 1603592 | tf_op jit(solution)/shard_map/ppermute | solution.py:272
  90.8 9.4 %collective-permute-start.21 = (bf16[4,24,2752]{2,1,0:T(8,128)(2,1)S(1)}, bf16[4,24,2752]{2,1,0:T(8,128)(2,1)S(1)}, u32[]{:S(2)}, u32[]{:S(2)}) collective-permute-start(bf16[4,24,2752]{2,1,0:T(8,128)(2,1)S(1)} %get-tuple-element.147), channel_id=1, source_target_pairs={{0,16},{8,24},{16,0},{24,8},{32,48},{40,56},{48,32},{56,40},{64,80... | collective-permute-start | bytes 1585160 | tf_op jit(solution)/shard_map/ppermute | solution.py:272
  108.4 2.8 %collective-permute-start.25 = (bf16[192,2752]{1,0:T(8,128)(2,1)S(1)}, bf16[192,2752]{1,0:T(8,128)(2,1)S(1)}, u32[]{:S(2)}, u32[]{:S(2)}) collective-permute-start(bf16[192,2752]{1,0:T(8,128)(2,1)S(1)} %bitcast.93), channel_id=1, source_target_pairs={{0,8},{8,0},{16,24},{24,16},{32,40},{40,32},{48,56},{56,48},{64,72... | collective-permute-start | bytes 3170312 | tf_op jit(solution)/shard_map/ppermute | solution.py:272
  111.2 7.5 %collective-permute-start.26 = (bf16[192,5568]{1,0:T(8,128)(2,1)S(1)}, bf16[192,5568]{1,0:T(8,128)(2,1)S(1)}, u32[]{:S(2)}, u32[]{:S(2)}) collective-permute-start(bf16[192,5568]{1,0:T(8,128)(2,1)S(1)} %bitcast.77), channel_id=1, source_target_pairs={{0,8},{8,0},{16,24},{24,16},{32,40},{40,32},{48,56},{56,48},{64,72... | collective-permute-start | bytes 6414344 | tf_op jit(solution)/shard_map/ppermute | solution.py:272
  111.3 7.3 %copy-start.3 = (bf16[512,2752]{0,1:T(8,128)(2,1)S(1)}, bf16[512,2752]{0,1:T(8,128)(2,1)}, u32[]{:S(2)}) copy-start(bf16[512,2752]{0,1:T(8,128)(2,1)} %param.13) | copy-start | bytes 8454148
  115.6 10.9 %collective-permute-start.27 = (bf16[4,48,512]{2,1,0:T(8,128)(2,1)S(1)}, bf16[4,48,512]{2,1,0:T(8,128)(2,1)S(1)}, u32[]{:S(2)}, u32[]{:S(2)}) collective-permute-start(bf16[4,48,512]{2,1,0:T(8,128)(2,1)S(1)} %bitcast.115), channel_id=1, source_target_pairs={{0,4},{1,5},{2,6},{3,7},{4,0},{5,1},{6,2},{7,3},{8,12},{9,13},{10,... | collective-permute-start | bytes 589832 | tf_op jit(solution)/shard_map/ppermute | solution.py:280
  123.2 8.7 %collective-permute-start.28 = (bf16[4,48,512]{2,1,0:T(8,128)(2,1)S(1)}, bf16[4,48,512]{2,1,0:T(8,128)(2,1)S(1)}, u32[]{:S(2)}, u32[]{:S(2)}) collective-permute-start(bf16[4,48,512]{2,1,0:T(8,128)(2,1)S(1)} %bitcast.116), channel_id=1, source_target_pairs={{0,4},{1,5},{2,6},{3,7},{4,0},{5,1},{6,2},{7,3},{8,12},{9,13},{10,... | collective-permute-start | bytes 589832 | tf_op jit(solution)/shard_map/ppermute | solution.py:280
  132.0 8.8 %collective-permute-start.29 = (bf16[2,48,512]{2,1,0:T(8,128)(2,1)S(1)}, bf16[2,48,512]{2,1,0:T(8,128)(2,1)S(1)}, u32[]{:S(2)}, u32[]{:S(2)}) collective-permute-start(bf16[2,48,512]{2,1,0:T(8,128)(2,1)S(1)} %get-tuple-element.131), channel_id=1, source_target_pairs={{0,1},{1,2},{2,3},{3,0},{4,5},{5,6},{6,7},{7,4},{8,9},{9,10},{10,1... | collective-permute-start | bytes 294920 | tf_op jit(solution)/shard_map/ppermute | solution.py:280
  134.8 6.1 %collective-permute-start.30 = (bf16[2,48,512]{2,1,0:T(8,128)(2,1)S(1)}, bf16[2,48,512]{2,1,0:T(8,128)(2,1)S(1)}, u32[]{:S(2)}, u32[]{:S(2)}) collective-permute-start(bf16[2,48,512]{2,1,0:T(8,128)(2,1)S(1)} %get-tuple-element.132), channel_id=1, source_target_pairs={{0,3},{1,0},{2,1},{3,2},{4,7},{5,4},{6,5},{7,6},{8,11},{9,8},{10,9... | collective-permute-start | bytes 294920 | tf_op jit(solution)/shard_map/ppermute | solution.py:280
  136.3 6.1 %collective-permute-start.31 = (bf16[2,48,512]{2,1,0:T(8,128)(2,1)S(1)}, bf16[2,48,512]{2,1,0:T(8,128)(2,1)S(1)}, u32[]{:S(2)}, u32[]{:S(2)}) collective-permute-start(bf16[2,48,512]{2,1,0:T(8,128)(2,1)S(1)} %pad_maximum_fusion.12), channel_id=1, source_target_pairs={{0,2},{1,3},{2,0},{3,1},{4,6},{5,7},{6,4},{7,5},{8,10},{9,11},{10,... | collective-permute-start | bytes 294920 | tf_op jit(solution)/shard_map/ppermute | solution.py:280

commit v8 on v6

--- a/solution.py
+++ b/solution.py
@@ -203,24 +203,19 @@
     return sent
 
 
-def backward_hidden(mine, other, x, weight, near, far, lefts, sort, index):
-    n, depth = weight.shape
-
-    def body(m_ref, o_ref, x_ref, near_ref, far_ref, l_ref, s_ref, i_ref, w_ref, out_ref, grad_hbm, grad_ref, sems):
-        sent = grads(m_ref, o_ref, 0, x_ref, grad_ref, grad_hbm, sems)
+def backward_hidden(mine, other, weight, near, far, lefts, sort, index):
+    def body(m_ref, o_ref, near_ref, far_ref, l_ref, s_ref, i_ref, w_ref, out_ref):
         total = through(m_ref, o_ref, 0, w_ref, near_ref, far_ref, l_ref, s_ref, 2)
         out_ref[...] = dot(pick(i_ref, SIZE), total.astype(BF), NN).astype(BF)
-        for copy in sent:
-            copy.wait()
 
     return pallas(
         body,
         "backward_hidden",
-        (mine, other, x, near, far, lefts, sort, index, weight),
-        [jax.ShapeDtypeStruct((SIZE, depth), BF), jax.ShapeDtypeStruct((n, depth), BF)],
-        [VMEM] * 9,
-        [VMEM, HBM],
-        [pltpu.VMEM((n, depth), BF), pltpu.SemaphoreType.DMA((len(cuts(n, STEP)),))],
+        (mine, other, near, far, lefts, sort, index, weight),
+        jax.ShapeDtypeStruct((SIZE, weight.shape[1]), BF),
+        [VMEM] * 8,
+        VMEM,
+        [],
     )
 
 
@@ -375,7 +370,7 @@
     near = jnp.stack([rights, rights_x], axis=1).reshape(64, -1)
     far = core_send(near)
 
-    *pair_z, up_x, leave = tie(*pair_z, up_x, leave)
+    *pair_z, up_x = tie(*pair_z, up_x)
     pair = plus(pair, pair_z).reshape(2, ROWS, -1)
     pair_x = x_send(pair[1].astype(BF))
     up = up[:, 0] + up_x.astype(F32)
@@ -393,16 +388,17 @@
     delta = jnp.stack([delta] + delta_z).reshape(HALF, -1)
     hidden_far, delta = tie(core_send(hidden), delta)
     delta_far = core_send(delta)
-    mixed, down_grad = backward_hidden(hidden, hidden_far, out, down_w, near, far, lefts, sort, leave)
+    mixed = backward_hidden(hidden, hidden_far, down_w, near, far, lefts, sort, leave)
     mixed = mixed.reshape(2, 4, 48, -1)
     mixed_h = col_send(mixed[1], 1, 0)
     delta_far, mixed = tie(delta_far, mixed)
     input_grad = backward_pair(delta, delta_far, gate_w, up_w, near, far, lefts, sort, leave)
     input_grad = input_grad.reshape(2, 4, 48, -1)
-    delta, leaving = tie(delta, input_grad[1])
+    delta, hidden, leaving = tie(delta, hidden, input_grad[1])
     input_h = col_send(leaving, 1, 0)
     up_grad = weight_grad(delta, delta_far, tok, padded(n), n)
-    input_h, delta, up_grad = tie(input_h, delta, up_grad)
+    down_grad = weight_grad(hidden, hidden_far, out, 0, n)
+    input_h, delta, up_grad, down_grad = tie(input_h, delta, up_grad, down_grad)
     both = [mixed[0].astype(F32) + mixed_h.astype(F32), input_grad[0].astype(F32) + input_h.astype(F32)]
     leaving = [jnp.stack([part[d] for part in both]).astype(BF) for d in (1, 3, 2)]
     delta, *leaving = tie(delta, *leaving)

time: 141 us -> 141 us (level)
    ppermute x9, waiting for transfers between devices: 8.15 us -> 6.68 us  [col_send(): return lax.ppermute(x, 'col', pairs)]
    pallas_call x8 -> x9, Pallas kernels: 20.3 us -> 21.1 us  [pallas(): pl.pallas_call(body, out_shape=outs, in_specs=in_specs, out_specs=out_spe...]
  transfers between devices with their start and end apart: 34 -> 34, of which waited for: 20 -> 21; matrix products, arithmetic and copies ran while one was open for 3% -> 3% of each run, Pallas kernels for 12% -> 13%
where the time goes in v8:
time: 141 us; the launch traced here: 140 us
  waiting for transfers between devices  58.6 us (42%)
  starting transfers between devices  49.5 us (35%)
  Pallas kernels  21.1 us (15%)
  local copies, waits for them, and re-layouts  4.93 us (3%)
  other arithmetic  4.83 us (3%)
    ppermute x25, waiting for transfers between devices, row_send(): return lax.ppermute(x, 'row', pairs)  51.9 us
    ppermute x25, starting transfers between devices, row_send(): return lax.ppermute(x, 'row', pairs)  32.3 us
    pallas_call x9, Pallas kernels, pallas(): pl.pallas_call(body, out_shape=outs, in_specs=in_specs, out_specs=out_spe...  21.1 us
    ppermute x9, starting transfers between devices, col_send(): return lax.ppermute(x, 'col', pairs)  17.2 us
    ppermute x9, waiting for transfers between devices, col_send(): return lax.ppermute(x, 'col', pairs)  6.68 us
    unnamed x14, local copies, waits for them, and re-layouts  3.62 us
  transfers between devices with their start and end apart: 34, of which 21 were waited for; matrix products, arithmetic and copies ran while one was open for 3% of the time, Pallas kernels for 13%

profile of v8, /device:TPU:0, one launch (start us, length us, event | category | flops | bytes accessed | tf_op | source)
XLA Modules:
  0.0 140.4 jit_solution(8051157728712169535)
XLA Ops:
  0.7 0.8 pad_maximum_fusion.11
  1.5 3.1 %collective-permute-start = (bf16[48,512]{1,0:T(8,128)(2,1)S(1)}, bf16[48,512]{1,0:T(8,128)(2,1)S(1)}, u32[]{:S(2)}, u32[]{:S(2)}) collective-permute-start(bf16[48,512]{1,0:T(8,128)(2,1)S(1)} %pad_maximum_fusion.11), channel_id=1, source_target_pairs={{0,4},{1,5},{2,6},{3,7},{4,0},{5,1},{6,2},{7,3},{8,12},{9,13},{10,... | collective-permute-start | bytes 147464 | tf_op jit(solution)/shard_map/ppermute | solution.py:275
  5.5 0.9 concatenate.6
  6.4 0.7 collective-permute-done
  7.1 1.8 %copy-done = bf16[512,2752]{0,1:T(8,128)(2,1)S(1)} copy-done((bf16[512,2752]{0,1:T(8,128)(2,1)S(1)}, bf16[512,2752]{0,1:T(8,128)(2,1)}, u32[]{:S(2)}) %copy-start) | copy-done | bytes 2818072
  8.9 1.8 %copy-done.2 = bf16[512,2752]{0,1:T(8,128)(2,1)S(1)} copy-done((bf16[512,2752]{0,1:T(8,128)(2,1)S(1)}, bf16[512,2752]{0,1:T(8,128)(2,1)}, u32[]{:S(2)}) %copy-start.2) | copy-done | bytes 2818072
  10.7 2.5 %forward_theirs.1 = (bf16[192,5568]{1,0:T(8,128)(2,1)S(1)}, bf16[384,512]{1,0:T(8,128)(2,1)S(1)}, bf16[384,512]{1,0:T(8,128)(2,1)S(1)}) custom-call(bf16[384,512]{1,0:T(8,128)(2,1)S(1)} %copy-done.5, bf16[384,512]{1,0:T(8,128)(2,1)S(1)} %copy-done.6, s32[384,1]{1,0:T(8,128)S(1)} %fusion.22.i_ref, bf16[2752,512]{1,0:T(8,128)(2,1)S(1)} %bitcast.80, ...), custom_call_target="tpu_custom_call" | custom-call | tf_op jit(solution)/shard_map/forward_theirs/pallas_call | solution.py:46
  13.4 3.4 %collective-permute-start.6 = (bf16[2,48,512]{2,1,0:T(8,128)(2,1)S(1)}, bf16[2,48,512]{2,1,0:T(8,128)(2,1)S(1)}, u32[]{:S(2)}, u32[]{:S(2)}) collective-permute-start(bf16[2,48,512]{2,1,0:T(8,128)(2,1)S(1)} %get-tuple-element.161), channel_id=1, source_target_pairs={{0,2},{1,3},{2,0},{3,1},{4,6},{5,7},{6,4},{7,5},{8,10},{9,11},{10,... | collective-permute-start | bytes 294920 | tf_op jit(solution)/shard_map/ppermute | solution.py:275
  17.4 2.6 %collective-permute-start.7 = (bf16[2,48,512]{2,1,0:T(8,128)(2,1)S(1)}, bf16[2,48,512]{2,1,0:T(8,128)(2,1)S(1)}, u32[]{:S(2)}, u32[]{:S(2)}) collective-permute-start(bf16[2,48,512]{2,1,0:T(8,128)(2,1)S(1)} %get-tuple-element.161), channel_id=1, source_target_pairs={{0,3},{1,0},{2,1},{3,2},{4,7},{5,4},{6,5},{7,6},{8,11},{9,8},{10,9... | collective-permute-start | bytes 294920 | tf_op jit(solution)/shard_map/ppermute | solution.py:275
  20.0 1.9 %collective-permute-start.11 = (bf16[8,8448]{1,0:T(8,128)(2,1)S(1)}, bf16[8,8448]{1,0:T(8,128)(2,1)S(1)}, u32[]{:S(2)}, u32[]{:S(2)}) collective-permute-start(bf16[8,8448]{1,0:T(8,128)(2,1)S(1)} %concatenate.6), channel_id=1, source_target_pairs={{0,32},{8,40},{16,48},{24,56},{32,64},{40,72},{48,80},{56,88},{64,... | collective-permute-start | bytes 405512 | tf_op jit(solution)/shard_map/ppermute | solution.py:267
  21.9 3.6 %collective-permute-start.10 = (bf16[8,8448]{1,0:T(8,128)(2,1)S(1)}, bf16[8,8448]{1,0:T(8,128)(2,1)S(1)}, u32[]{:S(2)}, u32[]{:S(2)}) collective-permute-start(bf16[8,8448]{1,0:T(8,128)(2,1)S(1)} %concatenate.6), channel_id=1, source_target_pairs={{0,64},{8,72},{16,80},{24,88},{32,96},{40,104},{48,112},{56,120},{... | collective-permute-start | bytes 405512 | tf_op jit(solution)/shard_map/ppermute | solution.py:267
  25.5 1.4 %collective-permute-start.9 = (bf16[8,8448]{1,0:T(8,128)(2,1)S(1)}, bf16[8,8448]{1,0:T(8,128)(2,1)S(1)}, u32[]{:S(2)}, u32[]{:S(2)}) collective-permute-start(bf16[8,8448]{1,0:T(8,128)(2,1)S(1)} %concatenate.6), channel_id=1, source_target_pairs={{0,96},{8,104},{16,112},{24,120},{32,0},{40,8},{48,16},{56,24},{64... | collective-permute-start | bytes 405512 | tf_op jit(solution)/shard_map/ppermute | solution.py:267
  27.3 2.0 %forward_mine.1 = (f32[48,5568]{1,0:T(8,128)S(1)}, bf16[48,5568]{1,0:T(8,128)(2,1)S(1)}, bf16[48,5568]{1,0:T(8,128)(2,1)S(1)}, bf16[48,5568]{1,0:T(8,128)(2,1)S(1)}) custom-call(bf16[384,512]{1,0:T(8,128)(2,1)S(1)} %get-tuple-element.96.t_ref.x_ref, bf16[384,512]{1,0:T(8,128)(2,1)S(1)} %get-tuple-element.89.o_ref.x_ref, bf16[2752,512]{1,0:T(8,128)(2,1)S(1)} %bitcast.81, ...), custom_call_target="tpu_custom_call" | custom-call | tf_op jit(solution)/shard_map/forward_mine/pallas_call | solution.py:46
  29.3 1.6 %forward_up.1 = (f32[192,3136]{1,0:T(8,128)S(1)}, bf16[192,3136]{1,0:T(8,128)(2,1)S(1)}) custom-call(bf16[384,512]{1,0:T(8,128)(2,1)S(1)} %get-tuple-element.96.t_ref.x_ref, bf16[384,512]{1,0:T(8,128)(2,1)S(1)} %get-tuple-element.89.o_ref.x_ref, bf16[384,512]{1,0:T(8,128)(2,1)S(1)} %convolution_convert_fusion.l_ref, bf16[2752,512]{1,0:T(8,128)(2,1)S(1)} %bitcast.87), custom_call_target="tpu_custom_call" | custom-call | tf_op jit(solution)/shard_map/forward_up/pallas_call | solution.py:46
  31.6 1.6 %collective-permute-start.12 = (bf16[4,8,8448]{2,1,0:T(8,128)(2,1)S(1)}, bf16[4,8,8448]{2,1,0:T(8,128)(2,1)S(1)}, u32[]{:S(2)}, u32[]{:S(2)}) collective-permute-start(bf16[4,8,8448]{2,1,0:T(8,128)(2,1)S(1)} %get-tuple-element.147), channel_id=1, source_target_pairs={{0,16},{8,24},{16,0},{24,8},{32,48},{40,56},{48,32},{56,40},{64,80... | collective-permute-start | bytes 1622024 | tf_op jit(solution)/shard_map/ppermute | solution.py:267
  33.1 1.5 %collective-permute-start.2 = (bf16[48,5568]{1,0:T(8,128)(2,1)S(1)}, bf16[48,5568]{1,0:T(8,128)(2,1)S(1)}, u32[]{:S(2)}, u32[]{:S(2)}) collective-permute-start(bf16[48,5568]{1,0:T(8,128)(2,1)S(1)} %get-tuple-element.93), channel_id=1, source_target_pairs={{0,32},{8,40},{16,48},{24,56},{32,64},{40,72},{48,80},{56,88},{64,... | collective-permute-start | bytes 1603592 | tf_op jit(solution)/shard_map/ppermute | solution.py:267
  34.6 1.8 %collective-permute-start.3 = (bf16[48,5568]{1,0:T(8,128)(2,1)S(1)}, bf16[48,5568]{1,0:T(8,128)(2,1)S(1)}, u32[]{:S(2)}, u32[]{:S(2)}) collective-permute-start(bf16[48,5568]{1,0:T(8,128)(2,1)S(1)} %get-tuple-element.94), channel_id=1, source_target_pairs={{0,96},{8,104},{16,112},{24,120},{32,0},{40,8},{48,16},{56,24},{64... | collective-permute-start | bytes 1603592 | tf_op jit(solution)/shard_map/ppermute | solution.py:267
  36.4 1.0 collective-permute-start.4
  37.4 8.5 %collective-permute-done.12 = bf16[4,8,8448]{2,1,0:T(8,128)(2,1)S(1)} collective-permute-done((bf16[4,8,8448]{2,1,0:T(8,128)(2,1)S(1)}, bf16[4,8,8448]{2,1,0:T(8,128)(2,1)S(1)}, u32[]{:S(2)}, u32[]{:S(2)}) %collective-permute-start.12) | collective-permute-done | bytes 540704 | tf_op jit(solution)/shard_map/ppermute | solution.py:267
  46.2 1.6 %collective-permute-start.13 = (bf16[4,24,3136]{2,1,0:T(8,128)(2,1)S(1)}, bf16[4,24,3136]{2,1,0:T(8,128)(2,1)S(1)}, u32[]{:S(2)}, u32[]{:S(2)}) collective-permute-start(bf16[4,24,3136]{2,1,0:T(8,128)(2,1)S(1)} %fusion.1), channel_id=1, source_target_pairs={{0,16},{8,24},{16,0},{24,8},{32,48},{40,56},{48,32},{56,40},{64,80... | collective-permute-start | bytes 1806344 | tf_op jit(solution)/shard_map/ppermute | solution.py:267
  48.0 2.4 %collective-permute-done.2 = bf16[48,5568]{1,0:T(8,128)(2,1)S(1)} collective-permute-done((bf16[48,5568]{1,0:T(8,128)(2,1)S(1)}, bf16[48,5568]{1,0:T(8,128)(2,1)S(1)}, u32[]{:S(2)}, u32[]{:S(2)}) %collective-permute-start.2) | collective-permute-done | bytes 534560 | tf_op jit(solution)/shard_map/ppermute | solution.py:267
  50.4 8.8 %collective-permute-done.3 = bf16[48,5568]{1,0:T(8,128)(2,1)S(1)} collective-permute-done((bf16[48,5568]{1,0:T(8,128)(2,1)S(1)}, bf16[48,5568]{1,0:T(8,128)(2,1)S(1)}, u32[]{:S(2)}, u32[]{:S(2)}) %collective-permute-start.3) | collective-permute-done | bytes 534560 | tf_op jit(solution)/shard_map/ppermute | solution.py:267
  59.9 1.3 collective-permute-done.13
  61.7 3.5 %collective-permute-start.16 = (bf16[24,3136]{1,0:T(8,128)(2,1)S(1)}, bf16[24,3136]{1,0:T(8,128)(2,1)S(1)}, u32[]{:S(2)}, u32[]{:S(2)}) collective-permute-start(bf16[24,3136]{1,0:T(8,128)(2,1)S(1)} %get-tuple-element.138), channel_id=1, source_target_pairs={{0,96},{8,104},{16,112},{24,120},{32,0},{40,8},{48,16},{56,24},{64... | collective-permute-start | bytes 451592 | tf_op jit(solution)/shard_map/ppermute | solution.py:267
  65.5 1.6 %collective-permute-start.14 = (bf16[24,5568]{1,0:T(8,128)(2,1)S(1)}, bf16[24,5568]{1,0:T(8,128)(2,1)S(1)}, u32[]{:S(2)}, u32[]{:S(2)}) collective-permute-start(bf16[24,5568]{1,0:T(8,128)(2,1)S(1)} %slice.177), channel_id=1, source_target_pairs={{0,16},{8,24},{16,0},{24,8},{32,48},{40,56},{48,32},{56,40},{64,80... | collective-permute-start | bytes 801800 | tf_op jit(solution)/shard_map/ppermute | solution.py:267
  67.1 1.8 %collective-permute-done.17.c_ref = bf16[24,3136]{1,0:T(8,128)(2,1)S(1)} collective-permute-done((bf16[24,3136]{1,0:T(8,128)(2,1)S(1)}, bf16[24,3136]{1,0:T(8,128)(2,1)S(1)}, u32[]{:S(2)}, u32[]{:S(2)}) %collective-permute-start.17) | collective-permute-done | bytes 150560 | tf_op jit(solution)/shard_map/ppermute | solution.py:267
  69.1 2.6 %collective-permute-done.15.a_ref = bf16[24,3136]{1,0:T(8,128)(2,1)S(1)} collective-permute-done((bf16[24,3136]{1,0:T(8,128)(2,1)S(1)}, bf16[24,3136]{1,0:T(8,128)(2,1)S(1)}, u32[]{:S(2)}, u32[]{:S(2)}) %collective-permute-start.15) | collective-permute-done | bytes 150560 | tf_op jit(solution)/shard_map/ppermute | solution.py:267
  72.7 1.6 %collective-permute-start.19 = (bf16[24,5568]{1,0:T(8,128)(2,1)S(1)}, bf16[24,5568]{1,0:T(8,128)(2,1)S(1)}, u32[]{:S(2)}, u32[]{:S(2)}) collective-permute-start(bf16[24,5568]{1,0:T(8,128)(2,1)S(1)} %get-tuple-element.111), channel_id=1, source_target_pairs={{0,16},{8,24},{16,0},{24,8},{32,48},{40,56},{48,32},{56,40},{64,80... | collective-permute-start | bytes 801800 | tf_op jit(solution)/shard_map/ppermute | solution.py:267
  74.3 4.9 %collective-permute-start.21 = (bf16[24,2752]{1,0:T(8,128)(2,1)S(1)}, bf16[24,2752]{1,0:T(8,128)(2,1)S(1)}, u32[]{:S(2)}, u32[]{:S(2)}) collective-permute-start(bf16[24,2752]{1,0:T(8,128)(2,1)S(1)} %get-tuple-element.110), channel_id=1, source_target_pairs={{0,64},{8,72},{16,80},{24,88},{32,96},{40,104},{48,112},{56,120},{... | collective-permute-start | bytes 396296 | tf_op jit(solution)/shard_map/ppermute | solution.py:267
  79.2 1.5 %collective-permute-done.22 = bf16[24,2752]{1,0:T(8,128)(2,1)S(1)} collective-permute-done((bf16[24,2752]{1,0:T(8,128)(2,1)S(1)}, bf16[24,2752]{1,0:T(8,128)(2,1)S(1)}, u32[]{:S(2)}, u32[]{:S(2)}) %collective-permute-start.22) | collective-permute-done | bytes 132128 | tf_op jit(solution)/shard_map/ppermute | solution.py:267
  80.7 3.0 %collective-permute-done.21 = bf16[24,2752]{1,0:T(8,128)(2,1)S(1)} collective-permute-done((bf16[24,2752]{1,0:T(8,128)(2,1)S(1)}, bf16[24,2752]{1,0:T(8,128)(2,1)S(1)}, u32[]{:S(2)}, u32[]{:S(2)}) %collective-permute-start.21) | collective-permute-done | bytes 132128 | tf_op jit(solution)/shard_map/ppermute | solution.py:267
  83.7 1.1 collective-permute-done.20
  84.9 2.4 %collective-permute-start.25 = (bf16[2,24,5568]{2,1,0:T(8,128)(2,1)S(1)}, bf16[2,24,5568]{2,1,0:T(8,128)(2,1)S(1)}, u32[]{:S(2)}, u32[]{:S(2)}) collective-permute-start(bf16[2,24,5568]{2,1,0:T(8,128)(2,1)S(1)} %get-tuple-element.143), channel_id=1, source_target_pairs={{0,64},{8,72},{16,80},{24,88},{32,96},{40,104},{48,112},{56,120},{... | collective-permute-start | bytes 1603592 | tf_op jit(solution)/shard_map/ppermute | solution.py:267
  87.3 2.5 %collective-permute-start.24 = (bf16[2,24,5568]{2,1,0:T(8,128)(2,1)S(1)}, bf16[2,24,5568]{2,1,0:T(8,128)(2,1)S(1)}, u32[]{:S(2)}, u32[]{:S(2)}) collective-permute-start(bf16[2,24,5568]{2,1,0:T(8,128)(2,1)S(1)} %get-tuple-element.143), channel_id=1, source_target_pairs={{0,96},{8,104},{16,112},{24,120},{32,0},{40,8},{48,16},{56,24},{64... | collective-permute-start | bytes 1603592 | tf_op jit(solution)/shard_map/ppermute | solution.py:267
  90.6 8.8 %collective-permute-done.23 = bf16[4,24,2752]{2,1,0:T(8,128)(2,1)S(1)} collective-permute-done((bf16[4,24,2752]{2,1,0:T(8,128)(2,1)S(1)}, bf16[4,24,2752]{2,1,0:T(8,128)(2,1)S(1)}, u32[]{:S(2)}, u32[]{:S(2)}) %collective-permute-start.23) | collective-permute-done | bytes 528416 | tf_op jit(solution)/shard_map/ppermute | solution.py:267
  99.4 7.7 %collective-permute-done.26 = bf16[2,24,5568]{2,1,0:T(8,128)(2,1)S(1)} collective-permute-done((bf16[2,24,5568]{2,1,0:T(8,128)(2,1)S(1)}, bf16[2,24,5568]{2,1,0:T(8,128)(2,1)S(1)}, u32[]{:S(2)}, u32[]{:S(2)}) %collective-permute-start.26) | collective-permute-done | bytes 534560 | tf_op jit(solution)/shard_map/ppermute | solution.py:267
  108.0 2.4 %collective-permute-done.27.o_ref = bf16[192,2752]{1,0:T(8,128)(2,1)S(1)} collective-permute-done((bf16[192,2752]{1,0:T(8,128)(2,1)S(1)}, bf16[192,2752]{1,0:T(8,128)(2,1)S(1)}, u32[]{:S(2)}, u32[]{:S(2)}) %collective-permute-start.27) | collective-permute-done | bytes 1056800 | tf_op jit(solution)/shard_map/ppermute | solution.py:267
  110.5 1.0 fusion.43.i_ref
  111.5 2.5 %backward_hidden.1 = bf16[384,512]{1,0:T(8,128)(2,1)S(1)} custom-call(bf16[192,2752]{1,0:T(8,128)(2,1)S(1)} %bitcast.90, bf16[192,2752]{1,0:T(8,128)(2,1)S(1)} %collective-permute-done.27.o_ref, bf16[64,8448]{1,0:T(8,128)(2,1)S(1)} %bitcast.85, bf16[64,8448]{1,0:T(8,128)(2,1)S(1)} %collective-permute-done.18.far_ref, ...), custom_call_target="tpu_custom_call" | custom-call | tf_op jit(solution)/shard_map/backward_hidden/pallas_call | solution.py:46
  114.1 2.8 %collective-permute-start.29 = (bf16[4,48,512]{2,1,0:T(8,128)(2,1)S(1)}, bf16[4,48,512]{2,1,0:T(8,128)(2,1)S(1)}, u32[]{:S(2)}, u32[]{:S(2)}) collective-permute-start(bf16[4,48,512]{2,1,0:T(8,128)(2,1)S(1)} %bitcast.110), channel_id=1, source_target_pairs={{0,4},{1,5},{2,6},{3,7},{4,0},{5,1},{6,2},{7,3},{8,12},{9,13},{10,... | collective-permute-start | bytes 589832 | tf_op jit(solution)/shard_map/ppermute | solution.py:275
  116.9 4.5 %backward_pair.1 = bf16[384,512]{1,0:T(8,128)(2,1)S(1)} custom-call(bf16[192,5568]{1,0:T(8,128)(2,1)S(1)} %bitcast.74, bf16[192,5568]{1,0:T(8,128)(2,1)S(1)} %collective-permute-done.28.o_ref, bf16[64,8448]{1,0:T(8,128)(2,1)S(1)} %bitcast.86, bf16[64,8448]{1,0:T(8,128)(2,1)S(1)} %collective-permute-done.18.far_ref, ...), custom_call_target="tpu_custom_call" | custom-call | tf_op jit(solution)/shard_map/backward_pair/pallas_call | solution.py:46
  121.4 1.1 collective-permute-start.30
  122.5 2.5 %weight_grad.4 = bf16[2752,512]{1,0:T(8,128)(2,1)} custom-call(bf16[192,2752]{1,0:T(8,128)(2,1)S(1)} %bitcast.91, bf16[192,2752]{1,0:T(8,128)(2,1)S(1)} %collective-permute-done.27.o_ref, bf16[384,512]{1,0:T(8,128)(2,1)S(1)} %get-tuple-element.89.o_ref.x_ref), custom_call_target="tpu_custom_call" | custom-call | tf_op jit(solution)/shard_map/weight_grad/pallas_call | solution.py:46
  125.0 2.5 %weight_grad.3 = bf16[2752,512]{1,0:T(8,128)(2,1)} custom-call(bf16[192,5568]{1,0:T(8,128)(2,1)S(1)} %bitcast.75, bf16[192,5568]{1,0:T(8,128)(2,1)S(1)} %collective-permute-done.28.o_ref, bf16[384,512]{1,0:T(8,128)(2,1)S(1)} %get-tuple-element.96.t_ref.x_ref), custom_call_target="tpu_custom_call" | custom-call | tf_op jit(solution)/shard_map/weight_grad/pallas_call | solution.py:46
  127.5 2.6 %collective-permute-done.30 = bf16[4,48,512]{2,1,0:T(8,128)(2,1)S(1)} collective-permute-done((bf16[4,48,512]{2,1,0:T(8,128)(2,1)S(1)}, bf16[4,48,512]{2,1,0:T(8,128)(2,1)S(1)}, u32[]{:S(2)}, u32[]{:S(2)}) %collective-permute-start.30) | collective-permute-done | bytes 196640 | tf_op jit(solution)/shard_map/ppermute | solution.py:275
  130.4 3.1 %collective-permute-start.32 = (bf16[2,48,512]{2,1,0:T(8,128)(2,1)S(1)}, bf16[2,48,512]{2,1,0:T(8,128)(2,1)S(1)}, u32[]{:S(2)}, u32[]{:S(2)}) collective-permute-start(bf16[2,48,512]{2,1,0:T(8,128)(2,1)S(1)} %get-tuple-element.130), channel_id=1, source_target_pairs={{0,3},{1,0},{2,1},{3,2},{4,7},{5,4},{6,5},{7,6},{8,11},{9,8},{10,9... | collective-permute-start | bytes 294920 | tf_op jit(solution)/shard_map/ppermute | solution.py:275
  133.8 2.5 %weight_grad.5 = bf16[2752,512]{1,0:T(8,128)(2,1)} custom-call(bf16[192,5568]{1,0:T(8,128)(2,1)S(1)} %bitcast.76, bf16[192,5568]{1,0:T(8,128)(2,1)S(1)} %collective-permute-done.28.o_ref, bf16[384,512]{1,0:T(8,128)(2,1)S(1)} %get-tuple-element.96.t_ref.x_ref), custom_call_target="tpu_custom_call" | custom-call | tf_op jit(solution)/shard_map/weight_grad/pallas_call | solution.py:46
  136.9 2.7 %collective-permute-done.33 = bf16[2,48,512]{2,1,0:T(8,128)(2,1)S(1)} collective-permute-done((bf16[2,48,512]{2,1,0:T(8,128)(2,1)S(1)}, bf16[2,48,512]{2,1,0:T(8,128)(2,1)S(1)}, u32[]{:S(2)}, u32[]{:S(2)}) %collective-permute-start.33) | collective-permute-done | bytes 98336 | tf_op jit(solution)/shard_map/ppermute | solution.py:275
  (80 shorter events, 9.6 us)
Async XLA Ops:
  0.6 6.5 %copy-start.6 = (bf16[384,512]{1,0:T(8,128)(2,1)S(1)}, bf16[384,512]{1,0:T(8,128)(2,1)}, u32[]{:S(2)}) copy-start(bf16[384,512]{1,0:T(8,128)(2,1)} %g_ref) | copy-start | bytes 1179652
  0.6 6.5 %copy-start.5 = (bf16[384,512]{1,0:T(8,128)(2,1)S(1)}, bf16[384,512]{1,0:T(8,128)(2,1)}, u32[]{:S(2)}) copy-start(bf16[384,512]{1,0:T(8,128)(2,1)} %t_ref) | copy-start | bytes 1179652
  1.5 5.6 %collective-permute-start = (bf16[48,512]{1,0:T(8,128)(2,1)S(1)}, bf16[48,512]{1,0:T(8,128)(2,1)S(1)}, u32[]{:S(2)}, u32[]{:S(2)}) collective-permute-start(bf16[48,512]{1,0:T(8,128)(2,1)S(1)} %pad_maximum_fusion.11), channel_id=1, source_target_pairs={{0,4},{1,5},{2,6},{3,7},{4,0},{5,1},{6,2},{7,3},{8,12},{9,13},{10,... | collective-permute-start | bytes 147464 | tf_op jit(solution)/shard_map/ppermute | solution.py:275
  7.1 1.8 %copy-start = (bf16[512,2752]{0,1:T(8,128)(2,1)S(1)}, bf16[512,2752]{0,1:T(8,128)(2,1)}, u32[]{:S(2)}) copy-start(bf16[512,2752]{0,1:T(8,128)(2,1)} %param.15) | copy-start | bytes 8454148
  8.9 1.8 %copy-start.2 = (bf16[512,2752]{0,1:T(8,128)(2,1)S(1)}, bf16[512,2752]{0,1:T(8,128)(2,1)}, u32[]{:S(2)}) copy-start(bf16[512,2752]{0,1:T(8,128)(2,1)} %param.13) | copy-start | bytes 8454148
  10.7 16.6 %copy-start.1 = (bf16[512,2752]{0,1:T(8,128)(2,1)S(1)}, bf16[512,2752]{0,1:T(8,128)(2,1)}, u32[]{:S(2)}) copy-start(bf16[512,2752]{0,1:T(8,128)(2,1)} %param.15) | copy-start | bytes 8454148
  13.3 14.1 %collective-permute-start.1 = (bf16[192,5568]{1,0:T(8,128)(2,1)S(1)}, bf16[192,5568]{1,0:T(8,128)(2,1)S(1)}, u32[]{:S(2)}, u32[]{:S(2)}) collective-permute-start(bf16[192,5568]{1,0:T(8,128)(2,1)S(1)} %get-tuple-element.90), channel_id=1, source_target_pairs={{0,8},{8,0},{16,24},{24,16},{32,40},{40,32},{48,56},{56,48},{64,72... | collective-permute-start | bytes 6414344 | tf_op jit(solution)/shard_map/ppermute | solution.py:267
  13.4 8.5 %collective-permute-start.6 = (bf16[2,48,512]{2,1,0:T(8,128)(2,1)S(1)}, bf16[2,48,512]{2,1,0:T(8,128)(2,1)S(1)}, u32[]{:S(2)}, u32[]{:S(2)}) collective-permute-start(bf16[2,48,512]{2,1,0:T(8,128)(2,1)S(1)} %get-tuple-element.161), channel_id=1, source_target_pairs={{0,2},{1,3},{2,0},{3,1},{4,6},{5,7},{6,4},{7,5},{8,10},{9,11},{10,... | collective-permute-start | bytes 294920 | tf_op jit(solution)/shard_map/ppermute | solution.py:275
  16.7 8.7 %collective-permute-start.5 = (bf16[2,48,512]{2,1,0:T(8,128)(2,1)S(1)}, bf16[2,48,512]{2,1,0:T(8,128)(2,1)S(1)}, u32[]{:S(2)}, u32[]{:S(2)}) collective-permute-start(bf16[2,48,512]{2,1,0:T(8,128)(2,1)S(1)} %get-tuple-element.161), channel_id=1, source_target_pairs={{0,1},{1,2},{2,3},{3,0},{4,5},{5,6},{6,7},{7,4},{8,9},{9,10},{10,1... | collective-permute-start | bytes 294920 | tf_op jit(solution)/shard_map/ppermute | solution.py:275
  17.4 9.5 %collective-permute-start.7 = (bf16[2,48,512]{2,1,0:T(8,128)(2,1)S(1)}, bf16[2,48,512]{2,1,0:T(8,128)(2,1)S(1)}, u32[]{:S(2)}, u32[]{:S(2)}) collective-permute-start(bf16[2,48,512]{2,1,0:T(8,128)(2,1)S(1)} %get-tuple-element.161), channel_id=1, source_target_pairs={{0,3},{1,0},{2,1},{3,2},{4,7},{5,4},{6,5},{7,6},{8,11},{9,8},{10,9... | collective-permute-start | bytes 294920 | tf_op jit(solution)/shard_map/ppermute | solution.py:275
  20.0 11.1 %collective-permute-start.11 = (bf16[8,8448]{1,0:T(8,128)(2,1)S(1)}, bf16[8,8448]{1,0:T(8,128)(2,1)S(1)}, u32[]{:S(2)}, u32[]{:S(2)}) collective-permute-start(bf16[8,8448]{1,0:T(8,128)(2,1)S(1)} %concatenate.6), channel_id=1, source_target_pairs={{0,32},{8,40},{16,48},{24,56},{32,64},{40,72},{48,80},{56,88},{64,... | collective-permute-start | bytes 405512 | tf_op jit(solution)/shard_map/ppermute | solution.py:267
  21.9 9.6 %collective-permute-start.10 = (bf16[8,8448]{1,0:T(8,128)(2,1)S(1)}, bf16[8,8448]{1,0:T(8,128)(2,1)S(1)}, u32[]{:S(2)}, u32[]{:S(2)}) collective-permute-start(bf16[8,8448]{1,0:T(8,128)(2,1)S(1)} %concatenate.6), channel_id=1, source_target_pairs={{0,64},{8,72},{16,80},{24,88},{32,96},{40,104},{48,112},{56,120},{... | collective-permute-start | bytes 405512 | tf_op jit(solution)/shard_map/ppermute | solution.py:267
  25.5 6.0 %collective-permute-start.9 = (bf16[8,8448]{1,0:T(8,128)(2,1)S(1)}, bf16[8,8448]{1,0:T(8,128)(2,1)S(1)}, u32[]{:S(2)}, u32[]{:S(2)}) collective-permute-start(bf16[8,8448]{1,0:T(8,128)(2,1)S(1)} %concatenate.6), channel_id=1, source_target_pairs={{0,96},{8,104},{16,112},{24,120},{32,0},{40,8},{48,16},{56,24},{64... | collective-permute-start | bytes 405512 | tf_op jit(solution)/shard_map/ppermute | solution.py:267
  27.3 2.0 %copy-start.4 = (bf16[512,2752]{0,1:T(8,128)(2,1)S(1)}, bf16[512,2752]{0,1:T(8,128)(2,1)}, u32[]{:S(2)}) copy-start(bf16[512,2752]{0,1:T(8,128)(2,1)} %param.14) | copy-start | bytes 8454148
  30.9 15.0 %collective-permute-start.8 = (bf16[192,3136]{1,0:T(8,128)(2,1)S(1)}, bf16[192,3136]{1,0:T(8,128)(2,1)S(1)}, u32[]{:S(2)}, u32[]{:S(2)}) collective-permute-start(bf16[192,3136]{1,0:T(8,128)(2,1)S(1)} %get-tuple-element.101), channel_id=1, source_target_pairs={{0,8},{8,0},{16,24},{24,16},{32,40},{40,32},{48,56},{56,48},{64,72... | collective-permute-start | bytes 3612680 | tf_op jit(solution)/shard_map/ppermute | solution.py:267
  31.6 14.3 %collective-permute-start.12 = (bf16[4,8,8448]{2,1,0:T(8,128)(2,1)S(1)}, bf16[4,8,8448]{2,1,0:T(8,128)(2,1)S(1)}, u32[]{:S(2)}, u32[]{:S(2)}) collective-permute-start(bf16[4,8,8448]{2,1,0:T(8,128)(2,1)S(1)} %get-tuple-element.147), channel_id=1, source_target_pairs={{0,16},{8,24},{16,0},{24,8},{32,48},{40,56},{48,32},{56,40},{64,80... | collective-permute-start | bytes 1622024 | tf_op jit(solution)/shard_map/ppermute | solution.py:267
  33.1 17.2 %collective-permute-start.2 = (bf16[48,5568]{1,0:T(8,128)(2,1)S(1)}, bf16[48,5568]{1,0:T(8,128)(2,1)S(1)}, u32[]{:S(2)}, u32[]{:S(2)}) collective-permute-start(bf16[48,5568]{1,0:T(8,128)(2,1)S(1)} %get-tuple-element.93), channel_id=1, source_target_pairs={{0,32},{8,40},{16,48},{24,56},{32,64},{40,72},{48,80},{56,88},{64,... | collective-permute-start | bytes 1603592 | tf_op jit(solution)/shard_map/ppermute | solution.py:267
  34.6 24.6 %collective-permute-start.3 = (bf16[48,5568]{1,0:T(8,128)(2,1)S(1)}, bf16[48,5568]{1,0:T(8,128)(2,1)S(1)}, u32[]{:S(2)}, u32[]{:S(2)}) collective-permute-start(bf16[48,5568]{1,0:T(8,128)(2,1)S(1)} %get-tuple-element.94), channel_id=1, source_target_pairs={{0,96},{8,104},{16,112},{24,120},{32,0},{40,8},{48,16},{56,24},{64... | collective-permute-start | bytes 1603592 | tf_op jit(solution)/shard_map/ppermute | solution.py:267
  36.4 23.5 %collective-permute-start.4 = (bf16[48,5568]{1,0:T(8,128)(2,1)S(1)}, bf16[48,5568]{1,0:T(8,128)(2,1)S(1)}, u32[]{:S(2)}, u32[]{:S(2)}) collective-permute-start(bf16[48,5568]{1,0:T(8,128)(2,1)S(1)} %get-tuple-element.95), channel_id=1, source_target_pairs={{0,64},{8,72},{16,80},{24,88},{32,96},{40,104},{48,112},{56,120},{... | collective-permute-start | bytes 1603592 | tf_op jit(solution)/shard_map/ppermute | solution.py:267
  46.2 15.1 %collective-permute-start.13 = (bf16[4,24,3136]{2,1,0:T(8,128)(2,1)S(1)}, bf16[4,24,3136]{2,1,0:T(8,128)(2,1)S(1)}, u32[]{:S(2)}, u32[]{:S(2)}) collective-permute-start(bf16[4,24,3136]{2,1,0:T(8,128)(2,1)S(1)} %fusion.1), channel_id=1, source_target_pairs={{0,16},{8,24},{16,0},{24,8},{32,48},{40,56},{48,32},{56,40},{64,80... | collective-permute-start | bytes 1806344 | tf_op jit(solution)/shard_map/ppermute | solution.py:267
  47.9 24.1 %collective-permute-start.18 = (bf16[64,8448]{1,0:T(8,128)(2,1)S(1)}, bf16[64,8448]{1,0:T(8,128)(2,1)S(1)}, u32[]{:S(2)}, u32[]{:S(2)}) collective-permute-start(bf16[64,8448]{1,0:T(8,128)(2,1)S(1)} %bitcast.83), channel_id=1, source_target_pairs={{0,8},{8,0},{16,24},{24,16},{32,40},{40,32},{48,56},{56,48},{64,72... | collective-permute-start | bytes 3244040 | tf_op jit(solution)/shard_map/ppermute | solution.py:267
  61.4 7.5 %collective-permute-start.17 = (bf16[24,3136]{1,0:T(8,128)(2,1)S(1)}, bf16[24,3136]{1,0:T(8,128)(2,1)S(1)}, u32[]{:S(2)}, u32[]{:S(2)}) collective-permute-start(bf16[24,3136]{1,0:T(8,128)(2,1)S(1)} %get-tuple-element.137), channel_id=1, source_target_pairs={{0,64},{8,72},{16,80},{24,88},{32,96},{40,104},{48,112},{56,120},{... | collective-permute-start | bytes 451592 | tf_op jit(solution)/shard_map/ppermute | solution.py:267
  61.7 7.3 %collective-permute-start.16 = (bf16[24,3136]{1,0:T(8,128)(2,1)S(1)}, bf16[24,3136]{1,0:T(8,128)(2,1)S(1)}, u32[]{:S(2)}, u32[]{:S(2)}) collective-permute-start(bf16[24,3136]{1,0:T(8,128)(2,1)S(1)} %get-tuple-element.138), channel_id=1, source_target_pairs={{0,96},{8,104},{16,112},{24,120},{32,0},{40,8},{48,16},{56,24},{64... | collective-permute-start | bytes 451592 | tf_op jit(solution)/shard_map/ppermute | solution.py:267
  65.2 6.4 %collective-permute-start.15 = (bf16[24,3136]{1,0:T(8,128)(2,1)S(1)}, bf16[24,3136]{1,0:T(8,128)(2,1)S(1)}, u32[]{:S(2)}, u32[]{:S(2)}) collective-permute-start(bf16[24,3136]{1,0:T(8,128)(2,1)S(1)} %get-tuple-element.139), channel_id=1, source_target_pairs={{0,32},{8,40},{16,48},{24,56},{32,64},{40,72},{48,80},{56,88},{64,... | collective-permute-start | bytes 451592 | tf_op jit(solution)/shard_map/ppermute | solution.py:267
  65.5 6.5 %collective-permute-start.14 = (bf16[24,5568]{1,0:T(8,128)(2,1)S(1)}, bf16[24,5568]{1,0:T(8,128)(2,1)S(1)}, u32[]{:S(2)}, u32[]{:S(2)}) collective-permute-start(bf16[24,5568]{1,0:T(8,128)(2,1)S(1)} %slice.177), channel_id=1, source_target_pairs={{0,16},{8,24},{16,0},{24,8},{32,48},{40,56},{48,32},{56,40},{64,80... | collective-permute-start | bytes 801800 | tf_op jit(solution)/shard_map/ppermute | solution.py:267
  72.7 12.1 %collective-permute-start.19 = (bf16[24,5568]{1,0:T(8,128)(2,1)S(1)}, bf16[24,5568]{1,0:T(8,128)(2,1)S(1)}, u32[]{:S(2)}, u32[]{:S(2)}) collective-permute-start(bf16[24,5568]{1,0:T(8,128)(2,1)S(1)} %get-tuple-element.111), channel_id=1, source_target_pairs={{0,16},{8,24},{16,0},{24,8},{32,48},{40,56},{48,32},{56,40},{64,80... | collective-permute-start | bytes 801800 | tf_op jit(solution)/shard_map/ppermute | solution.py:267
  74.2 6.4 %collective-permute-start.22 = (bf16[24,2752]{1,0:T(8,128)(2,1)S(1)}, bf16[24,2752]{1,0:T(8,128)(2,1)S(1)}, u32[]{:S(2)}, u32[]{:S(2)}) collective-permute-start(bf16[24,2752]{1,0:T(8,128)(2,1)S(1)} %get-tuple-element.110), channel_id=1, source_target_pairs={{0,32},{8,40},{16,48},{24,56},{32,64},{40,72},{48,80},{56,88},{64,... | collective-permute-start | bytes 396296 | tf_op jit(solution)/shard_map/ppermute | solution.py:267
  74.3 9.4 %collective-permute-start.21 = (bf16[24,2752]{1,0:T(8,128)(2,1)S(1)}, bf16[24,2752]{1,0:T(8,128)(2,1)S(1)}, u32[]{:S(2)}, u32[]{:S(2)}) collective-permute-start(bf16[24,2752]{1,0:T(8,128)(2,1)S(1)} %get-tuple-element.110), channel_id=1, source_target_pairs={{0,64},{8,72},{16,80},{24,88},{32,96},{40,104},{48,112},{56,120},{... | collective-permute-start | bytes 396296 | tf_op jit(solution)/shard_map/ppermute | solution.py:267
  79.2 5.6 %collective-permute-start.20 = (bf16[24,2752]{1,0:T(8,128)(2,1)S(1)}, bf16[24,2752]{1,0:T(8,128)(2,1)S(1)}, u32[]{:S(2)}, u32[]{:S(2)}) collective-permute-start(bf16[24,2752]{1,0:T(8,128)(2,1)S(1)} %get-tuple-element.110), channel_id=1, source_target_pairs={{0,96},{8,104},{16,112},{24,120},{32,0},{40,8},{48,16},{56,24},{64... | collective-permute-start | bytes 396296 | tf_op jit(solution)/shard_map/ppermute | solution.py:267
  84.9 22.2 %collective-permute-start.26 = (bf16[2,24,5568]{2,1,0:T(8,128)(2,1)S(1)}, bf16[2,24,5568]{2,1,0:T(8,128)(2,1)S(1)}, u32[]{:S(2)}, u32[]{:S(2)}) collective-permute-start(bf16[2,24,5568]{2,1,0:T(8,128)(2,1)S(1)} %get-tuple-element.143), channel_id=1, source_target_pairs={{0,32},{8,40},{16,48},{24,56},{32,64},{40,72},{48,80},{56,88},{64,... | collective-permute-start | bytes 1603592 | tf_op jit(solution)/shard_map/ppermute | solution.py:267
  84.9 22.1 %collective-permute-start.25 = (bf16[2,24,5568]{2,1,0:T(8,128)(2,1)S(1)}, bf16[2,24,5568]{2,1,0:T(8,128)(2,1)S(1)}, u32[]{:S(2)}, u32[]{:S(2)}) collective-permute-start(bf16[2,24,5568]{2,1,0:T(8,128)(2,1)S(1)} %get-tuple-element.143), channel_id=1, source_target_pairs={{0,64},{8,72},{16,80},{24,88},{32,96},{40,104},{48,112},{56,120},{... | collective-permute-start | bytes 1603592 | tf_op jit(solution)/shard_map/ppermute | solution.py:267
  87.3 20.1 %collective-permute-start.24 = (bf16[2,24,5568]{2,1,0:T(8,128)(2,1)S(1)}, bf16[2,24,5568]{2,1,0:T(8,128)(2,1)S(1)}, u32[]{:S(2)}, u32[]{:S(2)}) collective-permute-start(bf16[2,24,5568]{2,1,0:T(8,128)(2,1)S(1)} %get-tuple-element.143), channel_id=1, source_target_pairs={{0,96},{8,104},{16,112},{24,120},{32,0},{40,8},{48,16},{56,24},{64... | collective-permute-start | bytes 1603592 | tf_op jit(solution)/shard_map/ppermute | solution.py:267
  90.0 9.4 %collective-permute-start.23 = (bf16[4,24,2752]{2,1,0:T(8,128)(2,1)S(1)}, bf16[4,24,2752]{2,1,0:T(8,128)(2,1)S(1)}, u32[]{:S(2)}, u32[]{:S(2)}) collective-permute-start(bf16[4,24,2752]{2,1,0:T(8,128)(2,1)S(1)} %get-tuple-element.145), channel_id=1, source_target_pairs={{0,16},{8,24},{16,0},{24,8},{32,48},{40,56},{48,32},{56,40},{64,80... | collective-permute-start | bytes 1585160 | tf_op jit(solution)/shard_map/ppermute | solution.py:267
  107.6 2.8 %collective-permute-start.27 = (bf16[192,2752]{1,0:T(8,128)(2,1)S(1)}, bf16[192,2752]{1,0:T(8,128)(2,1)S(1)}, u32[]{:S(2)}, u32[]{:S(2)}) collective-permute-start(bf16[192,2752]{1,0:T(8,128)(2,1)S(1)} %bitcast.89), channel_id=1, source_target_pairs={{0,8},{8,0},{16,24},{24,16},{32,40},{40,32},{48,56},{56,48},{64,72... | collective-permute-start | bytes 3170312 | tf_op jit(solution)/shard_map/ppermute | solution.py:267
  110.4 6.5 %collective-permute-start.28 = (bf16[192,5568]{1,0:T(8,128)(2,1)S(1)}, bf16[192,5568]{1,0:T(8,128)(2,1)S(1)}, u32[]{:S(2)}, u32[]{:S(2)}) collective-permute-start(bf16[192,5568]{1,0:T(8,128)(2,1)S(1)} %bitcast.73), channel_id=1, source_target_pairs={{0,8},{8,0},{16,24},{24,16},{32,40},{40,32},{48,56},{56,48},{64,72... | collective-permute-start | bytes 6414344 | tf_op jit(solution)/shard_map/ppermute | solution.py:267
  111.5 5.3 %copy-start.3 = (bf16[512,2752]{0,1:T(8,128)(2,1)S(1)}, bf16[512,2752]{0,1:T(8,128)(2,1)}, u32[]{:S(2)}) copy-start(bf16[512,2752]{0,1:T(8,128)(2,1)} %param.13) | copy-start | bytes 8454148
  114.1 13.4 %collective-permute-start.29 = (bf16[4,48,512]{2,1,0:T(8,128)(2,1)S(1)}, bf16[4,48,512]{2,1,0:T(8,128)(2,1)S(1)}, u32[]{:S(2)}, u32[]{:S(2)}) collective-permute-start(bf16[4,48,512]{2,1,0:T(8,128)(2,1)S(1)} %bitcast.110), channel_id=1, source_target_pairs={{0,4},{1,5},{2,6},{3,7},{4,0},{5,1},{6,2},{7,3},{8,12},{9,13},{10,... | collective-permute-start | bytes 589832 | tf_op jit(solution)/shard_map/ppermute | solution.py:275
  121.4 8.7 %collective-permute-start.30 = (bf16[4,48,512]{2,1,0:T(8,128)(2,1)S(1)}, bf16[4,48,512]{2,1,0:T(8,128)(2,1)S(1)}, u32[]{:S(2)}, u32[]{:S(2)}) collective-permute-start(bf16[4,48,512]{2,1,0:T(8,128)(2,1)S(1)} %bitcast.111), channel_id=1, source_target_pairs={{0,4},{1,5},{2,6},{3,7},{4,0},{5,1},{6,2},{7,3},{8,12},{9,13},{10,... | collective-permute-start | bytes 589832 | tf_op jit(solution)/shard_map/ppermute | solution.py:275
  130.2 6.1 %collective-permute-start.31 = (bf16[2,48,512]{2,1,0:T(8,128)(2,1)S(1)}, bf16[2,48,512]{2,1,0:T(8,128)(2,1)S(1)}, u32[]{:S(2)}, u32[]{:S(2)}) collective-permute-start(bf16[2,48,512]{2,1,0:T(8,128)(2,1)S(1)} %get-tuple-element.129), channel_id=1, source_target_pairs={{0,1},{1,2},{2,3},{3,0},{4,5},{5,6},{6,7},{7,4},{8,9},{9,10},{10,1... | collective-permute-start | bytes 294920 | tf_op jit(solution)/shard_map/ppermute | solution.py:275
  130.4 6.5 %collective-permute-start.32 = (bf16[2,48,512]{2,1,0:T(8,128)(2,1)S(1)}, bf16[2,48,512]{2,1,0:T(8,128)(2,1)S(1)}, u32[]{:S(2)}, u32[]{:S(2)}) collective-permute-start(bf16[2,48,512]{2,1,0:T(8,128)(2,1)S(1)} %get-tuple-element.130), channel_id=1, source_target_pairs={{0,3},{1,0},{2,1},{3,2},{4,7},{5,4},{6,5},{7,6},{8,11},{9,8},{10,9... | collective-permute-start | bytes 294920 | tf_op jit(solution)/shard_map/ppermute | solution.py:275
  133.5 6.1 %collective-permute-start.33 = (bf16[2,48,512]{2,1,0:T(8,128)(2,1)S(1)}, bf16[2,48,512]{2,1,0:T(8,128)(2,1)S(1)}, u32[]{:S(2)}, u32[]{:S(2)}) collective-permute-start(bf16[2,48,512]{2,1,0:T(8,128)(2,1)S(1)} %pad_maximum_fusion.10), channel_id=1, source_target_pairs={{0,2},{1,3},{2,0},{3,1},{4,6},{5,7},{6,4},{7,5},{8,10},{9,11},{10,... | collective-permute-start | bytes 294920 | tf_op jit(solution)/shard_map/ppermute | solution.py:275
